TPU v7x, 32 devices: a whole 2x2x4 slice. The times are simulated.
32 devices in a mesh: gx: 4 (over y, x), gy: 4 (over z), gz: 2 (over core).
Axes of the slice: x: 2, y: 2, z: 4, core: 2. Of those that a mesh axis runs over, the one named last changes fastest.
Arguments:
- fields: float32 [4, 256, 256, 256], P(None, 'gx', 'gy', 'gz'), may hold values from -6 to 6
- sources: bfloat16 [4, 256, 256, 256], P(None, 'gx', 'gy', 'gz'), may hold values from -6 to 6
- material: int32 [256, 256, 256], P('gx', 'gy', 'gz'), may hold values from 0 to 3
- shift_real: float32 [4], replicated, may hold values from -2 to -0.5
- shift_imag: float32 [4], replicated, may hold values from 0.5 to 2
- design_share: float32 [4], replicated, may hold values from 0.2 to 1
- density: float32 [256, 256], P('gx', 'gy'), may hold values from 0 to 1
- owner_map: int32 [4, 4, 64, 1], P('gx', 'gy'), may hold values from 0 to 15; in each aligned block of 64 rows (0 to 63, 64 to 127, ..., all dimensions but the last counted through in order) at most 8 rows name the same one
Outputs:
- fields_out: float32 [4, 256, 256, 256], P(None, 'gx', 'gy', 'gz')
- owner_gradient: float32 [16, 16, 512], P(('gx', 'gy'))
Inputs may be any that keep to these rules, and one draw needn't show every extreme that they name: `owner_map`: within the 64 tiles of one column (aligned blocks of the map's rows), no owner is named more than 8 times, and in some column some owner is named exactly 8 times.
All inputs are finite; a program needn't handle non-finite values.
Results may differ from a plain program's by a relative error of at most 0.0003.
Values may be sent and summed in bfloat16 or wider, within the bound.
No kernel may reach another device: no remote copies, remote signals or barrier semaphores. Data moves between devices by JAX's collectives and lax.ppermute only.
A program may use at most 320 MiB of HBM per device.

v0:
```python
import math

import jax
import jax.numpy as jnp
from jax import lax
from jax.sharding import PartitionSpec as P

R = 8
TS = 8
MOST = 8


RELAXATION = 0.8
SHARPNESS = 8.0
THRESHOLD = 0.5


def extended(array, sides, width):
    for axis, dim in sides:
        count, length = (lax.axis_size(axis), array.shape[dim])
        up = [(i, (i + 1) % count) for i in range(count - 1)]
        down = [(j, i) for i, j in up]
        last = lax.slice_in_dim(array, length - width, length, axis=dim)
        leading = lax.slice_in_dim(array, 0, width, axis=dim)
        before = lax.ppermute(last, axis, up)
        after = lax.ppermute(leading, axis, down)
        array = jnp.concatenate([before, array, after], axis=dim)
    return array


def lookup(material, level_table):
    result = jnp.zeros(material.shape, jnp.float32)
    for level_index in range(level_table.shape[0]):
        result = result + jnp.where(
            material == level_index, level_table[level_index], jnp.float32(0.0)
        )
    return result


def coef_fields(material, shift_real, shift_imag):
    diag_real = 6.0 + shift_real
    magnitude = diag_real * diag_real + shift_imag * shift_imag
    return (
        lookup(material, diag_real),
        lookup(material, shift_imag),
        lookup(material, diag_real / magnitude),
        lookup(material, -shift_imag / magnitude),
    )


def sweep_box(padded, source, coefficients):
    diag_real, diag_imag, inverse_real, inverse_imag = coefficients
    center = padded[:, 1:-1, 1:-1, 1:-1]
    beside = (
        padded[:, 2:, 1:-1, 1:-1]
        + padded[:, :-2, 1:-1, 1:-1]
        + padded[:, 1:-1, 2:, 1:-1]
        + padded[:, 1:-1, :-2, 1:-1]
        + padded[:, 1:-1, 1:-1, 2:]
        + padded[:, 1:-1, 1:-1, :-2]
    )
    real_part = center[0::2]
    imag_part = center[1::2]
    applied_real = diag_real * real_part - diag_imag * imag_part - beside[0::2]
    applied_imag = diag_real * imag_part + diag_imag * real_part - beside[1::2]
    residual_real = source[0::2] - applied_real
    residual_imag = source[1::2] - applied_imag
    new_real = real_part + RELAXATION * (
        inverse_real * residual_real - inverse_imag * residual_imag
    )
    new_imag = imag_part + RELAXATION * (
        inverse_real * residual_imag + inverse_imag * residual_real
    )
    return jnp.stack([new_real[0], new_imag[0], new_real[1], new_imag[1]])


def band_matrix(cell_count):
    row_index = jnp.arange(cell_count)[:, None]
    col_index = jnp.arange(cell_count + 2 * R)[None, :]
    offset = jnp.abs(col_index - R - row_index)
    weight = jnp.maximum(R + 1 - offset, 0).astype(jnp.float32)
    return weight / float((R + 1) * (R + 1))


def filter_box(padded, band_rows, band_cols):
    partial_rows = jnp.dot(
        band_rows, padded, precision=lax.Precision.HIGHEST, preferred_element_type=jnp.float32
    )
    return jnp.dot(
        partial_rows,
        band_cols.T,
        precision=lax.Precision.HIGHEST,
        preferred_element_type=jnp.float32,
    )


def projection_slope(filtered):
    tangent = jnp.tanh(SHARPNESS * (filtered - THRESHOLD))
    scale_total = math.tanh(SHARPNESS * THRESHOLD) + math.tanh(SHARPNESS * (1.0 - THRESHOLD))
    return SHARPNESS * (1.0 - tangent * tangent) / scale_total


def select_matrix(route_list, owner_count):
    tile_count = route_list.shape[0]
    earlier = jnp.arange(tile_count)[None, :] < jnp.arange(tile_count)[:, None]
    same_owner = route_list[None, :] == route_list[:, None]
    rank_within = jnp.sum(jnp.where(same_owner & earlier, 1, 0), axis=1).astype(jnp.int32)
    slot_index = route_list * MOST + rank_within
    slot_range = jnp.arange(owner_count * MOST)
    return jnp.where(slot_range[:, None] == slot_index[None, :], 1.0, 0.0).astype(jnp.float32)


def on_device(fields, sources, material, shift_real, shift_imag, design_share, density, owner_map):
    rows_here, cols_here, depth_here = material.shape
    coefficients = coef_fields(material, shift_real, shift_imag)
    source = sources.astype(jnp.float32)
    current = fields
    for sweep_turn in range(2):
        padded = extended(current, (("gx", 1), ("gy", 2), ("gz", 3)), 1)
        current = sweep_box(padded, source, coefficients)
    share_field = lookup(material, design_share)
    product = current[0] * current[2] - current[1] * current[3]
    partial_value = jnp.sum(share_field * product, axis=2) / math.sqrt(
        depth_here * lax.axis_size("gz")
    )
    band_rows = band_matrix(rows_here)
    band_cols = band_matrix(cols_here)
    padded_density = extended(density, (("gx", 0), ("gy", 1)), R)
    filtered = filter_box(padded_density, band_rows, band_cols)
    weighted = projection_slope(filtered) * partial_value
    padded_weight = extended(weighted, (("gx", 0), ("gy", 1)), R)
    gradient = filter_box(padded_weight, band_rows, band_cols)
    tile_rows = gradient.reshape(rows_here // TS, TS, cols_here // TS, TS)
    tile_rows = jnp.transpose(tile_rows, (0, 2, 1, 3)).reshape(-1, TS * TS)
    owner_count = lax.axis_size("gx") * lax.axis_size("gy")
    selector = select_matrix(owner_map.reshape(-1), owner_count)
    packed = jnp.dot(
        selector, tile_rows, precision=lax.Precision.HIGHEST, preferred_element_type=jnp.float32
    )
    packed = packed.reshape(owner_count, MOST * TS * TS)
    received = lax.all_to_all(packed, ("gx", "gy"), split_axis=0, concat_axis=0, tiled=True)
    received = lax.psum(received, "gz")
    return (current, received[None])


def solution(mesh):
    placed = (
        P(None, "gx", "gy", "gz"),
        P(None, "gx", "gy", "gz"),
        P("gx", "gy", "gz"),
        P(),
        P(),
        P(),
        P("gx", "gy"),
        P("gx", "gy", None, None),
    )
    return jax.shard_map(
        on_device,
        mesh=mesh,
        in_specs=placed,
        out_specs=(P(None, "gx", "gy", "gz"), P(("gx", "gy"), None, None)),
        check_vma=False,
    )
```

profile of v0, /device:TPU:0, one launch (start us, length us, event | category | flops | bytes accessed | tf_op | source)
XLA Modules:
  0.0 366.0 jit_solution(4372399030370552370)
XLA Ops:
  1.6 1.3 collective-permute-start
  2.9 5.5 %collective-permute-start.1 = (f32[4,1,64,128]{3,2,1,0:T(8,128)S(1)}, f32[4,1,64,128]{3,2,1,0:T(8,128)S(1)}, u32[]{:S(2)}, u32[]{:S(2)}) collective-permute-start(f32[4,1,64,128]{3,2,1,0:T(8,128)S(1)} %get-tuple-element.29), channel_id=1, source_target_pairs={{0,8},{8,16},{16,24},{1,9},{9,17},{17,25},{2,10},{10,18},{18,26},{... | collective-permute-start | bytes 393224 | tf_op jit(solution)/shard_map/ppermute | solution.py:25
  8.4 1.3 fusion.84
  9.7 4.8 %collective-permute-start.12 = (f32[8,64]{1,0:T(8,128)S(1)}, f32[8,64]{1,0:T(8,128)S(1)}, u32[]{:S(2)}, u32[]{:S(2)}) collective-permute-start(f32[8,64]{1,0:T(8,128)S(1)} %get-tuple-element.51), channel_id=1, source_target_pairs={{0,8},{8,16},{16,24},{1,9},{9,17},{17,25},{2,10},{10,18},{18,26},{... | collective-permute-start | bytes 6152 | tf_op jit(solution)/shard_map/ppermute | solution.py:25
  14.5 1.3 collective-permute-start.13
  15.8 1.5 fusion.87
  18.6 8.0 %copy_convert_fusion = f32[4,64,64,128]{3,1,2,0:T(8,128)} fusion(bf16[4,64,64,128]{3,2,1,0:T(8,128)(2,1)} %param.9), kind=kLoop, calls=%fused_computation.66 | loop fusion | flops 2097152 | bytes 12582912 | tf_op jit(solution)/shard_map/convert_element_type | solution.py:116
  28.0 5.0 %select_add_fusion.3 = (f32[64,64,128]{2,0,1:T(8,128)S(1)}, pred[64,64,128]{2,0,1:T(8,128)(4,1)S(1)}, pred[64,64,128]{2,0,1:T(8,128)(4,1)S(1)}, pred[64,64,128]{2,0,1:T(8,128)(4,1)S(1)}, pred[64,64,128]{2,0,1:T(8,128)(4,1)S(1)}) fusion(f32[]{:T(128)} %bitcast.3, f32[]{:T(128)} %bitcast.2, f32[]{:T(128)} %bitcast.1, f32[]{:T(128)} %bitcast, ...), kind=kLoop, calls=%fused_computation.80 | loop fusion | flops 5767168 | bytes 6291472 | tf_op jit(solution)/shard_map/add | solution.py:34
  33.1 11.4 %select_add_fusion.2 = (f32[64,64,128]{2,0,1:T(8,128)}, f32[64,64,128]{2,0,1:T(8,128)}, f32[64,64,128]{2,0,1:T(8,128)}) fusion(pred[64,64,128]{2,0,1:T(8,128)(4,1)S(1)} %get-tuple-element.18, pred[64,64,128]{2,0,1:T(8,128)(4,1)S(1)} %get-tuple-element.17, pred[64,64,128]{2,0,1:T(8,128)(4,1)S(1)} %get-tuple-element.16, ...), kind=kLoop, calls=%fused_computation.79 | loop fusion | flops 11010048 | bytes 8388656 | tf_op jit(solution)/shard_map/add | solution.py:34
  45.0 4.9 %copy.71 = f32[4,64,64,128]{3,1,2,0:T(8,128)S(1)} copy(f32[4,64,64,128]{3,2,1,0:T(8,128)S(1)} %bitcast.46) | data formatting | bytes 16777216 | tf_op args[0]
  50.6 1.3 collective-permute-start.2
  51.9 14.7 %collective-permute-start.3 = (f32[4,66,1,128]{3,1,2,0:T(8,128)S(1)}, f32[4,66,1,128]{3,1,2,0:T(8,128)S(1)}, u32[]{:S(2)}, u32[]{:S(2)}) collective-permute-start(f32[4,66,1,128]{3,1,2,0:T(8,128)S(1)} %get-tuple-element.25), channel_id=1, source_target_pairs={{0,2},{2,4},{4,6},{1,3},{3,5},{5,7},{8,10},{10,12},{12,14},{9,11},... | collective-permute-start | bytes 405512 | tf_op jit(solution)/shard_map/ppermute | solution.py:25
  66.7 2.6 collective-permute-done.3
  69.3 2.2 pad_maximum_fusion.2
  71.6 7.7 %fusion.74 = (f32[4,66,66,1]{3,1,2,0:T(8,128)}, f32[4,66,66,1]{3,1,2,0:T(8,128)}) fusion(f32[4,66,66,128]{3,1,2,0:T(8,128)S(1)} %pad_maximum_fusion.2), kind=kLoop, calls=%fused_computation.172 | loop fusion | bytes 278784 | tf_op jit(solution)/shard_map/slice | solution.py:24
  79.3 6.9 %copy.87 = f32[4,66,66,1]{2,1,3,0:T(8,128)} copy(f32[4,66,66,1]{3,1,2,0:T(8,128)} %get-tuple-element.22) | data formatting | bytes 139392 | tf_op jit(solution)/shard_map/slice | solution.py:23
  86.3 1.9 collective-permute-start.5
  88.2 6.9 %copy.85 = f32[4,66,66,1]{2,1,3,0:T(8,128)} copy(f32[4,66,66,1]{3,1,2,0:T(8,128)} %get-tuple-element.21) | data formatting | bytes 139392 | tf_op jit(solution)/shard_map/slice | solution.py:24
  97.7 6.5 %copy.88 = f32[4,66,66,1]{3,1,2,0:T(8,128)} copy(f32[4,66,66,1]{2,1,3,0:T(8,128)} %collective-permute-done.5) | data formatting | bytes 139392 | tf_op jit(solution)/shard_map/ppermute | solution.py:25
  104.2 6.4 %copy.86 = f32[4,66,66,1]{3,1,2,0:T(8,128)} copy(f32[4,66,66,1]{2,1,3,0:T(8,128)} %collective-permute-done.4) | data formatting | bytes 139392 | tf_op jit(solution)/shard_map/ppermute | solution.py:26
  110.6 31.5 %fusion.5 = f32[4,64,64,128]{3,1,2,0:T(8,128)} fusion(f32[4,66,66,1]{3,1,2,0:T(8,128)} %copy.88, f32[4,66,1,128]{3,1,2,0:T(8,128)S(1)} %collective-permute-done.2, f32[4,66,1,128]{3,1,2,0:T(8,128)} %copy-done.17, f32[4,1,64,128]{3,1,2,0:T(1,128)S(1)} %bitcast.49, f32[4,64,64,128]{3,1,2,0:T(8,128)} %copy-done, f32[4,1,64,128]{3,1,2,0:T(1,128)S(1)} %bitcast.52, ...), kind=kLoop, calls=%fused_computation.42 | loop fusion | flops 48234496 | bytes 17449088 | tf_op jit(solution)/shard_map/add | solution.py:55
  142.0 16.2 %multiply_add_fusion.3 = (f32[2,64,64,128]{3,1,2,0:T(8,128)}, f32[2,64,64,128]{3,1,2,0:T(8,128)}, f32[2,64,64,128]{3,1,2,0:T(8,128)}) fusion(f32[4,64,64,128]{3,1,2,0:T(8,128)} %copy-done, f32[64,64,128]{2,0,1:T(8,128)S(1)} %copy-done.6, f32[64,64,128]{2,0,1:T(8,128)S(1)} %get-tuple-element.14, f32[4,64,64,128]{3,1,2,0:T(8,128)} %fusion.5, ...), kind=kLoop, calls=%fused_computation.72 | loop fusion | flops 15728640 | bytes 46137344 | tf_op jit(solution)/shard_map/add | solution.py:68
  158.2 8.7 %multiply_add_fusion.2 = f32[2,64,64,128]{3,1,2,0:T(8,128)} fusion(f32[2,64,64,128]{3,1,2,0:T(8,128)} %get-tuple-element.13, f32[2,64,64,128]{3,1,2,0:T(8,128)} %get-tuple-element.12, f32[4,64,64,128]{3,1,2,0:T(8,128)} %copy-done, f32[64,64,128]{2,0,1:T(8,128)S(1)} %copy-done.6, f32[64,64,128]{2,0,1:T(8,128)S(1)} %get-tuple-element.14), kind=kLoop, calls=%fused_computation.71 | loop fusion | flops 5242880 | bytes 20971520 | tf_op jit(solution)/shard_map/add | solution.py:71
  166.9 2.8 fusion.80
  173.5 5.2 %collective-permute-start.7 = (f32[4,1,64,128]{3,2,1,0:T(8,128)S(1)}, f32[4,1,64,128]{3,2,1,0:T(8,128)S(1)}, u32[]{:S(2)}, u32[]{:S(2)}) collective-permute-start(f32[4,1,64,128]{3,2,1,0:T(8,128)S(1)} %bitcast.61), channel_id=1, source_target_pairs={{0,8},{8,16},{16,24},{1,9},{9,17},{17,25},{2,10},{10,18},{18,26},{... | collective-permute-start | bytes 393224 | tf_op jit(solution)/shard_map/ppermute | solution.py:25
  180.1 5.0 %collective-permute-start.14 = (f32[80,8]{1,0:T(8,128)S(1)}, f32[80,8]{1,0:T(8,128)S(1)}, u32[]{:S(2)}, u32[]{:S(2)}) collective-permute-start(f32[80,8]{1,0:T(8,128)S(1)} %get-tuple-element.46), channel_id=1, source_target_pairs={{0,2},{2,4},{4,6},{1,3},{3,5},{5,7},{8,10},{10,12},{12,14},{9,11},... | collective-permute-start | bytes 7688 | tf_op jit(solution)/shard_map/ppermute | solution.py:25
  186.5 5.0 %collective-permute-start.9 = (f32[4,66,1,128]{3,1,2,0:T(8,128)S(1)}, f32[4,66,1,128]{3,1,2,0:T(8,128)S(1)}, u32[]{:S(2)}, u32[]{:S(2)}) collective-permute-start(f32[4,66,1,128]{3,1,2,0:T(8,128)S(1)} %get-tuple-element.23), channel_id=1, source_target_pairs={{0,2},{2,4},{4,6},{1,3},{3,5},{5,7},{8,10},{10,12},{12,14},{9,11},... | collective-permute-start | bytes 405512 | tf_op jit(solution)/shard_map/ppermute | solution.py:25
  193.6 1.7 collective-permute-done.9
  195.9 3.4 pad_maximum_fusion.3
  199.4 7.7 %fusion.73 = (f32[4,66,66,1]{3,1,2,0:T(8,128)}, f32[4,66,66,1]{3,1,2,0:T(8,128)}) fusion(f32[4,66,66,128]{3,1,2,0:T(8,128)S(1)} %pad_maximum_fusion.3), kind=kLoop, calls=%fused_computation.171 | loop fusion | bytes 278784 | tf_op jit(solution)/shard_map/slice | solution.py:24
  207.1 6.9 %copy.97 = f32[4,66,66,1]{2,1,3,0:T(8,128)} copy(f32[4,66,66,1]{3,1,2,0:T(8,128)} %get-tuple-element.20) | data formatting | bytes 139392 | tf_op jit(solution)/shard_map/slice | solution.py:23
  214.0 2.6 collective-permute-start.11
  216.6 6.9 %copy.95 = f32[4,66,66,1]{2,1,3,0:T(8,128)} copy(f32[4,66,66,1]{3,1,2,0:T(8,128)} %get-tuple-element.19) | data formatting | bytes 139392 | tf_op jit(solution)/shard_map/slice | solution.py:24
  224.8 17.6 %pad_maximum_fusion = (f32[4,66,66,129]{3,1,2,0:T(8,128)}, f32[4,66,66,129]{3,1,2,0:T(8,128)}) fusion(f32[1,64,64,128]{3,1,2,0:T(8,128)} %copy-done.2, f32[1,64,64,128]{3,1,2,0:T(8,128)S(1)} %get-tuple-element.39, f32[1,64,64,128]{3,1,2,0:T(8,128)} %copy-done.1), kind=kLoop, calls=%fused_computation | loop fusion | flops 8990784 | bytes 24273024 | tf_op jit(solution)/shard_map/stack | solution.py:74
  242.5 6.4 %copy.98 = f32[4,66,66,1]{3,1,2,0:T(8,128)} copy(f32[4,66,66,1]{2,1,3,0:T(8,128)} %collective-permute-done.11) | data formatting | bytes 139392 | tf_op jit(solution)/shard_map/ppermute | solution.py:25
  248.8 6.5 %copy.96 = f32[4,66,66,1]{3,1,2,0:T(8,128)} copy(f32[4,66,66,1]{2,1,3,0:T(8,128)} %collective-permute-done.10) | data formatting | bytes 139392 | tf_op jit(solution)/shard_map/ppermute | solution.py:26
  255.3 31.8 %fusion = f32[4,64,64,128]{3,1,2,0:T(8,128)} fusion(f32[4,66,66,1]{3,1,2,0:T(8,128)} %copy.98, f32[4,66,1,128]{3,1,2,0:T(8,128)S(1)} %collective-permute-done.8, f32[4,66,1,128]{3,1,2,0:T(8,128)} %copy-done.16, f32[4,1,64,128]{3,1,2,0:T(1,128)S(1)} %bitcast.55, f32[4,1,64,128]{3,1,2,0:T(1,128)S(1)} %bitcast.58, f32[1,64,64,128]{3,1,2,0:T(8,128)} %copy-done.8, ...), kind=kLoop, calls=%fused_computation.5 | loop fusion | flops 77594624 | bytes 34226304 | tf_op jit(solution)/shard_map/add | solution.py:55
  287.1 17.5 %multiply_add_fusion.1 = (f32[2,64,64,128]{3,1,2,0:T(8,128)}, f32[2,64,64,128]{3,1,2,0:T(8,128)}, f32[2,64,64,128]{3,1,2,0:T(8,128)}) fusion(f32[4,64,64,128]{3,1,2,0:T(8,128)} %copy-done.3, f32[64,64,128]{2,0,1:T(8,128)} %get-tuple-element.42, f32[64,64,128]{2,0,1:T(8,128)S(1)} %copy-done.5, f32[4,64,64,128]{3,1,2,0:T(8,128)} %fusion, ...), kind=kLoop, calls=%fused_computation.68 | loop fusion | flops 15728640 | bytes 46137344 | tf_op jit(solution)/shard_map/add | solution.py:68
  304.7 8.8 %multiply_add_fusion = f32[2,64,64,128]{3,1,2,0:T(8,128)} fusion(f32[2,64,64,128]{3,1,2,0:T(8,128)} %get-tuple-element.10, f32[2,64,64,128]{3,1,2,0:T(8,128)} %get-tuple-element.9, f32[4,64,64,128]{3,1,2,0:T(8,128)} %copy-done.3, f32[64,64,128]{2,0,1:T(8,128)S(1)} %copy-done.7, f32[64,64,128]{2,0,1:T(8,128)S(1)} %copy-done.5), kind=kLoop, calls=%fused_computation.67 | loop fusion | flops 5242880 | bytes 20971520 | tf_op jit(solution)/shard_map/add | solution.py:71
  313.5 7.4 %fusion.10 = f32[64,64]{0,1:T(8,128)S(1)} fusion(pred[64,64,128]{2,0,1:T(8,128)(4,1)S(1)} %copy-done.14, pred[64,64,128]{2,0,1:T(8,128)(4,1)S(1)} %copy-done.12, pred[64,64,128]{2,0,1:T(8,128)(4,1)S(1)} %get-tuple-element.16, pred[64,64,128]{2,0,1:T(8,128)(4,1)S(1)} %get-tuple-element.15, f32[]{:T(128)} %bitcast.30, f32[]{:T(128)} %bitcast.29, f32[]{:T(128)} %bitcast.28, ...), kind=kLoop, calls=%fused_computation.76 | loop fusion | flops 6287360 | bytes 10502160 | tf_op jit(solution)/shard_map/reduce_sum | solution.py:123
  322.6 5.1 %collective-permute-start.16 = (f32[8,64]{1,0:T(8,128)S(1)}, f32[8,64]{1,0:T(8,128)S(1)}, u32[]{:S(2)}, u32[]{:S(2)}) collective-permute-start(f32[8,64]{1,0:T(8,128)S(1)} %get-tuple-element.48), channel_id=1, source_target_pairs={{0,8},{8,16},{16,24},{1,9},{9,17},{17,25},{2,10},{10,18},{18,26},{... | collective-permute-start | bytes 6152 | tf_op jit(solution)/shard_map/ppermute | solution.py:25
  327.7 4.0 %fusion.78 = (f32[1,64,64,128]{3,1,2,0:T(8,128)S(1)}, f32[1,64,64,128]{3,1,2,0:T(8,128)}) fusion(f32[2,64,64,128]{3,1,2,0:T(8,128)} %multiply_add_fusion), kind=kLoop, calls=%fused_computation.176 | loop fusion | bytes 8388608 | tf_op jit(solution)/shard_map/slice | solution.py:74
  333.1 5.0 %collective-permute-start.18 = (f32[80,8]{1,0:T(8,128)S(1)}, f32[80,8]{1,0:T(8,128)S(1)}, u32[]{:S(2)}, u32[]{:S(2)}) collective-permute-start(f32[80,8]{1,0:T(8,128)S(1)} %get-tuple-element.44), channel_id=1, source_target_pairs={{0,2},{2,4},{4,6},{1,3},{3,5},{5,7},{8,10},{10,12},{12,14},{9,11},... | collective-permute-start | bytes 7688 | tf_op jit(solution)/shard_map/ppermute | solution.py:25
  338.2 2.3 fusion.77
  342.2 8.2 %all-to-all-start = ((f32[16,1,512]{2,1,0:T(1,128)}), f32[16,1,512]{2,1,0:T(1,128)S(1)}, u32[]{:S(2)}, u32[]{:S(2)}) async-start(f32[16,1,512]{2,1,0:T(1,128)} %all_to_all.11), calls=%async_computation | async-start | bytes 65536 | tf_op jit(solution)/shard_map/all_to_all | solution.py:141
  350.3 3.2 pad_maximum_fusion.55
  353.5 8.3 %copy.103 = f32[4,64,64,128]{3,2,1,0:T(8,128)} copy(f32[4,64,64,128]{3,1,2,0:T(8,128)S(1)} %pad_maximum_fusion.55) | data formatting | bytes 16777216
  361.8 3.4 psum.7
  (116 shorter events, 23.4 us)
Async XLA Ops:
  1.6 48.9 %collective-permute-start = (f32[4,1,64,128]{3,2,1,0:T(8,128)S(1)}, f32[4,1,64,128]{3,2,1,0:T(8,128)S(1)}, u32[]{:S(2)}, u32[]{:S(2)}) collective-permute-start(f32[4,1,64,128]{3,2,1,0:T(8,128)S(1)} %get-tuple-element.30), channel_id=1, source_target_pairs={{8,0},{16,8},{24,16},{9,1},{17,9},{25,17},{10,2},{18,10},{26,18},{... | collective-permute-start | bytes 393224 | tf_op jit(solution)/shard_map/ppermute | solution.py:26
  2.9 47.7 %collective-permute-start.1 = (f32[4,1,64,128]{3,2,1,0:T(8,128)S(1)}, f32[4,1,64,128]{3,2,1,0:T(8,128)S(1)}, u32[]{:S(2)}, u32[]{:S(2)}) collective-permute-start(f32[4,1,64,128]{3,2,1,0:T(8,128)S(1)} %get-tuple-element.29), channel_id=1, source_target_pairs={{0,8},{8,16},{16,24},{1,9},{9,17},{17,25},{2,10},{10,18},{18,26},{... | collective-permute-start | bytes 393224 | tf_op jit(solution)/shard_map/ppermute | solution.py:25
  9.7 57.0 %collective-permute-start.12 = (f32[8,64]{1,0:T(8,128)S(1)}, f32[8,64]{1,0:T(8,128)S(1)}, u32[]{:S(2)}, u32[]{:S(2)}) collective-permute-start(f32[8,64]{1,0:T(8,128)S(1)} %get-tuple-element.51), channel_id=1, source_target_pairs={{0,8},{8,16},{16,24},{1,9},{9,17},{17,25},{2,10},{10,18},{18,26},{... | collective-permute-start | bytes 6152 | tf_op jit(solution)/shard_map/ppermute | solution.py:25
  14.5 81.9 %collective-permute-start.13 = (f32[8,64]{1,0:T(8,128)}, f32[8,64]{1,0:T(8,128)}, u32[]{:S(2)}, u32[]{:S(2)}) collective-permute-start(f32[8,64]{1,0:T(8,128)} %get-tuple-element.50), channel_id=1, source_target_pairs={{8,0},{16,8},{24,16},{9,1},{17,9},{25,17},{10,2},{18,10},{26,18},{... | collective-permute-start | bytes 6152 | tf_op jit(solution)/shard_map/ppermute | solution.py:26
  18.6 8.0 %copy-start.26 = (s32[1,1,64,1]{2,3,1,0:T(1,128)S(1)}, s32[1,1,64,1]{2,3,1,0:T(1,128)}, u32[]{:S(2)}) copy-start(s32[1,1,64,1]{2,3,1,0:T(1,128)} %param.15) | copy-start | bytes 772
  18.6 9.4 %copy-start.15 = (s32[64,64,128]{2,1,0:T(8,128)S(1)}, s32[64,64,128]{2,1,0:T(8,128)}, u32[]{:S(2)}) copy-start(s32[64,64,128]{2,1,0:T(8,128)} %param.10) | copy-start | bytes 6291460
  18.6 26.3 %slice-start = ((s8[8388608]{0:T(1024)(128)(4,1)}), s8[4194304]{0:T(1024)(128)(4,1)S(1)}, s32[]{:S(2)}) async-start(s8[8388608]{0:T(1024)(128)(4,1)} %bitcast.45), calls=%async_computation.1 | async-start | bytes 8388608
  28.0 16.9 %slice-start.1 = ((s8[8388608]{0:T(1024)(128)(4,1)}), s8[4194304]{0:T(1024)(128)(4,1)S(1)}, s32[]{:S(2)}) async-start(s8[8388608]{0:T(1024)(128)(4,1)} %bitcast.45), calls=%async_computation.2 | async-start | bytes 8388608
  33.1 11.4 %copy-start.11 = (pred[64,64,128]{2,0,1:T(8,128)(4,1)}, pred[64,64,128]{2,0,1:T(8,128)(4,1)S(1)}, u32[]{:S(2)}) copy-start(pred[64,64,128]{2,0,1:T(8,128)(4,1)S(1)} %get-tuple-element.17) | copy-start | bytes 1572868
  33.1 11.4 %copy-start.13 = (pred[64,64,128]{2,0,1:T(8,128)(4,1)}, pred[64,64,128]{2,0,1:T(8,128)(4,1)S(1)}, u32[]{:S(2)}) copy-start(pred[64,64,128]{2,0,1:T(8,128)(4,1)S(1)} %get-tuple-element.18) | copy-start | bytes 1572868
  33.1 125.2 %copy-start.4 = (f32[64,64,128]{2,0,1:T(8,128)}, f32[64,64,128]{2,0,1:T(8,128)S(1)}, u32[]{:S(2)}) copy-start(f32[64,64,128]{2,0,1:T(8,128)S(1)} %get-tuple-element.14) | copy-start | bytes 6291460
  45.0 4.9 %copy-start.22 = (f32[4]{0:T(128)S(1)}, f32[4]{0:T(128)}, u32[]{:S(2)}) copy-start(f32[4]{0:T(128)} %param.13) | copy-start | bytes 52
  49.8 19.5 %copy-start = (f32[4,64,64,128]{3,1,2,0:T(8,128)}, f32[4,64,64,128]{3,1,2,0:T(8,128)S(1)}, u32[]{:S(2)}) copy-start(f32[4,64,64,128]{3,1,2,0:T(8,128)S(1)} %copy.71) | copy-start | bytes 25165828
  50.6 16.1 %copy-start.20 = (f32[64,64]{1,0:T(8,128)S(1)}, f32[64,64]{1,0:T(8,128)}, u32[]{:S(2)}) copy-start(f32[64,64]{1,0:T(8,128)} %param.14) | copy-start | bytes 49156
  50.6 16.1 %collective-permute-start.2 = (f32[4,66,1,128]{3,1,2,0:T(8,128)S(1)}, f32[4,66,1,128]{3,1,2,0:T(8,128)S(1)}, u32[]{:S(2)}, u32[]{:S(2)}) collective-permute-start(f32[4,66,1,128]{3,1,2,0:T(8,128)S(1)} %get-tuple-element.26), channel_id=1, source_target_pairs={{2,0},{4,2},{6,4},{3,1},{5,3},{7,5},{10,8},{12,10},{14,12},{11,9},... | collective-permute-start | bytes 405512 | tf_op jit(solution)/shard_map/ppermute | solution.py:26
  51.9 17.4 %collective-permute-start.3 = (f32[4,66,1,128]{3,1,2,0:T(8,128)S(1)}, f32[4,66,1,128]{3,1,2,0:T(8,128)S(1)}, u32[]{:S(2)}, u32[]{:S(2)}) collective-permute-start(f32[4,66,1,128]{3,1,2,0:T(8,128)S(1)} %get-tuple-element.25), channel_id=1, source_target_pairs={{0,2},{2,4},{4,6},{1,3},{3,5},{5,7},{8,10},{10,12},{12,14},{9,11},... | collective-permute-start | bytes 405512 | tf_op jit(solution)/shard_map/ppermute | solution.py:25
  66.7 4.9 %copy-start.18 = (f32[80,64]{1,0:T(8,128)}, f32[80,64]{1,0:T(8,128)S(1)}, u32[]{:S(2)}) copy-start(f32[80,64]{1,0:T(8,128)S(1)} %constant_dynamic-update-slice_fusion.1) | copy-start | bytes 61444
  86.3 11.4 %collective-permute-start.5 = (f32[4,66,66,1]{2,1,3,0:T(8,128)}, f32[4,66,66,1]{2,1,3,0:T(8,128)}, u32[]{:S(2)}, u32[]{:S(2)}) collective-permute-start(f32[4,66,66,1]{2,1,3,0:T(8,128)} %copy.87), channel_id=1, source_target_pairs={{0,1},{2,3},{4,5},{6,7},{8,9},{10,11},{12,13},{14,15},{16,17},{18,... | collective-permute-start | bytes 209096 | tf_op jit(solution)/shard_map/ppermute | solution.py:25
  95.1 9.0 %collective-permute-start.4 = (f32[4,66,66,1]{2,1,3,0:T(8,128)}, f32[4,66,66,1]{2,1,3,0:T(8,128)}, u32[]{:S(2)}, u32[]{:S(2)}) collective-permute-start(f32[4,66,66,1]{2,1,3,0:T(8,128)} %copy.85), channel_id=1, source_target_pairs={{1,0},{3,2},{5,4},{7,6},{9,8},{11,10},{13,12},{15,14},{17,16},{19,... | collective-permute-start | bytes 209096 | tf_op jit(solution)/shard_map/ppermute | solution.py:26
  110.6 31.5 %copy-start.6 = (f32[64,64,128]{2,0,1:T(8,128)S(1)}, f32[64,64,128]{2,0,1:T(8,128)}, u32[]{:S(2)}) copy-start(f32[64,64,128]{2,0,1:T(8,128)} %get-tuple-element.42) | copy-start | bytes 6291460
  166.9 3.4 copy-start.10
  169.7 25.6 %copy-start.8 = (f32[1,64,64,128]{3,1,2,0:T(8,128)}, f32[1,64,64,128]{3,1,2,0:T(8,128)S(1)}, u32[]{:S(2)}) copy-start(f32[1,64,64,128]{3,1,2,0:T(8,128)S(1)} %get-tuple-element.40) | copy-start | bytes 6291460
  170.9 24.3 %copy-start.1 = (f32[1,64,64,128]{3,1,2,0:T(8,128)}, f32[1,64,64,128]{3,1,2,0:T(8,128)S(1)}, u32[]{:S(2)}) copy-start(f32[1,64,64,128]{3,1,2,0:T(8,128)S(1)} %get-tuple-element.37) | copy-start | bytes 6291460
  170.9 24.3 %copy-start.2 = (f32[1,64,64,128]{3,1,2,0:T(8,128)}, f32[1,64,64,128]{3,1,2,0:T(8,128)S(1)}, u32[]{:S(2)}) copy-start(f32[1,64,64,128]{3,1,2,0:T(8,128)S(1)} %get-tuple-element.38) | copy-start | bytes 6291460
  171.0 7.8 %copy-start.19 = (f32[80,64]{1,0:T(8,128)S(1)}, f32[80,64]{1,0:T(8,128)}, u32[]{:S(2)}) copy-start(f32[80,64]{1,0:T(8,128)} %constant_dynamic-update-slice_fusion) | copy-start | bytes 61444
  172.0 13.2 %copy-start.3 = (f32[4,64,64,128]{3,1,2,0:T(8,128)}, f32[4,64,64,128]{3,1,2,0:T(8,128)S(1)}, u32[]{:S(2)}) copy-start(f32[4,64,64,128]{3,1,2,0:T(8,128)S(1)} %pad_maximum_fusion.54) | copy-start | bytes 25165828
  172.2 12.9 %collective-permute-start.6 = (f32[4,1,64,128]{3,2,1,0:T(8,128)S(1)}, f32[4,1,64,128]{3,2,1,0:T(8,128)S(1)}, u32[]{:S(2)}, u32[]{:S(2)}) collective-permute-start(f32[4,1,64,128]{3,2,1,0:T(8,128)S(1)} %bitcast.62), channel_id=1, source_target_pairs={{8,0},{16,8},{24,16},{9,1},{17,9},{25,17},{10,2},{18,10},{26,18},{... | collective-permute-start | bytes 393224 | tf_op jit(solution)/shard_map/ppermute | solution.py:26
  173.5 11.6 %collective-permute-start.7 = (f32[4,1,64,128]{3,2,1,0:T(8,128)S(1)}, f32[4,1,64,128]{3,2,1,0:T(8,128)S(1)}, u32[]{:S(2)}, u32[]{:S(2)}) collective-permute-start(f32[4,1,64,128]{3,2,1,0:T(8,128)S(1)} %bitcast.61), channel_id=1, source_target_pairs={{0,8},{8,16},{16,24},{1,9},{9,17},{17,25},{2,10},{10,18},{18,26},{... | collective-permute-start | bytes 393224 | tf_op jit(solution)/shard_map/ppermute | solution.py:25
  178.8 12.7 %collective-permute-start.15 = (f32[80,8]{1,0:T(8,128)S(1)}, f32[80,8]{1,0:T(8,128)S(1)}, u32[]{:S(2)}, u32[]{:S(2)}) collective-permute-start(f32[80,8]{1,0:T(8,128)S(1)} %get-tuple-element.47), channel_id=1, source_target_pairs={{2,0},{4,2},{6,4},{3,1},{5,3},{7,5},{10,8},{12,10},{14,12},{11,9},... | collective-permute-start | bytes 7688 | tf_op jit(solution)/shard_map/ppermute | solution.py:26
  180.1 11.4 %collective-permute-start.14 = (f32[80,8]{1,0:T(8,128)S(1)}, f32[80,8]{1,0:T(8,128)S(1)}, u32[]{:S(2)}, u32[]{:S(2)}) collective-permute-start(f32[80,8]{1,0:T(8,128)S(1)} %get-tuple-element.46), channel_id=1, source_target_pairs={{0,2},{2,4},{4,6},{1,3},{3,5},{5,7},{8,10},{10,12},{12,14},{9,11},... | collective-permute-start | bytes 7688 | tf_op jit(solution)/shard_map/ppermute | solution.py:25
  185.1 6.4 %copy-start.23 = (s32[80]{0:T(128)S(1)}, s32[80]{0:T(128)}, u32[]{:S(2)}) copy-start(s32[80]{0:T(128)} %iota_add_fusion) | copy-start | bytes 964
  185.2 8.4 %collective-permute-start.8 = (f32[4,66,1,128]{3,1,2,0:T(8,128)S(1)}, f32[4,66,1,128]{3,1,2,0:T(8,128)S(1)}, u32[]{:S(2)}, u32[]{:S(2)}) collective-permute-start(f32[4,66,1,128]{3,1,2,0:T(8,128)S(1)} %get-tuple-element.24), channel_id=1, source_target_pairs={{2,0},{4,2},{6,4},{3,1},{5,3},{7,5},{10,8},{12,10},{14,12},{11,9},... | collective-permute-start | bytes 405512 | tf_op jit(solution)/shard_map/ppermute | solution.py:26
  186.5 8.8 %collective-permute-start.9 = (f32[4,66,1,128]{3,1,2,0:T(8,128)S(1)}, f32[4,66,1,128]{3,1,2,0:T(8,128)S(1)}, u32[]{:S(2)}, u32[]{:S(2)}) collective-permute-start(f32[4,66,1,128]{3,1,2,0:T(8,128)S(1)} %get-tuple-element.23), channel_id=1, source_target_pairs={{0,2},{2,4},{4,6},{1,3},{3,5},{5,7},{8,10},{10,12},{12,14},{9,11},... | collective-permute-start | bytes 405512 | tf_op jit(solution)/shard_map/ppermute | solution.py:25
  214.0 28.4 %collective-permute-start.11 = (f32[4,66,66,1]{2,1,3,0:T(8,128)}, f32[4,66,66,1]{2,1,3,0:T(8,128)}, u32[]{:S(2)}, u32[]{:S(2)}) collective-permute-start(f32[4,66,66,1]{2,1,3,0:T(8,128)} %copy.97), channel_id=1, source_target_pairs={{0,1},{2,3},{4,5},{6,7},{8,9},{10,11},{12,13},{14,15},{16,17},{18,... | collective-permute-start | bytes 209096 | tf_op jit(solution)/shard_map/ppermute | solution.py:25
  223.5 25.3 %collective-permute-start.10 = (f32[4,66,66,1]{2,1,3,0:T(8,128)}, f32[4,66,66,1]{2,1,3,0:T(8,128)}, u32[]{:S(2)}, u32[]{:S(2)}) collective-permute-start(f32[4,66,66,1]{2,1,3,0:T(8,128)} %copy.95), channel_id=1, source_target_pairs={{1,0},{3,2},{5,4},{7,6},{9,8},{11,10},{13,12},{15,14},{17,16},{19,... | collective-permute-start | bytes 209096 | tf_op jit(solution)/shard_map/ppermute | solution.py:26
  255.3 31.8 %copy-start.5 = (f32[64,64,128]{2,0,1:T(8,128)S(1)}, f32[64,64,128]{2,0,1:T(8,128)}, u32[]{:S(2)}) copy-start(f32[64,64,128]{2,0,1:T(8,128)} %copy-done.4) | copy-start | bytes 6291460
  287.1 17.6 %copy-start.7 = (f32[64,64,128]{2,0,1:T(8,128)S(1)}, f32[64,64,128]{2,0,1:T(8,128)}, u32[]{:S(2)}) copy-start(f32[64,64,128]{2,0,1:T(8,128)} %get-tuple-element.42) | copy-start | bytes 6291460
  304.7 8.8 %copy-start.12 = (pred[64,64,128]{2,0,1:T(8,128)(4,1)S(1)}, pred[64,64,128]{2,0,1:T(8,128)(4,1)}, u32[]{:S(2)}) copy-start(pred[64,64,128]{2,0,1:T(8,128)(4,1)} %copy-done.11) | copy-start | bytes 1572868
  304.7 8.8 %copy-start.14 = (pred[64,64,128]{2,0,1:T(8,128)(4,1)S(1)}, pred[64,64,128]{2,0,1:T(8,128)(4,1)}, u32[]{:S(2)}) copy-start(pred[64,64,128]{2,0,1:T(8,128)(4,1)} %copy-done.13) | copy-start | bytes 1572868
  313.5 7.5 %copy-start.21 = (f32[64,80]{1,0:T(8,128)S(1)}, f32[64,80]{1,0:T(8,128)}, u32[]{:S(2)}) copy-start(f32[64,80]{1,0:T(8,128)} %fusion.19) | copy-start | bytes 61444
  313.5 7.5 %copy-start.24 = (s32[80]{0:T(128)S(1)}, s32[80]{0:T(128)}, u32[]{:S(2)}) copy-start(s32[80]{0:T(128)} %iota_add_fusion) | copy-start | bytes 964
  321.3 10.5 %collective-permute-start.17 = (f32[8,64]{1,0:T(8,128)S(1)}, f32[8,64]{1,0:T(8,128)S(1)}, u32[]{:S(2)}, u32[]{:S(2)}) collective-permute-start(f32[8,64]{1,0:T(8,128)S(1)} %get-tuple-element.49), channel_id=1, source_target_pairs={{8,0},{16,8},{24,16},{9,1},{17,9},{25,17},{10,2},{18,10},{26,18},{... | collective-permute-start | bytes 6152 | tf_op jit(solution)/shard_map/ppermute | solution.py:26
  322.6 15.6 %copy-start.9 = (f32[2,64,64,128]{3,1,2,0:T(8,128)S(1)}, f32[2,64,64,128]{3,1,2,0:T(8,128)}, u32[]{:S(2)}) copy-start(f32[2,64,64,128]{3,1,2,0:T(8,128)} %get-tuple-element.8) | copy-start | bytes 12582916
  322.6 9.2 %collective-permute-start.16 = (f32[8,64]{1,0:T(8,128)S(1)}, f32[8,64]{1,0:T(8,128)S(1)}, u32[]{:S(2)}, u32[]{:S(2)}) collective-permute-start(f32[8,64]{1,0:T(8,128)S(1)} %get-tuple-element.48), channel_id=1, source_target_pairs={{0,8},{8,16},{16,24},{1,9},{9,17},{17,25},{2,10},{10,18},{18,26},{... | collective-permute-start | bytes 6152 | tf_op jit(solution)/shard_map/ppermute | solution.py:25
  331.8 8.6 %collective-permute-start.19 = (f32[80,8]{1,0:T(8,128)S(1)}, f32[80,8]{1,0:T(8,128)S(1)}, u32[]{:S(2)}, u32[]{:S(2)}) collective-permute-start(f32[80,8]{1,0:T(8,128)S(1)} %get-tuple-element.45), channel_id=1, source_target_pairs={{2,0},{4,2},{6,4},{3,1},{5,3},{7,5},{10,8},{12,10},{14,12},{11,9},... | collective-permute-start | bytes 7688 | tf_op jit(solution)/shard_map/ppermute | solution.py:26
  333.1 8.1 %copy-start.25 = (s32[64]{0:T(128)S(1)}, s32[64]{0:T(128)}, u32[]{:S(2)}) copy-start(s32[64]{0:T(128)} %multiply_add_fusion.4) | copy-start | bytes 772
  333.1 7.3 %collective-permute-start.18 = (f32[80,8]{1,0:T(8,128)S(1)}, f32[80,8]{1,0:T(8,128)S(1)}, u32[]{:S(2)}, u32[]{:S(2)}) collective-permute-start(f32[80,8]{1,0:T(8,128)S(1)} %get-tuple-element.44), channel_id=1, source_target_pairs={{0,2},{2,4},{4,6},{1,3},{3,5},{5,7},{8,10},{10,12},{12,14},{9,11},... | collective-permute-start | bytes 7688 | tf_op jit(solution)/shard_map/ppermute | solution.py:25
  342.2 19.6 %all-to-all-start = ((f32[16,1,512]{2,1,0:T(1,128)}), f32[16,1,512]{2,1,0:T(1,128)S(1)}, u32[]{:S(2)}, u32[]{:S(2)}) async-start(f32[16,1,512]{2,1,0:T(1,128)} %all_to_all.11), calls=%async_computation | async-start | bytes 65536 | tf_op jit(solution)/shard_map/all_to_all | solution.py:141
  (2 other events, 2.9 us)
where the time goes:
time: 371 us; the launch traced here: 366 us
  other arithmetic  176 us (47%)
  local copies, waits for them, and re-layouts  102 us (27%)
  starting transfers between devices  75.9 us (20%)
  waiting for transfers between devices  5.54 us (1%)
    add x2, other arithmetic, sweep_box(): padded[:, 2:, 1:-1, 1:-1] + padded[:, :-2, 1:-1, 1:-1]  63.3 us
    ppermute x10, starting transfers between devices, extended(): before = lax.ppermute(last, axis, up)  54.9 us
    add x2, other arithmetic, sweep_box(): real_part + RELAXATION * (inverse_real * residual_real - inverse_imag * r...  33.7 us
    slice x5, local copies, waits for them, and re-layouts, extended(): leading = lax.slice_in_dim(array, 0, width, axis=dim)  30.6 us
    another operation x3, other arithmetic, sweep_box(): return jnp.stack([new_real[0], new_imag[0], new_real[1], new_imag[1]])  21.9 us
    add x2, other arithmetic, sweep_box(): imag_part + RELAXATION * (inverse_real * residual_imag + inverse_imag * r...  17.4 us
    add x2, other arithmetic, lookup(): result + jnp.where(material == level_index, level_table[level_index], jnp...  16.4 us
    slice x7, local copies, waits for them, and re-layouts, extended(): last = lax.slice_in_dim(array, length - width, length, axis=dim)  15.2 us
  transfers between devices with their start and end apart: 21, of which 3 were waited for; matrix products, arithmetic and copies ran while one was open for 32% of the time, Pallas kernels for 0%

commit v1 on v0

v1 whole, which is shorter than its diff:
```python
import functools
import math

import jax
import jax.numpy as jnp
from jax import lax
from jax.experimental import pallas as pl
from jax.experimental.pallas import tpu as pltpu
from jax.sharding import PartitionSpec as P

R = 8
TS = 8
MOST = 8
RELAXATION = 0.8
SHARPNESS = 8.0
THRESHOLD = 0.5
XB = 16
F32 = jnp.float32
BF16 = jnp.bfloat16


def lanes_of(shape):
    return lax.broadcasted_iota(jnp.int32, shape, len(shape) - 1)


def put_faces(c, x, xx, new, gs, ylo, yhi):
    ylo[c, pl.ds(xx, 1), :] = new[0:1, :]
    yhi[c, pl.ds(xx, 1), :] = new[-1:, :]
    turned = pltpu.roll(new, 2 * x + 1, 1)
    gs[c] = jnp.where(lanes_of(new.shape) // 2 == x, turned, gs[c])


def pack_kernel(v_ref, xlo_ref, xhi_ref, ylo_ref, yhi_ref, g_ref, gs, ylo, yhi):
    step, steps = pl.program_id(0), pl.num_programs(0)

    @pl.when(step == 0)
    def _():
        gs[...] = jnp.zeros_like(gs)
        xlo_ref[...] = v_ref[:, 0].astype(BF16)

    def plane(xx, carry):
        for c in range(4):
            put_faces(c, step * XB + xx, xx, v_ref[c, xx], gs, ylo, yhi)
        return carry

    lax.fori_loop(0, XB, plane, 0)
    ylo_ref[...] = ylo[...].astype(BF16)
    yhi_ref[...] = yhi[...].astype(BF16)

    @pl.when(step == steps - 1)
    def _():
        g_ref[...] = gs[...].astype(BF16)
        xhi_ref[...] = v_ref[:, XB - 1].astype(BF16)


def sweep_kernel(last, nz, *refs):
    (sr_ref, si_ref, sh_ref, v_ref, vp_ref, vn_ref, s_ref, m_ref, xl_ref, xr_ref,
     yl_ref, yr_ref, gl_ref, gr_ref) = refs[:14]
    if last:
        o_ref, sens_ref, hs, yl, yr, sens = refs[14:]
    else:
        o_ref, xlo_ref, xhi_ref, ylo_ref, yhi_ref, g_ref, hs, yl, yr, gs, ylo, yhi = refs[14:]
    step, steps = pl.program_id(0), pl.num_programs(0)
    rows, depth = v_ref.shape[2:]
    lane = lanes_of((rows, depth))

    @pl.when(step == 0)
    def _():
        if nz == 2:
            here = lax.axis_index("gz").astype(F32)
            keep_l, keep_r = here, 1.0 - here
        else:
            keep_l, keep_r = 1.0, 1.0
        for c in range(4):
            left = pltpu.roll(gl_ref[c].astype(F32), 1, 1) * keep_l
            right = pltpu.roll(gr_ref[c].astype(F32), depth - 1, 1) * keep_r
            hs[c] = jnp.where(lane % 2 == 1, left, right)
        if last:
            sens[...] = jnp.zeros_like(sens)
        else:
            gs[...] = jnp.zeros_like(gs)

    yl[...] = yl_ref[...].astype(F32)
    yr[...] = yr_ref[...].astype(F32)

    levels = sr_ref.shape[0]
    tile = (8, depth)
    wr, wi, share = [], [], []
    for m in range(levels):
        d = 6.0 + jnp.full(tile, sr_ref[m], F32)
        s = jnp.full(tile, si_ref[m], F32)
        mag = d * d + s * s
        wr.append(RELAXATION * d / mag)
        wi.append(-RELAXATION * s / mag)
        if last:
            share.append(jnp.full(tile, sh_ref[m], F32))

    def lookup(masks, table):
        out = jnp.broadcast_to(table[0], (rows // 8, 8, depth))
        for mask, value in zip(masks, table[1:]):
            out = jnp.where(mask, value, out)
        return out.reshape(rows, depth)

    row8 = lax.broadcasted_iota(jnp.int32, tile, 0)

    def plane(xx, before, after):
        x = step * XB + xx
        mat = m_ref[xx].reshape(rows // 8, 8, depth)
        masks = [mat == m for m in range(1, levels)]
        w_r, w_i = lookup(masks, wr), lookup(masks, wi)

        def drive(c):
            v = v_ref[c, xx]
            total = before(c) + after(c) + s_ref[c, xx].astype(F32)
            up = pltpu.roll(v, 1, 0)
            down = pltpu.roll(v, rows - 1, 0)
            top = jnp.where(row8 == 0, yl[c, pl.ds(xx, 1), :], up[:8])
            low = jnp.where(row8 == 7, yr[c, pl.ds(xx, 1), :], down[-8:])
            total = total + jnp.concatenate([top, up[8:]], 0) + jnp.concatenate([down[:-8], low], 0)
            h = pltpu.roll(hs[c], depth - 1 - 2 * x, 1)
            total = total + jnp.where(lane == 0, h, pltpu.roll(v, 1, 1))
            return v, total + jnp.where(lane == depth - 1, h, pltpu.roll(v, depth - 1, 1))

        news = []
        for re in (0, 2):
            v_r, t_r = drive(re)
            v_i, t_i = drive(re + 1)
            keep = 1.0 - RELAXATION
            n_r = keep * v_r + (w_r * t_r - w_i * t_i)
            n_i = keep * v_i + (w_r * t_i + w_i * t_r)
            o_ref[re, xx] = n_r
            o_ref[re + 1, xx] = n_i
            if last:
                news += [n_r, n_i]
            else:
                put_faces(re, x, xx, n_r, gs, ylo, yhi)
                put_faces(re + 1, x, xx, n_i, gs, ylo, yhi)
        if last:
            value = lookup(masks, share) * (news[0] * news[2] - news[1] * news[3])
            column = jnp.sum(value, axis=1, keepdims=True)
            sens[...] = jnp.where(lane == x, column, sens[...])

    plane(
        0,
        lambda c: jnp.where(step == 0, xl_ref[c].astype(F32), vp_ref[c, 0]),
        lambda c: v_ref[c, 1],
    )

    def middle(xx, carry):
        plane(xx, lambda c: v_ref[c, xx - 1], lambda c: v_ref[c, xx + 1])
        return carry

    lax.fori_loop(1, XB - 1, middle, 0)
    plane(
        XB - 1,
        lambda c: v_ref[c, XB - 2],
        lambda c: jnp.where(step == steps - 1, xr_ref[c].astype(F32), vn_ref[c, 0]),
    )
    if not last:
        ylo_ref[...] = ylo[...].astype(BF16)
        yhi_ref[...] = yhi[...].astype(BF16)

        @pl.when(step == 0)
        def _():
            xlo_ref[...] = o_ref[:, 0].astype(BF16)

    @pl.when(step == steps - 1)
    def _():
        if last:
            half = rows // 2
            both = pltpu.roll(sens[half:], depth // 2, 1)
            sens_ref[...] = jnp.where(lane[:half] < depth // 2, sens[:half], both)
        else:
            g_ref[...] = gs[...].astype(BF16)
            xhi_ref[...] = o_ref[:, XB - 1].astype(BF16)


def whole(shape):
    return pl.BlockSpec(shape, lambda i: (0,) * len(shape))


SMEM_SPEC = pl.BlockSpec(memory_space=pltpu.SMEM)


def face_outs(nx, ny, nz):
    shapes = [(4, ny, nz), (4, ny, nz), (4, nx, nz), (4, nx, nz), (4, ny, nz)]
    y_spec = pl.BlockSpec((4, XB, nz), lambda i: (0, i, 0))
    specs = [whole((4, ny, nz)), whole((4, ny, nz)), y_spec, y_spec, whole((4, ny, nz))]
    return [jax.ShapeDtypeStruct(s, BF16) for s in shapes], specs


def face_scratch(ny, nz):
    return [
        pltpu.VMEM((4, ny, nz), F32),
        pltpu.VMEM((4, XB, nz), F32),
        pltpu.VMEM((4, XB, nz), F32),
    ]


def pack(fields):
    _, nx, ny, nz = fields.shape
    shapes, specs = face_outs(nx, ny, nz)
    return pl.pallas_call(
        pack_kernel,
        grid=(nx // XB,),
        in_specs=[pl.BlockSpec((4, XB, ny, nz), lambda i: (0, i, 0, 0))],
        out_specs=specs,
        out_shape=shapes,
        scratch_shapes=face_scratch(ny, nz),
        compiler_params=pltpu.CompilerParams(vmem_limit_bytes=24 << 20),
        cost_estimate=pl.CostEstimate(
            flops=fields.size * 4, bytes_accessed=fields.size * 4, transcendentals=0
        ),
        name="pack_faces",
    )(fields)


def sweep(last, tables, current, sources, material, halos):
    _, nx, ny, nz = current.shape
    steps = nx // XB
    block = pl.BlockSpec((4, XB, ny, nz), lambda i: (0, i, 0, 0))
    y_spec = pl.BlockSpec((4, XB, nz), lambda i: (0, i, 0))
    x_spec = whole((4, ny, nz))
    in_specs = [SMEM_SPEC] * 3 + [
        block,
        pl.BlockSpec((4, 1, ny, nz), lambda i: (0, jnp.maximum(i * XB - 1, 0), 0, 0)),
        pl.BlockSpec((4, 1, ny, nz), lambda i: (0, jnp.minimum(i * XB + XB, nx - 1), 0, 0)),
        block,
        pl.BlockSpec((XB, ny, nz), lambda i: (i, 0, 0)),
        x_spec,
        x_spec,
        y_spec,
        y_spec,
        x_spec,
        x_spec,
    ]
    scratch = [
        pltpu.VMEM((4, ny, nz), F32),
        pltpu.VMEM((4, XB, nz), F32),
        pltpu.VMEM((4, XB, nz), F32),
    ]
    shapes, specs = [jax.ShapeDtypeStruct(current.shape, F32)], [block]
    if last:
        shapes.append(jax.ShapeDtypeStruct((ny // 2, nz), F32))
        specs.append(whole((ny // 2, nz)))
        scratch.append(pltpu.VMEM((ny, nz), F32))
    else:
        more_shapes, more_specs = face_outs(nx, ny, nz)
        shapes += more_shapes
        specs += more_specs
        scratch += face_scratch(ny, nz)
    return pl.pallas_call(
        functools.partial(sweep_kernel, last, lax.axis_size("gz")),
        grid=(steps,),
        in_specs=in_specs,
        out_specs=specs,
        out_shape=shapes,
        scratch_shapes=scratch,
        compiler_params=pltpu.CompilerParams(vmem_limit_bytes=32 << 20),
        cost_estimate=pl.CostEstimate(
            flops=current.size * 24, bytes_accessed=current.size * 11, transcendentals=0
        ),
        name="sweep_last" if last else "sweep_first",
    )(*tables, current, current, current, sources, material, *halos)


def exchange(xlo, xhi, ylo, yhi, g):
    out = []
    for axis, low, high in (("gx", xlo, xhi), ("gy", ylo, yhi)):
        count = lax.axis_size(axis)
        up = [(i, i + 1) for i in range(count - 1)]
        out.append(lax.ppermute(high, axis, up))
        out.append(lax.ppermute(low, axis, [(j, i) for i, j in up]))
    count = lax.axis_size("gz")
    if count == 2:
        other = lax.ppermute(g, "gz", [(0, 1), (1, 0)])
        return out + [other, other]
    up = [(i, i + 1) for i in range(count - 1)]
    return out + [lax.ppermute(g, "gz", up), lax.ppermute(g, "gz", [(j, i) for i, j in up])]


def split(value):
    high = value.astype(BF16)
    return high, (value - high.astype(F32)).astype(BF16)


def mm(a, b):
    return lax.dot_general(a, b, (((1,), (0,)), ((), ())), preferred_element_type=F32)


def plane_kernel(ngx, ngy, scale, me_ref, sens_ref, den_ref, own_ref, out_ref, w_ref, d_ref):
    cells = 64
    nx, ny = ngx * cells, ngy * cells
    columns = ngx * ngy
    half = cells // 2
    for cx in range(ngx):
        for cy in range(ngy):
            c = cx * ngy + cy
            for part in range(2):
                w_ref[pl.ds(cy * cells + part * half, half), pl.ds(cx * cells, cells)] = sens_ref[
                    c, :, pl.ds(part * cells, cells)
                ]
            d_ref[pl.ds(cx * cells, cells), pl.ds(cy * cells, cells)] = den_ref[c]

    def band(n):
        i = lax.broadcasted_iota(jnp.int32, (n, n), 0)
        j = lax.broadcasted_iota(jnp.int32, (n, n), 1)
        return jnp.maximum(R + 1 - jnp.abs(i - j), 0).astype(F32).astype(BF16)

    band_x, band_y = band(nx), band(ny)
    unit = float((R + 1) ** 4)

    def twice(value, right):
        high, low = split(value)
        return mm(high, right) + mm(low, right)

    def left_twice(left, value):
        high, low = split(value)
        return mm(left, high) + mm(left, low)

    density = jnp.transpose(d_ref[...], (1, 0))
    filtered = left_twice(band_y, twice(density, band_x)) / unit
    tangent = jnp.tanh(SHARPNESS * (filtered - THRESHOLD))
    total = math.tanh(SHARPNESS * THRESHOLD) + math.tanh(SHARPNESS * (1.0 - THRESHOLD))
    slope = SHARPNESS * (1.0 - tangent * tangent) / total
    weighted = twice(slope * w_ref[...] * scale, band_x)

    tiles = own_ref.shape[1]
    mine = own_ref[...] == me_ref[0].astype(F32)
    flag = jnp.where(mine, 1.0, 0.0)
    a = lax.broadcasted_iota(jnp.int32, (tiles, tiles), 0)
    b = lax.broadcasted_iota(jnp.int32, (tiles, tiles), 1)
    rank = mm(flag.astype(BF16), jnp.where(a < b, 1.0, 0.0).astype(BF16))
    number = lanes_of((columns, tiles))
    column = lax.broadcasted_iota(jnp.int32, (columns, 1), 0)
    rows, blocks = [], []
    for k in range(MOST):
        chosen = mine & (rank == float(k))
        tile = jnp.sum(jnp.where(chosen, number, 0), axis=1, keepdims=True)
        there = jnp.sum(jnp.where(chosen, 1, 0), axis=1, keepdims=True)
        rows.append((column % ngy) * cells + (tile % (cells // TS)) * TS)
        block = (column // ngy) * (cells // TS) + tile // (cells // TS)
        blocks.append(jnp.where(there > 0, block, -1))
    row = jnp.concatenate(rows, 0)
    block = jnp.concatenate(blocks, 0)
    slots = MOST * columns
    across = lax.broadcasted_iota(jnp.int32, (slots, ny), 1)
    lefts = [
        jnp.maximum(R + 1 - jnp.abs(row + j - across), 0).astype(F32).astype(BF16)
        for j in range(TS)
    ]
    lines = left_twice(jnp.concatenate(lefts, 0), weighted)
    keep = lanes_of((slots, nx)) // TS == block
    from_x = lax.broadcasted_iota(jnp.int32, (nx, TS * TS), 0) % TS
    to_q = lanes_of((nx, TS * TS))
    out = jnp.zeros((slots, TS * TS), F32)
    for j in range(TS):
        fold = jnp.where(to_q == from_x * TS + j, 1.0, 0.0).astype(BF16)
        out = out + twice(jnp.where(keep, lines[j * slots : (j + 1) * slots], 0.0), fold)
    out = out / unit
    for k in range(MOST):
        out_ref[0, :, pl.ds(k * TS * TS, TS * TS)] = out[k * columns : (k + 1) * columns]


def on_device(fields, sources, material, shift_real, shift_imag, design_share, density, owner_map):
    ngx, ngy, ngz = (lax.axis_size(a) for a in ("gx", "gy", "gz"))
    columns = ngx * ngy
    cells = density.shape[0]
    tables = (shift_real, shift_imag, design_share)
    known = jnp.concatenate([density, owner_map.reshape(1, -1).astype(F32)], 0)
    known = lax.all_gather(known, ("gx", "gy"))
    halos = exchange(*pack(fields))
    middle, *faces = sweep(False, tables, fields, sources, material, halos)
    final, partial = sweep(True, tables, middle, sources, material, exchange(*faces))
    partial = jnp.sum(lax.all_gather(partial, "gz"), 0)
    copies = jnp.broadcast_to(partial[None], (columns, *partial.shape))
    plane = lax.all_to_all(copies, ("gx", "gy"), split_axis=0, concat_axis=0)
    me = (lax.axis_index("gx") * ngy + lax.axis_index("gy")).reshape(1)
    vmem = pl.BlockSpec(memory_space=pltpu.VMEM)
    owned = pl.pallas_call(
        functools.partial(
            plane_kernel, ngx, ngy, 1.0 / math.sqrt(material.shape[2] * ngz)
        ),
        in_specs=[SMEM_SPEC, vmem, vmem, vmem],
        out_specs=vmem,
        out_shape=jax.ShapeDtypeStruct((1, columns, MOST * TS * TS), F32),
        scratch_shapes=[
            pltpu.VMEM((ngy * cells, ngx * cells), F32),
            pltpu.VMEM((ngx * cells, ngy * cells), F32),
        ],
        compiler_params=pltpu.CompilerParams(vmem_limit_bytes=32 << 20),
        name="plane",
    )(me, plane, known[:, :cells], known[:, cells])
    return (final, owned)


def solution(mesh):
    placed = (
        P(None, "gx", "gy", "gz"),
        P(None, "gx", "gy", "gz"),
        P("gx", "gy", "gz"),
        P(),
        P(),
        P(),
        P("gx", "gy"),
        P("gx", "gy", None, None),
    )
    return jax.shard_map(
        on_device,
        mesh=mesh,
        in_specs=placed,
        out_specs=(P(None, "gx", "gy", "gz"), P(("gx", "gy"), None, None)),
        check_vma=False,
    )
```

time: 371 us -> 145 us (0.39); the launches traced: 366 us -> 145 us
  other arithmetic: 176 us -> 0.09 us
  local copies, waits for them, and re-layouts: 102 us -> 4.92 us
  Pallas kernels: 0 us -> 52.9 us
  starting transfers between devices: 75.9 us -> 28.5 us
  blocking collectives: 3.39 us -> 47.8 us
  waiting for transfers between devices: 5.54 us -> 9.54 us
    add x9 -> x0, other arithmetic: 131 us -> none  [the longest x2 63.3 us: sweep_box(): padded[:, 2:, 1:-1, 1:-1] + padded[:, :-2, 1:-1, 1:-1]]
    slice x20 -> x1, local copies, waits for them, and re-layouts: 58.9 us -> 0.2 us  [on_device(): known[:, cells]]
    pallas_call x0 -> x4, Pallas kernels: none -> 52.9 us  [the longest x2 42.8 us: sweep(): pl.pallas_call(functools.partial(sweep_kernel, last, lax.axis_size('gz'))...]
    all_gather x0 -> x2, blocking collectives: none -> 47.8 us  [the longest x1 46 us: on_device(): known = lax.all_gather(known, ('gx', 'gy'))]
    ppermute x20 -> x10, starting transfers between devices: 67.7 us -> 21.7 us  [the longest x4 16.4 us: exchange(): out.append(lax.ppermute(high, axis, up))]
    ppermute x4 -> x0, local copies, waits for them, and re-layouts: 25.8 us -> none  [the longest x2 12.9 us: extended(): after = lax.ppermute(leading, axis, down)]
    another operation x3 -> x0, other arithmetic: 21.9 us -> none  [sweep_box(): return jnp.stack([new_real[0], new_imag[0], new_real[1], new_imag[1]])]
    unnamed x63 -> x19, local copies, waits for them, and re-layouts: 15.1 us -> 3.89 us
  transfers between devices with their start and end apart: 21 -> 11, of which waited for: 3 -> 5; matrix products, arithmetic and copies ran while one was open for 32% -> 1% of each run, Pallas kernels for 0% -> 0%
where the time goes in v1:
time: 145 us
  Pallas kernels  52.9 us (36%)
  blocking collectives  47.8 us (33%)
  starting transfers between devices  28.5 us (20%)
  waiting for transfers between devices  9.54 us (7%)
  local copies, waits for them, and re-layouts  4.92 us (3%)
    all_gather x1, blocking collectives, on_device(): known = lax.all_gather(known, ('gx', 'gy'))  46 us
    pallas_call x2, Pallas kernels, sweep(): pl.pallas_call(functools.partial(sweep_kernel, last, lax.axis_size('gz'))...  42.8 us
    ppermute x4, starting transfers between devices, exchange(): out.append(lax.ppermute(high, axis, up))  16.4 us
    ppermute x4, waiting for transfers between devices, exchange(): out.append(lax.ppermute(low, axis, [(j, i) for i, j in up]))  8.91 us
    pallas_call x1, Pallas kernels, pack(): pl.pallas_call(pack_kernel, grid=(nx // XB,), in_specs=[pl.BlockSpec((4,...  7.26 us
    all_to_all x1, starting transfers between devices, on_device(): plane = lax.all_to_all(copies, ('gx', 'gy'), split_axis=0, concat_axis=0)  6.86 us
    ppermute x4, starting transfers between devices, exchange(): out.append(lax.ppermute(low, axis, [(j, i) for i, j in up]))  5.17 us
    unnamed x19, local copies, waits for them, and re-layouts  3.89 us
  transfers between devices with their start and end apart: 11, of which 5 were waited for; matrix products, arithmetic and copies ran while one was open for 1% of the time, Pallas kernels for 0%

profile of v1, /device:TPU:0, one launch (start us, length us, event | category | flops | bytes accessed | tf_op | source)
XLA Modules:
  0.0 144.7 jit_solution(17783893835089002052)
XLA Ops:
  0.6 0.0 copy-start
  0.6 3.4 %copy-done = f32[4,64,64,128]{3,2,1,0:T(8,128)S(1)} copy-done((f32[4,64,64,128]{3,2,1,0:T(8,128)S(1)}, f32[4,64,64,128]{3,2,1,0:T(8,128)}, u32[]{:S(2)}) %copy-start) | copy-done | bytes 8388632
  4.0 0.0 copy-start.1
  4.0 0.0 copy-start.2
  4.0 0.0 copy-start.4
  4.0 0.0 copy-start.5
  4.0 7.3 %pack_faces.1 = (bf16[4,64,128]{2,1,0:T(8,128)(2,1)S(1)}, bf16[4,64,128]{2,1,0:T(8,128)(2,1)S(1)}, bf16[4,64,128]{2,1,0:T(8,128)(2,1)S(1)}, bf16[4,64,128]{2,1,0:T(8,128)(2,1)S(1)}, bf16[4,64,128]{2,1,0:T(8,128)(2,1)S(1)}) custom-call(f32[4,64,64,128]{3,2,1,0:T(8,128)S(1)} %copy-done), custom_call_target="tpu_custom_call" | custom-call | flops 8388608 | bytes 8388608 | tf_op jit(solution)/shard_map/pack_faces/pallas_call | solution.py:203
  11.3 4.8 %collective-permute-start = (bf16[4,64,128]{2,1,0:T(8,128)(2,1)S(1)}, bf16[4,64,128]{2,1,0:T(8,128)(2,1)S(1)}, u32[]{:S(2)}, u32[]{:S(2)}) collective-permute-start(bf16[4,64,128]{2,1,0:T(8,128)(2,1)S(1)} %get-tuple-element.15), channel_id=1, source_target_pairs={{0,8},{8,16},{16,24},{1,9},{9,17},{17,25},{2,10},{10,18},{18,26},{... | collective-permute-start | bytes 196616 | tf_op jit(solution)/shard_map/ppermute | solution.py:272
  16.2 1.3 collective-permute-start.1
  17.5 3.5 %collective-permute-start.2 = (bf16[4,64,128]{2,1,0:T(8,128)(2,1)S(1)}, bf16[4,64,128]{2,1,0:T(8,128)(2,1)S(1)}, u32[]{:S(2)}, u32[]{:S(2)}) collective-permute-start(bf16[4,64,128]{2,1,0:T(8,128)(2,1)S(1)} %get-tuple-element.17), channel_id=1, source_target_pairs={{0,2},{2,4},{4,6},{1,3},{3,5},{5,7},{8,10},{10,12},{12,14},{9,11},... | collective-permute-start | bytes 196616 | tf_op jit(solution)/shard_map/ppermute | solution.py:272
  21.0 1.3 collective-permute-start.3
  22.3 0.1 collective-permute-start.4
  22.3 0.0 collective-permute-done.refs_8_
  22.3 0.0 collective-permute-done.1.refs_9_
  22.4 0.5 collective-permute-done.2.refs_10_
  22.8 4.3 %collective-permute-done.3.refs_11_ = bf16[4,64,128]{2,1,0:T(8,128)(2,1)S(1)} collective-permute-done((bf16[4,64,128]{2,1,0:T(8,128)(2,1)S(1)}, bf16[4,64,128]{2,1,0:T(8,128)(2,1)S(1)}, u32[]{:S(2)}, u32[]{:S(2)}) %collective-permute-start.3) | collective-permute-done | bytes 65568 | tf_op jit(solution)/shard_map/ppermute | solution.py:273
  27.1 0.0 collective-permute-done.4.refs_12_.refs_13_
  27.1 0.0 copy-done.1
  27.1 0.0 copy-done.2
  27.1 0.0 copy-done.3
  27.1 0.0 copy-done.4
  27.1 0.0 copy-done.5
  27.2 22.9 %sweep_first.1 = (f32[4,64,64,128]{3,2,1,0:T(8,128)S(1)}, bf16[4,64,128]{2,1,0:T(8,128)(2,1)S(1)}, bf16[4,64,128]{2,1,0:T(8,128)(2,1)S(1)}, bf16[4,64,128]{2,1,0...) custom-call(f32[4]{0:T(128)S(1)} %copy-done.3, f32[4]{0:T(128)S(1)} %copy-done.4, ...), custom_call_target="tpu_custom_call" | custom-call | flops 50331648 | bytes 23068672 | tf_op jit(solution)/shard_map/sweep_first/pallas_call | solution.py:252
  50.1 4.5 %collective-permute-start.5 = (bf16[4,64,128]{2,1,0:T(8,128)(2,1)S(1)}, bf16[4,64,128]{2,1,0:T(8,128)(2,1)S(1)}, u32[]{:S(2)}, u32[]{:S(2)}) collective-permute-start(bf16[4,64,128]{2,1,0:T(8,128)(2,1)S(1)} %get-tuple-element.21), channel_id=1, source_target_pairs={{0,8},{8,16},{16,24},{1,9},{9,17},{17,25},{2,10},{10,18},{18,26},{... | collective-permute-start | bytes 196616 | tf_op jit(solution)/shard_map/ppermute | solution.py:272
  54.7 1.3 collective-permute-start.6
  56.0 3.5 %collective-permute-start.7 = (bf16[4,64,128]{2,1,0:T(8,128)(2,1)S(1)}, bf16[4,64,128]{2,1,0:T(8,128)(2,1)S(1)}, u32[]{:S(2)}, u32[]{:S(2)}) collective-permute-start(bf16[4,64,128]{2,1,0:T(8,128)(2,1)S(1)} %get-tuple-element.23), channel_id=1, source_target_pairs={{0,2},{2,4},{4,6},{1,3},{3,5},{5,7},{8,10},{10,12},{12,14},{9,11},... | collective-permute-start | bytes 196616 | tf_op jit(solution)/shard_map/ppermute | solution.py:272
  59.4 1.3 collective-permute-start.8
  60.7 0.1 collective-permute-start.9
  60.8 0.0 collective-permute-done.5.refs_8_
  60.8 0.4 collective-permute-done.6.refs_9_
  61.2 0.1 collective-permute-done.7.refs_10_
  61.3 4.3 %collective-permute-done.8.refs_11_ = bf16[4,64,128]{2,1,0:T(8,128)(2,1)S(1)} collective-permute-done((bf16[4,64,128]{2,1,0:T(8,128)(2,1)S(1)}, bf16[4,64,128]{2,1,0:T(8,128)(2,1)S(1)}, u32[]{:S(2)}, u32[]{:S(2)}) %collective-permute-start.8) | collective-permute-done | bytes 65568 | tf_op jit(solution)/shard_map/ppermute | solution.py:273
  65.6 0.0 collective-permute-done.9.refs_12_.refs_13_
  65.6 19.8 %sweep_last.1 = (f32[4,64,64,128]{3,2,1,0:T(8,128)}, f32[32,128]{1,0:T(8,128)S(1)}) custom-call(f32[4]{0:T(128)S(1)} %copy-done.3, f32[4]{0:T(128)S(1)} %copy-done.4, f32[4]{0:T(128)S(1)} %copy-done.5, f32[4,64,64,128]{3,2,1,0:T(8,128)S(1)} %get-tuple-element.20.refs_3_.refs_4_.refs_5_, f32[4,64,64,128]{3,2,1,0:T(8,128)S(1)} %get-tuple-element.20.refs_3_.refs_4_.refs_5_, ...), custom_call_target="tpu_custom_call" | custom-call | flops 50331648 | bytes 23068672 | tf_op jit(solution)/shard_map/sweep_last/pallas_call | solution.py:252
  85.4 1.8 %all-gather = f32[64,128]{1,0:T(8,128)S(1)} all-gather(f32[32,128]{1,0:T(8,128)S(1)} %get-tuple-element.27), channel_id=2, replica_groups=mesh['gx'=4,'gy'=4,'gz'=2] {'gz'}, dimensions={0}, use_global_device_ids=true | all-gather | bytes 49152 | tf_op jit(solution)/shard_map/all_gather | solution.py:375
  87.3 0.7 broadcast_in_dim.2
  88.0 6.9 %all-to-all-start = ((f32[16,32,128]{2,1,0:T(8,128)}), f32[16,32,128]{2,1,0:T(8,128)S(1)}, u32[]{:S(2)}, u32[]{:S(2)}) async-start(f32[16,32,128]{2,1,0:T(8,128)} %broadcast_in_dim.2), calls=%async_computation | async-start | bytes 524288 | tf_op jit(solution)/shard_map/all_to_all | solution.py:377
  94.9 0.0 copy-done.7
  94.9 0.1 copy.16
  95.0 0.0 copy-done.6
  95.0 0.1 copy.15
  95.1 0.1 maximum_bitcast_fusion
  95.2 46.0 %all-gather.2 = f32[16,65,64]{1,2,0:T(8,128)S(1)} all-gather(f32[1,65,64]{1,2,0:T(8,128)S(1)} %maximum_bitcast_fusion), channel_id=3, replica_groups=mesh['gx'=4,'gy'=4,'gz'=2] {'gx','gy'}, dimensions={0}, use_global_device_ids=true | all-gather | bytes 282880 | tf_op jit(solution)/shard_map/all_gather | solution.py:371
  141.1 0.2 slice.9
  141.3 0.2 copy.20
  141.5 0.2 copy.19.den_ref
  141.8 0.0 all-to-all-done.sens_ref
  141.8 2.9 %plane.1 = f32[1,16,512]{2,1,0:T(8,128)} custom-call(s32[1]{0:T(128)} %bitcast.me_ref, f32[16,32,128]{2,1,0:T(8,128)S(1)} %all-to-all-done.sens_ref, f32[16,64,64]{2,1,0:T(8,128)S(1)} %copy.19.den_ref, f32[16,64]{1,0:T(8,128)S(1)} %bitcast.8), custom_call_target="tpu_custom_call" | custom-call | tf_op jit(solution)/shard_map/plane/pallas_call | solution.py:380
  (5 shorter events, 0.0 us)
Async XLA Ops:
  0.6 3.4 %copy-start = (f32[4,64,64,128]{3,2,1,0:T(8,128)S(1)}, f32[4,64,64,128]{3,2,1,0:T(8,128)}, u32[]{:S(2)}) copy-start(f32[4,64,64,128]{3,2,1,0:T(8,128)} %refs_5_.1) | copy-start | bytes 25165828
  4.0 23.1 %copy-start.1 = (bf16[4,64,64,128]{3,2,1,0:T(8,128)(2,1)S(1)}, bf16[4,64,64,128]{3,2,1,0:T(8,128)(2,1)}, u32[]{:S(2)}) copy-start(bf16[4,64,64,128]{3,2,1,0:T(8,128)(2,1)} %refs_6_.3) | copy-start | bytes 12582916
  4.0 23.1 %copy-start.2 = (s32[64,64,128]{2,1,0:T(8,128)S(1)}, s32[64,64,128]{2,1,0:T(8,128)}, u32[]{:S(2)}) copy-start(s32[64,64,128]{2,1,0:T(8,128)} %refs_7_.3) | copy-start | bytes 6291460
  4.0 23.1 %copy-start.3 = (f32[4]{0:T(128)S(1)}, f32[4]{0:T(128)}, u32[]{:S(2)}) copy-start(f32[4]{0:T(128)} %refs_0_.3) | copy-start | bytes 52
  4.0 23.1 %copy-start.4 = (f32[4]{0:T(128)S(1)}, f32[4]{0:T(128)}, u32[]{:S(2)}) copy-start(f32[4]{0:T(128)} %refs_1_.3) | copy-start | bytes 52
  4.0 23.1 %copy-start.5 = (f32[4]{0:T(128)S(1)}, f32[4]{0:T(128)}, u32[]{:S(2)}) copy-start(f32[4]{0:T(128)} %refs_2_.3) | copy-start | bytes 52
  11.3 11.0 %collective-permute-start = (bf16[4,64,128]{2,1,0:T(8,128)(2,1)S(1)}, bf16[4,64,128]{2,1,0:T(8,128)(2,1)S(1)}, u32[]{:S(2)}, u32[]{:S(2)}) collective-permute-start(bf16[4,64,128]{2,1,0:T(8,128)(2,1)S(1)} %get-tuple-element.15), channel_id=1, source_target_pairs={{0,8},{8,16},{16,24},{1,9},{9,17},{17,25},{2,10},{10,18},{18,26},{... | collective-permute-start | bytes 196616 | tf_op jit(solution)/shard_map/ppermute | solution.py:272
  16.2 6.2 %collective-permute-start.1 = (bf16[4,64,128]{2,1,0:T(8,128)(2,1)S(1)}, bf16[4,64,128]{2,1,0:T(8,128)(2,1)S(1)}, u32[]{:S(2)}, u32[]{:S(2)}) collective-permute-start(bf16[4,64,128]{2,1,0:T(8,128)(2,1)S(1)} %get-tuple-element.16), channel_id=1, source_target_pairs={{8,0},{16,8},{24,16},{9,1},{17,9},{25,17},{10,2},{18,10},{26,18},{... | collective-permute-start | bytes 196616 | tf_op jit(solution)/shard_map/ppermute | solution.py:273
  17.5 5.4 %collective-permute-start.2 = (bf16[4,64,128]{2,1,0:T(8,128)(2,1)S(1)}, bf16[4,64,128]{2,1,0:T(8,128)(2,1)S(1)}, u32[]{:S(2)}, u32[]{:S(2)}) collective-permute-start(bf16[4,64,128]{2,1,0:T(8,128)(2,1)S(1)} %get-tuple-element.17), channel_id=1, source_target_pairs={{0,2},{2,4},{4,6},{1,3},{3,5},{5,7},{8,10},{10,12},{12,14},{9,11},... | collective-permute-start | bytes 196616 | tf_op jit(solution)/shard_map/ppermute | solution.py:272
  21.0 6.2 %collective-permute-start.3 = (bf16[4,64,128]{2,1,0:T(8,128)(2,1)S(1)}, bf16[4,64,128]{2,1,0:T(8,128)(2,1)S(1)}, u32[]{:S(2)}, u32[]{:S(2)}) collective-permute-start(bf16[4,64,128]{2,1,0:T(8,128)(2,1)S(1)} %get-tuple-element.18), channel_id=1, source_target_pairs={{2,0},{4,2},{6,4},{3,1},{5,3},{7,5},{10,8},{12,10},{14,12},{11,9},... | collective-permute-start | bytes 196616 | tf_op jit(solution)/shard_map/ppermute | solution.py:273
  22.3 4.9 %collective-permute-start.4 = (bf16[4,64,128]{2,1,0:T(8,128)(2,1)S(1)}, bf16[4,64,128]{2,1,0:T(8,128)(2,1)S(1)}, u32[]{:S(2)}, u32[]{:S(2)}) collective-permute-start(bf16[4,64,128]{2,1,0:T(8,128)(2,1)S(1)} %get-tuple-element.19), channel_id=1, source_target_pairs={{0,1},{1,0},{2,3},{3,2},{4,5},{5,4},{6,7},{7,6},{8,9},{9,8},{10,11... | collective-permute-start | bytes 196616 | tf_op jit(solution)/shard_map/ppermute | solution.py:276
  50.1 10.7 %collective-permute-start.5 = (bf16[4,64,128]{2,1,0:T(8,128)(2,1)S(1)}, bf16[4,64,128]{2,1,0:T(8,128)(2,1)S(1)}, u32[]{:S(2)}, u32[]{:S(2)}) collective-permute-start(bf16[4,64,128]{2,1,0:T(8,128)(2,1)S(1)} %get-tuple-element.21), channel_id=1, source_target_pairs={{0,8},{8,16},{16,24},{1,9},{9,17},{17,25},{2,10},{10,18},{18,26},{... | collective-permute-start | bytes 196616 | tf_op jit(solution)/shard_map/ppermute | solution.py:272
  54.7 6.5 %collective-permute-start.6 = (bf16[4,64,128]{2,1,0:T(8,128)(2,1)S(1)}, bf16[4,64,128]{2,1,0:T(8,128)(2,1)S(1)}, u32[]{:S(2)}, u32[]{:S(2)}) collective-permute-start(bf16[4,64,128]{2,1,0:T(8,128)(2,1)S(1)} %get-tuple-element.22), channel_id=1, source_target_pairs={{8,0},{16,8},{24,16},{9,1},{17,9},{25,17},{10,2},{18,10},{26,18},{... | collective-permute-start | bytes 196616 | tf_op jit(solution)/shard_map/ppermute | solution.py:273
  56.0 5.4 %collective-permute-start.7 = (bf16[4,64,128]{2,1,0:T(8,128)(2,1)S(1)}, bf16[4,64,128]{2,1,0:T(8,128)(2,1)S(1)}, u32[]{:S(2)}, u32[]{:S(2)}) collective-permute-start(bf16[4,64,128]{2,1,0:T(8,128)(2,1)S(1)} %get-tuple-element.23), channel_id=1, source_target_pairs={{0,2},{2,4},{4,6},{1,3},{3,5},{5,7},{8,10},{10,12},{12,14},{9,11},... | collective-permute-start | bytes 196616 | tf_op jit(solution)/shard_map/ppermute | solution.py:272
  59.4 6.2 %collective-permute-start.8 = (bf16[4,64,128]{2,1,0:T(8,128)(2,1)S(1)}, bf16[4,64,128]{2,1,0:T(8,128)(2,1)S(1)}, u32[]{:S(2)}, u32[]{:S(2)}) collective-permute-start(bf16[4,64,128]{2,1,0:T(8,128)(2,1)S(1)} %get-tuple-element.24), channel_id=1, source_target_pairs={{2,0},{4,2},{6,4},{3,1},{5,3},{7,5},{10,8},{12,10},{14,12},{11,9},... | collective-permute-start | bytes 196616 | tf_op jit(solution)/shard_map/ppermute | solution.py:273
  60.7 4.9 %collective-permute-start.9 = (bf16[4,64,128]{2,1,0:T(8,128)(2,1)S(1)}, bf16[4,64,128]{2,1,0:T(8,128)(2,1)S(1)}, u32[]{:S(2)}, u32[]{:S(2)}) collective-permute-start(bf16[4,64,128]{2,1,0:T(8,128)(2,1)S(1)} %get-tuple-element.25), channel_id=1, source_target_pairs={{0,1},{1,0},{2,3},{3,2},{4,5},{5,4},{6,7},{7,6},{8,9},{9,8},{10,11... | collective-permute-start | bytes 196616 | tf_op jit(solution)/shard_map/ppermute | solution.py:276
  65.6 29.3 %copy-start.7 = (s32[1,1,64,1]{2,3,1,0:T(1,128)S(1)}, s32[1,1,64,1]{2,3,1,0:T(1,128)}, u32[]{:S(2)}) copy-start(s32[1,1,64,1]{2,3,1,0:T(1,128)} %param.15) | copy-start | bytes 772
  65.6 29.4 %copy-start.6 = (f32[64,64]{1,0:T(8,128)S(1)}, f32[64,64]{1,0:T(8,128)}, u32[]{:S(2)}) copy-start(f32[64,64]{1,0:T(8,128)} %param.14) | copy-start | bytes 49156
  88.0 53.8 %all-to-all-start = ((f32[16,32,128]{2,1,0:T(8,128)}), f32[16,32,128]{2,1,0:T(8,128)S(1)}, u32[]{:S(2)}, u32[]{:S(2)}) async-start(f32[16,32,128]{2,1,0:T(8,128)} %broadcast_in_dim.2), calls=%async_computation | async-start | bytes 524288 | tf_op jit(solution)/shard_map/all_to_all | solution.py:377

commit v2 on v1

--- a/solution.py
+++ b/solution.py
@@ -15,6 +15,7 @@
 SHARPNESS = 8.0
 THRESHOLD = 0.5
 XB = 16
+PB = 8
 F32 = jnp.float32
 BF16 = jnp.bfloat16
 
@@ -23,27 +24,67 @@
     return lax.broadcasted_iota(jnp.int32, shape, len(shape) - 1)
 
 
-def put_faces(c, x, xx, new, gs, ylo, yhi):
-    ylo[c, pl.ds(xx, 1), :] = new[0:1, :]
-    yhi[c, pl.ds(xx, 1), :] = new[-1:, :]
-    turned = pltpu.roll(new, 2 * x + 1, 1)
-    gs[c] = jnp.where(lanes_of(new.shape) // 2 == x, turned, gs[c])
-
-
-def pack_kernel(v_ref, xlo_ref, xhi_ref, ylo_ref, yhi_ref, g_ref, gs, ylo, yhi):
+def put_faces(first, xx, ref, ends, gs, ylo, yhi):
+    rows, depth = ref.shape[2:]
+    value = ref[:, pl.ds(xx, PB)]
+    for p in range(PB):
+        for c in range(4):
+            ylo[c, pl.ds(xx + p, 1), :] = value[c, p, 0:1, :]
+            yhi[c, pl.ds(xx + p, 1), :] = value[c, p, rows - 1 :, :]
+    picked = mm(value.astype(BF16).reshape(4 * PB * rows, depth), ends).reshape(4, PB, rows, depth)
+    pair = lanes_of((rows, depth)) // 2
+    for c in range(4):
+        g = gs[c]
+        for p in range(PB):
+            g = jnp.where(pair == first + xx + p, picked[c, p], g)
+        gs[c] = g
+
+
+def ends_matrix(depth):
+    z = lax.broadcasted_iota(jnp.int32, (depth, depth), 0)
+    j = lax.broadcasted_iota(jnp.int32, (depth, depth), 1)
+    even = (z == 0) & (j % 2 == 0)
+    odd = (z == depth - 1) & (j % 2 == 1)
+    return jnp.where(even | odd, 1.0, 0.0).astype(BF16)
+
+
+def beside_matrix(depth):
+    z = lax.broadcasted_iota(jnp.int32, (depth, depth), 0)
+    j = lax.broadcasted_iota(jnp.int32, (depth, depth), 1)
+    return jnp.where(jnp.abs(z - j) == 1, 1.0, 0.0).astype(BF16)
+
+
+def halo_matrix(depth):
+    j = lax.broadcasted_iota(jnp.int32, (depth, depth), 0)
+    z = lax.broadcasted_iota(jnp.int32, (depth, depth), 1)
+    even = (z == 0) & (j % 2 == 0)
+    odd = (z == depth - 1) & (j % 2 == 1)
+    return jnp.where(even | odd, 1.0, 0.0).astype(BF16)
+
+
+def split(value):
+    high = value.astype(BF16)
+    return high, (value - high.astype(F32)).astype(BF16)
+
+
+def mm(a, b):
+    return lax.dot_general(a, b, (((1,), (0,)), ((), ())), preferred_element_type=F32)
+
+
+def pack_kernel(v_ref, xlo_ref, xhi_ref, ylo_ref, yhi_ref, g_ref, gs, ylo, yhi, ends):
     step, steps = pl.program_id(0), pl.num_programs(0)
 
     @pl.when(step == 0)
     def _():
         gs[...] = jnp.zeros_like(gs)
+        ends[...] = ends_matrix(v_ref.shape[3])
         xlo_ref[...] = v_ref[:, 0].astype(BF16)
 
-    def plane(xx, carry):
-        for c in range(4):
-            put_faces(c, step * XB + xx, xx, v_ref[c, xx], gs, ylo, yhi)
+    def planes(i, carry):
+        put_faces(step * XB, i * PB, v_ref, ends[...], gs, ylo, yhi)
         return carry
 
-    lax.fori_loop(0, XB, plane, 0)
+    lax.fori_loop(0, XB // PB, planes, 0)
     ylo_ref[...] = ylo[...].astype(BF16)
     yhi_ref[...] = yhi[...].astype(BF16)
 
@@ -57,9 +98,9 @@
     (sr_ref, si_ref, sh_ref, v_ref, vp_ref, vn_ref, s_ref, m_ref, xl_ref, xr_ref,
      yl_ref, yr_ref, gl_ref, gr_ref) = refs[:14]
     if last:
-        o_ref, sens_ref, hs, yl, yr, sens = refs[14:]
+        o_ref, sens_ref, hs, yl, yr, near, far, zt, sens, value = refs[14:]
     else:
-        o_ref, xlo_ref, xhi_ref, ylo_ref, yhi_ref, g_ref, hs, yl, yr, gs, ylo, yhi = refs[14:]
+        o_ref, xlo_ref, xhi_ref, ylo_ref, yhi_ref, g_ref, hs, yl, yr, near, far, zt, gs, ylo, yhi, ends = refs[14:]
     step, steps = pl.program_id(0), pl.num_programs(0)
     rows, depth = v_ref.shape[2:]
     lane = lanes_of((rows, depth))
@@ -72,13 +113,16 @@
         else:
             keep_l, keep_r = 1.0, 1.0
         for c in range(4):
-            left = pltpu.roll(gl_ref[c].astype(F32), 1, 1) * keep_l
-            right = pltpu.roll(gr_ref[c].astype(F32), depth - 1, 1) * keep_r
-            hs[c] = jnp.where(lane % 2 == 1, left, right)
+            left = pltpu.roll(gl_ref[c].astype(F32), depth - 1, 1) * keep_l
+            right = pltpu.roll(gr_ref[c].astype(F32), 1, 1) * keep_r
+            hs[c] = jnp.where(lane % 2 == 0, left, right)
+        near[...] = jnp.concatenate([beside_matrix(depth)] * 2, 0)
+        far[...] = halo_matrix(depth)
         if last:
             sens[...] = jnp.zeros_like(sens)
         else:
             gs[...] = jnp.zeros_like(gs)
+            ends[...] = ends_matrix(depth)
 
     yl[...] = yl_ref[...].astype(F32)
     yr[...] = yr_ref[...].astype(F32)
@@ -103,7 +147,17 @@
 
     row8 = lax.broadcasted_iota(jnp.int32, tile, 0)
 
-    def plane(xx, before, after):
+    def along_z(xx):
+        v = v_ref[:, pl.ds(xx, PB)].reshape(4 * PB * rows, depth)
+        masked = [
+            jnp.where(lane // 2 == step * XB + xx + p, hs[c], 0.0).astype(BF16)
+            for c in range(4)
+            for p in range(PB)
+        ]
+        out = mm(jnp.concatenate(split(v), 1), near[...]) + mm(jnp.concatenate(masked, 0), far[...])
+        zt[...] = out.reshape(4, PB, rows, depth)
+
+    def plane(xx, slot, before, after):
         x = step * XB + xx
         mat = m_ref[xx].reshape(rows // 8, 8, depth)
         masks = [mat == m for m in range(1, levels)]
@@ -117,9 +171,7 @@
             top = jnp.where(row8 == 0, yl[c, pl.ds(xx, 1), :], up[:8])
             low = jnp.where(row8 == 7, yr[c, pl.ds(xx, 1), :], down[-8:])
             total = total + jnp.concatenate([top, up[8:]], 0) + jnp.concatenate([down[:-8], low], 0)
-            h = pltpu.roll(hs[c], depth - 1 - 2 * x, 1)
-            total = total + jnp.where(lane == 0, h, pltpu.roll(v, 1, 1))
-            return v, total + jnp.where(lane == depth - 1, h, pltpu.roll(v, depth - 1, 1))
+            return v, total + zt[c, slot]
 
         news = []
         for re in (0, 2):
@@ -130,32 +182,49 @@
             n_i = keep * v_i + (w_r * t_i + w_i * t_r)
             o_ref[re, xx] = n_r
             o_ref[re + 1, xx] = n_i
-            if last:
-                news += [n_r, n_i]
-            else:
-                put_faces(re, x, xx, n_r, gs, ylo, yhi)
-                put_faces(re + 1, x, xx, n_i, gs, ylo, yhi)
+            news += [n_r, n_i]
         if last:
-            value = lookup(masks, share) * (news[0] * news[2] - news[1] * news[3])
-            column = jnp.sum(value, axis=1, keepdims=True)
-            sens[...] = jnp.where(lane == x, column, sens[...])
-
-    plane(
-        0,
-        lambda c: jnp.where(step == 0, xl_ref[c].astype(F32), vp_ref[c, 0]),
-        lambda c: v_ref[c, 1],
-    )
-
-    def middle(xx, carry):
-        plane(xx, lambda c: v_ref[c, xx - 1], lambda c: v_ref[c, xx + 1])
+            value[slot] = lookup(masks, share) * (news[0] * news[2] - news[1] * news[3])
+
+    def before(xx):
+        return lambda c: v_ref[c, xx - 1]
+
+    def after(xx):
+        return lambda c: v_ref[c, xx + 1]
+
+    def first(c):
+        return jnp.where(step == 0, xl_ref[c].astype(F32), vp_ref[c, 0])
+
+    def final(c):
+        return jnp.where(step == steps - 1, xr_ref[c].astype(F32), vn_ref[c, 0])
+
+    def planes(xx, start=False, end=False):
+        along_z(xx)
+        for p in range(PB):
+            plane(
+                xx + p,
+                p,
+                first if start and p == 0 else before(xx + p),
+                final if end and p == PB - 1 else after(xx + p),
+            )
+        if last:
+            ones = jnp.ones((2 * depth, depth), BF16)
+            parts = split(value[...].reshape(PB * rows, depth))
+            sums = mm(jnp.concatenate(parts, 1), ones).reshape(PB, rows, depth)
+            held = sens[...]
+            for p in range(PB):
+                held = jnp.where(lane == step * XB + xx + p, sums[p], held)
+            sens[...] = held
+        else:
+            put_faces(step * XB, xx, o_ref, ends[...], gs, ylo, yhi)
+
+    def middle(i, carry):
+        planes(i * PB)
         return carry
 
-    lax.fori_loop(1, XB - 1, middle, 0)
-    plane(
-        XB - 1,
-        lambda c: v_ref[c, XB - 2],
-        lambda c: jnp.where(step == steps - 1, xr_ref[c].astype(F32), vn_ref[c, 0]),
-    )
+    planes(0, start=True)
+    lax.fori_loop(1, XB // PB - 1, middle, 0)
+    planes(XB - PB, end=True)
     if not last:
         ylo_ref[...] = ylo[...].astype(BF16)
         yhi_ref[...] = yhi[...].astype(BF16)
@@ -194,6 +263,7 @@
         pltpu.VMEM((4, ny, nz), F32),
         pltpu.VMEM((4, XB, nz), F32),
         pltpu.VMEM((4, XB, nz), F32),
+        pltpu.VMEM((nz, nz), BF16),
     ]
 
 
@@ -238,12 +308,15 @@
         pltpu.VMEM((4, ny, nz), F32),
         pltpu.VMEM((4, XB, nz), F32),
         pltpu.VMEM((4, XB, nz), F32),
+        pltpu.VMEM((2 * nz, nz), BF16),
+        pltpu.VMEM((nz, nz), BF16),
+        pltpu.VMEM((4, PB, ny, nz), F32),
     ]
     shapes, specs = [jax.ShapeDtypeStruct(current.shape, F32)], [block]
     if last:
         shapes.append(jax.ShapeDtypeStruct((ny // 2, nz), F32))
         specs.append(whole((ny // 2, nz)))
-        scratch.append(pltpu.VMEM((ny, nz), F32))
+        scratch += [pltpu.VMEM((ny, nz), F32), pltpu.VMEM((PB, ny, nz), F32)]
     else:
         more_shapes, more_specs = face_outs(nx, ny, nz)
         shapes += more_shapes
@@ -279,16 +352,7 @@
     return out + [lax.ppermute(g, "gz", up), lax.ppermute(g, "gz", [(j, i) for i, j in up])]
 
 
-def split(value):
-    high = value.astype(BF16)
-    return high, (value - high.astype(F32)).astype(BF16)
-
-
-def mm(a, b):
-    return lax.dot_general(a, b, (((1,), (0,)), ((), ())), preferred_element_type=F32)
-
-
-def plane_kernel(ngx, ngy, scale, me_ref, sens_ref, den_ref, own_ref, out_ref, w_ref, d_ref):
+def plane_kernel(ngx, ngy, scale, me_ref, got_ref, out_ref, w_ref, d_ref):
     cells = 64
     nx, ny = ngx * cells, ngy * cells
     columns = ngx * ngy
@@ -297,10 +361,13 @@
         for cy in range(ngy):
             c = cx * ngy + cy
             for part in range(2):
-                w_ref[pl.ds(cy * cells + part * half, half), pl.ds(cx * cells, cells)] = sens_ref[
-                    c, :, pl.ds(part * cells, cells)
+                lanes = pl.ds(part * cells, cells)
+                w_ref[pl.ds(cy * cells + part * half, half), pl.ds(cx * cells, cells)] = got_ref[
+                    c, pl.ds(0, half), lanes
                 ]
-            d_ref[pl.ds(cx * cells, cells), pl.ds(cy * cells, cells)] = den_ref[c]
+                d_ref[pl.ds(cx * cells + part * half, half), pl.ds(cy * cells, cells)] = got_ref[
+                    c, pl.ds(half, half), lanes
+                ]
 
     def band(n):
         i = lax.broadcasted_iota(jnp.int32, (n, n), 0)
@@ -325,8 +392,9 @@
     slope = SHARPNESS * (1.0 - tangent * tangent) / total
     weighted = twice(slope * w_ref[...] * scale, band_x)
 
-    tiles = own_ref.shape[1]
-    mine = own_ref[...] == me_ref[0].astype(F32)
+    tiles = cells
+    owner = jnp.concatenate([got_ref[c, pl.ds(2 * half, 1), pl.ds(0, tiles)] for c in range(columns)], 0)
+    mine = owner == me_ref[0].astype(F32)
     flag = jnp.where(mine, 1.0, 0.0)
     a = lax.broadcasted_iota(jnp.int32, (tiles, tiles), 0)
     b = lax.broadcasted_iota(jnp.int32, (tiles, tiles), 1)
@@ -367,12 +435,14 @@
     columns = ngx * ngy
     cells = density.shape[0]
     tables = (shift_real, shift_imag, design_share)
-    known = jnp.concatenate([density, owner_map.reshape(1, -1).astype(F32)], 0)
-    known = lax.all_gather(known, ("gx", "gy"))
+    half = cells // 2
+    packed = jnp.concatenate([density[:half], density[half:]], 1)
+    owners = jnp.pad(owner_map.reshape(1, -1).astype(F32), ((0, 7), (0, cells)))
     halos = exchange(*pack(fields))
     middle, *faces = sweep(False, tables, fields, sources, material, halos)
     final, partial = sweep(True, tables, middle, sources, material, exchange(*faces))
     partial = jnp.sum(lax.all_gather(partial, "gz"), 0)
+    partial = jnp.concatenate([partial, packed, owners], 0)
     copies = jnp.broadcast_to(partial[None], (columns, *partial.shape))
     plane = lax.all_to_all(copies, ("gx", "gy"), split_axis=0, concat_axis=0)
     me = (lax.axis_index("gx") * ngy + lax.axis_index("gy")).reshape(1)
@@ -381,7 +451,7 @@
         functools.partial(
             plane_kernel, ngx, ngy, 1.0 / math.sqrt(material.shape[2] * ngz)
         ),
-        in_specs=[SMEM_SPEC, vmem, vmem, vmem],
+        in_specs=[SMEM_SPEC, vmem],
         out_specs=vmem,
         out_shape=jax.ShapeDtypeStruct((1, columns, MOST * TS * TS), F32),
         scratch_shapes=[
@@ -390,7 +460,7 @@
         ],
         compiler_params=pltpu.CompilerParams(vmem_limit_bytes=32 << 20),
         name="plane",
-    )(me, plane, known[:, :cells], known[:, cells])
+    )(me, plane)
     return (final, owned)
 
 

time: 145 us -> 92 us (0.63)
  blocking collectives: 47.8 us -> 1.82 us
  Pallas kernels: 52.9 us -> 28.5 us
  waiting for transfers between devices: 9.54 us -> 27.4 us
    all_gather x1 -> x0, blocking collectives: 46 us -> none  [on_device(): known = lax.all_gather(known, ('gx', 'gy'))]
    pallas_call x2, Pallas kernels: 42.8 us -> 22.6 us  [sweep(): pl.pallas_call(functools.partial(sweep_kernel, last, lax.axis_size('gz'))...]
    all_to_all x1, waiting for transfers between devices: 0.01 us -> 17.9 us  [on_device(): plane = lax.all_to_all(copies, ('gx', 'gy'), split_axis=0, concat_axis=0)]
    pallas_call x1, Pallas kernels: 7.26 us -> 2.98 us  [pack(): pl.pallas_call(pack_kernel, grid=(nx // XB,), in_specs=[pl.BlockSpec((4,...]
    unnamed x19 -> x16, local copies, waits for them, and re-layouts: 3.89 us -> 3.41 us
  transfers between devices with their start and end apart: 11 -> 11, of which waited for: 5 -> 6; matrix products, arithmetic and copies ran while one was open for 1% -> 0% of each run, Pallas kernels for 0% -> 0%
where the time goes in v2:
time: 92 us; the launch traced here: 91.5 us
  starting transfers between devices  28.6 us (31%)
  Pallas kernels  28.5 us (31%)
  waiting for transfers between devices  27.4 us (30%)
  local copies, waits for them, and re-layouts  4.28 us (5%)
  blocking collectives  1.82 us (2%)
    pallas_call x2, Pallas kernels, sweep(): pl.pallas_call(functools.partial(sweep_kernel, last, lax.axis_size('gz'))...  22.6 us
    all_to_all x1, waiting for transfers between devices, on_device(): plane = lax.all_to_all(copies, ('gx', 'gy'), split_axis=0, concat_axis=0)  17.9 us
    ppermute x4, starting transfers between devices, exchange(): out.append(lax.ppermute(high, axis, up))  16.4 us
    ppermute x4, waiting for transfers between devices, exchange(): out.append(lax.ppermute(low, axis, [(j, i) for i, j in up]))  8.88 us
    all_to_all x1, starting transfers between devices, on_device(): plane = lax.all_to_all(copies, ('gx', 'gy'), split_axis=0, concat_axis=0)  6.88 us
    ppermute x4, starting transfers between devices, exchange(): out.append(lax.ppermute(low, axis, [(j, i) for i, j in up]))  5.17 us
    unnamed x16, local copies, waits for them, and re-layouts  3.41 us
    pallas_call x1, Pallas kernels, pack(): pl.pallas_call(pack_kernel, grid=(nx // XB,), in_specs=[pl.BlockSpec((4,...  2.98 us
  transfers between devices with their start and end apart: 11, of which 6 were waited for; matrix products, arithmetic and copies ran while one was open for 0% of the time, Pallas kernels for 0%

profile of v2, /device:TPU:0, one launch (start us, length us, event | category | flops | bytes accessed | tf_op | source)
XLA Modules:
  0.0 91.5 jit_solution(13087794925290862610)
XLA Ops:
  0.6 0.0 copy-start
  0.6 3.4 %copy-done = f32[4,64,64,128]{3,2,1,0:T(8,128)S(1)} copy-done((f32[4,64,64,128]{3,2,1,0:T(8,128)S(1)}, f32[4,64,64,128]{3,2,1,0:T(8,128)}, u32[]{:S(2)}) %copy-start) | copy-done | bytes 8388632
  4.0 0.0 copy-start.6
  4.0 0.0 copy-start.1
  4.0 0.0 copy-start.2
  4.0 0.0 copy-start.3
  4.0 0.0 copy-start.4
  4.0 0.0 copy-start.5
  4.0 3.0 %pack_faces.1 = (bf16[4,64,128]{2,1,0:T(8,128)(2,1)S(1)}, bf16[4,64,128]{2,1,0:T(8,128)(2,1)S(1)}, bf16[4,64,128]{2,1,0:T(8,128)(2,1)S(1)}, bf16[4,64,128]{2,1,0:T(8,128)(2,1)S(1)}, bf16[4,64,128]{2,1,0:T(8,128)(2,1)S(1)}) custom-call(f32[4,64,64,128]{3,2,1,0:T(8,128)S(1)} %copy-done), custom_call_target="tpu_custom_call" | custom-call | flops 8388608 | bytes 8388608 | tf_op jit(solution)/shard_map/pack_faces/pallas_call | solution.py:273
  7.0 4.9 %collective-permute-start = (bf16[4,64,128]{2,1,0:T(8,128)(2,1)S(1)}, bf16[4,64,128]{2,1,0:T(8,128)(2,1)S(1)}, u32[]{:S(2)}, u32[]{:S(2)}) collective-permute-start(bf16[4,64,128]{2,1,0:T(8,128)(2,1)S(1)} %get-tuple-element.15), channel_id=1, source_target_pairs={{0,8},{8,16},{16,24},{1,9},{9,17},{17,25},{2,10},{10,18},{18,26},{... | collective-permute-start | bytes 196616 | tf_op jit(solution)/shard_map/ppermute | solution.py:345
  11.9 1.3 %collective-permute-start.1 = (bf16[4,64,128]{2,1,0:T(8,128)(2,1)S(1)}, bf16[4,64,128]{2,1,0:T(8,128)(2,1)S(1)}, u32[]{:S(2)}, u32[]{:S(2)}) collective-permute-start(bf16[4,64,128]{2,1,0:T(8,128)(2,1)S(1)} %get-tuple-element.16), channel_id=1, source_target_pairs={{8,0},{16,8},{24,16},{9,1},{17,9},{25,17},{10,2},{18,10},{26,18},{... | collective-permute-start | bytes 196616 | tf_op jit(solution)/shard_map/ppermute | solution.py:346
  13.2 3.5 %collective-permute-start.2 = (bf16[4,64,128]{2,1,0:T(8,128)(2,1)S(1)}, bf16[4,64,128]{2,1,0:T(8,128)(2,1)S(1)}, u32[]{:S(2)}, u32[]{:S(2)}) collective-permute-start(bf16[4,64,128]{2,1,0:T(8,128)(2,1)S(1)} %get-tuple-element.17), channel_id=1, source_target_pairs={{0,2},{2,4},{4,6},{1,3},{3,5},{5,7},{8,10},{10,12},{12,14},{9,11},... | collective-permute-start | bytes 196616 | tf_op jit(solution)/shard_map/ppermute | solution.py:345
  16.7 1.3 %collective-permute-start.3 = (bf16[4,64,128]{2,1,0:T(8,128)(2,1)S(1)}, bf16[4,64,128]{2,1,0:T(8,128)(2,1)S(1)}, u32[]{:S(2)}, u32[]{:S(2)}) collective-permute-start(bf16[4,64,128]{2,1,0:T(8,128)(2,1)S(1)} %get-tuple-element.18), channel_id=1, source_target_pairs={{2,0},{4,2},{6,4},{3,1},{5,3},{7,5},{10,8},{12,10},{14,12},{11,9},... | collective-permute-start | bytes 196616 | tf_op jit(solution)/shard_map/ppermute | solution.py:346
  18.0 0.1 collective-permute-start.4
  18.1 0.0 copy-done.6
  18.1 0.0 copy-start.7
  18.1 0.0 collective-permute-done.refs_8_
  18.1 0.0 collective-permute-done.1.refs_9_
  18.1 0.5 collective-permute-done.2.refs_10_
  18.6 4.3 %collective-permute-done.3.refs_11_ = bf16[4,64,128]{2,1,0:T(8,128)(2,1)S(1)} collective-permute-done((bf16[4,64,128]{2,1,0:T(8,128)(2,1)S(1)}, bf16[4,64,128]{2,1,0:T(8,128)(2,1)S(1)}, u32[]{:S(2)}, u32[]{:S(2)}) %collective-permute-start.3) | collective-permute-done | bytes 65568 | tf_op jit(solution)/shard_map/ppermute | solution.py:346
  22.8 0.0 collective-permute-done.4.refs_12_.refs_13_
  22.8 0.0 copy-done.1
  22.9 0.0 copy-done.2
  22.9 0.0 copy-done.3
  22.9 0.0 copy-done.4
  22.9 0.0 copy-done.5
  22.9 11.0 %sweep_first.1 = (f32[4,64,64,128]{3,2,1,0:T(8,128)S(1)}, bf16[4,64,128]{2,1,0:T(8,128)(2,1)S(1)}, bf16[4,64,128]{2,1,0:T(8,128)(2,1)S(1)}, bf16[4,64,128]{2,1,0...) custom-call(f32[4]{0:T(128)S(1)} %copy-done.3, f32[4]{0:T(128)S(1)} %copy-done.4, ...), custom_call_target="tpu_custom_call" | custom-call | flops 50331648 | bytes 23068672 | tf_op jit(solution)/shard_map/sweep_first/pallas_call | solution.py:325
  33.9 4.5 %collective-permute-start.5 = (bf16[4,64,128]{2,1,0:T(8,128)(2,1)S(1)}, bf16[4,64,128]{2,1,0:T(8,128)(2,1)S(1)}, u32[]{:S(2)}, u32[]{:S(2)}) collective-permute-start(bf16[4,64,128]{2,1,0:T(8,128)(2,1)S(1)} %get-tuple-element.21), channel_id=1, source_target_pairs={{0,8},{8,16},{16,24},{1,9},{9,17},{17,25},{2,10},{10,18},{18,26},{... | collective-permute-start | bytes 196616 | tf_op jit(solution)/shard_map/ppermute | solution.py:345
  38.5 1.3 %collective-permute-start.6 = (bf16[4,64,128]{2,1,0:T(8,128)(2,1)S(1)}, bf16[4,64,128]{2,1,0:T(8,128)(2,1)S(1)}, u32[]{:S(2)}, u32[]{:S(2)}) collective-permute-start(bf16[4,64,128]{2,1,0:T(8,128)(2,1)S(1)} %get-tuple-element.22), channel_id=1, source_target_pairs={{8,0},{16,8},{24,16},{9,1},{17,9},{25,17},{10,2},{18,10},{26,18},{... | collective-permute-start | bytes 196616 | tf_op jit(solution)/shard_map/ppermute | solution.py:346
  39.8 3.5 %collective-permute-start.7 = (bf16[4,64,128]{2,1,0:T(8,128)(2,1)S(1)}, bf16[4,64,128]{2,1,0:T(8,128)(2,1)S(1)}, u32[]{:S(2)}, u32[]{:S(2)}) collective-permute-start(bf16[4,64,128]{2,1,0:T(8,128)(2,1)S(1)} %get-tuple-element.23), channel_id=1, source_target_pairs={{0,2},{2,4},{4,6},{1,3},{3,5},{5,7},{8,10},{10,12},{12,14},{9,11},... | collective-permute-start | bytes 196616 | tf_op jit(solution)/shard_map/ppermute | solution.py:345
  43.3 1.3 %collective-permute-start.8 = (bf16[4,64,128]{2,1,0:T(8,128)(2,1)S(1)}, bf16[4,64,128]{2,1,0:T(8,128)(2,1)S(1)}, u32[]{:S(2)}, u32[]{:S(2)}) collective-permute-start(bf16[4,64,128]{2,1,0:T(8,128)(2,1)S(1)} %get-tuple-element.24), channel_id=1, source_target_pairs={{2,0},{4,2},{6,4},{3,1},{5,3},{7,5},{10,8},{12,10},{14,12},{11,9},... | collective-permute-start | bytes 196616 | tf_op jit(solution)/shard_map/ppermute | solution.py:346
  44.6 0.1 collective-permute-start.9
  44.6 0.0 copy-done.7
  44.7 0.0 collective-permute-done.5.refs_8_
  44.7 0.3 collective-permute-done.6.refs_9_
  45.0 0.1 collective-permute-done.7.refs_10_
  45.1 4.3 %collective-permute-done.8.refs_11_ = bf16[4,64,128]{2,1,0:T(8,128)(2,1)S(1)} collective-permute-done((bf16[4,64,128]{2,1,0:T(8,128)(2,1)S(1)}, bf16[4,64,128]{2,1,0:T(8,128)(2,1)S(1)}, u32[]{:S(2)}, u32[]{:S(2)}) %collective-permute-start.8) | collective-permute-done | bytes 65568 | tf_op jit(solution)/shard_map/ppermute | solution.py:346
  49.4 0.0 collective-permute-done.9.refs_12_.refs_13_
  49.4 11.6 %sweep_last.1 = (f32[4,64,64,128]{3,2,1,0:T(8,128)}, f32[32,128]{1,0:T(8,128)S(1)}) custom-call(f32[4]{0:T(128)S(1)} %copy-done.3, f32[4]{0:T(128)S(1)} %copy-done.4, f32[4]{0:T(128)S(1)} %copy-done.5, f32[4,64,64,128]{3,2,1,0:T(8,128)S(1)} %get-tuple-element.20.refs_3_.refs_4_.refs_5_, f32[4,64,64,128]{3,2,1,0:T(8,128)S(1)} %get-tuple-element.20.refs_3_.refs_4_.refs_5_, ...), custom_call_target="tpu_custom_call" | custom-call | flops 50331648 | bytes 23068672 | tf_op jit(solution)/shard_map/sweep_last/pallas_call | solution.py:325
  61.0 1.8 %all-gather = f32[64,128]{1,0:T(8,128)S(1)} all-gather(f32[32,128]{1,0:T(8,128)S(1)} %get-tuple-element.27), channel_id=2, replica_groups=mesh['gx'=4,'gy'=4,'gz'=2] {'gz'}, dimensions={0}, use_global_device_ids=true | all-gather | bytes 49152 | tf_op jit(solution)/shard_map/all_gather | solution.py:444
  62.9 0.1 select_maximum_fusion
  62.9 0.9 broadcast_in_dim.2
  63.8 6.9 %all-to-all-start = ((f32[16,72,128]{2,1,0:T(8,128)}), f32[16,72,128]{2,1,0:T(8,128)S(1)}, u32[]{:S(2)}, u32[]{:S(2)}) async-start(f32[16,72,128]{2,1,0:T(8,128)} %broadcast_in_dim.2), calls=%async_computation | async-start | bytes 1179648 | tf_op jit(solution)/shard_map/all_to_all | solution.py:447
  70.7 17.9 %all-to-all-done.got_ref = f32[16,72,128]{2,1,0:T(8,128)S(1)} async-done(((f32[16,72,128]{2,1,0:T(8,128)}), f32[16,72,128]{2,1,0:T(8,128)S(1)}, u32[]{:S(2)}, u32[]{:S(2)}) %all-to-all-start) | async-done | bytes 589856 | tf_op jit(solution)/shard_map/all_to_all | solution.py:447
  88.6 2.9 %plane.1 = f32[1,16,512]{2,1,0:T(8,128)} custom-call(s32[1]{0:T(128)} %bitcast.me_ref, f32[16,72,128]{2,1,0:T(8,128)S(1)} %all-to-all-done.got_ref), custom_call_target="tpu_custom_call" | custom-call | tf_op jit(solution)/shard_map/plane/pallas_call | solution.py:450
  (3 shorter events, 0.0 us)
Async XLA Ops:
  0.6 3.4 %copy-start = (f32[4,64,64,128]{3,2,1,0:T(8,128)S(1)}, f32[4,64,64,128]{3,2,1,0:T(8,128)}, u32[]{:S(2)}) copy-start(f32[4,64,64,128]{3,2,1,0:T(8,128)} %refs_5_.1) | copy-start | bytes 25165828
  4.0 14.0 %copy-start.6 = (f32[64,64]{1,0:T(8,128)S(1)}, f32[64,64]{1,0:T(8,128)}, u32[]{:S(2)}) copy-start(f32[64,64]{1,0:T(8,128)} %param.14) | copy-start | bytes 49156
  4.0 18.8 %copy-start.1 = (bf16[4,64,64,128]{3,2,1,0:T(8,128)(2,1)S(1)}, bf16[4,64,64,128]{3,2,1,0:T(8,128)(2,1)}, u32[]{:S(2)}) copy-start(bf16[4,64,64,128]{3,2,1,0:T(8,128)(2,1)} %refs_6_.3) | copy-start | bytes 12582916
  4.0 18.8 %copy-start.2 = (s32[64,64,128]{2,1,0:T(8,128)S(1)}, s32[64,64,128]{2,1,0:T(8,128)}, u32[]{:S(2)}) copy-start(s32[64,64,128]{2,1,0:T(8,128)} %refs_7_.3) | copy-start | bytes 6291460
  4.0 18.8 %copy-start.3 = (f32[4]{0:T(128)S(1)}, f32[4]{0:T(128)}, u32[]{:S(2)}) copy-start(f32[4]{0:T(128)} %refs_0_.3) | copy-start | bytes 52
  4.0 18.8 %copy-start.4 = (f32[4]{0:T(128)S(1)}, f32[4]{0:T(128)}, u32[]{:S(2)}) copy-start(f32[4]{0:T(128)} %refs_1_.3) | copy-start | bytes 52
  4.0 18.8 %copy-start.5 = (f32[4]{0:T(128)S(1)}, f32[4]{0:T(128)}, u32[]{:S(2)}) copy-start(f32[4]{0:T(128)} %refs_2_.3) | copy-start | bytes 52
  7.0 11.1 %collective-permute-start = (bf16[4,64,128]{2,1,0:T(8,128)(2,1)S(1)}, bf16[4,64,128]{2,1,0:T(8,128)(2,1)S(1)}, u32[]{:S(2)}, u32[]{:S(2)}) collective-permute-start(bf16[4,64,128]{2,1,0:T(8,128)(2,1)S(1)} %get-tuple-element.15), channel_id=1, source_target_pairs={{0,8},{8,16},{16,24},{1,9},{9,17},{17,25},{2,10},{10,18},{18,26},{... | collective-permute-start | bytes 196616 | tf_op jit(solution)/shard_map/ppermute | solution.py:345
  11.9 6.2 %collective-permute-start.1 = (bf16[4,64,128]{2,1,0:T(8,128)(2,1)S(1)}, bf16[4,64,128]{2,1,0:T(8,128)(2,1)S(1)}, u32[]{:S(2)}, u32[]{:S(2)}) collective-permute-start(bf16[4,64,128]{2,1,0:T(8,128)(2,1)S(1)} %get-tuple-element.16), channel_id=1, source_target_pairs={{8,0},{16,8},{24,16},{9,1},{17,9},{25,17},{10,2},{18,10},{26,18},{... | collective-permute-start | bytes 196616 | tf_op jit(solution)/shard_map/ppermute | solution.py:346
  13.2 5.4 %collective-permute-start.2 = (bf16[4,64,128]{2,1,0:T(8,128)(2,1)S(1)}, bf16[4,64,128]{2,1,0:T(8,128)(2,1)S(1)}, u32[]{:S(2)}, u32[]{:S(2)}) collective-permute-start(bf16[4,64,128]{2,1,0:T(8,128)(2,1)S(1)} %get-tuple-element.17), channel_id=1, source_target_pairs={{0,2},{2,4},{4,6},{1,3},{3,5},{5,7},{8,10},{10,12},{12,14},{9,11},... | collective-permute-start | bytes 196616 | tf_op jit(solution)/shard_map/ppermute | solution.py:345
  16.7 6.2 %collective-permute-start.3 = (bf16[4,64,128]{2,1,0:T(8,128)(2,1)S(1)}, bf16[4,64,128]{2,1,0:T(8,128)(2,1)S(1)}, u32[]{:S(2)}, u32[]{:S(2)}) collective-permute-start(bf16[4,64,128]{2,1,0:T(8,128)(2,1)S(1)} %get-tuple-element.18), channel_id=1, source_target_pairs={{2,0},{4,2},{6,4},{3,1},{5,3},{7,5},{10,8},{12,10},{14,12},{11,9},... | collective-permute-start | bytes 196616 | tf_op jit(solution)/shard_map/ppermute | solution.py:346
  18.0 4.9 %collective-permute-start.4 = (bf16[4,64,128]{2,1,0:T(8,128)(2,1)S(1)}, bf16[4,64,128]{2,1,0:T(8,128)(2,1)S(1)}, u32[]{:S(2)}, u32[]{:S(2)}) collective-permute-start(bf16[4,64,128]{2,1,0:T(8,128)(2,1)S(1)} %get-tuple-element.19), channel_id=1, source_target_pairs={{0,1},{1,0},{2,3},{3,2},{4,5},{5,4},{6,7},{7,6},{8,9},{9,8},{10,11... | collective-permute-start | bytes 196616 | tf_op jit(solution)/shard_map/ppermute | solution.py:349
  18.1 26.6 %copy-start.7 = (s32[1,1,64,1]{2,3,1,0:T(1,128)S(1)}, s32[1,1,64,1]{2,3,1,0:T(1,128)}, u32[]{:S(2)}) copy-start(s32[1,1,64,1]{2,3,1,0:T(1,128)} %param.15) | copy-start | bytes 772
  33.9 10.8 %collective-permute-start.5 = (bf16[4,64,128]{2,1,0:T(8,128)(2,1)S(1)}, bf16[4,64,128]{2,1,0:T(8,128)(2,1)S(1)}, u32[]{:S(2)}, u32[]{:S(2)}) collective-permute-start(bf16[4,64,128]{2,1,0:T(8,128)(2,1)S(1)} %get-tuple-element.21), channel_id=1, source_target_pairs={{0,8},{8,16},{16,24},{1,9},{9,17},{17,25},{2,10},{10,18},{18,26},{... | collective-permute-start | bytes 196616 | tf_op jit(solution)/shard_map/ppermute | solution.py:345
  38.5 6.5 %collective-permute-start.6 = (bf16[4,64,128]{2,1,0:T(8,128)(2,1)S(1)}, bf16[4,64,128]{2,1,0:T(8,128)(2,1)S(1)}, u32[]{:S(2)}, u32[]{:S(2)}) collective-permute-start(bf16[4,64,128]{2,1,0:T(8,128)(2,1)S(1)} %get-tuple-element.22), channel_id=1, source_target_pairs={{8,0},{16,8},{24,16},{9,1},{17,9},{25,17},{10,2},{18,10},{26,18},{... | collective-permute-start | bytes 196616 | tf_op jit(solution)/shard_map/ppermute | solution.py:346
  39.8 5.4 %collective-permute-start.7 = (bf16[4,64,128]{2,1,0:T(8,128)(2,1)S(1)}, bf16[4,64,128]{2,1,0:T(8,128)(2,1)S(1)}, u32[]{:S(2)}, u32[]{:S(2)}) collective-permute-start(bf16[4,64,128]{2,1,0:T(8,128)(2,1)S(1)} %get-tuple-element.23), channel_id=1, source_target_pairs={{0,2},{2,4},{4,6},{1,3},{3,5},{5,7},{8,10},{10,12},{12,14},{9,11},... | collective-permute-start | bytes 196616 | tf_op jit(solution)/shard_map/ppermute | solution.py:345
  43.3 6.2 %collective-permute-start.8 = (bf16[4,64,128]{2,1,0:T(8,128)(2,1)S(1)}, bf16[4,64,128]{2,1,0:T(8,128)(2,1)S(1)}, u32[]{:S(2)}, u32[]{:S(2)}) collective-permute-start(bf16[4,64,128]{2,1,0:T(8,128)(2,1)S(1)} %get-tuple-element.24), channel_id=1, source_target_pairs={{2,0},{4,2},{6,4},{3,1},{5,3},{7,5},{10,8},{12,10},{14,12},{11,9},... | collective-permute-start | bytes 196616 | tf_op jit(solution)/shard_map/ppermute | solution.py:346
  44.6 4.9 %collective-permute-start.9 = (bf16[4,64,128]{2,1,0:T(8,128)(2,1)S(1)}, bf16[4,64,128]{2,1,0:T(8,128)(2,1)S(1)}, u32[]{:S(2)}, u32[]{:S(2)}) collective-permute-start(bf16[4,64,128]{2,1,0:T(8,128)(2,1)S(1)} %get-tuple-element.25), channel_id=1, source_target_pairs={{0,1},{1,0},{2,3},{3,2},{4,5},{5,4},{6,7},{7,6},{8,9},{9,8},{10,11... | collective-permute-start | bytes 196616 | tf_op jit(solution)/shard_map/ppermute | solution.py:349
  63.8 24.8 %all-to-all-start = ((f32[16,72,128]{2,1,0:T(8,128)}), f32[16,72,128]{2,1,0:T(8,128)S(1)}, u32[]{:S(2)}, u32[]{:S(2)}) async-start(f32[16,72,128]{2,1,0:T(8,128)} %broadcast_in_dim.2), calls=%async_computation | async-start | bytes 1179648 | tf_op jit(solution)/shard_map/all_to_all | solution.py:447

commit v3 on v2

v3 whole, which is shorter than its diff:
```python
import functools
import math

import jax
import jax.numpy as jnp
from jax import lax
from jax.experimental import pallas as pl
from jax.experimental.pallas import tpu as pltpu
from jax.sharding import PartitionSpec as P

R = 8
TS = 8
MOST = 8
RELAXATION = 0.8
SHARPNESS = 8.0
THRESHOLD = 0.5
PB = 8
F32 = jnp.float32
BF16 = jnp.bfloat16


def lanes_of(shape):
    return lax.broadcasted_iota(jnp.int32, shape, len(shape) - 1)


def ends_matrix(depth):
    z = lax.broadcasted_iota(jnp.int32, (depth, depth), 0)
    j = lax.broadcasted_iota(jnp.int32, (depth, depth), 1)
    even = (z == 0) & (j % 2 == 0)
    odd = (z == depth - 1) & (j % 2 == 1)
    return jnp.where(even | odd, 1.0, 0.0).astype(BF16)


def beside_matrix(depth):
    z = lax.broadcasted_iota(jnp.int32, (depth, depth), 0)
    j = lax.broadcasted_iota(jnp.int32, (depth, depth), 1)
    return jnp.where(jnp.abs(z - j) == 1, 1.0, 0.0).astype(BF16)


def halo_matrix(depth):
    j = lax.broadcasted_iota(jnp.int32, (depth, depth), 0)
    z = lax.broadcasted_iota(jnp.int32, (depth, depth), 1)
    even = (z == 0) & (j % 2 == 0)
    odd = (z == depth - 1) & (j % 2 == 1)
    return jnp.where(even | odd, 1.0, 0.0).astype(BF16)


def split(value):
    high = value.astype(BF16)
    return high, (value - high.astype(F32)).astype(BF16)


def mm(a, b):
    return lax.dot_general(a, b, (((1,), (0,)), ((), ())), preferred_element_type=F32)


def put_faces(first, ref, start, ends, gs, ylo, yhi):
    rows, depth = ref.shape[2:]
    value = ref[:, pl.ds(start, PB)]
    for p in range(PB):
        for c in range(4):
            ylo[c, pl.ds(first + p, 1), :] = value[c, p, 0:1, :]
            yhi[c, pl.ds(first + p, 1), :] = value[c, p, rows - 1 :, :]
    picked = mm(value.astype(BF16).reshape(4 * PB * rows, depth), ends).reshape(4, PB, rows, depth)
    pair = lanes_of((rows, depth)) // 2
    for c in range(4):
        g = gs[c]
        for p in range(PB):
            g = jnp.where(pair == first + p, picked[c, p], g)
        gs[c] = g


def put_plane(out_ref, value):
    rows = value.shape[1]
    out_ref[: 4 * rows] = value.astype(BF16).reshape(4 * rows, value.shape[2])


def paired(value):
    high = value.astype(BF16).astype(F32)
    return jnp.concatenate([high, value - high], 1)


def pack_kernel(v_ref, d_ref, xlo_ref, xhi_ref, ylo_ref, yhi_ref, g_ref, gs, ylo, yhi, ends):
    step, steps = pl.program_id(0), pl.num_programs(0)
    rows, depth = v_ref.shape[2:]

    @pl.when(step == 0)
    def _():
        gs[...] = jnp.zeros_like(gs)
        ends[...] = ends_matrix(depth)
        put_plane(xlo_ref, v_ref[:, 0])
        cells = d_ref.shape[0]
        none = jnp.zeros((R, depth), F32)
        for out_ref, start in ((xlo_ref, 0), (xhi_ref, cells - R)):
            strip = jnp.concatenate([paired(d_ref[start : start + R, :]), none], 0)
            out_ref[4 * rows :] = strip.astype(BF16)

    put_faces(step * PB, v_ref, 0, ends[...], gs, ylo, yhi)

    @pl.when(step == steps - 1)
    def _():
        g_ref[...] = gs[...].astype(BF16)
        ylo_ref[...] = ylo[...].astype(BF16)
        yhi_ref[...] = yhi[...].astype(BF16)
        put_plane(xhi_ref, v_ref[:, PB - 1])


def sweep_kernel(last, nz, scale, *refs):
    sr_ref, si_ref, v_ref, s_ref, m_ref, xl_ref, xr_ref, yl_ref, yr_ref, gl_ref, gr_ref = refs[:11]
    if last:
        sh_ref, mid_ref, own_ref, o_ref, sens_ref = refs[11:16]
        hs, yl, yr, near, far, zt, sens, value, news, sems = refs[16:]
    else:
        d_ref, o_ref, xlo_ref, xhi_ref, ylo_ref, yhi_ref, g_ref = refs[11:18]
        hs, yl, yr, near, far, zt, gs, ylo, yhi, ends = refs[18:]
    planes_here, rows, depth = v_ref.shape[1:]
    lane = lanes_of((rows, depth))

    if nz == 2:
        here = lax.axis_index("gz").astype(F32)
        keep_l, keep_r = here, 1.0 - here
    else:
        keep_l, keep_r = 1.0, 1.0
    for c in range(4):
        left = pltpu.roll(gl_ref[c].astype(F32), depth - 1, 1) * keep_l
        right = pltpu.roll(gr_ref[c].astype(F32), 1, 1) * keep_r
        hs[c] = jnp.where(lane % 2 == 0, left, right)
    near[...] = jnp.concatenate([beside_matrix(depth)] * 2, 0)
    far[...] = halo_matrix(depth)
    if last:
        sens[...] = jnp.zeros_like(sens)
    else:
        gs[...] = jnp.zeros_like(gs)
        ends[...] = ends_matrix(depth)
    yl[...] = yl_ref[:4].astype(F32)
    yr[...] = yr_ref[:4].astype(F32)

    levels = sr_ref.shape[0]
    tile = (8, depth)
    wr, wi, share = [], [], []
    for m in range(levels):
        d = 6.0 + jnp.full(tile, sr_ref[m], F32)
        s = jnp.full(tile, si_ref[m], F32)
        mag = d * d + s * s
        wr.append(RELAXATION * d / mag)
        wi.append(-RELAXATION * s / mag)
        if last:
            share.append(jnp.full(tile, sh_ref[m], F32))

    def lookup(masks, table):
        out = jnp.broadcast_to(table[0], (rows // 8, 8, depth))
        for mask, entry in zip(masks, table[1:]):
            out = jnp.where(mask, entry, out)
        return out.reshape(rows, depth)

    row8 = lax.broadcasted_iota(jnp.int32, tile, 0)

    def along_z(first):
        v = v_ref[:, pl.ds(first, PB)].reshape(4 * PB * rows, depth)
        masked = [
            jnp.where(lane // 2 == first + p, hs[c], 0.0).astype(BF16)
            for c in range(4)
            for p in range(PB)
        ]
        out = mm(jnp.concatenate(split(v), 1), near[...]) + mm(jnp.concatenate(masked, 0), far[...])
        zt[...] = out.reshape(4, PB, rows, depth)

    def plane(first, p, put):
        x = first + p
        mat = m_ref[x].reshape(rows // 8, 8, depth)
        masks = [mat == m for m in range(1, levels)]
        w_r, w_i = lookup(masks, wr), lookup(masks, wi)

        def drive(c):
            v = v_ref[c, x]
            if p == 0:
                before = v_ref[c, jnp.maximum(x - 1, 0)]
                before = jnp.where(x == 0, xl_ref[c * rows : (c + 1) * rows].astype(F32), before)
            else:
                before = v_ref[c, x - 1]
            if p == PB - 1:
                after = v_ref[c, jnp.minimum(x + 1, planes_here - 1)]
                edge = xr_ref[c * rows : (c + 1) * rows].astype(F32)
                after = jnp.where(x == planes_here - 1, edge, after)
            else:
                after = v_ref[c, x + 1]
            total = before + after + s_ref[c, x].astype(F32) + zt[c, p]
            up = pltpu.roll(v, 1, 0)
            down = pltpu.roll(v, rows - 1, 0)
            top = jnp.where(row8 == 0, yl[c, pl.ds(x, 1), :], up[:8])
            low = jnp.where(row8 == 7, yr[c, pl.ds(x, 1), :], down[-8:])
            total = total + jnp.concatenate([top, up[8:]], 0)
            return v, total + jnp.concatenate([down[:-8], low], 0)

        new = []
        for re in (0, 2):
            v_r, t_r = drive(re)
            v_i, t_i = drive(re + 1)
            keep = 1.0 - RELAXATION
            n_r = keep * v_r + (w_r * t_r - w_i * t_i)
            n_i = keep * v_i + (w_r * t_i + w_i * t_r)
            put(re, n_r)
            put(re + 1, n_i)
            new += [n_r, n_i]
        if last:
            value[p] = lookup(masks, share) * (new[0] * new[2] - new[1] * new[3])

    groups = planes_here // PB

    def store(slot, first):
        return pltpu.make_async_copy(
            news.at[slot], o_ref.at[:, pl.ds(first, PB)], sems.at[slot]
        )

    def group(i, carry):
        first = i * PB
        along_z(first)
        if last:
            slot = i % 2

            @pl.when(i >= 2)
            def _():
                store(slot, first - 2 * PB).wait()

        for p in range(PB):

            def put(c, new, p=p):
                if last:
                    news[slot, c, p] = new
                else:
                    o_ref[c, first + p] = new

            plane(first, p, put)
        if last:
            store(slot, first).start()
            ones = jnp.ones((2 * depth, depth), BF16)
            parts = split(value[...].reshape(PB * rows, depth))
            sums = mm(jnp.concatenate(parts, 1), ones).reshape(PB, rows, depth)
            held = sens[...]
            for p in range(PB):
                held = jnp.where(lane == first + p, sums[p], held)
            sens[...] = held
        else:
            put_faces(first, o_ref, first, ends[...], gs, ylo, yhi)
        return carry

    lax.fori_loop(0, groups, group, 0)

    if not last:
        put_plane(xlo_ref, o_ref[:, 0])
        put_plane(xhi_ref, o_ref[:, planes_here - 1])
        g_ref[...] = gs[...].astype(BF16)
        xlo_ref[4 * rows :] = jnp.zeros((2 * R, depth), BF16)
        xhi_ref[4 * rows :] = jnp.zeros((2 * R, depth), BF16)
        cells = d_ref.shape[0]
        strips = [r[4 * rows : 4 * rows + 2 * R].astype(F32)[:R] for r in (xl_ref, xr_ref)]
        filler = jnp.zeros((2 * cells - cells - 2 * R, depth), F32)
        tall = jnp.concatenate([strips[0], paired(d_ref[...]), strips[1], filler], 0)
        tall = tall.astype(BF16).reshape(2, cells, depth)
        for out_ref, rows_out in ((ylo_ref, ylo), (yhi_ref, yhi)):
            out_ref[:4] = rows_out[...].astype(BF16)
            out_ref[4:] = tall
    else:
        cells = rows
        row = lax.broadcasted_iota(jnp.int32, (cells, 2 * cells), 0)
        col = lanes_of((cells, 2 * cells))
        half_sum = jnp.zeros((cells, 2 * cells), F32)
        for shift, ref in ((-cells, yl_ref), (0, mid_ref), (cells, yr_ref)):
            weight = jnp.maximum(R + 1 - jnp.abs(col % cells + shift - row), 0)
            tall = ref[4:].reshape(2 * cells, depth)
            half_sum = half_sum + lax.dot_general(
                weight.astype(F32).astype(BF16),
                tall,
                (((1,), (1,)), ((), ())),
                preferred_element_type=F32,
            )
        row = lax.broadcasted_iota(jnp.int32, (2 * cells, depth), 0)
        col = lanes_of((2 * cells, depth))
        weight = jnp.maximum(R + 1 - jnp.abs(row - R - col), 0).astype(F32).astype(BF16)
        filtered = twice(half_sum, weight) / float((R + 1) ** 4)
        tangent = jnp.tanh(SHARPNESS * (filtered - THRESHOLD))
        total = math.tanh(SHARPNESS * THRESHOLD) + math.tanh(SHARPNESS * (1.0 - THRESHOLD))
        slope = SHARPNESS * (1.0 - tangent * tangent) / total
        weighted = slope * sens[...] * scale
        half = rows // 2
        both = pltpu.roll(weighted[half:], depth // 2, 1)
        sens_ref[:half] = jnp.where(lane[:half] < depth // 2, weighted[:half], both)
        mine = jnp.where(lax.axis_index("gz") == 0, own_ref[...].astype(F32), 0.0)
        sens_ref[half:] = jnp.concatenate([mine, jnp.zeros((8, depth - rows), F32)], 1)
        store((groups - 2) % 2, (groups - 2) * PB).wait()
        store((groups - 1) % 2, (groups - 1) * PB).wait()


def twice(value, right):
    high, low = split(value)
    return mm(high, right) + mm(low, right)


def left_twice(left, value):
    high, low = split(value)
    return mm(left, high) + mm(left, low)


def whole(shape):
    return pl.BlockSpec(shape, lambda i: (0,) * len(shape))


SMEM_SPEC = pl.BlockSpec(memory_space=pltpu.SMEM)
VMEM_SPEC = pl.BlockSpec(memory_space=pltpu.VMEM)


def message_shapes(nx, ny, nz, parts):
    tall = (4 * ny + 2 * R, nz)
    return [tall, tall, (parts, nx, nz), (parts, nx, nz), (4, ny, nz)]


def face_scratch(nx, ny, nz):
    return [
        pltpu.VMEM((4, ny, nz), F32),
        pltpu.VMEM((4, nx, nz), F32),
        pltpu.VMEM((4, nx, nz), F32),
        pltpu.VMEM((nz, nz), BF16),
    ]


def pack(fields, density):
    _, nx, ny, nz = fields.shape
    shapes = message_shapes(nx, ny, nz, 4)
    return pl.pallas_call(
        pack_kernel,
        grid=(nx // PB,),
        in_specs=[
            pl.BlockSpec((4, PB, ny, nz), lambda i: (0, i, 0, 0)),
            whole(density.shape),
        ],
        out_specs=[whole(s) for s in shapes],
        out_shape=[jax.ShapeDtypeStruct(s, BF16) for s in shapes],
        scratch_shapes=face_scratch(nx, ny, nz),
        compiler_params=pltpu.CompilerParams(vmem_limit_bytes=12 << 20),
        cost_estimate=pl.CostEstimate(
            flops=fields.size * 4, bytes_accessed=fields.size * 4, transcendentals=0
        ),
        name="pack_faces",
    )(pltpu.with_memory_space_constraint(fields, pltpu.HBM), density)


def sweep(last, tables, current, sources, material, halos, more):
    _, nx, ny, nz = current.shape
    scratch = [
        pltpu.VMEM((4, ny, nz), F32),
        pltpu.VMEM((4, nx, nz), F32),
        pltpu.VMEM((4, nx, nz), F32),
        pltpu.VMEM((2 * nz, nz), BF16),
        pltpu.VMEM((nz, nz), BF16),
        pltpu.VMEM((4, PB, ny, nz), F32),
    ]
    if last:
        shapes = [
            jax.ShapeDtypeStruct(current.shape, F32),
            jax.ShapeDtypeStruct((ny // 2 + 8, nz), F32),
        ]
        specs = [pl.BlockSpec(memory_space=pltpu.HBM), VMEM_SPEC]
        more_specs = [SMEM_SPEC, VMEM_SPEC, VMEM_SPEC]
        scratch += [
            pltpu.VMEM((ny, nz), F32),
            pltpu.VMEM((PB, ny, nz), F32),
            pltpu.VMEM((2, 4, PB, ny, nz), F32),
            pltpu.SemaphoreType.DMA((2,)),
        ]
    else:
        faces = message_shapes(nx, ny, nz, 6)
        shapes = [pltpu.VMEM(current.shape, F32)]
        shapes += [jax.ShapeDtypeStruct(s, BF16) for s in faces]
        specs = [VMEM_SPEC] * len(shapes)
        more_specs = [VMEM_SPEC]
        scratch += face_scratch(nx, ny, nz)

    def near(value):
        return pltpu.with_memory_space_constraint(value, pltpu.VMEM)

    return pl.pallas_call(
        functools.partial(
            sweep_kernel,
            last,
            lax.axis_size("gz"),
            1.0 / math.sqrt(nz * lax.axis_size("gz")),
        ),
        in_specs=[SMEM_SPEC] * 2 + [VMEM_SPEC] * 9 + more_specs,
        out_specs=specs,
        out_shape=shapes,
        scratch_shapes=scratch,
        compiler_params=pltpu.CompilerParams(vmem_limit_bytes=20 << 20),
        cost_estimate=pl.CostEstimate(
            flops=current.size * 24, bytes_accessed=current.size * 11, transcendentals=0
        ),
        name="sweep_last" if last else "sweep_first",
    )(*tables, near(current), near(sources), near(material), *halos, *more)


def exchange(xlo, xhi, ylo, yhi, g):
    out = []
    for axis, low, high in (("gx", xlo, xhi), ("gy", ylo, yhi)):
        count = lax.axis_size(axis)
        up = [(i, i + 1) for i in range(count - 1)]
        out.append(lax.ppermute(high, axis, up))
        out.append(lax.ppermute(low, axis, [(j, i) for i, j in up]))
    count = lax.axis_size("gz")
    if count == 2:
        other = lax.ppermute(g, "gz", [(0, 1), (1, 0)])
        return out + [other, other]
    up = [(i, i + 1) for i in range(count - 1)]
    return out + [lax.ppermute(g, "gz", up), lax.ppermute(g, "gz", [(j, i) for i, j in up])]


def plane_kernel(ngx, ngy, me_ref, got_ref, out_ref, w_ref):
    cells = 64
    nx, ny = ngx * cells, ngy * cells
    columns = ngx * ngy
    half = cells // 2
    for cx in range(ngx):
        for cy in range(ngy):
            c = cx * ngy + cy
            for part in range(2):
                lanes = pl.ds(part * cells, cells)
                w_ref[pl.ds(cy * cells + part * half, half), pl.ds(cx * cells, cells)] = got_ref[
                    c, pl.ds(0, half), lanes
                ]

    def band(n):
        i = lax.broadcasted_iota(jnp.int32, (n, n), 0)
        j = lax.broadcasted_iota(jnp.int32, (n, n), 1)
        return jnp.maximum(R + 1 - jnp.abs(i - j), 0).astype(F32).astype(BF16)

    unit = float((R + 1) ** 4)
    weighted = twice(w_ref[...], band(nx))

    tiles = cells
    owner = jnp.concatenate([got_ref[c, pl.ds(half, 1), pl.ds(0, tiles)] for c in range(columns)], 0)
    mine = owner == me_ref[0].astype(F32)
    flag = jnp.where(mine, 1.0, 0.0)
    a = lax.broadcasted_iota(jnp.int32, (tiles, tiles), 0)
    b = lax.broadcasted_iota(jnp.int32, (tiles, tiles), 1)
    rank = mm(flag.astype(BF16), jnp.where(a < b, 1.0, 0.0).astype(BF16))
    number = lanes_of((columns, tiles))
    column = lax.broadcasted_iota(jnp.int32, (columns, 1), 0)
    rows, blocks = [], []
    for k in range(MOST):
        chosen = mine & (rank == float(k))
        tile = jnp.sum(jnp.where(chosen, number, 0), axis=1, keepdims=True)
        there = jnp.sum(jnp.where(chosen, 1, 0), axis=1, keepdims=True)
        rows.append((column % ngy) * cells + (tile % (cells // TS)) * TS)
        block = (column // ngy) * (cells // TS) + tile // (cells // TS)
        blocks.append(jnp.where(there > 0, block, -1))
    row = jnp.concatenate(rows, 0)
    block = jnp.concatenate(blocks, 0)
    slots = MOST * columns
    across = lax.broadcasted_iota(jnp.int32, (slots, ny), 1)
    lefts = [
        jnp.maximum(R + 1 - jnp.abs(row + j - across), 0).astype(F32).astype(BF16)
        for j in range(TS)
    ]
    lines = left_twice(jnp.concatenate(lefts, 0), weighted)
    keep = lanes_of((slots, nx)) // TS == block
    from_x = lax.broadcasted_iota(jnp.int32, (nx, TS * TS), 0) % TS
    to_q = lanes_of((nx, TS * TS))
    out = jnp.zeros((slots, TS * TS), F32)
    for j in range(TS):
        fold = jnp.where(to_q == from_x * TS + j, 1.0, 0.0).astype(BF16)
        out = out + twice(jnp.where(keep, lines[j * slots : (j + 1) * slots], 0.0), fold)
    out = out / unit
    for k in range(MOST):
        out_ref[0, :, pl.ds(k * TS * TS, TS * TS)] = out[k * columns : (k + 1) * columns]


def on_device(fields, sources, material, shift_real, shift_imag, design_share, density, owner_map):
    ngx, ngy = lax.axis_size("gx"), lax.axis_size("gy")
    columns = ngx * ngy
    cells = density.shape[0]
    tables = (shift_real, shift_imag)
    owners = jnp.broadcast_to(owner_map.reshape(1, -1), (8, cells))
    halos = exchange(*pack(fields, density))
    middle, *faces = sweep(False, tables, fields, sources, material, halos, [density])
    final, partial = sweep(
        True, tables, middle, sources, material, exchange(*faces), [design_share, faces[2], owners]
    )
    partial = jnp.sum(lax.all_gather(partial, "gz"), 0)
    copies = jnp.broadcast_to(partial[None], (columns, *partial.shape))
    plane = lax.all_to_all(copies, ("gx", "gy"), split_axis=0, concat_axis=0)
    me = (lax.axis_index("gx") * ngy + lax.axis_index("gy")).reshape(1)
    owned = pl.pallas_call(
        functools.partial(plane_kernel, ngx, ngy),
        in_specs=[SMEM_SPEC, VMEM_SPEC],
        out_specs=VMEM_SPEC,
        out_shape=jax.ShapeDtypeStruct((1, columns, MOST * TS * TS), F32),
        scratch_shapes=[pltpu.VMEM((ngy * cells, ngx * cells), F32)],
        compiler_params=pltpu.CompilerParams(vmem_limit_bytes=16 << 20),
        name="plane",
    )(me, plane)
    return (final, owned)


def solution(mesh):
    placed = (
        P(None, "gx", "gy", "gz"),
        P(None, "gx", "gy", "gz"),
        P("gx", "gy", "gz"),
        P(),
        P(),
        P(),
        P("gx", "gy"),
        P("gx", "gy", None, None),
    )
    return jax.shard_map(
        on_device,
        mesh=mesh,
        in_specs=placed,
        out_specs=(P(None, "gx", "gy", "gz"), P(("gx", "gy"), None, None)),
        check_vma=False,
    )
```

time: 92 us -> 92.8 us (level)
  waiting for transfers between devices: 27.4 us -> 22.3 us
  Pallas kernels: 28.5 us -> 32.8 us
  local copies, waits for them, and re-layouts: 4.28 us -> 5.45 us
    all_to_all x1, waiting for transfers between devices: 17.9 us -> 12.3 us  [on_device(): plane = lax.all_to_all(copies, ('gx', 'gy'), split_axis=0, concat_axis=0)]
    pallas_call x4, Pallas kernels: 28.5 us -> 32.8 us  [the longest x2 23.3 us: sweep(): pl.pallas_call(functools.partial(sweep_kernel, last, lax.axis_size('gz'),...]
    unnamed x16 -> x22, local copies, waits for them, and re-layouts: 3.41 us -> 4.71 us
    ppermute x2, waiting for transfers between devices: 0.01 us -> 1.24 us  [exchange(): other = lax.ppermute(g, 'gz', [(0, 1), (1, 0)])]
    ppermute x4, starting transfers between devices: 16.4 us -> 17.4 us  [exchange(): out.append(lax.ppermute(high, axis, up))]
  transfers between devices with their start and end apart: 11 -> 11, of which waited for: 6 -> 5; matrix products, arithmetic and copies ran while one was open for 0% -> 0% of each run, Pallas kernels for 0% -> 0%
where the time goes in v3:
time: 92.8 us; the launch traced here: 92.3 us
  Pallas kernels  32.8 us (35%)
  starting transfers between devices  29 us (31%)
  waiting for transfers between devices  22.3 us (24%)
  local copies, waits for them, and re-layouts  5.45 us (6%)
  blocking collectives  1.83 us (2%)
    pallas_call x2, Pallas kernels, sweep(): pl.pallas_call(functools.partial(sweep_kernel, last, lax.axis_size('gz'),...  23.3 us
    ppermute x4, starting transfers between devices, exchange(): out.append(lax.ppermute(high, axis, up))  17.4 us
    all_to_all x1, waiting for transfers between devices, on_device(): plane = lax.all_to_all(copies, ('gx', 'gy'), split_axis=0, concat_axis=0)  12.3 us
    ppermute x4, waiting for transfers between devices, exchange(): out.append(lax.ppermute(low, axis, [(j, i) for i, j in up]))  8.22 us
    pallas_call x1, Pallas kernels, pack(): pl.pallas_call(pack_kernel, grid=(nx // PB,), in_specs=[pl.BlockSpec((4,...  7.26 us
    all_to_all x1, starting transfers between devices, on_device(): plane = lax.all_to_all(copies, ('gx', 'gy'), split_axis=0, concat_axis=0)  6.31 us
    ppermute x4, starting transfers between devices, exchange(): out.append(lax.ppermute(low, axis, [(j, i) for i, j in up]))  5.16 us
    unnamed x22, local copies, waits for them, and re-layouts  4.71 us
  transfers between devices with their start and end apart: 11, of which 5 were waited for; matrix products, arithmetic and copies ran while one was open for 0% of the time, Pallas kernels for 0%

profile of v3, /device:TPU:0, one launch (start us, length us, event | category | flops | bytes accessed | tf_op | source)
XLA Modules:
  0.0 92.3 jit_solution(340184137656049631)
XLA Ops:
  0.6 0.0 copy-start
  0.6 0.0 copy-start.5
  0.7 0.9 copy-done.5
  1.5 0.0 copy-start.6
  1.6 0.0 copy-start.7
  1.6 0.0 copy-start.8
  1.6 7.3 %pack_faces.1 = (bf16[272,128]{1,0:T(8,128)(2,1)S(1)}, bf16[272,128]{1,0:T(8,128)(2,1)S(1)}, bf16[4,64,128]{2,1,0:T(8,128)(2,1)S(1)}, bf16[4,64,128]{2,1,0:T(8,128)(2,1)S(1)}, bf16[4,64,128]{2,1,0:T(8,128)(2,1)S(1)}) custom-call(f32[4,64,64,128]{3,2,1,0:T(8,128)} %refs_2_.1, f32[64,64]{1,0:T(8,128)S(1)} %copy-done.5), custom_call_target="tpu_custom_call" | custom-call | flops 8388608 | bytes 8388608 | tf_op jit(solution)/shard_map/pack_faces/pallas_call | solution.py:329
  8.8 0.0 copy-start.10
  8.8 0.0 copy-start.9
  8.8 4.8 %collective-permute-start = (bf16[272,128]{1,0:T(8,128)(2,1)S(1)}, bf16[272,128]{1,0:T(8,128)(2,1)S(1)}, u32[]{:S(2)}, u32[]{:S(2)}) collective-permute-start(bf16[272,128]{1,0:T(8,128)(2,1)S(1)} %get-tuple-element.15), channel_id=1, source_target_pairs={{0,8},{8,16},{16,24},{1,9},{9,17},{17,25},{2,10},{10,18},{18,26},{... | collective-permute-start | bytes 208904 | tf_op jit(solution)/shard_map/ppermute | solution.py:405
  13.7 1.3 %collective-permute-start.1 = (bf16[272,128]{1,0:T(8,128)(2,1)S(1)}, bf16[272,128]{1,0:T(8,128)(2,1)S(1)}, u32[]{:S(2)}, u32[]{:S(2)}) collective-permute-start(bf16[272,128]{1,0:T(8,128)(2,1)S(1)} %get-tuple-element.16), channel_id=1, source_target_pairs={{8,0},{16,8},{24,16},{9,1},{17,9},{25,17},{10,2},{18,10},{26,18},{... | collective-permute-start | bytes 208904 | tf_op jit(solution)/shard_map/ppermute | solution.py:406
  15.0 3.5 %collective-permute-start.2 = (bf16[4,64,128]{2,1,0:T(8,128)(2,1)S(1)}, bf16[4,64,128]{2,1,0:T(8,128)(2,1)S(1)}, u32[]{:S(2)}, u32[]{:S(2)}) collective-permute-start(bf16[4,64,128]{2,1,0:T(8,128)(2,1)S(1)} %get-tuple-element.17), channel_id=1, source_target_pairs={{0,2},{2,4},{4,6},{1,3},{3,5},{5,7},{8,10},{10,12},{12,14},{9,11},... | collective-permute-start | bytes 196616 | tf_op jit(solution)/shard_map/ppermute | solution.py:405
  18.5 1.3 %collective-permute-start.3 = (bf16[4,64,128]{2,1,0:T(8,128)(2,1)S(1)}, bf16[4,64,128]{2,1,0:T(8,128)(2,1)S(1)}, u32[]{:S(2)}, u32[]{:S(2)}) collective-permute-start(bf16[4,64,128]{2,1,0:T(8,128)(2,1)S(1)} %get-tuple-element.18), channel_id=1, source_target_pairs={{2,0},{4,2},{6,4},{3,1},{5,3},{7,5},{10,8},{12,10},{14,12},{11,9},... | collective-permute-start | bytes 196616 | tf_op jit(solution)/shard_map/ppermute | solution.py:406
  19.8 0.1 collective-permute-start.4
  19.9 0.5 collective-permute-done.2.refs_7_
  20.4 4.3 %collective-permute-done.3.refs_8_ = bf16[4,64,128]{2,1,0:T(8,128)(2,1)S(1)} collective-permute-done((bf16[4,64,128]{2,1,0:T(8,128)(2,1)S(1)}, bf16[4,64,128]{2,1,0:T(8,128)(2,1)S(1)}, u32[]{:S(2)}, u32[]{:S(2)}) %collective-permute-start.3) | collective-permute-done | bytes 65568 | tf_op jit(solution)/shard_map/ppermute | solution.py:406
  24.7 0.0 collective-permute-done.4.refs_9_.refs_10_
  24.7 0.0 collective-permute-done.refs_5_
  24.7 0.0 collective-permute-done.1.refs_6_
  24.7 0.0 copy-done
  24.7 0.0 copy-done.6
  24.7 0.0 copy-done.7
  24.7 0.0 copy-done.8
  24.7 0.0 copy-start.1
  24.7 2.2 %copy-done.1 = bf16[4,64,64,128]{3,2,1,0:T(8,128)(2,1)S(1)} copy-done((bf16[4,64,64,128]{3,2,1,0:T(8,128)(2,1)S(1)}, bf16[4,64,64,128]{3,2,1,0:T(8,128)(2,1)}, u32[]{:S(2)}) %copy-start.1) | copy-done | bytes 4194328
  26.9 0.0 copy-start.3
  26.9 1.6 %copy-done.3 = s32[64,64,128]{2,1,0:T(8,128)S(1)} copy-done((s32[64,64,128]{2,1,0:T(8,128)S(1)}, s32[64,64,128]{2,1,0:T(8,128)}, u32[]{:S(2)}) %copy-start.3) | copy-done | bytes 2097176
  28.5 9.7 %sweep_first.1 = (f32[4,64,64,128]{3,2,1,0:T(8,128)S(1)}, bf16[272,128]{1,0:T(8,128)(2,1)S(1)}, bf16[272,128]{1,0:T(8,128)(2,1)S(1)}, bf16[6,64,128]{2,1,0:T(8,1...) custom-call(f32[4]{0:T(128)S(1)} %copy-done.7, f32[4]{0:T(128)S(1)} %copy-done.8, ...), custom_call_target="tpu_custom_call" | custom-call | flops 50331648 | bytes 23068672 | tf_op jit(solution)/shard_map/sweep_first/pallas_call | solution.py:381
  38.2 1.3 %collective-permute-start.8 = (bf16[6,64,128]{2,1,0:T(8,128)(2,1)S(1)}, bf16[6,64,128]{2,1,0:T(8,128)(2,1)S(1)}, u32[]{:S(2)}, u32[]{:S(2)}) collective-permute-start(bf16[6,64,128]{2,1,0:T(8,128)(2,1)S(1)} %get-tuple-element.24.refs_12_), channel_id=1, source_target_pairs={{2,0},{4,2},{6,4},{3,1},{5,3},{7,5},{10,8},{12,10},{14,12},{11,9},... | collective-permute-start | bytes 294920 | tf_op jit(solution)/shard_map/ppermute | solution.py:406
  39.5 4.6 %collective-permute-start.7 = (bf16[6,64,128]{2,1,0:T(8,128)(2,1)S(1)}, bf16[6,64,128]{2,1,0:T(8,128)(2,1)S(1)}, u32[]{:S(2)}, u32[]{:S(2)}) collective-permute-start(bf16[6,64,128]{2,1,0:T(8,128)(2,1)S(1)} %get-tuple-element.23), channel_id=1, source_target_pairs={{0,2},{2,4},{4,6},{1,3},{3,5},{5,7},{8,10},{10,12},{12,14},{9,11},... | collective-permute-start | bytes 294920 | tf_op jit(solution)/shard_map/ppermute | solution.py:405
  44.0 4.6 %collective-permute-start.5 = (bf16[272,128]{1,0:T(8,128)(2,1)S(1)}, bf16[272,128]{1,0:T(8,128)(2,1)S(1)}, u32[]{:S(2)}, u32[]{:S(2)}) collective-permute-start(bf16[272,128]{1,0:T(8,128)(2,1)S(1)} %get-tuple-element.21), channel_id=1, source_target_pairs={{0,8},{8,16},{16,24},{1,9},{9,17},{17,25},{2,10},{10,18},{18,26},{... | collective-permute-start | bytes 208904 | tf_op jit(solution)/shard_map/ppermute | solution.py:405
  48.6 1.3 %collective-permute-start.6 = (bf16[272,128]{1,0:T(8,128)(2,1)S(1)}, bf16[272,128]{1,0:T(8,128)(2,1)S(1)}, u32[]{:S(2)}, u32[]{:S(2)}) collective-permute-start(bf16[272,128]{1,0:T(8,128)(2,1)S(1)} %get-tuple-element.22), channel_id=1, source_target_pairs={{8,0},{16,8},{24,16},{9,1},{17,9},{25,17},{10,2},{18,10},{26,18},{... | collective-permute-start | bytes 208904 | tf_op jit(solution)/shard_map/ppermute | solution.py:406
  49.9 0.1 collective-permute-start.9
  50.0 1.2 %collective-permute-done.9.refs_9_.refs_10_ = bf16[4,64,128]{2,1,0:T(8,128)(2,1)S(1)} collective-permute-done((bf16[4,64,128]{2,1,0:T(8,128)(2,1)S(1)}, bf16[4,64,128]{2,1,0:T(8,128)(2,1)S(1)}, u32[]{:S(2)}, u32[]{:S(2)}) %collective-permute-start.9) | collective-permute-done | bytes 65568 | tf_op jit(solution)/shard_map/ppermute | solution.py:409
  51.2 0.0 collective-permute-done.5.refs_5_
  51.2 3.9 %collective-permute-done.6.refs_6_ = bf16[272,128]{1,0:T(8,128)(2,1)S(1)} collective-permute-done((bf16[272,128]{1,0:T(8,128)(2,1)S(1)}, bf16[272,128]{1,0:T(8,128)(2,1)S(1)}, u32[]{:S(2)}, u32[]{:S(2)}) %collective-permute-start.6) | collective-permute-done | bytes 69664 | tf_op jit(solution)/shard_map/ppermute | solution.py:406
  55.2 0.0 collective-permute-done.8.refs_8_
  55.2 0.0 collective-permute-done.7.refs_7_
  55.2 0.0 copy-done.10
  55.2 0.0 copy-done.9
  55.2 0.0 copy-done.2
  55.2 0.0 copy-done.4
  55.2 13.6 %sweep_last.1 = (f32[4,64,64,128]{3,2,1,0:T(8,128)}, f32[40,128]{1,0:T(8,128)S(1)}) custom-call(f32[4]{0:T(128)S(1)} %copy-done.7, f32[4]{0:T(128)S(1)} %copy-done.8, f32[4,64,64,128]{3,2,1,0:T(8,128)S(1)} %get-tuple-element.20.refs_2_, bf16[4,64,64,128]{3,2,1,0:T(8,128)(2,1)S(1)} %copy-done.2, s32[64,64,128]{2,1,0:T(8,128)S(1)} %copy-done.4, ...), custom_call_target="tpu_custom_call" | custom-call | flops 50331648 | bytes 23068672 | tf_op jit(solution)/shard_map/sweep_last/pallas_call | solution.py:381
  68.8 1.8 %all-gather = f32[80,128]{1,0:T(8,128)S(1)} all-gather(f32[40,128]{1,0:T(8,128)S(1)} %get-tuple-element.27), channel_id=2, replica_groups=mesh['gx'=4,'gy'=4,'gz'=2] {'gz'}, dimensions={0}, use_global_device_ids=true | all-gather | bytes 61440 | tf_op jit(solution)/shard_map/all_gather | solution.py:486
  70.6 0.7 broadcast_in_dim.15
  71.4 6.3 %all-to-all-start = ((f32[16,40,128]{2,1,0:T(8,128)}), f32[16,40,128]{2,1,0:T(8,128)S(1)}, u32[]{:S(2)}, u32[]{:S(2)}) async-start(f32[16,40,128]{2,1,0:T(8,128)} %broadcast_in_dim.15), calls=%async_computation | async-start | bytes 655360 | tf_op jit(solution)/shard_map/all_to_all | solution.py:488
  77.7 12.3 %all-to-all-done.got_ref = f32[16,40,128]{2,1,0:T(8,128)S(1)} async-done(((f32[16,40,128]{2,1,0:T(8,128)}), f32[16,40,128]{2,1,0:T(8,128)S(1)}, u32[]{:S(2)}, u32[]{:S(2)}) %all-to-all-start) | async-done | bytes 327712 | tf_op jit(solution)/shard_map/all_to_all | solution.py:488
  90.0 2.2 %plane.1 = f32[1,16,512]{2,1,0:T(8,128)} custom-call(s32[1]{0:T(128)} %bitcast.1.me_ref, f32[16,40,128]{2,1,0:T(8,128)S(1)} %all-to-all-done.got_ref), custom_call_target="tpu_custom_call" | custom-call | tf_op jit(solution)/shard_map/plane/pallas_call | solution.py:490
  (4 shorter events, 0.0 us)
Async XLA Ops:
  0.6 24.0 %copy-start = (f32[4,64,64,128]{3,2,1,0:T(8,128)S(1)}, f32[4,64,64,128]{3,2,1,0:T(8,128)}, u32[]{:S(2)}) copy-start(f32[4,64,64,128]{3,2,1,0:T(8,128)} %refs_2_.1) | copy-start | bytes 25165828
  0.6 0.9 copy-start.5
  1.5 23.1 %copy-start.6 = (f32[64,64]{1,0:T(8,128)S(1)}, f32[64,64]{1,0:T(8,128)}, u32[]{:S(2)}) copy-start(f32[64,64]{1,0:T(8,128)} %refs_11_.2) | copy-start | bytes 49156
  1.6 23.1 %copy-start.7 = (f32[4]{0:T(128)S(1)}, f32[4]{0:T(128)}, u32[]{:S(2)}) copy-start(f32[4]{0:T(128)} %refs_0_.3) | copy-start | bytes 52
  1.6 23.1 %copy-start.8 = (f32[4]{0:T(128)S(1)}, f32[4]{0:T(128)}, u32[]{:S(2)}) copy-start(f32[4]{0:T(128)} %refs_1_.3) | copy-start | bytes 52
  8.8 46.3 %copy-start.10 = (s32[1,1,64,1]{2,3,1,0:T(1,128)S(1)}, s32[1,1,64,1]{2,3,1,0:T(1,128)}, u32[]{:S(2)}) copy-start(s32[1,1,64,1]{2,3,1,0:T(1,128)} %param.15) | copy-start | bytes 772
  8.8 46.4 %copy-start.9 = (f32[4]{0:T(128)S(1)}, f32[4]{0:T(128)}, u32[]{:S(2)}) copy-start(f32[4]{0:T(128)} %refs_11_.3) | copy-start | bytes 52
  8.8 15.8 %collective-permute-start = (bf16[272,128]{1,0:T(8,128)(2,1)S(1)}, bf16[272,128]{1,0:T(8,128)(2,1)S(1)}, u32[]{:S(2)}, u32[]{:S(2)}) collective-permute-start(bf16[272,128]{1,0:T(8,128)(2,1)S(1)} %get-tuple-element.15), channel_id=1, source_target_pairs={{0,8},{8,16},{16,24},{1,9},{9,17},{17,25},{2,10},{10,18},{18,26},{... | collective-permute-start | bytes 208904 | tf_op jit(solution)/shard_map/ppermute | solution.py:405
  13.7 11.0 %collective-permute-start.1 = (bf16[272,128]{1,0:T(8,128)(2,1)S(1)}, bf16[272,128]{1,0:T(8,128)(2,1)S(1)}, u32[]{:S(2)}, u32[]{:S(2)}) collective-permute-start(bf16[272,128]{1,0:T(8,128)(2,1)S(1)} %get-tuple-element.16), channel_id=1, source_target_pairs={{8,0},{16,8},{24,16},{9,1},{17,9},{25,17},{10,2},{18,10},{26,18},{... | collective-permute-start | bytes 208904 | tf_op jit(solution)/shard_map/ppermute | solution.py:406
  15.0 5.4 %collective-permute-start.2 = (bf16[4,64,128]{2,1,0:T(8,128)(2,1)S(1)}, bf16[4,64,128]{2,1,0:T(8,128)(2,1)S(1)}, u32[]{:S(2)}, u32[]{:S(2)}) collective-permute-start(bf16[4,64,128]{2,1,0:T(8,128)(2,1)S(1)} %get-tuple-element.17), channel_id=1, source_target_pairs={{0,2},{2,4},{4,6},{1,3},{3,5},{5,7},{8,10},{10,12},{12,14},{9,11},... | collective-permute-start | bytes 196616 | tf_op jit(solution)/shard_map/ppermute | solution.py:405
  18.5 6.2 %collective-permute-start.3 = (bf16[4,64,128]{2,1,0:T(8,128)(2,1)S(1)}, bf16[4,64,128]{2,1,0:T(8,128)(2,1)S(1)}, u32[]{:S(2)}, u32[]{:S(2)}) collective-permute-start(bf16[4,64,128]{2,1,0:T(8,128)(2,1)S(1)} %get-tuple-element.18), channel_id=1, source_target_pairs={{2,0},{4,2},{6,4},{3,1},{5,3},{7,5},{10,8},{12,10},{14,12},{11,9},... | collective-permute-start | bytes 196616 | tf_op jit(solution)/shard_map/ppermute | solution.py:406
  19.8 4.9 %collective-permute-start.4 = (bf16[4,64,128]{2,1,0:T(8,128)(2,1)S(1)}, bf16[4,64,128]{2,1,0:T(8,128)(2,1)S(1)}, u32[]{:S(2)}, u32[]{:S(2)}) collective-permute-start(bf16[4,64,128]{2,1,0:T(8,128)(2,1)S(1)} %get-tuple-element.19), channel_id=1, source_target_pairs={{0,1},{1,0},{2,3},{3,2},{4,5},{5,4},{6,7},{7,6},{8,9},{9,8},{10,11... | collective-permute-start | bytes 196616 | tf_op jit(solution)/shard_map/ppermute | solution.py:409
  24.7 2.2 %copy-start.1 = (bf16[4,64,64,128]{3,2,1,0:T(8,128)(2,1)S(1)}, bf16[4,64,64,128]{3,2,1,0:T(8,128)(2,1)}, u32[]{:S(2)}) copy-start(bf16[4,64,64,128]{3,2,1,0:T(8,128)(2,1)} %refs_3_.3) | copy-start | bytes 12582916
  26.9 1.6 %copy-start.3 = (s32[64,64,128]{2,1,0:T(8,128)S(1)}, s32[64,64,128]{2,1,0:T(8,128)}, u32[]{:S(2)}) copy-start(s32[64,64,128]{2,1,0:T(8,128)} %refs_4_.3) | copy-start | bytes 6291460
  28.5 26.7 %copy-start.2 = (bf16[4,64,64,128]{3,2,1,0:T(8,128)(2,1)S(1)}, bf16[4,64,64,128]{3,2,1,0:T(8,128)(2,1)}, u32[]{:S(2)}) copy-start(bf16[4,64,64,128]{3,2,1,0:T(8,128)(2,1)} %refs_3_.3) | copy-start | bytes 12582916
  28.5 26.7 %copy-start.4 = (s32[64,64,128]{2,1,0:T(8,128)S(1)}, s32[64,64,128]{2,1,0:T(8,128)}, u32[]{:S(2)}) copy-start(s32[64,64,128]{2,1,0:T(8,128)} %refs_4_.3) | copy-start | bytes 6291460
  38.2 17.0 %collective-permute-start.8 = (bf16[6,64,128]{2,1,0:T(8,128)(2,1)S(1)}, bf16[6,64,128]{2,1,0:T(8,128)(2,1)S(1)}, u32[]{:S(2)}, u32[]{:S(2)}) collective-permute-start(bf16[6,64,128]{2,1,0:T(8,128)(2,1)S(1)} %get-tuple-element.24.refs_12_), channel_id=1, source_target_pairs={{2,0},{4,2},{6,4},{3,1},{5,3},{7,5},{10,8},{12,10},{14,12},{11,9},... | collective-permute-start | bytes 294920 | tf_op jit(solution)/shard_map/ppermute | solution.py:406
  39.5 15.7 %collective-permute-start.7 = (bf16[6,64,128]{2,1,0:T(8,128)(2,1)S(1)}, bf16[6,64,128]{2,1,0:T(8,128)(2,1)S(1)}, u32[]{:S(2)}, u32[]{:S(2)}) collective-permute-start(bf16[6,64,128]{2,1,0:T(8,128)(2,1)S(1)} %get-tuple-element.23), channel_id=1, source_target_pairs={{0,2},{2,4},{4,6},{1,3},{3,5},{5,7},{8,10},{10,12},{12,14},{9,11},... | collective-permute-start | bytes 294920 | tf_op jit(solution)/shard_map/ppermute | solution.py:405
  44.0 7.2 %collective-permute-start.5 = (bf16[272,128]{1,0:T(8,128)(2,1)S(1)}, bf16[272,128]{1,0:T(8,128)(2,1)S(1)}, u32[]{:S(2)}, u32[]{:S(2)}) collective-permute-start(bf16[272,128]{1,0:T(8,128)(2,1)S(1)} %get-tuple-element.21), channel_id=1, source_target_pairs={{0,8},{8,16},{16,24},{1,9},{9,17},{17,25},{2,10},{10,18},{18,26},{... | collective-permute-start | bytes 208904 | tf_op jit(solution)/shard_map/ppermute | solution.py:405
  48.6 6.6 %collective-permute-start.6 = (bf16[272,128]{1,0:T(8,128)(2,1)S(1)}, bf16[272,128]{1,0:T(8,128)(2,1)S(1)}, u32[]{:S(2)}, u32[]{:S(2)}) collective-permute-start(bf16[272,128]{1,0:T(8,128)(2,1)S(1)} %get-tuple-element.22), channel_id=1, source_target_pairs={{8,0},{16,8},{24,16},{9,1},{17,9},{25,17},{10,2},{18,10},{26,18},{... | collective-permute-start | bytes 208904 | tf_op jit(solution)/shard_map/ppermute | solution.py:406
  49.9 1.3 %collective-permute-start.9 = (bf16[4,64,128]{2,1,0:T(8,128)(2,1)S(1)}, bf16[4,64,128]{2,1,0:T(8,128)(2,1)S(1)}, u32[]{:S(2)}, u32[]{:S(2)}) collective-permute-start(bf16[4,64,128]{2,1,0:T(8,128)(2,1)S(1)} %get-tuple-element.25), channel_id=1, source_target_pairs={{0,1},{1,0},{2,3},{3,2},{4,5},{5,4},{6,7},{7,6},{8,9},{9,8},{10,11... | collective-permute-start | bytes 196616 | tf_op jit(solution)/shard_map/ppermute | solution.py:409
  71.4 18.6 %all-to-all-start = ((f32[16,40,128]{2,1,0:T(8,128)}), f32[16,40,128]{2,1,0:T(8,128)S(1)}, u32[]{:S(2)}, u32[]{:S(2)}) async-start(f32[16,40,128]{2,1,0:T(8,128)} %broadcast_in_dim.15), calls=%async_computation | async-start | bytes 655360 | tf_op jit(solution)/shard_map/all_to_all | solution.py:488

commit v4 on v3

--- a/solution.py
+++ b/solution.py
@@ -15,6 +15,7 @@
 SHARPNESS = 8.0
 THRESHOLD = 0.5
 PB = 8
+RC = 16
 F32 = jnp.float32
 BF16 = jnp.bfloat16
 
@@ -24,10 +25,10 @@
 
 
 def ends_matrix(depth):
-    z = lax.broadcasted_iota(jnp.int32, (depth, depth), 0)
-    j = lax.broadcasted_iota(jnp.int32, (depth, depth), 1)
-    even = (z == 0) & (j % 2 == 0)
-    odd = (z == depth - 1) & (j % 2 == 1)
+    k = lax.broadcasted_iota(jnp.int32, (PB * depth, depth), 0)
+    j = lax.broadcasted_iota(jnp.int32, (PB * depth, depth), 1) % (2 * PB)
+    even = (k % depth == 0) & (j == 2 * (k // depth))
+    odd = (k % depth == depth - 1) & (j == 2 * (k // depth) + 1)
     return jnp.where(even | odd, 1.0, 0.0).astype(BF16)
 
 
@@ -43,6 +44,12 @@
     even = (z == 0) & (j % 2 == 0)
     odd = (z == depth - 1) & (j % 2 == 1)
     return jnp.where(even | odd, 1.0, 0.0).astype(BF16)
+
+
+def sum_matrix(depth):
+    k = lax.broadcasted_iota(jnp.int32, (2 * PB * depth, depth), 0) // (2 * depth)
+    j = lax.broadcasted_iota(jnp.int32, (2 * PB * depth, depth), 1) % PB
+    return jnp.where(k == j, 1.0, 0.0).astype(BF16)
 
 
 def split(value):
@@ -61,13 +68,12 @@
         for c in range(4):
             ylo[c, pl.ds(first + p, 1), :] = value[c, p, 0:1, :]
             yhi[c, pl.ds(first + p, 1), :] = value[c, p, rows - 1 :, :]
-    picked = mm(value.astype(BF16).reshape(4 * PB * rows, depth), ends).reshape(4, PB, rows, depth)
-    pair = lanes_of((rows, depth)) // 2
+    high = value.astype(BF16)
+    beside = [high[:, p].reshape(4 * rows, depth) for p in range(PB)]
+    picked = mm(jnp.concatenate(beside, 1), ends).reshape(4, rows, depth)
+    here = lanes_of((rows, depth)) // (2 * PB) == first // PB
     for c in range(4):
-        g = gs[c]
-        for p in range(PB):
-            g = jnp.where(pair == first + p, picked[c, p], g)
-        gs[c] = g
+        gs[c] = jnp.where(here, picked[c], gs[c])
 
 
 def put_plane(out_ref, value):
@@ -80,39 +86,46 @@
     return jnp.concatenate([high, value - high], 1)
 
 
-def pack_kernel(v_ref, d_ref, xlo_ref, xhi_ref, ylo_ref, yhi_ref, g_ref, gs, ylo, yhi, ends):
-    step, steps = pl.program_id(0), pl.num_programs(0)
+def x_kernel(v_ref, d_ref, xlo_ref, xhi_ref, planes, sems):
+    far = v_ref.shape[1] - 1
     rows, depth = v_ref.shape[2:]
-
-    @pl.when(step == 0)
-    def _():
-        gs[...] = jnp.zeros_like(gs)
-        ends[...] = ends_matrix(depth)
-        put_plane(xlo_ref, v_ref[:, 0])
-        cells = d_ref.shape[0]
-        none = jnp.zeros((R, depth), F32)
-        for out_ref, start in ((xlo_ref, 0), (xhi_ref, cells - R)):
-            strip = jnp.concatenate([paired(d_ref[start : start + R, :]), none], 0)
-            out_ref[4 * rows :] = strip.astype(BF16)
-
-    put_faces(step * PB, v_ref, 0, ends[...], gs, ylo, yhi)
-
-    @pl.when(step == steps - 1)
-    def _():
-        g_ref[...] = gs[...].astype(BF16)
-        ylo_ref[...] = ylo[...].astype(BF16)
-        yhi_ref[...] = yhi[...].astype(BF16)
-        put_plane(xhi_ref, v_ref[:, PB - 1])
+    copies = [
+        pltpu.make_async_copy(v_ref.at[:, x], planes.at[i], sems.at[i])
+        for i, x in enumerate((0, far))
+    ]
+    for copy in copies:
+        copy.start()
+    cells = d_ref.shape[0]
+    none = jnp.zeros((R, depth), F32)
+    for i, (out_ref, start) in enumerate(((xlo_ref, 0), (xhi_ref, cells - R))):
+        strip = jnp.concatenate([paired(d_ref[start : start + R, :]), none], 0)
+        out_ref[4 * rows :] = strip.astype(BF16)
+        copies[i].wait()
+        put_plane(out_ref, planes[i])
+
+
+def pack_kernel(v_ref, ylo_ref, yhi_ref, g_ref, gs, ylo, yhi, ends):
+    gs[...] = jnp.zeros_like(gs)
+    ends[...] = ends_matrix(v_ref.shape[3])
+
+    def group(i, carry):
+        put_faces(i * PB, v_ref, i * PB, ends[...], gs, ylo, yhi)
+        return carry
+
+    lax.fori_loop(0, v_ref.shape[1] // PB, group, 0)
+    g_ref[...] = gs[...].astype(BF16)
+    ylo_ref[...] = ylo[...].astype(BF16)
+    yhi_ref[...] = yhi[...].astype(BF16)
 
 
 def sweep_kernel(last, nz, scale, *refs):
     sr_ref, si_ref, v_ref, s_ref, m_ref, xl_ref, xr_ref, yl_ref, yr_ref, gl_ref, gr_ref = refs[:11]
     if last:
         sh_ref, mid_ref, own_ref, o_ref, sens_ref = refs[11:16]
-        hs, yl, yr, near, far, zt, sens, value, news, sems = refs[16:]
+        hs, yl, yr, near, far, zt0, zt1, sens, value, news, sums, sems = refs[16:]
     else:
         d_ref, o_ref, xlo_ref, xhi_ref, ylo_ref, yhi_ref, g_ref = refs[11:18]
-        hs, yl, yr, near, far, zt, gs, ylo, yhi, ends = refs[18:]
+        hs, yl, yr, near, far, zt0, zt1, gs, ylo, yhi, ends = refs[18:]
     planes_here, rows, depth = v_ref.shape[1:]
     lane = lanes_of((rows, depth))
 
@@ -129,6 +142,7 @@
     far[...] = halo_matrix(depth)
     if last:
         sens[...] = jnp.zeros_like(sens)
+        sums[...] = sum_matrix(depth)
     else:
         gs[...] = jnp.zeros_like(gs)
         ends[...] = ends_matrix(depth)
@@ -148,14 +162,14 @@
             share.append(jnp.full(tile, sh_ref[m], F32))
 
     def lookup(masks, table):
-        out = jnp.broadcast_to(table[0], (rows // 8, 8, depth))
+        out = jnp.broadcast_to(table[0], (RC // 8, 8, depth))
         for mask, entry in zip(masks, table[1:]):
             out = jnp.where(mask, entry, out)
-        return out.reshape(rows, depth)
+        return out.reshape(RC, depth)
 
     row8 = lax.broadcasted_iota(jnp.int32, tile, 0)
 
-    def along_z(first):
+    def along_z(first, zt):
         v = v_ref[:, pl.ds(first, PB)].reshape(4 * PB * rows, depth)
         masked = [
             jnp.where(lane // 2 == first + p, hs[c], 0.0).astype(BF16)
@@ -165,32 +179,44 @@
         out = mm(jnp.concatenate(split(v), 1), near[...]) + mm(jnp.concatenate(masked, 0), far[...])
         zt[...] = out.reshape(4, PB, rows, depth)
 
-    def plane(first, p, put):
+    def plane(first, p, zt, put):
+        for low in range(0, rows, RC):
+            chunk(first, p, low, zt, put)
+
+    def chunk(first, p, low, zt, put):
         x = first + p
-        mat = m_ref[x].reshape(rows // 8, 8, depth)
+        span = slice(low, low + RC)
+        mat = m_ref[x, span].reshape(RC // 8, 8, depth)
         masks = [mat == m for m in range(1, levels)]
         w_r, w_i = lookup(masks, wr), lookup(masks, wi)
 
         def drive(c):
-            v = v_ref[c, x]
+            v = v_ref[c, x, span]
+            part = slice(c * rows + low, c * rows + low + RC)
             if p == 0:
-                before = v_ref[c, jnp.maximum(x - 1, 0)]
-                before = jnp.where(x == 0, xl_ref[c * rows : (c + 1) * rows].astype(F32), before)
+                before = v_ref[c, jnp.maximum(x - 1, 0), span]
+                before = jnp.where(x == 0, xl_ref[part].astype(F32), before)
             else:
-                before = v_ref[c, x - 1]
+                before = v_ref[c, x - 1, span]
             if p == PB - 1:
-                after = v_ref[c, jnp.minimum(x + 1, planes_here - 1)]
-                edge = xr_ref[c * rows : (c + 1) * rows].astype(F32)
-                after = jnp.where(x == planes_here - 1, edge, after)
+                after = v_ref[c, jnp.minimum(x + 1, planes_here - 1), span]
+                after = jnp.where(x == planes_here - 1, xr_ref[part].astype(F32), after)
             else:
-                after = v_ref[c, x + 1]
-            total = before + after + s_ref[c, x].astype(F32) + zt[c, p]
-            up = pltpu.roll(v, 1, 0)
-            down = pltpu.roll(v, rows - 1, 0)
-            top = jnp.where(row8 == 0, yl[c, pl.ds(x, 1), :], up[:8])
-            low = jnp.where(row8 == 7, yr[c, pl.ds(x, 1), :], down[-8:])
-            total = total + jnp.concatenate([top, up[8:]], 0)
-            return v, total + jnp.concatenate([down[:-8], low], 0)
+                after = v_ref[c, x + 1, span]
+            total = before + after + s_ref[c, x, span].astype(F32) + zt[c, p, span]
+            if low == 0:
+                up = pltpu.roll(v, 1, 0)
+                top = jnp.where(row8 == 0, yl[c, pl.ds(x, 1), :], up[:8])
+                up = jnp.concatenate([top, up[8:]], 0)
+            else:
+                up = v_ref[c, x, low - 1 : low - 1 + RC]
+            if low == rows - RC:
+                down = pltpu.roll(v, RC - 1, 0)
+                tail = jnp.where(row8 == 7, yr[c, pl.ds(x, 1), :], down[-8:])
+                down = jnp.concatenate([down[:-8], tail], 0)
+            else:
+                down = v_ref[c, x, low + 1 : low + 1 + RC]
+            return v, total + up + down
 
         new = []
         for re in (0, 2):
@@ -199,52 +225,44 @@
             keep = 1.0 - RELAXATION
             n_r = keep * v_r + (w_r * t_r - w_i * t_i)
             n_i = keep * v_i + (w_r * t_i + w_i * t_r)
-            put(re, n_r)
-            put(re + 1, n_i)
+            put(re, span, n_r)
+            put(re + 1, span, n_i)
             new += [n_r, n_i]
         if last:
-            value[p] = lookup(masks, share) * (new[0] * new[2] - new[1] * new[3])
+            value[p, span] = lookup(masks, share) * (new[0] * new[2] - new[1] * new[3])
 
     groups = planes_here // PB
 
-    def store(slot, first):
-        return pltpu.make_async_copy(
-            news.at[slot], o_ref.at[:, pl.ds(first, PB)], sems.at[slot]
-        )
-
-    def group(i, carry):
+    def store(i):
+        part = pl.ds(i * PB, PB)
+        return pltpu.make_async_copy(news.at[:, part], o_ref.at[:, part], sems.at[i])
+
+    result = news if last else o_ref
+
+    def group(i, zt, zt_next):
         first = i * PB
-        along_z(first)
+        along_z(jnp.minimum(first + PB, planes_here - PB), zt_next)
+        for p in range(PB):
+
+            def put(c, span, new, p=p):
+                result[c, first + p, span] = new
+
+            plane(first, p, zt, put)
         if last:
-            slot = i % 2
-
-            @pl.when(i >= 2)
-            def _():
-                store(slot, first - 2 * PB).wait()
-
-        for p in range(PB):
-
-            def put(c, new, p=p):
-                if last:
-                    news[slot, c, p] = new
-                else:
-                    o_ref[c, first + p] = new
-
-            plane(first, p, put)
-        if last:
-            store(slot, first).start()
-            ones = jnp.ones((2 * depth, depth), BF16)
-            parts = split(value[...].reshape(PB * rows, depth))
-            sums = mm(jnp.concatenate(parts, 1), ones).reshape(PB, rows, depth)
-            held = sens[...]
-            for p in range(PB):
-                held = jnp.where(lane == first + p, sums[p], held)
-            sens[...] = held
+            store(i).start()
+            parts = [part for p in range(PB) for part in split(value[p])]
+            picked = mm(jnp.concatenate(parts, 1), sums[...])
+            sens[...] = jnp.where(lane // PB == i, picked, sens[...])
         else:
             put_faces(first, o_ref, first, ends[...], gs, ylo, yhi)
+
+    def two(i, carry):
+        group(2 * i, zt0, zt1)
+        group(2 * i + 1, zt1, zt0)
         return carry
 
-    lax.fori_loop(0, groups, group, 0)
+    along_z(0, zt0)
+    lax.fori_loop(0, groups // 2, two, 0)
 
     if not last:
         put_plane(xlo_ref, o_ref[:, 0])
@@ -287,8 +305,8 @@
         sens_ref[:half] = jnp.where(lane[:half] < depth // 2, weighted[:half], both)
         mine = jnp.where(lax.axis_index("gz") == 0, own_ref[...].astype(F32), 0.0)
         sens_ref[half:] = jnp.concatenate([mine, jnp.zeros((8, depth - rows), F32)], 1)
-        store((groups - 2) % 2, (groups - 2) * PB).wait()
-        store((groups - 1) % 2, (groups - 1) * PB).wait()
+        for i in range(groups):
+            store(i).wait()
 
 
 def twice(value, right):
@@ -319,29 +337,41 @@
         pltpu.VMEM((4, ny, nz), F32),
         pltpu.VMEM((4, nx, nz), F32),
         pltpu.VMEM((4, nx, nz), F32),
-        pltpu.VMEM((nz, nz), BF16),
+        pltpu.VMEM((PB * nz, nz), BF16),
     ]
+
+
+def near(value):
+    return pltpu.with_memory_space_constraint(value, pltpu.VMEM)
 
 
 def pack(fields, density):
     _, nx, ny, nz = fields.shape
-    shapes = message_shapes(nx, ny, nz, 4)
-    return pl.pallas_call(
+    shapes = [jax.ShapeDtypeStruct(s, BF16) for s in message_shapes(nx, ny, nz, 4)]
+    xlo, xhi = pl.pallas_call(
+        x_kernel,
+        in_specs=[pl.BlockSpec(memory_space=pltpu.HBM), VMEM_SPEC],
+        out_specs=[VMEM_SPEC] * 2,
+        out_shape=shapes[:2],
+        scratch_shapes=[pltpu.VMEM((2, 4, ny, nz), F32), pltpu.SemaphoreType.DMA((2,))],
+        compiler_params=pltpu.CompilerParams(vmem_limit_bytes=4 << 20),
+        cost_estimate=pl.CostEstimate(flops=ny * nz * 8, bytes_accessed=ny * nz * 48, transcendentals=0),
+        name="x_faces",
+    )(pltpu.with_memory_space_constraint(fields, pltpu.HBM), density)
+    held = near(fields)
+    ylo, yhi, g = pl.pallas_call(
         pack_kernel,
-        grid=(nx // PB,),
-        in_specs=[
-            pl.BlockSpec((4, PB, ny, nz), lambda i: (0, i, 0, 0)),
-            whole(density.shape),
-        ],
-        out_specs=[whole(s) for s in shapes],
-        out_shape=[jax.ShapeDtypeStruct(s, BF16) for s in shapes],
+        in_specs=[VMEM_SPEC],
+        out_specs=[VMEM_SPEC] * 3,
+        out_shape=shapes[2:],
         scratch_shapes=face_scratch(nx, ny, nz),
         compiler_params=pltpu.CompilerParams(vmem_limit_bytes=12 << 20),
         cost_estimate=pl.CostEstimate(
             flops=fields.size * 4, bytes_accessed=fields.size * 4, transcendentals=0
         ),
         name="pack_faces",
-    )(pltpu.with_memory_space_constraint(fields, pltpu.HBM), density)
+    )(held)
+    return held, (xlo, xhi, ylo, yhi, g)
 
 
 def sweep(last, tables, current, sources, material, halos, more):
@@ -352,6 +382,7 @@
         pltpu.VMEM((4, nx, nz), F32),
         pltpu.VMEM((2 * nz, nz), BF16),
         pltpu.VMEM((nz, nz), BF16),
+        pltpu.VMEM((4, PB, ny, nz), F32),
         pltpu.VMEM((4, PB, ny, nz), F32),
     ]
     if last:
@@ -364,8 +395,9 @@
         scratch += [
             pltpu.VMEM((ny, nz), F32),
             pltpu.VMEM((PB, ny, nz), F32),
-            pltpu.VMEM((2, 4, PB, ny, nz), F32),
-            pltpu.SemaphoreType.DMA((2,)),
+            pltpu.VMEM(current.shape, F32),
+            pltpu.VMEM((2 * PB * nz, nz), BF16),
+            pltpu.SemaphoreType.DMA((nx // PB,)),
         ]
     else:
         faces = message_shapes(nx, ny, nz, 6)
@@ -374,9 +406,6 @@
         specs = [VMEM_SPEC] * len(shapes)
         more_specs = [VMEM_SPEC]
         scratch += face_scratch(nx, ny, nz)
-
-    def near(value):
-        return pltpu.with_memory_space_constraint(value, pltpu.VMEM)
 
     return pl.pallas_call(
         functools.partial(
@@ -478,8 +507,9 @@
     cells = density.shape[0]
     tables = (shift_real, shift_imag)
     owners = jnp.broadcast_to(owner_map.reshape(1, -1), (8, cells))
-    halos = exchange(*pack(fields, density))
-    middle, *faces = sweep(False, tables, fields, sources, material, halos, [density])
+    held, faces = pack(fields, density)
+    halos = exchange(*faces)
+    middle, *faces = sweep(False, tables, held, sources, material, halos, [density])
     final, partial = sweep(
         True, tables, middle, sources, material, exchange(*faces), [design_share, faces[2], owners]
     )

time: 92.8 us -> 84.5 us (0.911)
  Pallas kernels: 32.8 us -> 28.1 us
  local copies, waits for them, and re-layouts: 5.45 us -> 1.69 us
    unnamed x22 -> x18, local copies, waits for them, and re-layouts: 4.71 us -> 0.94 us
    pallas_call x1 -> x2, Pallas kernels: 7.26 us -> 3.82 us  [the longest x1 2.42 us: pack(): pl.pallas_call(pack_kernel, in_specs=[VMEM_SPEC], out_specs=[VMEM_SPEC] *...]
    pallas_call x2, Pallas kernels: 23.3 us -> 22 us  [sweep(): pl.pallas_call(functools.partial(sweep_kernel, last, lax.axis_size('gz'),...]
  transfers between devices with their start and end apart: 11 -> 11, of which waited for: 5 -> 5; matrix products, arithmetic and copies ran while one was open for 0% -> 0% of each run, Pallas kernels for 0% -> 3%
where the time goes in v4:
time: 84.5 us; the launch traced here: 84.1 us
  starting transfers between devices  29.3 us (35%)
  Pallas kernels  28.1 us (33%)
  waiting for transfers between devices  22.3 us (26%)
  blocking collectives  1.83 us (2%)
  local copies, waits for them, and re-layouts  1.69 us (2%)
  between operations  0.87 us (1%)
    pallas_call x2, Pallas kernels, sweep(): pl.pallas_call(functools.partial(sweep_kernel, last, lax.axis_size('gz'),...  22 us
    ppermute x4, starting transfers between devices, exchange(): out.append(lax.ppermute(high, axis, up))  17.7 us
    all_to_all x1, waiting for transfers between devices, on_device(): plane = lax.all_to_all(copies, ('gx', 'gy'), split_axis=0, concat_axis=0)  12.3 us
    ppermute x4, waiting for transfers between devices, exchange(): out.append(lax.ppermute(low, axis, [(j, i) for i, j in up]))  8.23 us
    all_to_all x1, starting transfers between devices, on_device(): plane = lax.all_to_all(copies, ('gx', 'gy'), split_axis=0, concat_axis=0)  6.32 us
    ppermute x4, starting transfers between devices, exchange(): out.append(lax.ppermute(low, axis, [(j, i) for i, j in up]))  5.16 us
    pallas_call x1, Pallas kernels, pack(): pl.pallas_call(pack_kernel, in_specs=[VMEM_SPEC], out_specs=[VMEM_SPEC] *...  2.42 us
    pallas_call x1, Pallas kernels, on_device(): pl.pallas_call(functools.partial(plane_kernel, ngx, ngy), in_specs=[SMEM_...  2.24 us
  transfers between devices with their start and end apart: 11, of which 5 were waited for; matrix products, arithmetic and copies ran while one was open for 0% of the time, Pallas kernels for 3%

profile of v4, /device:TPU:0, one launch (start us, length us, event | category | flops | bytes accessed | tf_op | source)
XLA Modules:
  0.0 84.1 jit_solution(12707906404835222158)
XLA Ops:
  0.6 0.0 copy-start
  0.6 0.0 copy-start.2
  0.7 0.0 copy-start.1
  0.7 0.0 copy-start.3
  0.7 0.9 %copy-done.3 = f32[64,64]{1,0:T(8,128)S(1)} copy-done((f32[64,64]{1,0:T(8,128)S(1)}, f32[64,64]{1,0:T(8,128)}, u32[]{:S(2)}) %copy-start.3) | copy-done | bytes 16408
  1.6 0.0 copy-start.4
  1.6 0.0 copy-start.5
  1.6 0.0 copy-start.6
  1.6 1.4 %x_faces.1 = (bf16[272,128]{1,0:T(8,128)(2,1)S(1)}, bf16[272,128]{1,0:T(8,128)(2,1)S(1)}) custom-call(f32[4,64,64,128]{3,2,1,0:T(8,128)} %refs_2_.1, f32[64,64]{1,0:T(8,128)S(1)} %copy-done.3), custom_call_target="tpu_custom_call" | custom-call | flops 65536 | bytes 393216 | tf_op jit(solution)/shard_map/x_faces/pallas_call | solution.py:351
  3.0 5.1 %collective-permute-start = (bf16[272,128]{1,0:T(8,128)(2,1)S(1)}, bf16[272,128]{1,0:T(8,128)(2,1)S(1)}, u32[]{:S(2)}, u32[]{:S(2)}) collective-permute-start(bf16[272,128]{1,0:T(8,128)(2,1)S(1)} %get-tuple-element.15), channel_id=1, source_target_pairs={{0,8},{8,16},{16,24},{1,9},{9,17},{17,25},{2,10},{10,18},{18,26},{... | collective-permute-start | bytes 208904 | tf_op jit(solution)/shard_map/ppermute | solution.py:434
  8.1 1.3 %collective-permute-start.1 = (bf16[272,128]{1,0:T(8,128)(2,1)S(1)}, bf16[272,128]{1,0:T(8,128)(2,1)S(1)}, u32[]{:S(2)}, u32[]{:S(2)}) collective-permute-start(bf16[272,128]{1,0:T(8,128)(2,1)S(1)} %get-tuple-element.16), channel_id=1, source_target_pairs={{8,0},{16,8},{24,16},{9,1},{17,9},{25,17},{10,2},{18,10},{26,18},{... | collective-permute-start | bytes 208904 | tf_op jit(solution)/shard_map/ppermute | solution.py:435
  9.4 0.0 copy-done
  9.4 2.4 %pack_faces.1 = (bf16[4,64,128]{2,1,0:T(8,128)(2,1)S(1)}, bf16[4,64,128]{2,1,0:T(8,128)(2,1)S(1)}, bf16[4,64,128]{2,1,0:T(8,128)(2,1)S(1)}) custom-call(f32[4,64,64,128]{3,2,1,0:T(8,128)S(1)} %copy-done), custom_call_target="tpu_custom_call" | custom-call | flops 8388608 | bytes 8388608 | tf_op jit(solution)/shard_map/pack_faces/pallas_call | solution.py:362
  11.8 0.0 copy-start.8
  11.9 0.0 copy-start.7
  11.9 3.5 %collective-permute-start.2 = (bf16[4,64,128]{2,1,0:T(8,128)(2,1)S(1)}, bf16[4,64,128]{2,1,0:T(8,128)(2,1)S(1)}, u32[]{:S(2)}, u32[]{:S(2)}) collective-permute-start(bf16[4,64,128]{2,1,0:T(8,128)(2,1)S(1)} %get-tuple-element.17), channel_id=1, source_target_pairs={{0,2},{2,4},{4,6},{1,3},{3,5},{5,7},{8,10},{10,12},{12,14},{9,11},... | collective-permute-start | bytes 196616 | tf_op jit(solution)/shard_map/ppermute | solution.py:434
  15.4 1.3 %collective-permute-start.3 = (bf16[4,64,128]{2,1,0:T(8,128)(2,1)S(1)}, bf16[4,64,128]{2,1,0:T(8,128)(2,1)S(1)}, u32[]{:S(2)}, u32[]{:S(2)}) collective-permute-start(bf16[4,64,128]{2,1,0:T(8,128)(2,1)S(1)} %get-tuple-element.18), channel_id=1, source_target_pairs={{2,0},{4,2},{6,4},{3,1},{5,3},{7,5},{10,8},{12,10},{14,12},{11,9},... | collective-permute-start | bytes 196616 | tf_op jit(solution)/shard_map/ppermute | solution.py:435
  16.7 0.1 collective-permute-start.4
  16.7 0.5 collective-permute-done.2.refs_7_
  17.2 4.3 %collective-permute-done.3.refs_8_ = bf16[4,64,128]{2,1,0:T(8,128)(2,1)S(1)} collective-permute-done((bf16[4,64,128]{2,1,0:T(8,128)(2,1)S(1)}, bf16[4,64,128]{2,1,0:T(8,128)(2,1)S(1)}, u32[]{:S(2)}, u32[]{:S(2)}) %collective-permute-start.3) | collective-permute-done | bytes 65568 | tf_op jit(solution)/shard_map/ppermute | solution.py:435
  21.5 0.0 collective-permute-done.4.refs_9_.refs_10_
  21.5 0.0 collective-permute-done.refs_5_
  21.5 0.0 collective-permute-done.1.refs_6_
  21.5 0.0 copy-done.2
  21.5 0.0 copy-done.1
  21.6 0.0 copy-done.4
  21.6 0.0 copy-done.5
  21.6 0.0 copy-done.6
  21.6 10.7 %sweep_first.1 = (f32[4,64,64,128]{3,2,1,0:T(8,128)S(1)}, bf16[272,128]{1,0:T(8,128)(2,1)S(1)}, bf16[272,128]{1,0:T(8,128)(2,1)S(1)}, bf16[6,64,128]{2,1,0:T(8,1...) custom-call(f32[4]{0:T(128)S(1)} %copy-done.5, f32[4]{0:T(128)S(1)} %copy-done.6, ...), custom_call_target="tpu_custom_call" | custom-call | flops 50331648 | bytes 23068672 | tf_op jit(solution)/shard_map/sweep_first/pallas_call | solution.py:410
  32.2 1.3 %collective-permute-start.8 = (bf16[6,64,128]{2,1,0:T(8,128)(2,1)S(1)}, bf16[6,64,128]{2,1,0:T(8,128)(2,1)S(1)}, u32[]{:S(2)}, u32[]{:S(2)}) collective-permute-start(bf16[6,64,128]{2,1,0:T(8,128)(2,1)S(1)} %get-tuple-element.24.refs_12_), channel_id=1, source_target_pairs={{2,0},{4,2},{6,4},{3,1},{5,3},{7,5},{10,8},{12,10},{14,12},{11,9},... | collective-permute-start | bytes 294920 | tf_op jit(solution)/shard_map/ppermute | solution.py:435
  33.5 4.6 %collective-permute-start.7 = (bf16[6,64,128]{2,1,0:T(8,128)(2,1)S(1)}, bf16[6,64,128]{2,1,0:T(8,128)(2,1)S(1)}, u32[]{:S(2)}, u32[]{:S(2)}) collective-permute-start(bf16[6,64,128]{2,1,0:T(8,128)(2,1)S(1)} %get-tuple-element.23), channel_id=1, source_target_pairs={{0,2},{2,4},{4,6},{1,3},{3,5},{5,7},{8,10},{10,12},{12,14},{9,11},... | collective-permute-start | bytes 294920 | tf_op jit(solution)/shard_map/ppermute | solution.py:434
  38.1 4.6 %collective-permute-start.5 = (bf16[272,128]{1,0:T(8,128)(2,1)S(1)}, bf16[272,128]{1,0:T(8,128)(2,1)S(1)}, u32[]{:S(2)}, u32[]{:S(2)}) collective-permute-start(bf16[272,128]{1,0:T(8,128)(2,1)S(1)} %get-tuple-element.21), channel_id=1, source_target_pairs={{0,8},{8,16},{16,24},{1,9},{9,17},{17,25},{2,10},{10,18},{18,26},{... | collective-permute-start | bytes 208904 | tf_op jit(solution)/shard_map/ppermute | solution.py:434
  42.7 1.3 %collective-permute-start.6 = (bf16[272,128]{1,0:T(8,128)(2,1)S(1)}, bf16[272,128]{1,0:T(8,128)(2,1)S(1)}, u32[]{:S(2)}, u32[]{:S(2)}) collective-permute-start(bf16[272,128]{1,0:T(8,128)(2,1)S(1)} %get-tuple-element.22), channel_id=1, source_target_pairs={{8,0},{16,8},{24,16},{9,1},{17,9},{25,17},{10,2},{18,10},{26,18},{... | collective-permute-start | bytes 208904 | tf_op jit(solution)/shard_map/ppermute | solution.py:435
  44.0 0.1 collective-permute-start.9
  44.0 1.2 %collective-permute-done.9.refs_9_.refs_10_ = bf16[4,64,128]{2,1,0:T(8,128)(2,1)S(1)} collective-permute-done((bf16[4,64,128]{2,1,0:T(8,128)(2,1)S(1)}, bf16[4,64,128]{2,1,0:T(8,128)(2,1)S(1)}, u32[]{:S(2)}, u32[]{:S(2)}) %collective-permute-start.9) | collective-permute-done | bytes 65568 | tf_op jit(solution)/shard_map/ppermute | solution.py:438
  45.3 0.0 collective-permute-done.5.refs_5_
  45.3 4.0 %collective-permute-done.6.refs_6_ = bf16[272,128]{1,0:T(8,128)(2,1)S(1)} collective-permute-done((bf16[272,128]{1,0:T(8,128)(2,1)S(1)}, bf16[272,128]{1,0:T(8,128)(2,1)S(1)}, u32[]{:S(2)}, u32[]{:S(2)}) %collective-permute-start.6) | collective-permute-done | bytes 69664 | tf_op jit(solution)/shard_map/ppermute | solution.py:435
  49.2 0.0 collective-permute-done.8.refs_8_
  49.2 0.0 collective-permute-done.7.refs_7_
  49.2 0.0 copy-done.8
  49.3 0.0 copy-done.7
  49.3 11.4 %sweep_last.1 = (f32[4,64,64,128]{3,2,1,0:T(8,128)}, f32[40,128]{1,0:T(8,128)S(1)}) custom-call(f32[4]{0:T(128)S(1)} %copy-done.5, f32[4]{0:T(128)S(1)} %copy-done.6, f32[4,64,64,128]{3,2,1,0:T(8,128)S(1)} %get-tuple-element.20.refs_2_, bf16[4,64,64,128]{3,2,1,0:T(8,128)(2,1)S(1)} %copy-done.1, s32[64,64,128]{2,1,0:T(8,128)S(1)} %copy-done.2, ...), custom_call_target="tpu_custom_call" | custom-call | flops 50331648 | bytes 23068672 | tf_op jit(solution)/shard_map/sweep_last/pallas_call | solution.py:410
  60.6 1.8 %all-gather = f32[80,128]{1,0:T(8,128)S(1)} all-gather(f32[40,128]{1,0:T(8,128)S(1)} %get-tuple-element.27), channel_id=2, replica_groups=mesh['gx'=4,'gy'=4,'gz'=2] {'gz'}, dimensions={0}, use_global_device_ids=true | all-gather | bytes 61440 | tf_op jit(solution)/shard_map/all_gather | solution.py:516
  62.5 0.7 broadcast_in_dim.15
  63.2 6.3 %all-to-all-start = ((f32[16,40,128]{2,1,0:T(8,128)}), f32[16,40,128]{2,1,0:T(8,128)S(1)}, u32[]{:S(2)}, u32[]{:S(2)}) async-start(f32[16,40,128]{2,1,0:T(8,128)} %broadcast_in_dim.15), calls=%async_computation | async-start | bytes 655360 | tf_op jit(solution)/shard_map/all_to_all | solution.py:518
  69.6 12.3 %all-to-all-done.got_ref = f32[16,40,128]{2,1,0:T(8,128)S(1)} async-done(((f32[16,40,128]{2,1,0:T(8,128)}), f32[16,40,128]{2,1,0:T(8,128)S(1)}, u32[]{:S(2)}, u32[]{:S(2)}) %all-to-all-start) | async-done | bytes 327712 | tf_op jit(solution)/shard_map/all_to_all | solution.py:518
  81.9 2.2 %plane.1 = f32[1,16,512]{2,1,0:T(8,128)} custom-call(s32[1]{0:T(128)} %bitcast.1.me_ref, f32[16,40,128]{2,1,0:T(8,128)S(1)} %all-to-all-done.got_ref), custom_call_target="tpu_custom_call" | custom-call | tf_op jit(solution)/shard_map/plane/pallas_call | solution.py:520
  (2 shorter events, 0.0 us)
Async XLA Ops:
  0.6 8.8 %copy-start = (f32[4,64,64,128]{3,2,1,0:T(8,128)S(1)}, f32[4,64,64,128]{3,2,1,0:T(8,128)}, u32[]{:S(2)}) copy-start(f32[4,64,64,128]{3,2,1,0:T(8,128)} %refs_2_.1) | copy-start | bytes 25165828
  0.6 20.9 %copy-start.2 = (s32[64,64,128]{2,1,0:T(8,128)S(1)}, s32[64,64,128]{2,1,0:T(8,128)}, u32[]{:S(2)}) copy-start(s32[64,64,128]{2,1,0:T(8,128)} %refs_4_.3) | copy-start | bytes 6291460
  0.7 20.9 %copy-start.1 = (bf16[4,64,64,128]{3,2,1,0:T(8,128)(2,1)S(1)}, bf16[4,64,64,128]{3,2,1,0:T(8,128)(2,1)}, u32[]{:S(2)}) copy-start(bf16[4,64,64,128]{3,2,1,0:T(8,128)(2,1)} %refs_3_.3) | copy-start | bytes 12582916
  0.7 0.9 %copy-start.3 = (f32[64,64]{1,0:T(8,128)S(1)}, f32[64,64]{1,0:T(8,128)}, u32[]{:S(2)}) copy-start(f32[64,64]{1,0:T(8,128)} %refs_11_.2) | copy-start | bytes 49156
  1.6 20.0 %copy-start.4 = (f32[64,64]{1,0:T(8,128)S(1)}, f32[64,64]{1,0:T(8,128)}, u32[]{:S(2)}) copy-start(f32[64,64]{1,0:T(8,128)} %refs_11_.2) | copy-start | bytes 49156
  1.6 20.0 %copy-start.5 = (f32[4]{0:T(128)S(1)}, f32[4]{0:T(128)}, u32[]{:S(2)}) copy-start(f32[4]{0:T(128)} %refs_0_.3) | copy-start | bytes 52
  1.6 20.0 %copy-start.6 = (f32[4]{0:T(128)S(1)}, f32[4]{0:T(128)}, u32[]{:S(2)}) copy-start(f32[4]{0:T(128)} %refs_1_.3) | copy-start | bytes 52
  3.0 18.5 %collective-permute-start = (bf16[272,128]{1,0:T(8,128)(2,1)S(1)}, bf16[272,128]{1,0:T(8,128)(2,1)S(1)}, u32[]{:S(2)}, u32[]{:S(2)}) collective-permute-start(bf16[272,128]{1,0:T(8,128)(2,1)S(1)} %get-tuple-element.15), channel_id=1, source_target_pairs={{0,8},{8,16},{16,24},{1,9},{9,17},{17,25},{2,10},{10,18},{18,26},{... | collective-permute-start | bytes 208904 | tf_op jit(solution)/shard_map/ppermute | solution.py:434
  8.1 13.4 %collective-permute-start.1 = (bf16[272,128]{1,0:T(8,128)(2,1)S(1)}, bf16[272,128]{1,0:T(8,128)(2,1)S(1)}, u32[]{:S(2)}, u32[]{:S(2)}) collective-permute-start(bf16[272,128]{1,0:T(8,128)(2,1)S(1)} %get-tuple-element.16), channel_id=1, source_target_pairs={{8,0},{16,8},{24,16},{9,1},{17,9},{25,17},{10,2},{18,10},{26,18},{... | collective-permute-start | bytes 208904 | tf_op jit(solution)/shard_map/ppermute | solution.py:435
  11.8 37.4 %copy-start.8 = (s32[1,1,64,1]{2,3,1,0:T(1,128)S(1)}, s32[1,1,64,1]{2,3,1,0:T(1,128)}, u32[]{:S(2)}) copy-start(s32[1,1,64,1]{2,3,1,0:T(1,128)} %param.15) | copy-start | bytes 772
  11.9 37.4 %copy-start.7 = (f32[4]{0:T(128)S(1)}, f32[4]{0:T(128)}, u32[]{:S(2)}) copy-start(f32[4]{0:T(128)} %refs_11_.3) | copy-start | bytes 52
  11.9 5.4 %collective-permute-start.2 = (bf16[4,64,128]{2,1,0:T(8,128)(2,1)S(1)}, bf16[4,64,128]{2,1,0:T(8,128)(2,1)S(1)}, u32[]{:S(2)}, u32[]{:S(2)}) collective-permute-start(bf16[4,64,128]{2,1,0:T(8,128)(2,1)S(1)} %get-tuple-element.17), channel_id=1, source_target_pairs={{0,2},{2,4},{4,6},{1,3},{3,5},{5,7},{8,10},{10,12},{12,14},{9,11},... | collective-permute-start | bytes 196616 | tf_op jit(solution)/shard_map/ppermute | solution.py:434
  15.4 6.2 %collective-permute-start.3 = (bf16[4,64,128]{2,1,0:T(8,128)(2,1)S(1)}, bf16[4,64,128]{2,1,0:T(8,128)(2,1)S(1)}, u32[]{:S(2)}, u32[]{:S(2)}) collective-permute-start(bf16[4,64,128]{2,1,0:T(8,128)(2,1)S(1)} %get-tuple-element.18), channel_id=1, source_target_pairs={{2,0},{4,2},{6,4},{3,1},{5,3},{7,5},{10,8},{12,10},{14,12},{11,9},... | collective-permute-start | bytes 196616 | tf_op jit(solution)/shard_map/ppermute | solution.py:435
  16.7 4.9 %collective-permute-start.4 = (bf16[4,64,128]{2,1,0:T(8,128)(2,1)S(1)}, bf16[4,64,128]{2,1,0:T(8,128)(2,1)S(1)}, u32[]{:S(2)}, u32[]{:S(2)}) collective-permute-start(bf16[4,64,128]{2,1,0:T(8,128)(2,1)S(1)} %get-tuple-element.19), channel_id=1, source_target_pairs={{0,1},{1,0},{2,3},{3,2},{4,5},{5,4},{6,7},{7,6},{8,9},{9,8},{10,11... | collective-permute-start | bytes 196616 | tf_op jit(solution)/shard_map/ppermute | solution.py:438
  32.2 17.0 %collective-permute-start.8 = (bf16[6,64,128]{2,1,0:T(8,128)(2,1)S(1)}, bf16[6,64,128]{2,1,0:T(8,128)(2,1)S(1)}, u32[]{:S(2)}, u32[]{:S(2)}) collective-permute-start(bf16[6,64,128]{2,1,0:T(8,128)(2,1)S(1)} %get-tuple-element.24.refs_12_), channel_id=1, source_target_pairs={{2,0},{4,2},{6,4},{3,1},{5,3},{7,5},{10,8},{12,10},{14,12},{11,9},... | collective-permute-start | bytes 294920 | tf_op jit(solution)/shard_map/ppermute | solution.py:435
  33.5 15.7 %collective-permute-start.7 = (bf16[6,64,128]{2,1,0:T(8,128)(2,1)S(1)}, bf16[6,64,128]{2,1,0:T(8,128)(2,1)S(1)}, u32[]{:S(2)}, u32[]{:S(2)}) collective-permute-start(bf16[6,64,128]{2,1,0:T(8,128)(2,1)S(1)} %get-tuple-element.23), channel_id=1, source_target_pairs={{0,2},{2,4},{4,6},{1,3},{3,5},{5,7},{8,10},{10,12},{12,14},{9,11},... | collective-permute-start | bytes 294920 | tf_op jit(solution)/shard_map/ppermute | solution.py:434
  38.1 7.2 %collective-permute-start.5 = (bf16[272,128]{1,0:T(8,128)(2,1)S(1)}, bf16[272,128]{1,0:T(8,128)(2,1)S(1)}, u32[]{:S(2)}, u32[]{:S(2)}) collective-permute-start(bf16[272,128]{1,0:T(8,128)(2,1)S(1)} %get-tuple-element.21), channel_id=1, source_target_pairs={{0,8},{8,16},{16,24},{1,9},{9,17},{17,25},{2,10},{10,18},{18,26},{... | collective-permute-start | bytes 208904 | tf_op jit(solution)/shard_map/ppermute | solution.py:434
  42.7 6.6 %collective-permute-start.6 = (bf16[272,128]{1,0:T(8,128)(2,1)S(1)}, bf16[272,128]{1,0:T(8,128)(2,1)S(1)}, u32[]{:S(2)}, u32[]{:S(2)}) collective-permute-start(bf16[272,128]{1,0:T(8,128)(2,1)S(1)} %get-tuple-element.22), channel_id=1, source_target_pairs={{8,0},{16,8},{24,16},{9,1},{17,9},{25,17},{10,2},{18,10},{26,18},{... | collective-permute-start | bytes 208904 | tf_op jit(solution)/shard_map/ppermute | solution.py:435
  44.0 1.3 %collective-permute-start.9 = (bf16[4,64,128]{2,1,0:T(8,128)(2,1)S(1)}, bf16[4,64,128]{2,1,0:T(8,128)(2,1)S(1)}, u32[]{:S(2)}, u32[]{:S(2)}) collective-permute-start(bf16[4,64,128]{2,1,0:T(8,128)(2,1)S(1)} %get-tuple-element.25), channel_id=1, source_target_pairs={{0,1},{1,0},{2,3},{3,2},{4,5},{5,4},{6,7},{7,6},{8,9},{9,8},{10,11... | collective-permute-start | bytes 196616 | tf_op jit(solution)/shard_map/ppermute | solution.py:438
  63.2 18.6 %all-to-all-start = ((f32[16,40,128]{2,1,0:T(8,128)}), f32[16,40,128]{2,1,0:T(8,128)S(1)}, u32[]{:S(2)}, u32[]{:S(2)}) async-start(f32[16,40,128]{2,1,0:T(8,128)} %broadcast_in_dim.15), calls=%async_computation | async-start | bytes 655360 | tf_op jit(solution)/shard_map/all_to_all | solution.py:518

commit v5 on v4

--- a/solution.py
+++ b/solution.py
@@ -61,14 +61,9 @@
     return lax.dot_general(a, b, (((1,), (0,)), ((), ())), preferred_element_type=F32)
 
 
-def put_faces(first, ref, start, ends, gs, ylo, yhi):
+def put_ends(first, ref, ends, gs):
     rows, depth = ref.shape[2:]
-    value = ref[:, pl.ds(start, PB)]
-    for p in range(PB):
-        for c in range(4):
-            ylo[c, pl.ds(first + p, 1), :] = value[c, p, 0:1, :]
-            yhi[c, pl.ds(first + p, 1), :] = value[c, p, rows - 1 :, :]
-    high = value.astype(BF16)
+    high = ref[:, pl.ds(first, PB)].astype(BF16)
     beside = [high[:, p].reshape(4 * rows, depth) for p in range(PB)]
     picked = mm(jnp.concatenate(beside, 1), ends).reshape(4, rows, depth)
     here = lanes_of((rows, depth)) // (2 * PB) == first // PB
@@ -76,56 +71,102 @@
         gs[c] = jnp.where(here, picked[c], gs[c])
 
 
-def put_plane(out_ref, value):
-    rows = value.shape[1]
-    out_ref[: 4 * rows] = value.astype(BF16).reshape(4 * rows, value.shape[2])
-
-
 def paired(value):
     high = value.astype(BF16).astype(F32)
     return jnp.concatenate([high, value - high], 1)
 
 
-def x_kernel(v_ref, d_ref, xlo_ref, xhi_ref, planes, sems):
-    far = v_ref.shape[1] - 1
+PLANES = 13
+
+
+def x_kernel(v_ref, s_ref, m_ref, d_ref, xlo_ref, xhi_ref, vs, ss, ms, sems):
+    last = v_ref.shape[1] - 1
     rows, depth = v_ref.shape[2:]
-    copies = [
-        pltpu.make_async_copy(v_ref.at[:, x], planes.at[i], sems.at[i])
-        for i, x in enumerate((0, far))
-    ]
-    for copy in copies:
-        copy.start()
+    sides = ((0, 0, 1), (last, last - 1, 0))
+    copies = []
+    for i, (x, second, _) in enumerate(sides):
+        copies.append(
+            [
+                pltpu.make_async_copy(
+                    v_ref.at[:, pl.ds(min(x, second), 2)], vs.at[i], sems.at[3 * i]
+                ),
+                pltpu.make_async_copy(s_ref.at[:, x], ss.at[i], sems.at[3 * i + 1]),
+                pltpu.make_async_copy(m_ref.at[x], ms.at[i], sems.at[3 * i + 2]),
+            ]
+        )
+    for side in copies:
+        for copy in side:
+            copy.start()
     cells = d_ref.shape[0]
     none = jnp.zeros((R, depth), F32)
     for i, (out_ref, start) in enumerate(((xlo_ref, 0), (xhi_ref, cells - R))):
         strip = jnp.concatenate([paired(d_ref[start : start + R, :]), none], 0)
-        out_ref[4 * rows :] = strip.astype(BF16)
-        copies[i].wait()
-        put_plane(out_ref, planes[i])
-
-
-def pack_kernel(v_ref, ylo_ref, yhi_ref, g_ref, gs, ylo, yhi, ends):
+        out_ref[PLANES * rows :] = strip.astype(BF16)
+        for copy in copies[i]:
+            copy.wait()
+        inner = sides[i][2]
+        out_ref[: 4 * rows] = vs[i, :, 1 - inner].astype(BF16).reshape(4 * rows, depth)
+        out_ref[4 * rows : 8 * rows] = vs[i, :, inner].astype(BF16).reshape(4 * rows, depth)
+        out_ref[8 * rows : 12 * rows] = ss[i].reshape(4 * rows, depth)
+        out_ref[12 * rows : 13 * rows] = (ms[i] + 1).astype(F32).astype(BF16)
+
+
+def pack_kernel(v_ref, s_ref, m_ref, d_ref, xl_ref, xr_ref, ylo_ref, yhi_ref, g_ref, gs, ylo, yhi, ends):
+    rows, depth = v_ref.shape[2:]
     gs[...] = jnp.zeros_like(gs)
-    ends[...] = ends_matrix(v_ref.shape[3])
+    ends[...] = ends_matrix(depth)
 
     def group(i, carry):
-        put_faces(i * PB, v_ref, i * PB, ends[...], gs, ylo, yhi)
+        first = i * PB
+        put_ends(first, v_ref, ends[...], gs)
+        for p in range(PB):
+            x = first + p
+            here = pl.ds(x, 1)
+            level = (m_ref[x] + 1).astype(F32)
+            for out, edge, inner, low in ((ylo, 0, 1, 0), (yhi, rows - 1, rows - 2, rows - 16)):
+                for c in range(4):
+                    out[c, here, :] = v_ref[c, x, edge : edge + 1, :]
+                    out[4 + c, here, :] = v_ref[c, x, inner : inner + 1, :]
+                    near_edge = s_ref[c, x, low : low + 16, :].astype(F32)
+                    out[8 + c, here, :] = near_edge[edge - low : edge - low + 1]
+                out[12, here, :] = level[edge : edge + 1]
         return carry
 
     lax.fori_loop(0, v_ref.shape[1] // PB, group, 0)
     g_ref[...] = gs[...].astype(BF16)
-    ylo_ref[...] = ylo[...].astype(BF16)
-    yhi_ref[...] = yhi[...].astype(BF16)
+    nx = v_ref.shape[1]
+    cells = d_ref.shape[0]
+    strips = [r[PLANES * rows :].astype(F32)[:R] for r in (xl_ref, xr_ref)]
+    filler = jnp.zeros((cells - 2 * R, depth), F32)
+    tall = jnp.concatenate([strips[0], paired(d_ref[...]), strips[1], filler], 0).astype(BF16)
+    for out_ref, rows_out, edge, low in ((ylo_ref, ylo, 0, 0), (yhi_ref, yhi, rows - 1, rows - 16)):
+        out_ref[: PLANES * nx] = rows_out[...].astype(BF16).reshape(PLANES * nx, depth)
+        corners = [
+            r[c * rows + low : c * rows + low + 16].astype(F32)[edge - low : edge - low + 1]
+            for r in (xl_ref, xr_ref)
+            for c in range(4)
+        ]
+        corners.append(jnp.zeros((2 * R - 8, depth), F32))
+        out_ref[PLANES * nx : PLANES * nx + 2 * R] = jnp.concatenate(corners, 0).astype(BF16)
+        out_ref[PLANES * nx + 2 * R :] = tall
+
+
+def edge_kernel(g_ref, xl_ref, xr_ref, yl_ref, yr_ref, out_ref):
+    parts, rows, depth = g_ref.shape
+    beside = [r[: 4 * rows] for r in (xl_ref, xr_ref, yl_ref, yr_ref)]
+    picked = mm(jnp.concatenate(beside, 1), ends_matrix(depth)[: 4 * depth])
+    out_ref[:4] = g_ref[...]
+    out_ref[4:] = picked.astype(BF16).reshape(4, rows, depth)
 
 
 def sweep_kernel(last, nz, scale, *refs):
-    sr_ref, si_ref, v_ref, s_ref, m_ref, xl_ref, xr_ref, yl_ref, yr_ref, gl_ref, gr_ref = refs[:11]
+    sr_ref, si_ref, v_ref, s_ref, m_ref, gl_ref, gr_ref = refs[:7]
     if last:
-        sh_ref, mid_ref, own_ref, o_ref, sens_ref = refs[11:16]
-        hs, yl, yr, near, far, zt0, zt1, sens, value, news, sums, sems = refs[16:]
+        ext_ref, mid_ref, yl_ref, yr_ref, sh_ref, own_ref, o_ref, sens_ref = refs[7:15]
+        hs, yl, yr, near, far, zt0, zt1, sens, value, news, sums, sems = refs[15:]
     else:
-        d_ref, o_ref, xlo_ref, xhi_ref, ylo_ref, yhi_ref, g_ref = refs[11:18]
-        hs, yl, yr, near, far, zt0, zt1, gs, ylo, yhi, ends = refs[18:]
+        xl_ref, xr_ref, yl_ref, yr_ref, ylo_ref, yhi_ref, o_ref, ext_ref, g_ref = refs[7:16]
+        hs, yl, yr, near, far, zt0, zt1, gs, ends = refs[16:]
     planes_here, rows, depth = v_ref.shape[1:]
     lane = lanes_of((rows, depth))
 
@@ -134,7 +175,7 @@
         keep_l, keep_r = here, 1.0 - here
     else:
         keep_l, keep_r = 1.0, 1.0
-    for c in range(4):
+    for c in range(gl_ref.shape[0]):
         left = pltpu.roll(gl_ref[c].astype(F32), depth - 1, 1) * keep_l
         right = pltpu.roll(gr_ref[c].astype(F32), 1, 1) * keep_r
         hs[c] = jnp.where(lane % 2 == 0, left, right)
@@ -146,8 +187,18 @@
     else:
         gs[...] = jnp.zeros_like(gs)
         ends[...] = ends_matrix(depth)
-    yl[...] = yl_ref[:4].astype(F32)
-    yr[...] = yr_ref[:4].astype(F32)
+    face = 4 * rows
+    if last:
+        yl[...] = ext_ref[2 * face : 3 * face].reshape(4, rows, depth)
+        yr[...] = ext_ref[3 * face : 4 * face].reshape(4, rows, depth)
+    else:
+        yl[...] = yl_ref[:face].astype(F32).reshape(4, rows, depth)
+        yr[...] = yr_ref[:face].astype(F32).reshape(4, rows, depth)
+
+    def x_halo(side, low):
+        if last:
+            return ext_ref[side * face + low : side * face + low + RC]
+        return (xl_ref, xr_ref)[side][low : low + RC].astype(F32)
 
     levels = sr_ref.shape[0]
     tile = (8, depth)
@@ -162,10 +213,10 @@
             share.append(jnp.full(tile, sh_ref[m], F32))
 
     def lookup(masks, table):
-        out = jnp.broadcast_to(table[0], (RC // 8, 8, depth))
+        out = jnp.broadcast_to(table[0], masks[0].shape)
         for mask, entry in zip(masks, table[1:]):
             out = jnp.where(mask, entry, out)
-        return out.reshape(RC, depth)
+        return out.reshape(-1, depth)
 
     row8 = lax.broadcasted_iota(jnp.int32, tile, 0)
 
@@ -192,15 +243,14 @@
 
         def drive(c):
             v = v_ref[c, x, span]
-            part = slice(c * rows + low, c * rows + low + RC)
             if p == 0:
                 before = v_ref[c, jnp.maximum(x - 1, 0), span]
-                before = jnp.where(x == 0, xl_ref[part].astype(F32), before)
+                before = jnp.where(x == 0, x_halo(0, c * rows + low), before)
             else:
                 before = v_ref[c, x - 1, span]
             if p == PB - 1:
                 after = v_ref[c, jnp.minimum(x + 1, planes_here - 1), span]
-                after = jnp.where(x == planes_here - 1, xr_ref[part].astype(F32), after)
+                after = jnp.where(x == planes_here - 1, x_halo(1, c * rows + low), after)
             else:
                 after = v_ref[c, x + 1, span]
             total = before + after + s_ref[c, x, span].astype(F32) + zt[c, p, span]
@@ -254,7 +304,7 @@
             picked = mm(jnp.concatenate(parts, 1), sums[...])
             sens[...] = jnp.where(lane // PB == i, picked, sens[...])
         else:
-            put_faces(first, o_ref, first, ends[...], gs, ylo, yhi)
+            put_ends(first, o_ref, ends[...], gs)
 
     def two(i, carry):
         group(2 * i, zt0, zt1)
@@ -265,19 +315,50 @@
     lax.fori_loop(0, groups // 2, two, 0)
 
     if not last:
-        put_plane(xlo_ref, o_ref[:, 0])
-        put_plane(xhi_ref, o_ref[:, planes_here - 1])
         g_ref[...] = gs[...].astype(BF16)
-        xlo_ref[4 * rows :] = jnp.zeros((2 * R, depth), BF16)
-        xhi_ref[4 * rows :] = jnp.zeros((2 * R, depth), BF16)
-        cells = d_ref.shape[0]
-        strips = [r[4 * rows : 4 * rows + 2 * R].astype(F32)[:R] for r in (xl_ref, xr_ref)]
-        filler = jnp.zeros((2 * cells - cells - 2 * R, depth), F32)
-        tall = jnp.concatenate([strips[0], paired(d_ref[...]), strips[1], filler], 0)
-        tall = tall.astype(BF16).reshape(2, cells, depth)
-        for out_ref, rows_out in ((ylo_ref, ylo), (yhi_ref, yhi)):
-            out_ref[:4] = rows_out[...].astype(BF16)
-            out_ref[4:] = tall
+        sides = (xl_ref, xr_ref, yl_ref, yr_ref)
+        centres = jnp.concatenate([r[:face] for r in sides], 0)
+        masked = [
+            jnp.where(lane // 2 == e, hs[4 + c], 0.0).astype(BF16) for e in range(4) for c in range(4)
+        ]
+        along = mm(centres, near[:depth]) + mm(jnp.concatenate(masked, 0), far[...])
+        for e in range(4):
+            zt0[:, e] = along[e * face : (e + 1) * face].reshape(4, rows, depth)
+        block = PLANES * planes_here
+        corner_l = yl_ref[block : block + 2 * R].astype(F32)
+        corner_r = yr_ref[block : block + 2 * R].astype(F32)
+        zero = jnp.zeros(tile, F32)
+        for e, ref in enumerate(sides):
+            level = ref[3 * face : 3 * face + rows].astype(F32).reshape(rows // 8, 8, depth)
+            masks = [level == float(m + 1) for m in range(levels)]
+            w_r, w_i = lookup(masks, [zero] + wr), lookup(masks, [zero] + wi)
+
+            def near_plane(c, e=e, ref=ref):
+                part = slice(c * rows, (c + 1) * rows)
+                v = ref[part].astype(F32)
+                beyond = ref[face + c * rows : face + (c + 1) * rows].astype(F32)
+                if e < 2:
+                    inside = v_ref[c, 0 if e == 0 else planes_here - 1]
+                    top, low = corner_l[4 * e + c : 4 * e + c + 1], corner_r[4 * e + c : 4 * e + c + 1]
+                else:
+                    inside = (ylo_ref, yhi_ref)[e - 2][part].astype(F32)
+                    corner = corner_l if e == 2 else corner_r
+                    top, low = corner[c : c + 1], corner[4 + c : 5 + c]
+                source = ref[2 * face + c * rows : 2 * face + (c + 1) * rows].astype(F32)
+                total = beyond + inside + source + zt0[c, e]
+                up = pltpu.roll(v, 1, 0)
+                down = pltpu.roll(v, rows - 1, 0)
+                up = jnp.concatenate([jnp.where(row8 == 0, top, up[:8]), up[8:]], 0)
+                down = jnp.concatenate([down[:-8], jnp.where(row8 == 7, low, down[-8:])], 0)
+                return v, total + up + down
+
+            for re in (0, 2):
+                v_r, t_r = near_plane(re)
+                v_i, t_i = near_plane(re + 1)
+                keep = 1.0 - RELAXATION
+                at = e * face + re * rows
+                ext_ref[at : at + rows] = keep * v_r + (w_r * t_r - w_i * t_i)
+                ext_ref[at + rows : at + 2 * rows] = keep * v_i + (w_r * t_i + w_i * t_r)
     else:
         cells = rows
         row = lax.broadcasted_iota(jnp.int32, (cells, 2 * cells), 0)
@@ -285,7 +366,7 @@
         half_sum = jnp.zeros((cells, 2 * cells), F32)
         for shift, ref in ((-cells, yl_ref), (0, mid_ref), (cells, yr_ref)):
             weight = jnp.maximum(R + 1 - jnp.abs(col % cells + shift - row), 0)
-            tall = ref[4:].reshape(2 * cells, depth)
+            tall = ref[PLANES * planes_here + 2 * R :]
             half_sum = half_sum + lax.dot_general(
                 weight.astype(F32).astype(BF16),
                 tall,
@@ -319,126 +400,146 @@
     return mm(left, high) + mm(left, low)
 
 
-def whole(shape):
-    return pl.BlockSpec(shape, lambda i: (0,) * len(shape))
-
-
 SMEM_SPEC = pl.BlockSpec(memory_space=pltpu.SMEM)
 VMEM_SPEC = pl.BlockSpec(memory_space=pltpu.VMEM)
 
 
-def message_shapes(nx, ny, nz, parts):
-    tall = (4 * ny + 2 * R, nz)
-    return [tall, tall, (parts, nx, nz), (parts, nx, nz), (4, ny, nz)]
-
-
-def face_scratch(nx, ny, nz):
-    return [
-        pltpu.VMEM((4, ny, nz), F32),
-        pltpu.VMEM((4, nx, nz), F32),
-        pltpu.VMEM((4, nx, nz), F32),
-        pltpu.VMEM((PB * nz, nz), BF16),
-    ]
-
-
 def near(value):
     return pltpu.with_memory_space_constraint(value, pltpu.VMEM)
 
 
-def pack(fields, density):
+def far_away(value):
+    return pltpu.with_memory_space_constraint(value, pltpu.HBM)
+
+
+def local(kernel, name, operands, specs, shapes, out_specs, scratch, limit, cost):
+    return pl.pallas_call(
+        kernel,
+        in_specs=specs,
+        out_specs=out_specs,
+        out_shape=shapes,
+        scratch_shapes=scratch,
+        compiler_params=pltpu.CompilerParams(vmem_limit_bytes=limit << 20),
+        cost_estimate=pl.CostEstimate(flops=cost, bytes_accessed=cost, transcendentals=0),
+        name=name,
+    )(*operands)
+
+
+def shift(value, axis, up):
+    count = lax.axis_size(axis)
+    pairs = [(i, i + 1) for i in range(count - 1)]
+    return lax.ppermute(value, axis, pairs if up else [(j, i) for i, j in pairs])
+
+
+def shift_z(g):
+    if lax.axis_size("gz") == 2:
+        other = lax.ppermute(g, "gz", [(0, 1), (1, 0)])
+        return other, other
+    return shift(g, "gz", True), shift(g, "gz", False)
+
+
+def sweeps(tables, share, fields, sources, material, density, owners):
     _, nx, ny, nz = fields.shape
-    shapes = [jax.ShapeDtypeStruct(s, BF16) for s in message_shapes(nx, ny, nz, 4)]
-    xlo, xhi = pl.pallas_call(
+    nz_parts = lax.axis_size("gz")
+    hbm = pl.BlockSpec(memory_space=pltpu.HBM)
+    held = [near(a) for a in (fields, sources, material)]
+
+    x_shape = jax.ShapeDtypeStruct((PLANES * ny + 2 * R, nz), BF16)
+    y_shape = jax.ShapeDtypeStruct((PLANES * nx + 2 * R + 2 * nx, nz), BF16)
+    g_shape = jax.ShapeDtypeStruct((4, ny, nz), BF16)
+    wide_g = jax.ShapeDtypeStruct((8, ny, nz), BF16)
+    xlo, xhi = local(
         x_kernel,
-        in_specs=[pl.BlockSpec(memory_space=pltpu.HBM), VMEM_SPEC],
-        out_specs=[VMEM_SPEC] * 2,
-        out_shape=shapes[:2],
-        scratch_shapes=[pltpu.VMEM((2, 4, ny, nz), F32), pltpu.SemaphoreType.DMA((2,))],
-        compiler_params=pltpu.CompilerParams(vmem_limit_bytes=4 << 20),
-        cost_estimate=pl.CostEstimate(flops=ny * nz * 8, bytes_accessed=ny * nz * 48, transcendentals=0),
-        name="x_faces",
-    )(pltpu.with_memory_space_constraint(fields, pltpu.HBM), density)
-    held = near(fields)
-    ylo, yhi, g = pl.pallas_call(
+        "x_faces",
+        [far_away(a) for a in (fields, sources, material)] + [density],
+        [hbm] * 3 + [VMEM_SPEC],
+        [x_shape] * 2,
+        [VMEM_SPEC] * 2,
+        [
+            pltpu.VMEM((2, 4, 2, ny, nz), F32),
+            pltpu.VMEM((2, 4, ny, nz), BF16),
+            pltpu.VMEM((2, ny, nz), jnp.int32),
+            pltpu.SemaphoreType.DMA((6,)),
+        ],
+        8,
+        ny * nz * 100,
+    )
+    xl, xr = shift(xhi, "gx", True), shift(xlo, "gx", False)
+    ylo, yhi, g = local(
         pack_kernel,
-        in_specs=[VMEM_SPEC],
-        out_specs=[VMEM_SPEC] * 3,
-        out_shape=shapes[2:],
-        scratch_shapes=face_scratch(nx, ny, nz),
-        compiler_params=pltpu.CompilerParams(vmem_limit_bytes=12 << 20),
-        cost_estimate=pl.CostEstimate(
-            flops=fields.size * 4, bytes_accessed=fields.size * 4, transcendentals=0
-        ),
-        name="pack_faces",
-    )(held)
-    return held, (xlo, xhi, ylo, yhi, g)
-
-
-def sweep(last, tables, current, sources, material, halos, more):
-    _, nx, ny, nz = current.shape
-    scratch = [
-        pltpu.VMEM((4, ny, nz), F32),
-        pltpu.VMEM((4, nx, nz), F32),
-        pltpu.VMEM((4, nx, nz), F32),
-        pltpu.VMEM((2 * nz, nz), BF16),
-        pltpu.VMEM((nz, nz), BF16),
-        pltpu.VMEM((4, PB, ny, nz), F32),
-        pltpu.VMEM((4, PB, ny, nz), F32),
-    ]
-    if last:
-        shapes = [
-            jax.ShapeDtypeStruct(current.shape, F32),
+        "pack_faces",
+        held + [density, xl, xr],
+        [VMEM_SPEC] * 6,
+        [y_shape, y_shape, g_shape],
+        [VMEM_SPEC] * 3,
+        [
+            pltpu.VMEM((4, ny, nz), F32),
+            pltpu.VMEM((PLANES, nx, nz), F32),
+            pltpu.VMEM((PLANES, nx, nz), F32),
+            pltpu.VMEM((PB * nz, nz), BF16),
+        ],
+        12,
+        fields.size * 4,
+    )
+    yl, yr = shift(yhi, "gy", True), shift(ylo, "gy", False)
+    g = local(
+        edge_kernel,
+        "edge_faces",
+        [g, xl, xr, yl, yr],
+        [VMEM_SPEC] * 5,
+        wide_g,
+        VMEM_SPEC,
+        [],
+        8,
+        ny * nz * 40,
+    )
+    gl, gr = shift_z(g)
+
+    def scratch(parts):
+        return [
+            pltpu.VMEM((parts, ny, nz), F32),
+            pltpu.VMEM((4, nx, nz), F32),
+            pltpu.VMEM((4, nx, nz), F32),
+            pltpu.VMEM((2 * nz, nz), BF16),
+            pltpu.VMEM((nz, nz), BF16),
+            pltpu.VMEM((4, PB, ny, nz), F32),
+            pltpu.VMEM((4, PB, ny, nz), F32),
+        ]
+
+    scale = 1.0 / math.sqrt(nz * nz_parts)
+    middle, ext, g = local(
+        functools.partial(sweep_kernel, False, nz_parts, scale),
+        "sweep_first",
+        [*tables, *held, gl, gr, xl, xr, yl, yr, ylo, yhi],
+        [SMEM_SPEC] * 2 + [VMEM_SPEC] * 11,
+        [pltpu.VMEM(fields.shape, F32), jax.ShapeDtypeStruct((16 * ny, nz), F32), g_shape],
+        [VMEM_SPEC] * 3,
+        scratch(8) + [pltpu.VMEM((4, ny, nz), F32), pltpu.VMEM((PB * nz, nz), BF16)],
+        20,
+        fields.size * 20,
+    )
+    gl, gr = shift_z(g)
+    return local(
+        functools.partial(sweep_kernel, True, nz_parts, scale),
+        "sweep_last",
+        [*tables, near(middle), *held[1:], gl, gr, ext, ylo, yl, yr, share, owners],
+        [SMEM_SPEC] * 2 + [VMEM_SPEC] * 9 + [SMEM_SPEC, VMEM_SPEC],
+        [
+            jax.ShapeDtypeStruct(fields.shape, F32),
             jax.ShapeDtypeStruct((ny // 2 + 8, nz), F32),
-        ]
-        specs = [pl.BlockSpec(memory_space=pltpu.HBM), VMEM_SPEC]
-        more_specs = [SMEM_SPEC, VMEM_SPEC, VMEM_SPEC]
-        scratch += [
+        ],
+        [hbm, VMEM_SPEC],
+        scratch(4)
+        + [
             pltpu.VMEM((ny, nz), F32),
             pltpu.VMEM((PB, ny, nz), F32),
-            pltpu.VMEM(current.shape, F32),
+            pltpu.VMEM(fields.shape, F32),
             pltpu.VMEM((2 * PB * nz, nz), BF16),
             pltpu.SemaphoreType.DMA((nx // PB,)),
-        ]
-    else:
-        faces = message_shapes(nx, ny, nz, 6)
-        shapes = [pltpu.VMEM(current.shape, F32)]
-        shapes += [jax.ShapeDtypeStruct(s, BF16) for s in faces]
-        specs = [VMEM_SPEC] * len(shapes)
-        more_specs = [VMEM_SPEC]
-        scratch += face_scratch(nx, ny, nz)
-
-    return pl.pallas_call(
-        functools.partial(
-            sweep_kernel,
-            last,
-            lax.axis_size("gz"),
-            1.0 / math.sqrt(nz * lax.axis_size("gz")),
-        ),
-        in_specs=[SMEM_SPEC] * 2 + [VMEM_SPEC] * 9 + more_specs,
-        out_specs=specs,
-        out_shape=shapes,
-        scratch_shapes=scratch,
-        compiler_params=pltpu.CompilerParams(vmem_limit_bytes=20 << 20),
-        cost_estimate=pl.CostEstimate(
-            flops=current.size * 24, bytes_accessed=current.size * 11, transcendentals=0
-        ),
-        name="sweep_last" if last else "sweep_first",
-    )(*tables, near(current), near(sources), near(material), *halos, *more)
-
-
-def exchange(xlo, xhi, ylo, yhi, g):
-    out = []
-    for axis, low, high in (("gx", xlo, xhi), ("gy", ylo, yhi)):
-        count = lax.axis_size(axis)
-        up = [(i, i + 1) for i in range(count - 1)]
-        out.append(lax.ppermute(high, axis, up))
-        out.append(lax.ppermute(low, axis, [(j, i) for i, j in up]))
-    count = lax.axis_size("gz")
-    if count == 2:
-        other = lax.ppermute(g, "gz", [(0, 1), (1, 0)])
-        return out + [other, other]
-    up = [(i, i + 1) for i in range(count - 1)]
-    return out + [lax.ppermute(g, "gz", up), lax.ppermute(g, "gz", [(j, i) for i, j in up])]
+        ],
+        20,
+        fields.size * 20,
+    )
 
 
 def plane_kernel(ngx, ngy, me_ref, got_ref, out_ref, w_ref):
@@ -507,12 +608,7 @@
     cells = density.shape[0]
     tables = (shift_real, shift_imag)
     owners = jnp.broadcast_to(owner_map.reshape(1, -1), (8, cells))
-    held, faces = pack(fields, density)
-    halos = exchange(*faces)
-    middle, *faces = sweep(False, tables, held, sources, material, halos, [density])
-    final, partial = sweep(
-        True, tables, middle, sources, material, exchange(*faces), [design_share, faces[2], owners]
-    )
+    final, partial = sweeps(tables, design_share, fields, sources, material, density, owners)
     partial = jnp.sum(lax.all_gather(partial, "gz"), 0)
     copies = jnp.broadcast_to(partial[None], (columns, *partial.shape))
     plane = lax.all_to_all(copies, ("gx", "gy"), split_axis=0, concat_axis=0)

time: 84.5 us -> 79.2 us (0.937)
  starting transfers between devices: 29.3 us -> 19.4 us
  waiting for transfers between devices: 22.3 us -> 28.7 us
  Pallas kernels: 28.1 us -> 26.5 us
    ppermute x10 -> x6, starting transfers between devices: 23 us -> 12.5 us  [the longest x4 12.3 us: shift(): lax.ppermute(value, axis, pairs if up else [(j, i) for i, j in pairs])]
    ppermute x10 -> x6, waiting for transfers between devices: 9.99 us -> 16.4 us  [the longest x4 14 us: shift(): lax.ppermute(value, axis, pairs if up else [(j, i) for i, j in pairs])]
    pallas_call x4 -> x5, Pallas kernels: 25.8 us -> 24.2 us  [local(): pl.pallas_call(kernel, in_specs=specs, out_specs=out_specs, out_shape=sha...]
  transfers between devices with their start and end apart: 11 -> 7, of which waited for: 5 -> 7; matrix products, arithmetic and copies ran while one was open for 0% -> 0% of each run, Pallas kernels for 3% -> 0%
where the time goes in v5:
time: 79.2 us; the launch traced here: 78.9 us
  waiting for transfers between devices  28.7 us (36%)
  Pallas kernels  26.5 us (33%)
  starting transfers between devices  19.4 us (24%)
  blocking collectives  1.83 us (2%)
  local copies, waits for them, and re-layouts  1.69 us (2%)
  between operations  0.8 us (1%)
    pallas_call x5, Pallas kernels, local(): pl.pallas_call(kernel, in_specs=specs, out_specs=out_specs, out_shape=sha...  24.2 us
    ppermute x4, waiting for transfers between devices, shift(): lax.ppermute(value, axis, pairs if up else [(j, i) for i, j in pairs])  14 us
    all_to_all x1, waiting for transfers between devices, on_device(): plane = lax.all_to_all(copies, ('gx', 'gy'), split_axis=0, concat_axis=0)  12.3 us
    ppermute x4, starting transfers between devices, shift(): lax.ppermute(value, axis, pairs if up else [(j, i) for i, j in pairs])  12.3 us
    all_to_all x1, starting transfers between devices, on_device(): plane = lax.all_to_all(copies, ('gx', 'gy'), split_axis=0, concat_axis=0)  6.83 us
    ppermute x2, waiting for transfers between devices, shift_z(): other = lax.ppermute(g, 'gz', [(0, 1), (1, 0)])  2.44 us
    pallas_call x1, Pallas kernels, on_device(): pl.pallas_call(functools.partial(plane_kernel, ngx, ngy), in_specs=[SMEM_...  2.25 us
    all_gather x1, blocking collectives, on_device(): partial = jnp.sum(lax.all_gather(partial, 'gz'), 0)  1.83 us
  transfers between devices with their start and end apart: 7, of which 7 were waited for; matrix products, arithmetic and copies ran while one was open for 0% of the time, Pallas kernels for 0%

profile of v5, /device:TPU:0, one launch (start us, length us, event | category | flops | bytes accessed | tf_op | source)
XLA Modules:
  0.0 78.9 jit_solution(9437929015221584581)
XLA Ops:
  0.6 0.0 copy-start.2
  0.6 0.0 copy-start
  0.7 0.0 copy-start.1
  0.7 0.0 copy-start.3
  0.7 0.9 %copy-done.3 = f32[64,64]{1,0:T(8,128)S(1)} copy-done((f32[64,64]{1,0:T(8,128)S(1)}, f32[64,64]{1,0:T(8,128)}, u32[]{:S(2)}) %copy-start.3) | copy-done | bytes 16408
  1.6 0.0 copy-start.4
  1.6 1.6 %x_faces.1 = (bf16[848,128]{1,0:T(8,128)(2,1)S(1)}, bf16[848,128]{1,0:T(8,128)(2,1)S(1)}) custom-call(f32[4,64,64,128]{3,2,1,0:T(8,128)} %refs_2_.1, bf16[4,64,64,128]{3,2,1,0:T(8,128)(2,1)} %refs_3_.3, s32[64,64,128]{2,1,0:T(8,128)} %refs_4_.3, f32[64,64]{1,0:T(8,128)S(1)} %copy-done.3), custom_call_target="tpu_custom_call" | custom-call | flops 819200 | bytes 819200 | tf_op jit(solution)/shard_map/x_faces/pallas_call | solution.py:416
  3.2 0.0 copy-start.5
  3.2 0.0 copy-start.6
  3.2 5.1 %collective-permute-start = (bf16[848,128]{1,0:T(8,128)(2,1)S(1)}, bf16[848,128]{1,0:T(8,128)(2,1)S(1)}, u32[]{:S(2)}, u32[]{:S(2)}) collective-permute-start(bf16[848,128]{1,0:T(8,128)(2,1)S(1)} %get-tuple-element.12), channel_id=1, source_target_pairs={{0,8},{8,16},{16,24},{1,9},{9,17},{17,25},{2,10},{10,18},{18,26},{... | collective-permute-start | bytes 651272 | tf_op jit(solution)/shard_map/ppermute | solution.py:431
  8.3 1.3 %collective-permute-start.1 = (bf16[848,128]{1,0:T(8,128)(2,1)S(1)}, bf16[848,128]{1,0:T(8,128)(2,1)S(1)}, u32[]{:S(2)}, u32[]{:S(2)}) collective-permute-start(bf16[848,128]{1,0:T(8,128)(2,1)S(1)} %get-tuple-element.13), channel_id=1, source_target_pairs={{8,0},{16,8},{24,16},{9,1},{17,9},{25,17},{10,2},{18,10},{26,18},{... | collective-permute-start | bytes 651272 | tf_op jit(solution)/shard_map/ppermute | solution.py:431
  9.6 3.3 %collective-permute-done.xl_ref.refs_7_ = bf16[848,128]{1,0:T(8,128)(2,1)S(1)} collective-permute-done((bf16[848,128]{1,0:T(8,128)(2,1)S(1)}, bf16[848,128]{1,0:T(8,128)(2,1)S(1)}, u32[]{:S(2)}, u32[]{:S(2)}) %collective-permute-start) | collective-permute-done | bytes 217120 | tf_op jit(solution)/shard_map/ppermute | solution.py:431
  12.9 6.6 %collective-permute-done.1.xr_ref.refs_8_ = bf16[848,128]{1,0:T(8,128)(2,1)S(1)} collective-permute-done((bf16[848,128]{1,0:T(8,128)(2,1)S(1)}, bf16[848,128]{1,0:T(8,128)(2,1)S(1)}, u32[]{:S(2)}, u32[]{:S(2)}) %collective-permute-start.1) | collective-permute-done | bytes 217120 | tf_op jit(solution)/shard_map/ppermute | solution.py:431
  19.5 0.0 copy-done.2
  19.5 0.0 copy-done
  19.5 0.0 copy-done.1
  19.5 0.0 copy-done.4
  19.5 2.7 %pack_faces.1 = (bf16[976,128]{1,0:T(8,128)(2,1)S(1)}, bf16[976,128]{1,0:T(8,128)(2,1)S(1)}, bf16[4,64,128]{2,1,0:T(8,128)(2,1)S(1)}) custom-call(f32[4,64,64,128]{3,2,1,0:T(8,128)S(1)} %copy-done, bf16[4,64,64,128]{3,2,1,0:T(8,128)(2,1)S(1)} %copy-done.1, s32[64,64,128]{2,1,0:T(8,128)S(1)} %copy-done.2, f32[64,64]{1,0:T(8,128)S(1)} %copy-done.4, ...), custom_call_target="tpu_custom_call" | custom-call | flops 8388608 | bytes 8388608 | tf_op jit(solution)/shard_map/pack_faces/pallas_call | solution.py:416
  22.2 1.3 %collective-permute-start.3 = (bf16[976,128]{1,0:T(8,128)(2,1)S(1)}, bf16[976,128]{1,0:T(8,128)(2,1)S(1)}, u32[]{:S(2)}, u32[]{:S(2)}) collective-permute-start(bf16[976,128]{1,0:T(8,128)(2,1)S(1)} %get-tuple-element.16.refs_11_.refs_8_), channel_id=1, source_target_pairs={{2,0},{4,2},{6,4},{3,1},{5,3},{7,5},{10,8},{12,10},{14,12},{11,9},... | collective-permute-start | bytes 749576 | tf_op jit(solution)/shard_map/ppermute | solution.py:431
  23.5 4.6 %collective-permute-start.2 = (bf16[976,128]{1,0:T(8,128)(2,1)S(1)}, bf16[976,128]{1,0:T(8,128)(2,1)S(1)}, u32[]{:S(2)}, u32[]{:S(2)}) collective-permute-start(bf16[976,128]{1,0:T(8,128)(2,1)S(1)} %get-tuple-element.15.refs_12_), channel_id=1, source_target_pairs={{0,2},{2,4},{4,6},{1,3},{3,5},{5,7},{8,10},{10,12},{12,14},{9,11},... | collective-permute-start | bytes 749576 | tf_op jit(solution)/shard_map/ppermute | solution.py:431
  28.0 2.9 %collective-permute-done.3.yr_ref.refs_10_ = bf16[976,128]{1,0:T(8,128)(2,1)S(1)} collective-permute-done((bf16[976,128]{1,0:T(8,128)(2,1)S(1)}, bf16[976,128]{1,0:T(8,128)(2,1)S(1)}, u32[]{:S(2)}, u32[]{:S(2)}) %collective-permute-start.3) | collective-permute-done | bytes 249888 | tf_op jit(solution)/shard_map/ppermute | solution.py:431
  31.0 1.2 %collective-permute-done.2.yl_ref.refs_9_ = bf16[976,128]{1,0:T(8,128)(2,1)S(1)} collective-permute-done((bf16[976,128]{1,0:T(8,128)(2,1)S(1)}, bf16[976,128]{1,0:T(8,128)(2,1)S(1)}, u32[]{:S(2)}, u32[]{:S(2)}) %collective-permute-start.2) | collective-permute-done | bytes 249888 | tf_op jit(solution)/shard_map/ppermute | solution.py:431
  32.2 0.2 edge_faces.1
  32.4 0.0 copy-start.8
  32.4 0.0 copy-start.7
  32.4 0.1 collective-permute-start.4
  32.5 1.3 %collective-permute-done.4.refs_5_.refs_6_ = bf16[8,64,128]{2,1,0:T(8,128)(2,1)S(1)} collective-permute-done((bf16[8,64,128]{2,1,0:T(8,128)(2,1)S(1)}, bf16[8,64,128]{2,1,0:T(8,128)(2,1)S(1)}, u32[]{:S(2)}, u32[]{:S(2)}) %collective-permute-start.4) | collective-permute-done | bytes 131104 | tf_op jit(solution)/shard_map/ppermute | solution.py:436
  33.8 0.0 copy-done.5
  33.8 0.0 copy-done.6
  33.8 9.7 %sweep_first.1 = (f32[4,64,64,128]{3,2,1,0:T(8,128)S(1)}, f32[1024,128]{1,0:T(8,128)S(1)}, bf16[4,64,128]{2,1,0:T(8,128)(2,1)S(1)}) custom-call(f32[4]{0:T(128)S(1)} %copy-done.5, f32[4]{0:T(128)S(1)} %copy-done.6, f32[4,64,64,128]{3,2,1,0:T(8,128)S(1)} %copy-done, bf16[4,64,64,128]{3,2,1,0:T(8,128)(2,1)S(1)} %copy-done.1, s32[64,64,128]{2,1,0:T(8,128)S(1)} %copy-done.2, ...), custom_call_target="tpu_custom_call" | custom-call | flops 41943040 | bytes 41943040 | tf_op jit(solution)/shard_map/sweep_first/pallas_call | solution.py:416
  43.5 0.2 collective-permute-start.5
  43.7 1.1 %collective-permute-done.5.refs_5_.refs_6_ = bf16[4,64,128]{2,1,0:T(8,128)(2,1)S(1)} collective-permute-done((bf16[4,64,128]{2,1,0:T(8,128)(2,1)S(1)}, bf16[4,64,128]{2,1,0:T(8,128)(2,1)S(1)}, u32[]{:S(2)}, u32[]{:S(2)}) %collective-permute-start.5) | collective-permute-done | bytes 65568 | tf_op jit(solution)/shard_map/ppermute | solution.py:436
  44.8 0.0 copy-done.8
  44.8 0.0 copy-done.7
  44.8 10.1 %sweep_last.1 = (f32[4,64,64,128]{3,2,1,0:T(8,128)}, f32[40,128]{1,0:T(8,128)S(1)}) custom-call(f32[4]{0:T(128)S(1)} %copy-done.5, f32[4]{0:T(128)S(1)} %copy-done.6, f32[4,64,64,128]{3,2,1,0:T(8,128)S(1)} %get-tuple-element.17.refs_2_, bf16[4,64,64,128]{3,2,1,0:T(8,128)(2,1)S(1)} %copy-done.1, s32[64,64,128]{2,1,0:T(8,128)S(1)} %copy-done.2, ...), custom_call_target="tpu_custom_call" | custom-call | flops 41943040 | bytes 41943040 | tf_op jit(solution)/shard_map/sweep_last/pallas_call | solution.py:416
  54.9 1.8 %all-gather = f32[80,128]{1,0:T(8,128)S(1)} all-gather(f32[40,128]{1,0:T(8,128)S(1)} %get-tuple-element.21), channel_id=2, replica_groups=mesh['gx'=4,'gy'=4,'gz'=2] {'gz'}, dimensions={0}, use_global_device_ids=true | all-gather | bytes 61440 | tf_op jit(solution)/shard_map/all_gather | solution.py:612
  56.7 0.7 broadcast_in_dim.15
  57.5 6.8 %all-to-all-start = ((f32[16,40,128]{2,1,0:T(8,128)}), f32[16,40,128]{2,1,0:T(8,128)S(1)}, u32[]{:S(2)}, u32[]{:S(2)}) async-start(f32[16,40,128]{2,1,0:T(8,128)} %broadcast_in_dim.15), calls=%async_computation | async-start | bytes 655360 | tf_op jit(solution)/shard_map/all_to_all | solution.py:614
  64.3 12.3 %all-to-all-done.got_ref = f32[16,40,128]{2,1,0:T(8,128)S(1)} async-done(((f32[16,40,128]{2,1,0:T(8,128)}), f32[16,40,128]{2,1,0:T(8,128)S(1)}, u32[]{:S(2)}, u32[]{:S(2)}) %all-to-all-start) | async-done | bytes 327712 | tf_op jit(solution)/shard_map/all_to_all | solution.py:614
  76.6 2.2 %plane.1 = f32[1,16,512]{2,1,0:T(8,128)} custom-call(s32[1]{0:T(128)} %bitcast.1.me_ref, f32[16,40,128]{2,1,0:T(8,128)S(1)} %all-to-all-done.got_ref), custom_call_target="tpu_custom_call" | custom-call | tf_op jit(solution)/shard_map/plane/pallas_call | solution.py:616
  (2 shorter events, 0.0 us)
Async XLA Ops:
  0.6 18.8 %copy-start.2 = (s32[64,64,128]{2,1,0:T(8,128)S(1)}, s32[64,64,128]{2,1,0:T(8,128)}, u32[]{:S(2)}) copy-start(s32[64,64,128]{2,1,0:T(8,128)} %refs_4_.3) | copy-start | bytes 6291460
  0.6 18.8 %copy-start = (f32[4,64,64,128]{3,2,1,0:T(8,128)S(1)}, f32[4,64,64,128]{3,2,1,0:T(8,128)}, u32[]{:S(2)}) copy-start(f32[4,64,64,128]{3,2,1,0:T(8,128)} %refs_2_.1) | copy-start | bytes 25165828
  0.7 18.8 %copy-start.1 = (bf16[4,64,64,128]{3,2,1,0:T(8,128)(2,1)S(1)}, bf16[4,64,64,128]{3,2,1,0:T(8,128)(2,1)}, u32[]{:S(2)}) copy-start(bf16[4,64,64,128]{3,2,1,0:T(8,128)(2,1)} %refs_3_.3) | copy-start | bytes 12582916
  0.7 0.9 %copy-start.3 = (f32[64,64]{1,0:T(8,128)S(1)}, f32[64,64]{1,0:T(8,128)}, u32[]{:S(2)}) copy-start(f32[64,64]{1,0:T(8,128)} %d_ref.3) | copy-start | bytes 49156
  1.6 17.9 %copy-start.4 = (f32[64,64]{1,0:T(8,128)S(1)}, f32[64,64]{1,0:T(8,128)}, u32[]{:S(2)}) copy-start(f32[64,64]{1,0:T(8,128)} %d_ref.3) | copy-start | bytes 49156
  3.2 30.7 %copy-start.5 = (f32[4]{0:T(128)S(1)}, f32[4]{0:T(128)}, u32[]{:S(2)}) copy-start(f32[4]{0:T(128)} %refs_0_.3) | copy-start | bytes 52
  3.2 30.7 %copy-start.6 = (f32[4]{0:T(128)S(1)}, f32[4]{0:T(128)}, u32[]{:S(2)}) copy-start(f32[4]{0:T(128)} %refs_1_.3) | copy-start | bytes 52
  3.2 9.7 %collective-permute-start = (bf16[848,128]{1,0:T(8,128)(2,1)S(1)}, bf16[848,128]{1,0:T(8,128)(2,1)S(1)}, u32[]{:S(2)}, u32[]{:S(2)}) collective-permute-start(bf16[848,128]{1,0:T(8,128)(2,1)S(1)} %get-tuple-element.12), channel_id=1, source_target_pairs={{0,8},{8,16},{16,24},{1,9},{9,17},{17,25},{2,10},{10,18},{18,26},{... | collective-permute-start | bytes 651272 | tf_op jit(solution)/shard_map/ppermute | solution.py:431
  8.3 11.2 %collective-permute-start.1 = (bf16[848,128]{1,0:T(8,128)(2,1)S(1)}, bf16[848,128]{1,0:T(8,128)(2,1)S(1)}, u32[]{:S(2)}, u32[]{:S(2)}) collective-permute-start(bf16[848,128]{1,0:T(8,128)(2,1)S(1)} %get-tuple-element.13), channel_id=1, source_target_pairs={{8,0},{16,8},{24,16},{9,1},{17,9},{25,17},{10,2},{18,10},{26,18},{... | collective-permute-start | bytes 651272 | tf_op jit(solution)/shard_map/ppermute | solution.py:431
  22.2 8.8 %collective-permute-start.3 = (bf16[976,128]{1,0:T(8,128)(2,1)S(1)}, bf16[976,128]{1,0:T(8,128)(2,1)S(1)}, u32[]{:S(2)}, u32[]{:S(2)}) collective-permute-start(bf16[976,128]{1,0:T(8,128)(2,1)S(1)} %get-tuple-element.16.refs_11_.refs_8_), channel_id=1, source_target_pairs={{2,0},{4,2},{6,4},{3,1},{5,3},{7,5},{10,8},{12,10},{14,12},{11,9},... | collective-permute-start | bytes 749576 | tf_op jit(solution)/shard_map/ppermute | solution.py:431
  23.5 8.7 %collective-permute-start.2 = (bf16[976,128]{1,0:T(8,128)(2,1)S(1)}, bf16[976,128]{1,0:T(8,128)(2,1)S(1)}, u32[]{:S(2)}, u32[]{:S(2)}) collective-permute-start(bf16[976,128]{1,0:T(8,128)(2,1)S(1)} %get-tuple-element.15.refs_12_), channel_id=1, source_target_pairs={{0,2},{2,4},{4,6},{1,3},{3,5},{5,7},{8,10},{10,12},{12,14},{9,11},... | collective-permute-start | bytes 749576 | tf_op jit(solution)/shard_map/ppermute | solution.py:431
  32.4 12.4 %copy-start.8 = (s32[1,1,64,1]{2,3,1,0:T(1,128)S(1)}, s32[1,1,64,1]{2,3,1,0:T(1,128)}, u32[]{:S(2)}) copy-start(s32[1,1,64,1]{2,3,1,0:T(1,128)} %param.15) | copy-start | bytes 772
  32.4 12.4 %copy-start.7 = (f32[4]{0:T(128)S(1)}, f32[4]{0:T(128)}, u32[]{:S(2)}) copy-start(f32[4]{0:T(128)} %refs_11_.1) | copy-start | bytes 52
  32.4 1.4 %collective-permute-start.4 = (bf16[8,64,128]{2,1,0:T(8,128)(2,1)S(1)}, bf16[8,64,128]{2,1,0:T(8,128)(2,1)S(1)}, u32[]{:S(2)}, u32[]{:S(2)}) collective-permute-start(bf16[8,64,128]{2,1,0:T(8,128)(2,1)S(1)} %edge_faces.1), channel_id=1, source_target_pairs={{0,1},{1,0},{2,3},{3,2},{4,5},{5,4},{6,7},{7,6},{8,9},{9,8},{10,11... | collective-permute-start | bytes 393224 | tf_op jit(solution)/shard_map/ppermute | solution.py:436
  43.5 1.3 %collective-permute-start.5 = (bf16[4,64,128]{2,1,0:T(8,128)(2,1)S(1)}, bf16[4,64,128]{2,1,0:T(8,128)(2,1)S(1)}, u32[]{:S(2)}, u32[]{:S(2)}) collective-permute-start(bf16[4,64,128]{2,1,0:T(8,128)(2,1)S(1)} %get-tuple-element.18), channel_id=1, source_target_pairs={{0,1},{1,0},{2,3},{3,2},{4,5},{5,4},{6,7},{7,6},{8,9},{9,8},{10,11... | collective-permute-start | bytes 196616 | tf_op jit(solution)/shard_map/ppermute | solution.py:436
  57.5 19.1 %all-to-all-start = ((f32[16,40,128]{2,1,0:T(8,128)}), f32[16,40,128]{2,1,0:T(8,128)S(1)}, u32[]{:S(2)}, u32[]{:S(2)}) async-start(f32[16,40,128]{2,1,0:T(8,128)} %broadcast_in_dim.15), calls=%async_computation | async-start | bytes 655360 | tf_op jit(solution)/shard_map/all_to_all | solution.py:614

commit v6 on v5

--- a/solution.py
+++ b/solution.py
@@ -111,7 +111,7 @@
         out_ref[12 * rows : 13 * rows] = (ms[i] + 1).astype(F32).astype(BF16)
 
 
-def pack_kernel(v_ref, s_ref, m_ref, d_ref, xl_ref, xr_ref, ylo_ref, yhi_ref, g_ref, gs, ylo, yhi, ends):
+def pack_kernel(v_ref, s_ref, m_ref, ylo_ref, yhi_ref, g_ref, gs, ylo, yhi, ends):
     rows, depth = v_ref.shape[2:]
     gs[...] = jnp.zeros_like(gs)
     ends[...] = ends_matrix(depth)
@@ -134,24 +134,81 @@
 
     lax.fori_loop(0, v_ref.shape[1] // PB, group, 0)
     g_ref[...] = gs[...].astype(BF16)
-    nx = v_ref.shape[1]
+    for out_ref, rows_out in ((ylo_ref, ylo), (yhi_ref, yhi)):
+        out_ref[...] = rows_out[...].astype(BF16).reshape(out_ref.shape)
+
+
+def corner_kernel(lo_ref, hi_ref, d_ref, xl_ref, xr_ref, _, ylo_ref, yhi_ref):
+    block, depth = lo_ref.shape
     cells = d_ref.shape[0]
+    rows = (xl_ref.shape[0] - 2 * R) // PLANES
     strips = [r[PLANES * rows :].astype(F32)[:R] for r in (xl_ref, xr_ref)]
     filler = jnp.zeros((cells - 2 * R, depth), F32)
     tall = jnp.concatenate([strips[0], paired(d_ref[...]), strips[1], filler], 0).astype(BF16)
-    for out_ref, rows_out, edge, low in ((ylo_ref, ylo, 0, 0), (yhi_ref, yhi, rows - 1, rows - 16)):
-        out_ref[: PLANES * nx] = rows_out[...].astype(BF16).reshape(PLANES * nx, depth)
+    for out_ref, from_ref, edge, low in (
+        (ylo_ref, lo_ref, 0, 0),
+        (yhi_ref, hi_ref, rows - 1, rows - 16),
+    ):
+        out_ref[:block] = from_ref[...]
         corners = [
             r[c * rows + low : c * rows + low + 16].astype(F32)[edge - low : edge - low + 1]
             for r in (xl_ref, xr_ref)
             for c in range(4)
         ]
         corners.append(jnp.zeros((2 * R - 8, depth), F32))
-        out_ref[PLANES * nx : PLANES * nx + 2 * R] = jnp.concatenate(corners, 0).astype(BF16)
-        out_ref[PLANES * nx + 2 * R :] = tall
-
-
-def edge_kernel(g_ref, xl_ref, xr_ref, yl_ref, yr_ref, out_ref):
+        out_ref[block : block + 2 * R] = jnp.concatenate(corners, 0).astype(BF16)
+        out_ref[block + 2 * R :] = tall
+
+
+def inside_kernel(start, v_ref, s_ref, t_ref, token_ref, near, zt0, zt1):
+    planes_here, rows, depth = v_ref.shape[1:]
+    token_ref[...] = jnp.zeros_like(token_ref)
+    near[...] = jnp.concatenate([beside_matrix(depth)] * 2, 0)
+    row8 = lax.broadcasted_iota(jnp.int32, (8, depth), 0)
+    count = t_ref.shape[1]
+
+    def along_z(first, zt):
+        v = v_ref[:, pl.ds(first, PB)].reshape(4 * PB * rows, depth)
+        zt[...] = mm(jnp.concatenate(split(v), 1), near[...]).reshape(4, PB, rows, depth)
+
+    def group(i, zt, zt_next):
+        first = start + i * PB
+        along_z(jnp.minimum(first + PB, start + count - PB), zt_next)
+        for p in range(PB):
+            x = first + p
+            for low in range(0, rows, RC):
+                span = slice(low, low + RC)
+                for c in range(4):
+                    v = v_ref[c, x, span]
+                    before = v_ref[c, jnp.maximum(x - 1, 0), span]
+                    after = v_ref[c, jnp.minimum(x + 1, planes_here - 1), span]
+                    if p == 0:
+                        before = jnp.where(x == 0, 0.0, before)
+                    if p == PB - 1:
+                        after = jnp.where(x == planes_here - 1, 0.0, after)
+                    if low == 0:
+                        up = pltpu.roll(v, 1, 0)
+                        up = jnp.concatenate([jnp.where(row8 == 0, 0.0, up[:8]), up[8:]], 0)
+                    else:
+                        up = v_ref[c, x, low - 1 : low - 1 + RC]
+                    if low == rows - RC:
+                        down = pltpu.roll(v, RC - 1, 0)
+                        down = jnp.concatenate([down[:-8], jnp.where(row8 == 7, 0.0, down[-8:])], 0)
+                    else:
+                        down = v_ref[c, x, low + 1 : low + 1 + RC]
+                    total = before + after + s_ref[c, x, span].astype(F32) + zt[c, p, span]
+                    t_ref[c, i * PB + p, span] = total + up + down
+
+    def two(i, carry):
+        group(2 * i, zt0, zt1)
+        group(2 * i + 1, zt1, zt0)
+        return carry
+
+    along_z(start, zt0)
+    lax.fori_loop(0, count // (2 * PB), two, 0)
+
+
+def edge_kernel(g_ref, xl_ref, xr_ref, yl_ref, yr_ref, _, out_ref):
     parts, rows, depth = g_ref.shape
     beside = [r[: 4 * rows] for r in (xl_ref, xr_ref, yl_ref, yr_ref)]
     picked = mm(jnp.concatenate(beside, 1), ends_matrix(depth)[: 4 * depth])
@@ -165,8 +222,9 @@
         ext_ref, mid_ref, yl_ref, yr_ref, sh_ref, own_ref, o_ref, sens_ref = refs[7:15]
         hs, yl, yr, near, far, zt0, zt1, sens, value, news, sums, sems = refs[15:]
     else:
-        xl_ref, xr_ref, yl_ref, yr_ref, ylo_ref, yhi_ref, o_ref, ext_ref, g_ref = refs[7:16]
-        hs, yl, yr, near, far, zt0, zt1, gs, ends = refs[16:]
+        xl_ref, xr_ref, yl_ref, yr_ref, ylo_ref, yhi_ref = refs[7:13]
+        ta_ref, tb_ref, o_ref, ext_ref, g_ref = refs[13:18]
+        hs, yl, yr, near, far, zt0, zt1, gs, ends = refs[18:]
     planes_here, rows, depth = v_ref.shape[1:]
     lane = lanes_of((rows, depth))
 
@@ -221,27 +279,46 @@
     row8 = lax.broadcasted_iota(jnp.int32, tile, 0)
 
     def along_z(first, zt):
-        v = v_ref[:, pl.ds(first, PB)].reshape(4 * PB * rows, depth)
         masked = [
             jnp.where(lane // 2 == first + p, hs[c], 0.0).astype(BF16)
             for c in range(4)
             for p in range(PB)
         ]
-        out = mm(jnp.concatenate(split(v), 1), near[...]) + mm(jnp.concatenate(masked, 0), far[...])
+        out = mm(jnp.concatenate(masked, 0), far[...])
+        if last:
+            v = v_ref[:, pl.ds(first, PB)].reshape(4 * PB * rows, depth)
+            out = out + mm(jnp.concatenate(split(v), 1), near[...])
         zt[...] = out.reshape(4, PB, rows, depth)
 
-    def plane(first, p, zt, put):
+    def plane(first, p, zt, put, inside=None):
         for low in range(0, rows, RC):
-            chunk(first, p, low, zt, put)
-
-    def chunk(first, p, low, zt, put):
+            chunk(first, p, low, zt, put, inside)
+
+    def chunk(first, p, low, zt, put, inside):
         x = first + p
         span = slice(low, low + RC)
         mat = m_ref[x, span].reshape(RC // 8, 8, depth)
         masks = [mat == m for m in range(1, levels)]
         w_r, w_i = lookup(masks, wr), lookup(masks, wi)
 
+        def join(c):
+            t_ref, t_start = inside
+            total = t_ref[c, x - t_start, span] + zt[c, p, span]
+            if p == 0:
+                total = total + jnp.where(x == 0, x_halo(0, c * rows + low), 0.0)
+            if p == PB - 1:
+                total = total + jnp.where(x == planes_here - 1, x_halo(1, c * rows + low), 0.0)
+            if low == 0:
+                top = total[:8] + jnp.where(row8 == 0, yl[c, pl.ds(x, 1), :], 0.0)
+                total = jnp.concatenate([top, total[8:]], 0)
+            if low == rows - RC:
+                tail = total[-8:] + jnp.where(row8 == 7, yr[c, pl.ds(x, 1), :], 0.0)
+                total = jnp.concatenate([total[:-8], tail], 0)
+            return v_ref[c, x, span], total
+
         def drive(c):
+            if not last:
+                return join(c)
             v = v_ref[c, x, span]
             if p == 0:
                 before = v_ref[c, jnp.maximum(x - 1, 0), span]
@@ -289,7 +366,7 @@
 
     result = news if last else o_ref
 
-    def group(i, zt, zt_next):
+    def group(i, zt, zt_next, inside=None):
         first = i * PB
         along_z(jnp.minimum(first + PB, planes_here - PB), zt_next)
         for p in range(PB):
@@ -297,7 +374,7 @@
             def put(c, span, new, p=p):
                 result[c, first + p, span] = new
 
-            plane(first, p, zt, put)
+            plane(first, p, zt, put, inside)
         if last:
             store(i).start()
             parts = [part for p in range(PB) for part in split(value[p])]
@@ -306,13 +383,21 @@
         else:
             put_ends(first, o_ref, ends[...], gs)
 
-    def two(i, carry):
-        group(2 * i, zt0, zt1)
-        group(2 * i + 1, zt1, zt0)
-        return carry
+    def pairs(begin, end, inside=None):
+        def two(i, carry):
+            group(2 * i, zt0, zt1, inside)
+            group(2 * i + 1, zt1, zt0, inside)
+            return carry
+
+        lax.fori_loop(begin, end, two, 0)
 
     along_z(0, zt0)
-    lax.fori_loop(0, groups // 2, two, 0)
+    if last:
+        pairs(0, groups // 2)
+    else:
+        cut = ta_ref.shape[1]
+        pairs(0, cut // (2 * PB), (ta_ref, 0))
+        pairs(cut // (2 * PB), groups // 2, (tb_ref, cut))
 
     if not last:
         g_ref[...] = gs[...].astype(BF16)
@@ -465,12 +550,13 @@
         ny * nz * 100,
     )
     xl, xr = shift(xhi, "gx", True), shift(xlo, "gx", False)
-    ylo, yhi, g = local(
+    part_shape = jax.ShapeDtypeStruct((PLANES * nx, nz), BF16)
+    lo, hi, g = local(
         pack_kernel,
         "pack_faces",
-        held + [density, xl, xr],
-        [VMEM_SPEC] * 6,
-        [y_shape, y_shape, g_shape],
+        held,
+        [VMEM_SPEC] * 3,
+        [part_shape, part_shape, g_shape],
         [VMEM_SPEC] * 3,
         [
             pltpu.VMEM((4, ny, nz), F32),
@@ -481,12 +567,42 @@
         12,
         fields.size * 4,
     )
+    cut = nx // 2
+    inside = [
+        local(
+            functools.partial(inside_kernel, start),
+            "inside",
+            held[:2],
+            [VMEM_SPEC] * 2,
+            [pltpu.VMEM((4, cut, ny, nz), F32), jax.ShapeDtypeStruct((8, nz), F32)],
+            [VMEM_SPEC] * 2,
+            [
+                pltpu.VMEM((2 * nz, nz), BF16),
+                pltpu.VMEM((4, PB, ny, nz), F32),
+                pltpu.VMEM((4, PB, ny, nz), F32),
+            ],
+            8,
+            fields.size * 5,
+        )
+        for start in (0, cut)
+    ]
+    ylo, yhi = local(
+        corner_kernel,
+        "corners",
+        [lo, hi, density, xl, xr, inside[0][1]],
+        [VMEM_SPEC] * 6,
+        [y_shape] * 2,
+        [VMEM_SPEC] * 2,
+        [],
+        8,
+        ny * nz * 40,
+    )
     yl, yr = shift(yhi, "gy", True), shift(ylo, "gy", False)
     g = local(
         edge_kernel,
         "edge_faces",
-        [g, xl, xr, yl, yr],
-        [VMEM_SPEC] * 5,
+        [g, xl, xr, yl, yr, inside[1][1]],
+        [VMEM_SPEC] * 6,
         wide_g,
         VMEM_SPEC,
         [],
@@ -510,8 +626,8 @@
     middle, ext, g = local(
         functools.partial(sweep_kernel, False, nz_parts, scale),
         "sweep_first",
-        [*tables, *held, gl, gr, xl, xr, yl, yr, ylo, yhi],
-        [SMEM_SPEC] * 2 + [VMEM_SPEC] * 11,
+        [*tables, held[0], density, held[2], gl, gr, xl, xr, yl, yr, ylo, yhi, *(near(t) for t, _ in inside)],
+        [SMEM_SPEC] * 2 + [VMEM_SPEC] * 13,
         [pltpu.VMEM(fields.shape, F32), jax.ShapeDtypeStruct((16 * ny, nz), F32), g_shape],
         [VMEM_SPEC] * 3,
         scratch(8) + [pltpu.VMEM((4, ny, nz), F32), pltpu.VMEM((PB * nz, nz), BF16)],

time: 79.2 us -> 72.6 us (0.917)
  waiting for transfers between devices: 28.7 us -> 21.9 us
    ppermute x4, waiting for transfers between devices: 14 us -> 7.12 us  [shift(): lax.ppermute(value, axis, pairs if up else [(j, i) for i, j in pairs])]
    pallas_call x5 -> x8, Pallas kernels: 24.2 us -> 24.4 us  [local(): pl.pallas_call(kernel, in_specs=specs, out_specs=out_specs, out_shape=sha...]
  transfers between devices with their start and end apart: 7 -> 7, of which waited for: 7 -> 6; matrix products, arithmetic and copies ran while one was open for 0% -> 0% of each run, Pallas kernels for 0% -> 9%
where the time goes in v6:
time: 72.6 us; the launch traced here: 72.3 us
  Pallas kernels  26.7 us (37%)
  waiting for transfers between devices  21.9 us (30%)
  starting transfers between devices  19.4 us (27%)
  blocking collectives  1.83 us (3%)
  local copies, waits for them, and re-layouts  1.7 us (2%)
  between operations  0.84 us (1%)
    pallas_call x8, Pallas kernels, local(): pl.pallas_call(kernel, in_specs=specs, out_specs=out_specs, out_shape=sha...  24.4 us
    all_to_all x1, waiting for transfers between devices, on_device(): plane = lax.all_to_all(copies, ('gx', 'gy'), split_axis=0, concat_axis=0)  12.3 us
    ppermute x4, starting transfers between devices, shift(): lax.ppermute(value, axis, pairs if up else [(j, i) for i, j in pairs])  12.3 us
    ppermute x4, waiting for transfers between devices, shift(): lax.ppermute(value, axis, pairs if up else [(j, i) for i, j in pairs])  7.12 us
    all_to_all x1, starting transfers between devices, on_device(): plane = lax.all_to_all(copies, ('gx', 'gy'), split_axis=0, concat_axis=0)  6.83 us
    ppermute x2, waiting for transfers between devices, shift_z(): other = lax.ppermute(g, 'gz', [(0, 1), (1, 0)])  2.44 us
    pallas_call x1, Pallas kernels, on_device(): pl.pallas_call(functools.partial(plane_kernel, ngx, ngy), in_specs=[SMEM_...  2.25 us
    all_gather x1, blocking collectives, on_device(): partial = jnp.sum(lax.all_gather(partial, 'gz'), 0)  1.83 us
  transfers between devices with their start and end apart: 7, of which 6 were waited for; matrix products, arithmetic and copies ran while one was open for 0% of the time, Pallas kernels for 9%

profile of v6, /device:TPU:0, one launch (start us, length us, event | category | flops | bytes accessed | tf_op | source)
XLA Modules:
  0.0 72.3 jit_solution(16817742636656011251)
XLA Ops:
  0.6 0.0 copy-start.2
  0.6 0.0 copy-start
  0.6 0.0 copy-start.1
  0.7 0.0 copy-start.3
  0.7 0.9 %copy-done.3 = f32[64,64]{1,0:T(8,128)S(1)} copy-done((f32[64,64]{1,0:T(8,128)S(1)}, f32[64,64]{1,0:T(8,128)}, u32[]{:S(2)}) %copy-start.3) | copy-done | bytes 16408
  1.6 1.6 %x_faces.1 = (bf16[848,128]{1,0:T(8,128)(2,1)S(1)}, bf16[848,128]{1,0:T(8,128)(2,1)S(1)}) custom-call(f32[4,64,64,128]{3,2,1,0:T(8,128)} %refs_2_.1, bf16[4,64,64,128]{3,2,1,0:T(8,128)(2,1)} %refs_3_.3, s32[64,64,128]{2,1,0:T(8,128)} %refs_4_.3, f32[64,64]{1,0:T(8,128)S(1)} %copy-done.3), custom_call_target="tpu_custom_call" | custom-call | flops 819200 | bytes 819200 | tf_op jit(solution)/shard_map/x_faces/pallas_call | solution.py:501
  3.2 5.1 %collective-permute-start = (bf16[848,128]{1,0:T(8,128)(2,1)S(1)}, bf16[848,128]{1,0:T(8,128)(2,1)S(1)}, u32[]{:S(2)}, u32[]{:S(2)}) collective-permute-start(bf16[848,128]{1,0:T(8,128)(2,1)S(1)} %get-tuple-element.19), channel_id=1, source_target_pairs={{0,8},{8,16},{16,24},{1,9},{9,17},{17,25},{2,10},{10,18},{18,26},{... | collective-permute-start | bytes 651272 | tf_op jit(solution)/shard_map/ppermute | solution.py:516
  8.3 1.3 %collective-permute-start.1 = (bf16[848,128]{1,0:T(8,128)(2,1)S(1)}, bf16[848,128]{1,0:T(8,128)(2,1)S(1)}, u32[]{:S(2)}, u32[]{:S(2)}) collective-permute-start(bf16[848,128]{1,0:T(8,128)(2,1)S(1)} %get-tuple-element.20), channel_id=1, source_target_pairs={{8,0},{16,8},{24,16},{9,1},{17,9},{25,17},{10,2},{18,10},{26,18},{... | collective-permute-start | bytes 651272 | tf_op jit(solution)/shard_map/ppermute | solution.py:516
  9.6 0.0 copy-done.2
  9.6 0.0 copy-done
  9.6 0.0 copy-done.1
  9.6 2.6 %pack_faces.1 = (bf16[832,128]{1,0:T(8,128)(2,1)S(1)}, bf16[832,128]{1,0:T(8,128)(2,1)S(1)}, bf16[4,64,128]{2,1,0:T(8,128)(2,1)S(1)}) custom-call(f32[4,64,64,128]{3,2,1,0:T(8,128)S(1)} %copy-done, bf16[4,64,64,128]{3,2,1,0:T(8,128)(2,1)S(1)} %copy-done.1, s32[64,64,128]{2,1,0:T(8,128)S(1)} %copy-done.2), custom_call_target="tpu_custom_call" | custom-call | flops 8388608 | bytes 8388608 | tf_op jit(solution)/shard_map/pack_faces/pallas_call | solution.py:501
  12.2 0.0 copy-start.4
  12.3 2.1 %inside.2 = (f32[4,32,64,128]{3,2,1,0:T(8,128)S(1)}, f32[8,128]{1,0:T(8,128)S(1)}) custom-call(f32[4,64,64,128]{3,2,1,0:T(8,128)S(1)} %copy-done, bf16[4,64,64,128]{3,2,1,0:T(8,128)(2,1)S(1)} %copy-done.1), custom_call_target="tpu_custom_call" | custom-call | flops 10485760 | bytes 10485760 | tf_op jit(solution)/shard_map/inside/pallas_call | solution.py:501
  14.3 0.0 collective-permute-done.xl_ref.refs_7_
  14.4 5.1 %collective-permute-done.1.xr_ref.refs_8_ = bf16[848,128]{1,0:T(8,128)(2,1)S(1)} collective-permute-done((bf16[848,128]{1,0:T(8,128)(2,1)S(1)}, bf16[848,128]{1,0:T(8,128)(2,1)S(1)}, u32[]{:S(2)}, u32[]{:S(2)}) %collective-permute-start.1) | collective-permute-done | bytes 217120 | tf_op jit(solution)/shard_map/ppermute | solution.py:516
  19.4 0.0 copy-done.4
  19.5 0.1 corners.1
  19.5 1.3 %collective-permute-start.3 = (bf16[976,128]{1,0:T(8,128)(2,1)S(1)}, bf16[976,128]{1,0:T(8,128)(2,1)S(1)}, u32[]{:S(2)}, u32[]{:S(2)}) collective-permute-start(bf16[976,128]{1,0:T(8,128)(2,1)S(1)} %get-tuple-element.25.refs_11_.refs_8_), channel_id=1, source_target_pairs={{2,0},{4,2},{6,4},{3,1},{5,3},{7,5},{10,8},{12,10},{14,12},{11,9},... | collective-permute-start | bytes 749576 | tf_op jit(solution)/shard_map/ppermute | solution.py:516
  20.8 0.0 copy-start.5
  20.8 0.0 copy-start.6
  20.8 4.6 %collective-permute-start.2 = (bf16[976,128]{1,0:T(8,128)(2,1)S(1)}, bf16[976,128]{1,0:T(8,128)(2,1)S(1)}, u32[]{:S(2)}, u32[]{:S(2)}) collective-permute-start(bf16[976,128]{1,0:T(8,128)(2,1)S(1)} %get-tuple-element.24.refs_12_), channel_id=1, source_target_pairs={{0,2},{2,4},{4,6},{1,3},{3,5},{5,7},{8,10},{10,12},{12,14},{9,11},... | collective-permute-start | bytes 749576 | tf_op jit(solution)/shard_map/ppermute | solution.py:516
  25.4 2.1 %inside.3 = (f32[4,32,64,128]{3,2,1,0:T(8,128)S(1)}, f32[8,128]{1,0:T(8,128)S(1)}) custom-call(f32[4,64,64,128]{3,2,1,0:T(8,128)S(1)} %copy-done, bf16[4,64,64,128]{3,2,1,0:T(8,128)(2,1)S(1)} %copy-done.1), custom_call_target="tpu_custom_call" | custom-call | flops 10485760 | bytes 10485760 | tf_op jit(solution)/shard_map/inside/pallas_call | solution.py:501
  27.5 0.8 %collective-permute-done.3.yr_ref.refs_10_ = bf16[976,128]{1,0:T(8,128)(2,1)S(1)} collective-permute-done((bf16[976,128]{1,0:T(8,128)(2,1)S(1)}, bf16[976,128]{1,0:T(8,128)(2,1)S(1)}, u32[]{:S(2)}, u32[]{:S(2)}) %collective-permute-start.3) | collective-permute-done | bytes 249888 | tf_op jit(solution)/shard_map/ppermute | solution.py:516
  28.3 1.2 %collective-permute-done.2.yl_ref.refs_9_ = bf16[976,128]{1,0:T(8,128)(2,1)S(1)} collective-permute-done((bf16[976,128]{1,0:T(8,128)(2,1)S(1)}, bf16[976,128]{1,0:T(8,128)(2,1)S(1)}, u32[]{:S(2)}, u32[]{:S(2)}) %collective-permute-start.2) | collective-permute-done | bytes 249888 | tf_op jit(solution)/shard_map/ppermute | solution.py:516
  29.5 0.2 edge_faces.1
  29.8 0.1 collective-permute-start.4
  29.8 1.3 %collective-permute-done.4.refs_5_.refs_6_ = bf16[8,64,128]{2,1,0:T(8,128)(2,1)S(1)} collective-permute-done((bf16[8,64,128]{2,1,0:T(8,128)(2,1)S(1)}, bf16[8,64,128]{2,1,0:T(8,128)(2,1)S(1)}, u32[]{:S(2)}, u32[]{:S(2)}) %collective-permute-start.4) | collective-permute-done | bytes 131104 | tf_op jit(solution)/shard_map/ppermute | solution.py:521
  31.2 0.0 copy-done.5
  31.2 0.0 copy-done.6
  31.2 0.0 copy-start.8
  31.2 0.0 copy-start.7
  31.2 6.1 %sweep_first.1 = (f32[4,64,64,128]{3,2,1,0:T(8,128)S(1)}, f32[1024,128]{1,0:T(8,128)S(1)}, bf16[4,64,128]{2,1,0:T(8,128)(2,1)S(1)}) custom-call(f32[4]{0:T(128)S(1)} %copy-done.5, f32[4]{0:T(128)S(1)} %copy-done.6, f32[4,64,64,128]{3,2,1,0:T(8,128)S(1)} %copy-done, f32[64,64]{1,0:T(8,128)S(1)} %copy-done.4, s32[64,64,128]{2,1,0:T(8,128)S(1)} %copy-done.2, ...), custom_call_target="tpu_custom_call" | custom-call | flops 41943040 | bytes 41943040 | tf_op jit(solution)/shard_map/sweep_first/pallas_call | solution.py:501
  37.3 0.2 collective-permute-start.5
  37.5 1.1 %collective-permute-done.5.refs_5_.refs_6_ = bf16[4,64,128]{2,1,0:T(8,128)(2,1)S(1)} collective-permute-done((bf16[4,64,128]{2,1,0:T(8,128)(2,1)S(1)}, bf16[4,64,128]{2,1,0:T(8,128)(2,1)S(1)}, u32[]{:S(2)}, u32[]{:S(2)}) %collective-permute-start.5) | collective-permute-done | bytes 65568 | tf_op jit(solution)/shard_map/ppermute | solution.py:521
  38.6 0.0 copy-done.8
  38.6 0.0 copy-done.7
  38.6 9.7 %sweep_last.1 = (f32[4,64,64,128]{3,2,1,0:T(8,128)}, f32[40,128]{1,0:T(8,128)S(1)}) custom-call(f32[4]{0:T(128)S(1)} %copy-done.5, f32[4]{0:T(128)S(1)} %copy-done.6, f32[4,64,64,128]{3,2,1,0:T(8,128)S(1)} %get-tuple-element.29.refs_2_, bf16[4,64,64,128]{3,2,1,0:T(8,128)(2,1)S(1)} %copy-done.1, s32[64,64,128]{2,1,0:T(8,128)S(1)} %copy-done.2, ...), custom_call_target="tpu_custom_call" | custom-call | flops 41943040 | bytes 41943040 | tf_op jit(solution)/shard_map/sweep_last/pallas_call | solution.py:501
  48.3 1.8 %all-gather = f32[80,128]{1,0:T(8,128)S(1)} all-gather(f32[40,128]{1,0:T(8,128)S(1)} %get-tuple-element.33), channel_id=2, replica_groups=mesh['gx'=4,'gy'=4,'gz'=2] {'gz'}, dimensions={0}, use_global_device_ids=true | all-gather | bytes 61440 | tf_op jit(solution)/shard_map/all_gather | solution.py:728
  50.1 0.8 %broadcast_in_dim.15 = f32[16,40,128]{2,1,0:T(8,128)} broadcast(f32[40,128]{1,0:T(8,128)S(1)} %reduce_sum.9), dimensions={1,2} | broadcast | bytes 348160 | tf_op jit(solution)/shard_map/broadcast_in_dim | solution.py:729
  50.9 6.8 %all-to-all-start = ((f32[16,40,128]{2,1,0:T(8,128)}), f32[16,40,128]{2,1,0:T(8,128)S(1)}, u32[]{:S(2)}, u32[]{:S(2)}) async-start(f32[16,40,128]{2,1,0:T(8,128)} %broadcast_in_dim.15), calls=%async_computation | async-start | bytes 655360 | tf_op jit(solution)/shard_map/all_to_all | solution.py:730
  57.7 12.3 %all-to-all-done.got_ref = f32[16,40,128]{2,1,0:T(8,128)S(1)} async-done(((f32[16,40,128]{2,1,0:T(8,128)}), f32[16,40,128]{2,1,0:T(8,128)S(1)}, u32[]{:S(2)}, u32[]{:S(2)}) %all-to-all-start) | async-done | bytes 327712 | tf_op jit(solution)/shard_map/all_to_all | solution.py:730
  70.0 2.2 %plane.1 = f32[1,16,512]{2,1,0:T(8,128)} custom-call(s32[1]{0:T(128)} %bitcast.1.me_ref, f32[16,40,128]{2,1,0:T(8,128)S(1)} %all-to-all-done.got_ref), custom_call_target="tpu_custom_call" | custom-call | tf_op jit(solution)/shard_map/plane/pallas_call | solution.py:732
  (2 shorter events, 0.0 us)
Async XLA Ops:
  0.6 9.0 %copy-start.2 = (s32[64,64,128]{2,1,0:T(8,128)S(1)}, s32[64,64,128]{2,1,0:T(8,128)}, u32[]{:S(2)}) copy-start(s32[64,64,128]{2,1,0:T(8,128)} %refs_4_.3) | copy-start | bytes 6291460
  0.6 9.0 %copy-start = (f32[4,64,64,128]{3,2,1,0:T(8,128)S(1)}, f32[4,64,64,128]{3,2,1,0:T(8,128)}, u32[]{:S(2)}) copy-start(f32[4,64,64,128]{3,2,1,0:T(8,128)} %refs_2_.1) | copy-start | bytes 25165828
  0.6 9.0 %copy-start.1 = (bf16[4,64,64,128]{3,2,1,0:T(8,128)(2,1)S(1)}, bf16[4,64,64,128]{3,2,1,0:T(8,128)(2,1)}, u32[]{:S(2)}) copy-start(bf16[4,64,64,128]{3,2,1,0:T(8,128)(2,1)} %refs_3_.3) | copy-start | bytes 12582916
  0.7 0.9 %copy-start.3 = (f32[64,64]{1,0:T(8,128)S(1)}, f32[64,64]{1,0:T(8,128)}, u32[]{:S(2)}) copy-start(f32[64,64]{1,0:T(8,128)} %refs_3_.2) | copy-start | bytes 49156
  3.2 11.2 %collective-permute-start = (bf16[848,128]{1,0:T(8,128)(2,1)S(1)}, bf16[848,128]{1,0:T(8,128)(2,1)S(1)}, u32[]{:S(2)}, u32[]{:S(2)}) collective-permute-start(bf16[848,128]{1,0:T(8,128)(2,1)S(1)} %get-tuple-element.19), channel_id=1, source_target_pairs={{0,8},{8,16},{16,24},{1,9},{9,17},{17,25},{2,10},{10,18},{18,26},{... | collective-permute-start | bytes 651272 | tf_op jit(solution)/shard_map/ppermute | solution.py:516
  8.3 11.2 %collective-permute-start.1 = (bf16[848,128]{1,0:T(8,128)(2,1)S(1)}, bf16[848,128]{1,0:T(8,128)(2,1)S(1)}, u32[]{:S(2)}, u32[]{:S(2)}) collective-permute-start(bf16[848,128]{1,0:T(8,128)(2,1)S(1)} %get-tuple-element.20), channel_id=1, source_target_pairs={{8,0},{16,8},{24,16},{9,1},{17,9},{25,17},{10,2},{18,10},{26,18},{... | collective-permute-start | bytes 651272 | tf_op jit(solution)/shard_map/ppermute | solution.py:516
  12.2 7.2 %copy-start.4 = (f32[64,64]{1,0:T(8,128)S(1)}, f32[64,64]{1,0:T(8,128)}, u32[]{:S(2)}) copy-start(f32[64,64]{1,0:T(8,128)} %refs_3_.2) | copy-start | bytes 49156
  19.5 8.8 %collective-permute-start.3 = (bf16[976,128]{1,0:T(8,128)(2,1)S(1)}, bf16[976,128]{1,0:T(8,128)(2,1)S(1)}, u32[]{:S(2)}, u32[]{:S(2)}) collective-permute-start(bf16[976,128]{1,0:T(8,128)(2,1)S(1)} %get-tuple-element.25.refs_11_.refs_8_), channel_id=1, source_target_pairs={{2,0},{4,2},{6,4},{3,1},{5,3},{7,5},{10,8},{12,10},{14,12},{11,9},... | collective-permute-start | bytes 749576 | tf_op jit(solution)/shard_map/ppermute | solution.py:516
  20.8 10.4 %copy-start.5 = (f32[4]{0:T(128)S(1)}, f32[4]{0:T(128)}, u32[]{:S(2)}) copy-start(f32[4]{0:T(128)} %refs_0_.3) | copy-start | bytes 52
  20.8 10.3 %copy-start.6 = (f32[4]{0:T(128)S(1)}, f32[4]{0:T(128)}, u32[]{:S(2)}) copy-start(f32[4]{0:T(128)} %refs_1_.3) | copy-start | bytes 52
  20.8 8.7 %collective-permute-start.2 = (bf16[976,128]{1,0:T(8,128)(2,1)S(1)}, bf16[976,128]{1,0:T(8,128)(2,1)S(1)}, u32[]{:S(2)}, u32[]{:S(2)}) collective-permute-start(bf16[976,128]{1,0:T(8,128)(2,1)S(1)} %get-tuple-element.24.refs_12_), channel_id=1, source_target_pairs={{0,2},{2,4},{4,6},{1,3},{3,5},{5,7},{8,10},{10,12},{12,14},{9,11},... | collective-permute-start | bytes 749576 | tf_op jit(solution)/shard_map/ppermute | solution.py:516
  29.8 1.4 %collective-permute-start.4 = (bf16[8,64,128]{2,1,0:T(8,128)(2,1)S(1)}, bf16[8,64,128]{2,1,0:T(8,128)(2,1)S(1)}, u32[]{:S(2)}, u32[]{:S(2)}) collective-permute-start(bf16[8,64,128]{2,1,0:T(8,128)(2,1)S(1)} %edge_faces.1), channel_id=1, source_target_pairs={{0,1},{1,0},{2,3},{3,2},{4,5},{5,4},{6,7},{7,6},{8,9},{9,8},{10,11... | collective-permute-start | bytes 393224 | tf_op jit(solution)/shard_map/ppermute | solution.py:521
  31.2 7.4 %copy-start.8 = (s32[1,1,64,1]{2,3,1,0:T(1,128)S(1)}, s32[1,1,64,1]{2,3,1,0:T(1,128)}, u32[]{:S(2)}) copy-start(s32[1,1,64,1]{2,3,1,0:T(1,128)} %param.15) | copy-start | bytes 772
  31.2 7.4 %copy-start.7 = (f32[4]{0:T(128)S(1)}, f32[4]{0:T(128)}, u32[]{:S(2)}) copy-start(f32[4]{0:T(128)} %refs_11_.1) | copy-start | bytes 52
  37.3 1.3 %collective-permute-start.5 = (bf16[4,64,128]{2,1,0:T(8,128)(2,1)S(1)}, bf16[4,64,128]{2,1,0:T(8,128)(2,1)S(1)}, u32[]{:S(2)}, u32[]{:S(2)}) collective-permute-start(bf16[4,64,128]{2,1,0:T(8,128)(2,1)S(1)} %get-tuple-element.30), channel_id=1, source_target_pairs={{0,1},{1,0},{2,3},{3,2},{4,5},{5,4},{6,7},{7,6},{8,9},{9,8},{10,11... | collective-permute-start | bytes 196616 | tf_op jit(solution)/shard_map/ppermute | solution.py:521
  50.9 19.1 %all-to-all-start = ((f32[16,40,128]{2,1,0:T(8,128)}), f32[16,40,128]{2,1,0:T(8,128)S(1)}, u32[]{:S(2)}, u32[]{:S(2)}) async-start(f32[16,40,128]{2,1,0:T(8,128)} %broadcast_in_dim.15), calls=%async_computation | async-start | bytes 655360 | tf_op jit(solution)/shard_map/all_to_all | solution.py:730

commit v7 on v6

--- a/solution.py
+++ b/solution.py
@@ -46,12 +46,6 @@
     return jnp.where(even | odd, 1.0, 0.0).astype(BF16)
 
 
-def sum_matrix(depth):
-    k = lax.broadcasted_iota(jnp.int32, (2 * PB * depth, depth), 0) // (2 * depth)
-    j = lax.broadcasted_iota(jnp.int32, (2 * PB * depth, depth), 1) % PB
-    return jnp.where(k == j, 1.0, 0.0).astype(BF16)
-
-
 def split(value):
     high = value.astype(BF16)
     return high, (value - high.astype(F32)).astype(BF16)
@@ -76,7 +70,7 @@
     return jnp.concatenate([high, value - high], 1)
 
 
-PLANES = 13
+PLANES = 9
 
 
 def x_kernel(v_ref, s_ref, m_ref, d_ref, xlo_ref, xhi_ref, vs, ss, ms, sems):
@@ -106,9 +100,9 @@
             copy.wait()
         inner = sides[i][2]
         out_ref[: 4 * rows] = vs[i, :, 1 - inner].astype(BF16).reshape(4 * rows, depth)
-        out_ref[4 * rows : 8 * rows] = vs[i, :, inner].astype(BF16).reshape(4 * rows, depth)
-        out_ref[8 * rows : 12 * rows] = ss[i].reshape(4 * rows, depth)
-        out_ref[12 * rows : 13 * rows] = (ms[i] + 1).astype(F32).astype(BF16)
+        beyond = vs[i, :, inner] + ss[i].astype(F32)
+        out_ref[4 * rows : 8 * rows] = beyond.astype(BF16).reshape(4 * rows, depth)
+        out_ref[8 * rows : 9 * rows] = (ms[i] + 1).astype(F32).astype(BF16)
 
 
 def pack_kernel(v_ref, s_ref, m_ref, ylo_ref, yhi_ref, g_ref, gs, ylo, yhi, ends):
@@ -126,10 +120,9 @@
             for out, edge, inner, low in ((ylo, 0, 1, 0), (yhi, rows - 1, rows - 2, rows - 16)):
                 for c in range(4):
                     out[c, here, :] = v_ref[c, x, edge : edge + 1, :]
-                    out[4 + c, here, :] = v_ref[c, x, inner : inner + 1, :]
-                    near_edge = s_ref[c, x, low : low + 16, :].astype(F32)
-                    out[8 + c, here, :] = near_edge[edge - low : edge - low + 1]
-                out[12, here, :] = level[edge : edge + 1]
+                    source = s_ref[c, x, low : low + 16, :].astype(F32)[edge - low : edge - low + 1]
+                    out[4 + c, here, :] = v_ref[c, x, inner : inner + 1, :] + source
+                out[8, here, :] = level[edge : edge + 1]
         return carry
 
     lax.fori_loop(0, v_ref.shape[1] // PB, group, 0)
@@ -220,7 +213,7 @@
     sr_ref, si_ref, v_ref, s_ref, m_ref, gl_ref, gr_ref = refs[:7]
     if last:
         ext_ref, mid_ref, yl_ref, yr_ref, sh_ref, own_ref, o_ref, sens_ref = refs[7:15]
-        hs, yl, yr, near, far, zt0, zt1, sens, value, news, sums, sems = refs[15:]
+        hs, yl, yr, near, far, zt0, zt1, sens, news, sems = refs[15:]
     else:
         xl_ref, xr_ref, yl_ref, yr_ref, ylo_ref, yhi_ref = refs[7:13]
         ta_ref, tb_ref, o_ref, ext_ref, g_ref = refs[13:18]
@@ -241,7 +234,6 @@
     far[...] = halo_matrix(depth)
     if last:
         sens[...] = jnp.zeros_like(sens)
-        sums[...] = sum_matrix(depth)
     else:
         gs[...] = jnp.zeros_like(gs)
         ends[...] = ends_matrix(depth)
@@ -356,7 +348,9 @@
             put(re + 1, span, n_i)
             new += [n_r, n_i]
         if last:
-            value[p, span] = lookup(masks, share) * (new[0] * new[2] - new[1] * new[3])
+            value = lookup(masks, share) * (new[0] * new[2] - new[1] * new[3])
+            column = jnp.sum(value, axis=1, keepdims=True)
+            sens[span] = jnp.where(lane[:RC] == x, column, sens[span])
 
     groups = planes_here // PB
 
@@ -377,9 +371,6 @@
             plane(first, p, zt, put, inside)
         if last:
             store(i).start()
-            parts = [part for p in range(PB) for part in split(value[p])]
-            picked = mm(jnp.concatenate(parts, 1), sums[...])
-            sens[...] = jnp.where(lane // PB == i, picked, sens[...])
         else:
             put_ends(first, o_ref, ends[...], gs)
 
@@ -414,7 +405,7 @@
         corner_r = yr_ref[block : block + 2 * R].astype(F32)
         zero = jnp.zeros(tile, F32)
         for e, ref in enumerate(sides):
-            level = ref[3 * face : 3 * face + rows].astype(F32).reshape(rows // 8, 8, depth)
+            level = ref[2 * face : 2 * face + rows].astype(F32).reshape(rows // 8, 8, depth)
             masks = [level == float(m + 1) for m in range(levels)]
             w_r, w_i = lookup(masks, [zero] + wr), lookup(masks, [zero] + wi)
 
@@ -429,8 +420,7 @@
                     inside = (ylo_ref, yhi_ref)[e - 2][part].astype(F32)
                     corner = corner_l if e == 2 else corner_r
                     top, low = corner[c : c + 1], corner[4 + c : 5 + c]
-                source = ref[2 * face + c * rows : 2 * face + (c + 1) * rows].astype(F32)
-                total = beyond + inside + source + zt0[c, e]
+                total = beyond + inside + zt0[c, e]
                 up = pltpu.roll(v, 1, 0)
                 down = pltpu.roll(v, rows - 1, 0)
                 up = jnp.concatenate([jnp.where(row8 == 0, top, up[:8]), up[8:]], 0)
@@ -648,9 +638,7 @@
         scratch(4)
         + [
             pltpu.VMEM((ny, nz), F32),
-            pltpu.VMEM((PB, ny, nz), F32),
             pltpu.VMEM(fields.shape, F32),
-            pltpu.VMEM((2 * PB * nz, nz), BF16),
             pltpu.SemaphoreType.DMA((nx // PB,)),
         ],
         20,

time: 72.6 us -> 68.5 us (0.944)
  waiting for transfers between devices: 21.9 us -> 18 us
    ppermute x4, waiting for transfers between devices: 7.12 us -> 3.24 us  [shift(): lax.ppermute(value, axis, pairs if up else [(j, i) for i, j in pairs])]
  transfers between devices with their start and end apart: 7 -> 7, of which waited for: 6 -> 5; matrix products, arithmetic and copies ran while one was open for 0% -> 0% of each run, Pallas kernels for 9% -> 10%
where the time goes in v7:
time: 68.5 us; the launch traced here: 68.2 us
  Pallas kernels  26.5 us (39%)
  starting transfers between devices  19.3 us (28%)
  waiting for transfers between devices  18 us (26%)
  blocking collectives  1.83 us (3%)
  local copies, waits for them, and re-layouts  1.7 us (2%)
  between operations  0.84 us (1%)
    pallas_call x8, Pallas kernels, local(): pl.pallas_call(kernel, in_specs=specs, out_specs=out_specs, out_shape=sha...  24.3 us
    all_to_all x1, waiting for transfers between devices, on_device(): plane = lax.all_to_all(copies, ('gx', 'gy'), split_axis=0, concat_axis=0)  12.3 us
    ppermute x4, starting transfers between devices, shift(): lax.ppermute(value, axis, pairs if up else [(j, i) for i, j in pairs])  12.2 us
    all_to_all x1, starting transfers between devices, on_device(): plane = lax.all_to_all(copies, ('gx', 'gy'), split_axis=0, concat_axis=0)  6.82 us
    ppermute x4, waiting for transfers between devices, shift(): lax.ppermute(value, axis, pairs if up else [(j, i) for i, j in pairs])  3.24 us
    ppermute x2, waiting for transfers between devices, shift_z(): other = lax.ppermute(g, 'gz', [(0, 1), (1, 0)])  2.45 us
    pallas_call x1, Pallas kernels, on_device(): pl.pallas_call(functools.partial(plane_kernel, ngx, ngy), in_specs=[SMEM_...  2.25 us
    all_gather x1, blocking collectives, on_device(): partial = jnp.sum(lax.all_gather(partial, 'gz'), 0)  1.83 us
  transfers between devices with their start and end apart: 7, of which 5 were waited for; matrix products, arithmetic and copies ran while one was open for 0% of the time, Pallas kernels for 10%

profile of v7, /device:TPU:0, one launch (start us, length us, event | category | flops | bytes accessed | tf_op | source)
XLA Modules:
  0.0 68.2 jit_solution(16160949337042738779)
XLA Ops:
  0.6 0.0 copy-start.2
  0.6 0.0 copy-start
  0.6 0.0 copy-start.1
  0.7 0.0 copy-start.3
  0.7 0.9 %copy-done.3 = f32[64,64]{1,0:T(8,128)S(1)} copy-done((f32[64,64]{1,0:T(8,128)S(1)}, f32[64,64]{1,0:T(8,128)}, u32[]{:S(2)}) %copy-start.3) | copy-done | bytes 16408
  1.6 1.6 %x_faces.1 = (bf16[592,128]{1,0:T(8,128)(2,1)S(1)}, bf16[592,128]{1,0:T(8,128)(2,1)S(1)}) custom-call(f32[4,64,64,128]{3,2,1,0:T(8,128)} %refs_2_.1, bf16[4,64,64,128]{3,2,1,0:T(8,128)(2,1)} %refs_3_.3, s32[64,64,128]{2,1,0:T(8,128)} %refs_4_.3, f32[64,64]{1,0:T(8,128)S(1)} %copy-done.3), custom_call_target="tpu_custom_call" | custom-call | flops 819200 | bytes 819200 | tf_op jit(solution)/shard_map/x_faces/pallas_call | solution.py:491
  3.2 5.1 %collective-permute-start = (bf16[592,128]{1,0:T(8,128)(2,1)S(1)}, bf16[592,128]{1,0:T(8,128)(2,1)S(1)}, u32[]{:S(2)}, u32[]{:S(2)}) collective-permute-start(bf16[592,128]{1,0:T(8,128)(2,1)S(1)} %get-tuple-element.19), channel_id=1, source_target_pairs={{0,8},{8,16},{16,24},{1,9},{9,17},{17,25},{2,10},{10,18},{18,26},{... | collective-permute-start | bytes 454664 | tf_op jit(solution)/shard_map/ppermute | solution.py:506
  8.3 1.3 %collective-permute-start.1 = (bf16[592,128]{1,0:T(8,128)(2,1)S(1)}, bf16[592,128]{1,0:T(8,128)(2,1)S(1)}, u32[]{:S(2)}, u32[]{:S(2)}) collective-permute-start(bf16[592,128]{1,0:T(8,128)(2,1)S(1)} %get-tuple-element.20), channel_id=1, source_target_pairs={{8,0},{16,8},{24,16},{9,1},{17,9},{25,17},{10,2},{18,10},{26,18},{... | collective-permute-start | bytes 454664 | tf_op jit(solution)/shard_map/ppermute | solution.py:506
  9.6 0.0 copy-done.2
  9.6 0.0 copy-done
  9.6 0.0 copy-done.1
  9.6 2.6 %pack_faces.1 = (bf16[576,128]{1,0:T(8,128)(2,1)S(1)}, bf16[576,128]{1,0:T(8,128)(2,1)S(1)}, bf16[4,64,128]{2,1,0:T(8,128)(2,1)S(1)}) custom-call(f32[4,64,64,128]{3,2,1,0:T(8,128)S(1)} %copy-done, bf16[4,64,64,128]{3,2,1,0:T(8,128)(2,1)S(1)} %copy-done.1, s32[64,64,128]{2,1,0:T(8,128)S(1)} %copy-done.2), custom_call_target="tpu_custom_call" | custom-call | flops 8388608 | bytes 8388608 | tf_op jit(solution)/shard_map/pack_faces/pallas_call | solution.py:491
  12.2 0.0 copy-start.4
  12.2 2.1 %inside.2 = (f32[4,32,64,128]{3,2,1,0:T(8,128)S(1)}, f32[8,128]{1,0:T(8,128)S(1)}) custom-call(f32[4,64,64,128]{3,2,1,0:T(8,128)S(1)} %copy-done, bf16[4,64,64,128]{3,2,1,0:T(8,128)(2,1)S(1)} %copy-done.1), custom_call_target="tpu_custom_call" | custom-call | flops 10485760 | bytes 10485760 | tf_op jit(solution)/shard_map/inside/pallas_call | solution.py:491
  14.3 0.0 collective-permute-done.xl_ref.refs_7_
  14.3 2.3 %collective-permute-done.1.xr_ref.refs_8_ = bf16[592,128]{1,0:T(8,128)(2,1)S(1)} collective-permute-done((bf16[592,128]{1,0:T(8,128)(2,1)S(1)}, bf16[592,128]{1,0:T(8,128)(2,1)S(1)}, u32[]{:S(2)}, u32[]{:S(2)}) %collective-permute-start.1) | collective-permute-done | bytes 151584 | tf_op jit(solution)/shard_map/ppermute | solution.py:506
  16.6 0.0 copy-done.4
  16.6 0.1 corners.1
  16.7 1.3 %collective-permute-start.3 = (bf16[720,128]{1,0:T(8,128)(2,1)S(1)}, bf16[720,128]{1,0:T(8,128)(2,1)S(1)}, u32[]{:S(2)}, u32[]{:S(2)}) collective-permute-start(bf16[720,128]{1,0:T(8,128)(2,1)S(1)} %get-tuple-element.25.refs_11_.refs_8_), channel_id=1, source_target_pairs={{2,0},{4,2},{6,4},{3,1},{5,3},{7,5},{10,8},{12,10},{14,12},{11,9},... | collective-permute-start | bytes 552968 | tf_op jit(solution)/shard_map/ppermute | solution.py:506
  18.0 0.0 copy-start.5
  18.0 0.0 copy-start.6
  18.0 4.6 %collective-permute-start.2 = (bf16[720,128]{1,0:T(8,128)(2,1)S(1)}, bf16[720,128]{1,0:T(8,128)(2,1)S(1)}, u32[]{:S(2)}, u32[]{:S(2)}) collective-permute-start(bf16[720,128]{1,0:T(8,128)(2,1)S(1)} %get-tuple-element.24.refs_12_), channel_id=1, source_target_pairs={{0,2},{2,4},{4,6},{1,3},{3,5},{5,7},{8,10},{10,12},{12,14},{9,11},... | collective-permute-start | bytes 552968 | tf_op jit(solution)/shard_map/ppermute | solution.py:506
  22.6 2.1 %inside.3 = (f32[4,32,64,128]{3,2,1,0:T(8,128)S(1)}, f32[8,128]{1,0:T(8,128)S(1)}) custom-call(f32[4,64,64,128]{3,2,1,0:T(8,128)S(1)} %copy-done, bf16[4,64,64,128]{3,2,1,0:T(8,128)(2,1)S(1)} %copy-done.1), custom_call_target="tpu_custom_call" | custom-call | flops 10485760 | bytes 10485760 | tf_op jit(solution)/shard_map/inside/pallas_call | solution.py:491
  24.7 0.0 collective-permute-done.3.yr_ref.refs_10_
  24.7 0.9 %collective-permute-done.2.yl_ref.refs_9_ = bf16[720,128]{1,0:T(8,128)(2,1)S(1)} collective-permute-done((bf16[720,128]{1,0:T(8,128)(2,1)S(1)}, bf16[720,128]{1,0:T(8,128)(2,1)S(1)}, u32[]{:S(2)}, u32[]{:S(2)}) %collective-permute-start.2) | collective-permute-done | bytes 184352 | tf_op jit(solution)/shard_map/ppermute | solution.py:506
  25.6 0.2 edge_faces.1
  25.9 0.1 collective-permute-start.4
  25.9 1.3 %collective-permute-done.4.refs_5_.refs_6_ = bf16[8,64,128]{2,1,0:T(8,128)(2,1)S(1)} collective-permute-done((bf16[8,64,128]{2,1,0:T(8,128)(2,1)S(1)}, bf16[8,64,128]{2,1,0:T(8,128)(2,1)S(1)}, u32[]{:S(2)}, u32[]{:S(2)}) %collective-permute-start.4) | collective-permute-done | bytes 131104 | tf_op jit(solution)/shard_map/ppermute | solution.py:511
  27.3 0.0 copy-done.5
  27.3 0.0 copy-done.6
  27.3 0.0 copy-start.8
  27.3 0.0 copy-start.7
  27.3 6.0 %sweep_first.1 = (f32[4,64,64,128]{3,2,1,0:T(8,128)S(1)}, f32[1024,128]{1,0:T(8,128)S(1)}, bf16[4,64,128]{2,1,0:T(8,128)(2,1)S(1)}) custom-call(f32[4]{0:T(128)S(1)} %copy-done.5, f32[4]{0:T(128)S(1)} %copy-done.6, f32[4,64,64,128]{3,2,1,0:T(8,128)S(1)} %copy-done, f32[64,64]{1,0:T(8,128)S(1)} %copy-done.4, s32[64,64,128]{2,1,0:T(8,128)S(1)} %copy-done.2, ...), custom_call_target="tpu_custom_call" | custom-call | flops 41943040 | bytes 41943040 | tf_op jit(solution)/shard_map/sweep_first/pallas_call | solution.py:491
  33.3 0.2 collective-permute-start.5
  33.5 1.1 %collective-permute-done.5.refs_5_.refs_6_ = bf16[4,64,128]{2,1,0:T(8,128)(2,1)S(1)} collective-permute-done((bf16[4,64,128]{2,1,0:T(8,128)(2,1)S(1)}, bf16[4,64,128]{2,1,0:T(8,128)(2,1)S(1)}, u32[]{:S(2)}, u32[]{:S(2)}) %collective-permute-start.5) | collective-permute-done | bytes 65568 | tf_op jit(solution)/shard_map/ppermute | solution.py:511
  34.7 0.0 copy-done.8
  34.7 0.0 copy-done.7
  34.7 9.6 %sweep_last.1 = (f32[4,64,64,128]{3,2,1,0:T(8,128)}, f32[40,128]{1,0:T(8,128)S(1)}) custom-call(f32[4]{0:T(128)S(1)} %copy-done.5, f32[4]{0:T(128)S(1)} %copy-done.6, f32[4,64,64,128]{3,2,1,0:T(8,128)S(1)} %get-tuple-element.29.refs_2_, bf16[4,64,64,128]{3,2,1,0:T(8,128)(2,1)S(1)} %copy-done.1, s32[64,64,128]{2,1,0:T(8,128)S(1)} %copy-done.2, ...), custom_call_target="tpu_custom_call" | custom-call | flops 41943040 | bytes 41943040 | tf_op jit(solution)/shard_map/sweep_last/pallas_call | solution.py:491
  44.2 1.8 %all-gather = f32[80,128]{1,0:T(8,128)S(1)} all-gather(f32[40,128]{1,0:T(8,128)S(1)} %get-tuple-element.33), channel_id=2, replica_groups=mesh['gx'=4,'gy'=4,'gz'=2] {'gz'}, dimensions={0}, use_global_device_ids=true | all-gather | bytes 61440 | tf_op jit(solution)/shard_map/all_gather | solution.py:716
  46.1 0.8 %broadcast_in_dim.15 = f32[16,40,128]{2,1,0:T(8,128)} broadcast(f32[40,128]{1,0:T(8,128)S(1)} %reduce_sum.9), dimensions={1,2} | broadcast | bytes 348160 | tf_op jit(solution)/shard_map/broadcast_in_dim | solution.py:717
  46.8 6.8 %all-to-all-start = ((f32[16,40,128]{2,1,0:T(8,128)}), f32[16,40,128]{2,1,0:T(8,128)S(1)}, u32[]{:S(2)}, u32[]{:S(2)}) async-start(f32[16,40,128]{2,1,0:T(8,128)} %broadcast_in_dim.15), calls=%async_computation | async-start | bytes 655360 | tf_op jit(solution)/shard_map/all_to_all | solution.py:718
  53.7 12.3 %all-to-all-done.got_ref = f32[16,40,128]{2,1,0:T(8,128)S(1)} async-done(((f32[16,40,128]{2,1,0:T(8,128)}), f32[16,40,128]{2,1,0:T(8,128)S(1)}, u32[]{:S(2)}, u32[]{:S(2)}) %all-to-all-start) | async-done | bytes 327712 | tf_op jit(solution)/shard_map/all_to_all | solution.py:718
  66.0 2.2 %plane.1 = f32[1,16,512]{2,1,0:T(8,128)} custom-call(s32[1]{0:T(128)} %bitcast.1.me_ref, f32[16,40,128]{2,1,0:T(8,128)S(1)} %all-to-all-done.got_ref), custom_call_target="tpu_custom_call" | custom-call | tf_op jit(solution)/shard_map/plane/pallas_call | solution.py:720
  (2 shorter events, 0.0 us)
Async XLA Ops:
  0.6 9.0 %copy-start.2 = (s32[64,64,128]{2,1,0:T(8,128)S(1)}, s32[64,64,128]{2,1,0:T(8,128)}, u32[]{:S(2)}) copy-start(s32[64,64,128]{2,1,0:T(8,128)} %refs_4_.3) | copy-start | bytes 6291460
  0.6 9.0 %copy-start = (f32[4,64,64,128]{3,2,1,0:T(8,128)S(1)}, f32[4,64,64,128]{3,2,1,0:T(8,128)}, u32[]{:S(2)}) copy-start(f32[4,64,64,128]{3,2,1,0:T(8,128)} %refs_2_.1) | copy-start | bytes 25165828
  0.6 9.0 %copy-start.1 = (bf16[4,64,64,128]{3,2,1,0:T(8,128)(2,1)S(1)}, bf16[4,64,64,128]{3,2,1,0:T(8,128)(2,1)}, u32[]{:S(2)}) copy-start(bf16[4,64,64,128]{3,2,1,0:T(8,128)(2,1)} %refs_3_.3) | copy-start | bytes 12582916
  0.7 0.9 %copy-start.3 = (f32[64,64]{1,0:T(8,128)S(1)}, f32[64,64]{1,0:T(8,128)}, u32[]{:S(2)}) copy-start(f32[64,64]{1,0:T(8,128)} %refs_3_.2) | copy-start | bytes 49156
  3.2 11.2 %collective-permute-start = (bf16[592,128]{1,0:T(8,128)(2,1)S(1)}, bf16[592,128]{1,0:T(8,128)(2,1)S(1)}, u32[]{:S(2)}, u32[]{:S(2)}) collective-permute-start(bf16[592,128]{1,0:T(8,128)(2,1)S(1)} %get-tuple-element.19), channel_id=1, source_target_pairs={{0,8},{8,16},{16,24},{1,9},{9,17},{17,25},{2,10},{10,18},{18,26},{... | collective-permute-start | bytes 454664 | tf_op jit(solution)/shard_map/ppermute | solution.py:506
  8.3 8.4 %collective-permute-start.1 = (bf16[592,128]{1,0:T(8,128)(2,1)S(1)}, bf16[592,128]{1,0:T(8,128)(2,1)S(1)}, u32[]{:S(2)}, u32[]{:S(2)}) collective-permute-start(bf16[592,128]{1,0:T(8,128)(2,1)S(1)} %get-tuple-element.20), channel_id=1, source_target_pairs={{8,0},{16,8},{24,16},{9,1},{17,9},{25,17},{10,2},{18,10},{26,18},{... | collective-permute-start | bytes 454664 | tf_op jit(solution)/shard_map/ppermute | solution.py:506
  12.2 4.4 %copy-start.4 = (f32[64,64]{1,0:T(8,128)S(1)}, f32[64,64]{1,0:T(8,128)}, u32[]{:S(2)}) copy-start(f32[64,64]{1,0:T(8,128)} %refs_3_.2) | copy-start | bytes 49156
  16.7 8.0 %collective-permute-start.3 = (bf16[720,128]{1,0:T(8,128)(2,1)S(1)}, bf16[720,128]{1,0:T(8,128)(2,1)S(1)}, u32[]{:S(2)}, u32[]{:S(2)}) collective-permute-start(bf16[720,128]{1,0:T(8,128)(2,1)S(1)} %get-tuple-element.25.refs_11_.refs_8_), channel_id=1, source_target_pairs={{2,0},{4,2},{6,4},{3,1},{5,3},{7,5},{10,8},{12,10},{14,12},{11,9},... | collective-permute-start | bytes 552968 | tf_op jit(solution)/shard_map/ppermute | solution.py:506
  18.0 9.3 %copy-start.5 = (f32[4]{0:T(128)S(1)}, f32[4]{0:T(128)}, u32[]{:S(2)}) copy-start(f32[4]{0:T(128)} %refs_0_.3) | copy-start | bytes 52
  18.0 9.3 %copy-start.6 = (f32[4]{0:T(128)S(1)}, f32[4]{0:T(128)}, u32[]{:S(2)}) copy-start(f32[4]{0:T(128)} %refs_1_.3) | copy-start | bytes 52
  18.0 7.6 %collective-permute-start.2 = (bf16[720,128]{1,0:T(8,128)(2,1)S(1)}, bf16[720,128]{1,0:T(8,128)(2,1)S(1)}, u32[]{:S(2)}, u32[]{:S(2)}) collective-permute-start(bf16[720,128]{1,0:T(8,128)(2,1)S(1)} %get-tuple-element.24.refs_12_), channel_id=1, source_target_pairs={{0,2},{2,4},{4,6},{1,3},{3,5},{5,7},{8,10},{10,12},{12,14},{9,11},... | collective-permute-start | bytes 552968 | tf_op jit(solution)/shard_map/ppermute | solution.py:506
  25.9 1.4 %collective-permute-start.4 = (bf16[8,64,128]{2,1,0:T(8,128)(2,1)S(1)}, bf16[8,64,128]{2,1,0:T(8,128)(2,1)S(1)}, u32[]{:S(2)}, u32[]{:S(2)}) collective-permute-start(bf16[8,64,128]{2,1,0:T(8,128)(2,1)S(1)} %edge_faces.1), channel_id=1, source_target_pairs={{0,1},{1,0},{2,3},{3,2},{4,5},{5,4},{6,7},{7,6},{8,9},{9,8},{10,11... | collective-permute-start | bytes 393224 | tf_op jit(solution)/shard_map/ppermute | solution.py:511
  27.3 7.4 %copy-start.8 = (s32[1,1,64,1]{2,3,1,0:T(1,128)S(1)}, s32[1,1,64,1]{2,3,1,0:T(1,128)}, u32[]{:S(2)}) copy-start(s32[1,1,64,1]{2,3,1,0:T(1,128)} %param.15) | copy-start | bytes 772
  27.3 7.4 %copy-start.7 = (f32[4]{0:T(128)S(1)}, f32[4]{0:T(128)}, u32[]{:S(2)}) copy-start(f32[4]{0:T(128)} %refs_11_.1) | copy-start | bytes 52
  33.3 1.3 %collective-permute-start.5 = (bf16[4,64,128]{2,1,0:T(8,128)(2,1)S(1)}, bf16[4,64,128]{2,1,0:T(8,128)(2,1)S(1)}, u32[]{:S(2)}, u32[]{:S(2)}) collective-permute-start(bf16[4,64,128]{2,1,0:T(8,128)(2,1)S(1)} %get-tuple-element.30), channel_id=1, source_target_pairs={{0,1},{1,0},{2,3},{3,2},{4,5},{5,4},{6,7},{7,6},{8,9},{9,8},{10,11... | collective-permute-start | bytes 196616 | tf_op jit(solution)/shard_map/ppermute | solution.py:511
  46.8 19.1 %all-to-all-start = ((f32[16,40,128]{2,1,0:T(8,128)}), f32[16,40,128]{2,1,0:T(8,128)S(1)}, u32[]{:S(2)}, u32[]{:S(2)}) async-start(f32[16,40,128]{2,1,0:T(8,128)} %broadcast_in_dim.15), calls=%async_computation | async-start | bytes 655360 | tf_op jit(solution)/shard_map/all_to_all | solution.py:718

commit v8 on v7

--- a/solution.py
+++ b/solution.py
@@ -646,19 +646,41 @@
     )
 
 
+STEPS = 32767.0
+
+
+def share_kernel(got_ref, out_ref):
+    half = got_ref.shape[1] - 8
+    both = got_ref[0]
+    for part in range(1, got_ref.shape[0]):
+        both = both + got_ref[part]
+    value = both[:half]
+    top = jnp.max(jnp.abs(value), axis=0, keepdims=True)
+    power = jnp.floor(jnp.log(jnp.maximum(top, 1e-30)) * (1.0 / math.log(2.0))) + 1.0
+    steps = jnp.floor(value * (STEPS * jnp.exp2(-power)) + 0.5)
+    steps = jnp.clip(steps, -STEPS, STEPS)
+    power = jnp.broadcast_to(power, (8, value.shape[1]))
+    block = jnp.concatenate([steps, power, both[half:]], 0).astype(jnp.int32).astype(jnp.int16)
+    for c in range(out_ref.shape[0]):
+        out_ref[c] = block
+
+
 def plane_kernel(ngx, ngy, me_ref, got_ref, out_ref, w_ref):
     cells = 64
     nx, ny = ngx * cells, ngy * cells
     columns = ngx * ngy
     half = cells // 2
+    owners = []
     for cx in range(ngx):
         for cy in range(ngy):
             c = cx * ngy + cy
+            got = got_ref[c].astype(jnp.int32).astype(F32)
+            value = got[:half] * (jnp.exp2(got[half : half + 1]) * (1.0 / STEPS))
             for part in range(2):
-                lanes = pl.ds(part * cells, cells)
-                w_ref[pl.ds(cy * cells + part * half, half), pl.ds(cx * cells, cells)] = got_ref[
-                    c, pl.ds(0, half), lanes
+                w_ref[pl.ds(cy * cells + part * half, half), pl.ds(cx * cells, cells)] = value[
+                    :, part * cells : (part + 1) * cells
                 ]
+            owners.append(got[half + 8 : half + 9, :cells])
 
     def band(n):
         i = lax.broadcasted_iota(jnp.int32, (n, n), 0)
@@ -669,7 +691,7 @@
     weighted = twice(w_ref[...], band(nx))
 
     tiles = cells
-    owner = jnp.concatenate([got_ref[c, pl.ds(half, 1), pl.ds(0, tiles)] for c in range(columns)], 0)
+    owner = jnp.concatenate(owners, 0)
     mine = owner == me_ref[0].astype(F32)
     flag = jnp.where(mine, 1.0, 0.0)
     a = lax.broadcasted_iota(jnp.int32, (tiles, tiles), 0)
@@ -713,8 +735,18 @@
     tables = (shift_real, shift_imag)
     owners = jnp.broadcast_to(owner_map.reshape(1, -1), (8, cells))
     final, partial = sweeps(tables, design_share, fields, sources, material, density, owners)
-    partial = jnp.sum(lax.all_gather(partial, "gz"), 0)
-    copies = jnp.broadcast_to(partial[None], (columns, *partial.shape))
+    partial = lax.all_gather(partial, "gz")
+    copies = local(
+        share_kernel,
+        "share",
+        [partial],
+        [VMEM_SPEC],
+        jax.ShapeDtypeStruct((columns, partial.shape[1] + 8, partial.shape[2]), jnp.int16),
+        VMEM_SPEC,
+        [],
+        8,
+        partial.size * 16,
+    )
     plane = lax.all_to_all(copies, ("gx", "gy"), split_axis=0, concat_axis=0)
     me = (lax.axis_index("gx") * ngy + lax.axis_index("gy")).reshape(1)
     owned = pl.pallas_call(

time: 68.5 us -> 65.7 us (0.959)
  waiting for transfers between devices: 18 us -> 15.2 us
  local copies, waits for them, and re-layouts: 1.7 us -> 0.94 us
  Pallas kernels: 26.5 us -> 27.2 us
    all_to_all x1, waiting for transfers between devices: 12.3 us -> 9.5 us  [on_device(): plane = lax.all_to_all(copies, ('gx', 'gy'), split_axis=0, concat_axis=0)]
    broadcast_in_dim x1 -> x0, local copies, waits for them, and re-layouts: 0.76 us -> none  [on_device(): copies = jnp.broadcast_to(partial[None], (columns, *partial.shape))]
    pallas_call x8 -> x9, Pallas kernels: 24.3 us -> 25 us  [local(): pl.pallas_call(kernel, in_specs=specs, out_specs=out_specs, out_shape=sha...]
where the time goes in v8:
time: 65.7 us; the launch traced here: 65.4 us
  Pallas kernels  27.2 us (41%)
  starting transfers between devices  19.3 us (29%)
  waiting for transfers between devices  15.2 us (23%)
  blocking collectives  1.83 us (3%)
  local copies, waits for them, and re-layouts  0.94 us (1%)
  between operations  0.84 us (1%)
    pallas_call x9, Pallas kernels, local(): pl.pallas_call(kernel, in_specs=specs, out_specs=out_specs, out_shape=sha...  25 us
    ppermute x4, starting transfers between devices, shift(): lax.ppermute(value, axis, pairs if up else [(j, i) for i, j in pairs])  12.2 us
    all_to_all x1, waiting for transfers between devices, on_device(): plane = lax.all_to_all(copies, ('gx', 'gy'), split_axis=0, concat_axis=0)  9.5 us
    all_to_all x1, starting transfers between devices, on_device(): plane = lax.all_to_all(copies, ('gx', 'gy'), split_axis=0, concat_axis=0)  6.82 us
    ppermute x4, waiting for transfers between devices, shift(): lax.ppermute(value, axis, pairs if up else [(j, i) for i, j in pairs])  3.24 us
    ppermute x2, waiting for transfers between devices, shift_z(): other = lax.ppermute(g, 'gz', [(0, 1), (1, 0)])  2.45 us
    pallas_call x1, Pallas kernels, on_device(): pl.pallas_call(functools.partial(plane_kernel, ngx, ngy), in_specs=[SMEM_...  2.27 us
    all_gather x1, blocking collectives, on_device(): partial = lax.all_gather(partial, 'gz')  1.83 us
  transfers between devices with their start and end apart: 7, of which 5 were waited for; matrix products, arithmetic and copies ran while one was open for 0% of the time, Pallas kernels for 10%

profile of v8, /device:TPU:0, one launch (start us, length us, event | category | flops | bytes accessed | tf_op | source)
XLA Modules:
  0.0 65.4 jit_solution(6910606549530855740)
XLA Ops:
  0.6 0.0 copy-start.2
  0.6 0.0 copy-start
  0.6 0.0 copy-start.1
  0.7 0.0 copy-start.3
  0.7 0.9 %copy-done.3 = f32[64,64]{1,0:T(8,128)S(1)} copy-done((f32[64,64]{1,0:T(8,128)S(1)}, f32[64,64]{1,0:T(8,128)}, u32[]{:S(2)}) %copy-start.3) | copy-done | bytes 16408
  1.6 1.6 %x_faces.1 = (bf16[592,128]{1,0:T(8,128)(2,1)S(1)}, bf16[592,128]{1,0:T(8,128)(2,1)S(1)}) custom-call(f32[4,64,64,128]{3,2,1,0:T(8,128)} %refs_2_.1, bf16[4,64,64,128]{3,2,1,0:T(8,128)(2,1)} %refs_3_.3, s32[64,64,128]{2,1,0:T(8,128)} %refs_4_.3, f32[64,64]{1,0:T(8,128)S(1)} %copy-done.3), custom_call_target="tpu_custom_call" | custom-call | flops 819200 | bytes 819200 | tf_op jit(solution)/shard_map/x_faces/pallas_call | solution.py:491
  3.2 5.1 %collective-permute-start = (bf16[592,128]{1,0:T(8,128)(2,1)S(1)}, bf16[592,128]{1,0:T(8,128)(2,1)S(1)}, u32[]{:S(2)}, u32[]{:S(2)}) collective-permute-start(bf16[592,128]{1,0:T(8,128)(2,1)S(1)} %get-tuple-element.19), channel_id=1, source_target_pairs={{0,8},{8,16},{16,24},{1,9},{9,17},{17,25},{2,10},{10,18},{18,26},{... | collective-permute-start | bytes 454664 | tf_op jit(solution)/shard_map/ppermute | solution.py:506
  8.3 1.3 %collective-permute-start.1 = (bf16[592,128]{1,0:T(8,128)(2,1)S(1)}, bf16[592,128]{1,0:T(8,128)(2,1)S(1)}, u32[]{:S(2)}, u32[]{:S(2)}) collective-permute-start(bf16[592,128]{1,0:T(8,128)(2,1)S(1)} %get-tuple-element.20), channel_id=1, source_target_pairs={{8,0},{16,8},{24,16},{9,1},{17,9},{25,17},{10,2},{18,10},{26,18},{... | collective-permute-start | bytes 454664 | tf_op jit(solution)/shard_map/ppermute | solution.py:506
  9.6 0.0 copy-done.2
  9.6 0.0 copy-done
  9.6 0.0 copy-done.1
  9.6 2.6 %pack_faces.1 = (bf16[576,128]{1,0:T(8,128)(2,1)S(1)}, bf16[576,128]{1,0:T(8,128)(2,1)S(1)}, bf16[4,64,128]{2,1,0:T(8,128)(2,1)S(1)}) custom-call(f32[4,64,64,128]{3,2,1,0:T(8,128)S(1)} %copy-done, bf16[4,64,64,128]{3,2,1,0:T(8,128)(2,1)S(1)} %copy-done.1, s32[64,64,128]{2,1,0:T(8,128)S(1)} %copy-done.2), custom_call_target="tpu_custom_call" | custom-call | flops 8388608 | bytes 8388608 | tf_op jit(solution)/shard_map/pack_faces/pallas_call | solution.py:491
  12.2 0.0 copy-start.4
  12.2 2.1 %inside.2 = (f32[4,32,64,128]{3,2,1,0:T(8,128)S(1)}, f32[8,128]{1,0:T(8,128)S(1)}) custom-call(f32[4,64,64,128]{3,2,1,0:T(8,128)S(1)} %copy-done, bf16[4,64,64,128]{3,2,1,0:T(8,128)(2,1)S(1)} %copy-done.1), custom_call_target="tpu_custom_call" | custom-call | flops 10485760 | bytes 10485760 | tf_op jit(solution)/shard_map/inside/pallas_call | solution.py:491
  14.3 0.0 collective-permute-done.xl_ref.refs_7_
  14.3 2.3 %collective-permute-done.1.xr_ref.refs_8_ = bf16[592,128]{1,0:T(8,128)(2,1)S(1)} collective-permute-done((bf16[592,128]{1,0:T(8,128)(2,1)S(1)}, bf16[592,128]{1,0:T(8,128)(2,1)S(1)}, u32[]{:S(2)}, u32[]{:S(2)}) %collective-permute-start.1) | collective-permute-done | bytes 151584 | tf_op jit(solution)/shard_map/ppermute | solution.py:506
  16.6 0.0 copy-done.4
  16.6 0.1 corners.1
  16.7 1.3 %collective-permute-start.3 = (bf16[720,128]{1,0:T(8,128)(2,1)S(1)}, bf16[720,128]{1,0:T(8,128)(2,1)S(1)}, u32[]{:S(2)}, u32[]{:S(2)}) collective-permute-start(bf16[720,128]{1,0:T(8,128)(2,1)S(1)} %get-tuple-element.25.refs_11_.refs_8_), channel_id=1, source_target_pairs={{2,0},{4,2},{6,4},{3,1},{5,3},{7,5},{10,8},{12,10},{14,12},{11,9},... | collective-permute-start | bytes 552968 | tf_op jit(solution)/shard_map/ppermute | solution.py:506
  18.0 0.0 copy-start.5
  18.0 0.0 copy-start.6
  18.0 4.6 %collective-permute-start.2 = (bf16[720,128]{1,0:T(8,128)(2,1)S(1)}, bf16[720,128]{1,0:T(8,128)(2,1)S(1)}, u32[]{:S(2)}, u32[]{:S(2)}) collective-permute-start(bf16[720,128]{1,0:T(8,128)(2,1)S(1)} %get-tuple-element.24.refs_12_), channel_id=1, source_target_pairs={{0,2},{2,4},{4,6},{1,3},{3,5},{5,7},{8,10},{10,12},{12,14},{9,11},... | collective-permute-start | bytes 552968 | tf_op jit(solution)/shard_map/ppermute | solution.py:506
  22.6 2.1 %inside.3 = (f32[4,32,64,128]{3,2,1,0:T(8,128)S(1)}, f32[8,128]{1,0:T(8,128)S(1)}) custom-call(f32[4,64,64,128]{3,2,1,0:T(8,128)S(1)} %copy-done, bf16[4,64,64,128]{3,2,1,0:T(8,128)(2,1)S(1)} %copy-done.1), custom_call_target="tpu_custom_call" | custom-call | flops 10485760 | bytes 10485760 | tf_op jit(solution)/shard_map/inside/pallas_call | solution.py:491
  24.7 0.0 collective-permute-done.3.yr_ref.refs_10_
  24.7 0.9 %collective-permute-done.2.yl_ref.refs_9_ = bf16[720,128]{1,0:T(8,128)(2,1)S(1)} collective-permute-done((bf16[720,128]{1,0:T(8,128)(2,1)S(1)}, bf16[720,128]{1,0:T(8,128)(2,1)S(1)}, u32[]{:S(2)}, u32[]{:S(2)}) %collective-permute-start.2) | collective-permute-done | bytes 184352 | tf_op jit(solution)/shard_map/ppermute | solution.py:506
  25.6 0.2 edge_faces.1
  25.9 0.1 collective-permute-start.4
  25.9 1.3 %collective-permute-done.4.refs_5_.refs_6_ = bf16[8,64,128]{2,1,0:T(8,128)(2,1)S(1)} collective-permute-done((bf16[8,64,128]{2,1,0:T(8,128)(2,1)S(1)}, bf16[8,64,128]{2,1,0:T(8,128)(2,1)S(1)}, u32[]{:S(2)}, u32[]{:S(2)}) %collective-permute-start.4) | collective-permute-done | bytes 131104 | tf_op jit(solution)/shard_map/ppermute | solution.py:511
  27.3 0.0 copy-done.5
  27.3 0.0 copy-done.6
  27.3 0.0 copy-start.8
  27.3 0.0 copy-start.7
  27.3 6.0 %sweep_first.1 = (f32[4,64,64,128]{3,2,1,0:T(8,128)S(1)}, f32[1024,128]{1,0:T(8,128)S(1)}, bf16[4,64,128]{2,1,0:T(8,128)(2,1)S(1)}) custom-call(f32[4]{0:T(128)S(1)} %copy-done.5, f32[4]{0:T(128)S(1)} %copy-done.6, f32[4,64,64,128]{3,2,1,0:T(8,128)S(1)} %copy-done, f32[64,64]{1,0:T(8,128)S(1)} %copy-done.4, s32[64,64,128]{2,1,0:T(8,128)S(1)} %copy-done.2, ...), custom_call_target="tpu_custom_call" | custom-call | flops 41943040 | bytes 41943040 | tf_op jit(solution)/shard_map/sweep_first/pallas_call | solution.py:491
  33.3 0.2 collective-permute-start.5
  33.5 1.1 %collective-permute-done.5.refs_5_.refs_6_ = bf16[4,64,128]{2,1,0:T(8,128)(2,1)S(1)} collective-permute-done((bf16[4,64,128]{2,1,0:T(8,128)(2,1)S(1)}, bf16[4,64,128]{2,1,0:T(8,128)(2,1)S(1)}, u32[]{:S(2)}, u32[]{:S(2)}) %collective-permute-start.5) | collective-permute-done | bytes 65568 | tf_op jit(solution)/shard_map/ppermute | solution.py:511
  34.7 0.0 copy-done.8
  34.7 0.0 copy-done.7
  34.7 9.6 %sweep_last.1 = (f32[4,64,64,128]{3,2,1,0:T(8,128)}, f32[40,128]{1,0:T(8,128)S(1)}) custom-call(f32[4]{0:T(128)S(1)} %copy-done.5, f32[4]{0:T(128)S(1)} %copy-done.6, f32[4,64,64,128]{3,2,1,0:T(8,128)S(1)} %get-tuple-element.29.refs_2_, bf16[4,64,64,128]{3,2,1,0:T(8,128)(2,1)S(1)} %copy-done.1, s32[64,64,128]{2,1,0:T(8,128)S(1)} %copy-done.2, ...), custom_call_target="tpu_custom_call" | custom-call | flops 41943040 | bytes 41943040 | tf_op jit(solution)/shard_map/sweep_last/pallas_call | solution.py:491
  44.2 1.8 %all-gather = f32[80,128]{1,0:T(8,128)S(1)} all-gather(f32[40,128]{1,0:T(8,128)S(1)} %get-tuple-element.33), channel_id=2, replica_groups=mesh['gx'=4,'gy'=4,'gz'=2] {'gz'}, dimensions={0}, use_global_device_ids=true | all-gather | bytes 61440 | tf_op jit(solution)/shard_map/all_gather | solution.py:738
  46.1 0.7 %share.1 = s16[16,48,128]{2,1,0:T(8,128)(2,1)} custom-call(f32[2,40,128]{2,1,0:T(8,128)S(1)} %bitcast.3), custom_call_target="tpu_custom_call" | custom-call | flops 163840 | bytes 163840 | tf_op jit(solution)/shard_map/share/pallas_call | solution.py:491
  46.8 6.8 %all-to-all-start = ((s16[16,48,128]{2,1,0:T(8,128)(2,1)}), s16[16,48,128]{2,1,0:T(8,128)(2,1)S(1)}, u32[]{:S(2)}, u32[]{:S(2)}) async-start(s16[16,48,128]{2,1,0:T(8,128)(2,1)} %share.1), calls=%async_computation | async-start | bytes 393216 | tf_op jit(solution)/shard_map/all_to_all | solution.py:750
  53.6 9.5 %all-to-all-done.got_ref = s16[16,48,128]{2,1,0:T(8,128)(2,1)S(1)} async-done(((s16[16,48,128]{2,1,0:T(8,128)(2,1)}), s16[16,48,128]{2,1,0:T(8,128)(2,1)S(1)}, u32[]{:S(2)}, u32[]{:S(2)}) %all-to-all-start) | async-done | bytes 196640 | tf_op jit(solution)/shard_map/all_to_all | solution.py:750
  63.1 2.3 %plane.1 = f32[1,16,512]{2,1,0:T(8,128)} custom-call(s32[1]{0:T(128)} %bitcast.1.me_ref, s16[16,48,128]{2,1,0:T(8,128)(2,1)S(1)} %all-to-all-done.got_ref), custom_call_target="tpu_custom_call" | custom-call | tf_op jit(solution)/shard_map/plane/pallas_call | solution.py:752
  (1 shorter events, 0.0 us)
Async XLA Ops:
  0.6 9.0 %copy-start.2 = (s32[64,64,128]{2,1,0:T(8,128)S(1)}, s32[64,64,128]{2,1,0:T(8,128)}, u32[]{:S(2)}) copy-start(s32[64,64,128]{2,1,0:T(8,128)} %refs_4_.3) | copy-start | bytes 6291460
  0.6 9.0 %copy-start = (f32[4,64,64,128]{3,2,1,0:T(8,128)S(1)}, f32[4,64,64,128]{3,2,1,0:T(8,128)}, u32[]{:S(2)}) copy-start(f32[4,64,64,128]{3,2,1,0:T(8,128)} %refs_2_.1) | copy-start | bytes 25165828
  0.6 9.0 %copy-start.1 = (bf16[4,64,64,128]{3,2,1,0:T(8,128)(2,1)S(1)}, bf16[4,64,64,128]{3,2,1,0:T(8,128)(2,1)}, u32[]{:S(2)}) copy-start(bf16[4,64,64,128]{3,2,1,0:T(8,128)(2,1)} %refs_3_.3) | copy-start | bytes 12582916
  0.7 0.9 %copy-start.3 = (f32[64,64]{1,0:T(8,128)S(1)}, f32[64,64]{1,0:T(8,128)}, u32[]{:S(2)}) copy-start(f32[64,64]{1,0:T(8,128)} %refs_3_.2) | copy-start | bytes 49156
  3.2 11.2 %collective-permute-start = (bf16[592,128]{1,0:T(8,128)(2,1)S(1)}, bf16[592,128]{1,0:T(8,128)(2,1)S(1)}, u32[]{:S(2)}, u32[]{:S(2)}) collective-permute-start(bf16[592,128]{1,0:T(8,128)(2,1)S(1)} %get-tuple-element.19), channel_id=1, source_target_pairs={{0,8},{8,16},{16,24},{1,9},{9,17},{17,25},{2,10},{10,18},{18,26},{... | collective-permute-start | bytes 454664 | tf_op jit(solution)/shard_map/ppermute | solution.py:506
  8.3 8.4 %collective-permute-start.1 = (bf16[592,128]{1,0:T(8,128)(2,1)S(1)}, bf16[592,128]{1,0:T(8,128)(2,1)S(1)}, u32[]{:S(2)}, u32[]{:S(2)}) collective-permute-start(bf16[592,128]{1,0:T(8,128)(2,1)S(1)} %get-tuple-element.20), channel_id=1, source_target_pairs={{8,0},{16,8},{24,16},{9,1},{17,9},{25,17},{10,2},{18,10},{26,18},{... | collective-permute-start | bytes 454664 | tf_op jit(solution)/shard_map/ppermute | solution.py:506
  12.2 4.4 %copy-start.4 = (f32[64,64]{1,0:T(8,128)S(1)}, f32[64,64]{1,0:T(8,128)}, u32[]{:S(2)}) copy-start(f32[64,64]{1,0:T(8,128)} %refs_3_.2) | copy-start | bytes 49156
  16.7 8.0 %collective-permute-start.3 = (bf16[720,128]{1,0:T(8,128)(2,1)S(1)}, bf16[720,128]{1,0:T(8,128)(2,1)S(1)}, u32[]{:S(2)}, u32[]{:S(2)}) collective-permute-start(bf16[720,128]{1,0:T(8,128)(2,1)S(1)} %get-tuple-element.25.refs_11_.refs_8_), channel_id=1, source_target_pairs={{2,0},{4,2},{6,4},{3,1},{5,3},{7,5},{10,8},{12,10},{14,12},{11,9},... | collective-permute-start | bytes 552968 | tf_op jit(solution)/shard_map/ppermute | solution.py:506
  18.0 9.3 %copy-start.5 = (f32[4]{0:T(128)S(1)}, f32[4]{0:T(128)}, u32[]{:S(2)}) copy-start(f32[4]{0:T(128)} %refs_0_.3) | copy-start | bytes 52
  18.0 9.3 %copy-start.6 = (f32[4]{0:T(128)S(1)}, f32[4]{0:T(128)}, u32[]{:S(2)}) copy-start(f32[4]{0:T(128)} %refs_1_.3) | copy-start | bytes 52
  18.0 7.6 %collective-permute-start.2 = (bf16[720,128]{1,0:T(8,128)(2,1)S(1)}, bf16[720,128]{1,0:T(8,128)(2,1)S(1)}, u32[]{:S(2)}, u32[]{:S(2)}) collective-permute-start(bf16[720,128]{1,0:T(8,128)(2,1)S(1)} %get-tuple-element.24.refs_12_), channel_id=1, source_target_pairs={{0,2},{2,4},{4,6},{1,3},{3,5},{5,7},{8,10},{10,12},{12,14},{9,11},... | collective-permute-start | bytes 552968 | tf_op jit(solution)/shard_map/ppermute | solution.py:506
  25.9 1.4 %collective-permute-start.4 = (bf16[8,64,128]{2,1,0:T(8,128)(2,1)S(1)}, bf16[8,64,128]{2,1,0:T(8,128)(2,1)S(1)}, u32[]{:S(2)}, u32[]{:S(2)}) collective-permute-start(bf16[8,64,128]{2,1,0:T(8,128)(2,1)S(1)} %edge_faces.1), channel_id=1, source_target_pairs={{0,1},{1,0},{2,3},{3,2},{4,5},{5,4},{6,7},{7,6},{8,9},{9,8},{10,11... | collective-permute-start | bytes 393224 | tf_op jit(solution)/shard_map/ppermute | solution.py:511
  27.3 7.4 %copy-start.8 = (s32[1,1,64,1]{2,3,1,0:T(1,128)S(1)}, s32[1,1,64,1]{2,3,1,0:T(1,128)}, u32[]{:S(2)}) copy-start(s32[1,1,64,1]{2,3,1,0:T(1,128)} %param.15) | copy-start | bytes 772
  27.3 7.4 %copy-start.7 = (f32[4]{0:T(128)S(1)}, f32[4]{0:T(128)}, u32[]{:S(2)}) copy-start(f32[4]{0:T(128)} %refs_11_.1) | copy-start | bytes 52
  33.3 1.3 %collective-permute-start.5 = (bf16[4,64,128]{2,1,0:T(8,128)(2,1)S(1)}, bf16[4,64,128]{2,1,0:T(8,128)(2,1)S(1)}, u32[]{:S(2)}, u32[]{:S(2)}) collective-permute-start(bf16[4,64,128]{2,1,0:T(8,128)(2,1)S(1)} %get-tuple-element.30), channel_id=1, source_target_pairs={{0,1},{1,0},{2,3},{3,2},{4,5},{5,4},{6,7},{7,6},{8,9},{9,8},{10,11... | collective-permute-start | bytes 196616 | tf_op jit(solution)/shard_map/ppermute | solution.py:511
  46.8 16.3 %all-to-all-start = ((s16[16,48,128]{2,1,0:T(8,128)(2,1)}), s16[16,48,128]{2,1,0:T(8,128)(2,1)S(1)}, u32[]{:S(2)}, u32[]{:S(2)}) async-start(s16[16,48,128]{2,1,0:T(8,128)(2,1)} %share.1), calls=%async_computation | async-start | bytes 393216 | tf_op jit(solution)/shard_map/all_to_all | solution.py:750

commit v9 on v8

--- a/solution.py
+++ b/solution.py
@@ -73,7 +73,7 @@
 PLANES = 9
 
 
-def x_kernel(v_ref, s_ref, m_ref, d_ref, xlo_ref, xhi_ref, vs, ss, ms, sems):
+def x_kernel(v_ref, s_ref, m_ref, d_ref, xlo_ref, xhi_ref, vs, ss, ms, ds, sems):
     last = v_ref.shape[1] - 1
     rows, depth = v_ref.shape[2:]
     sides = ((0, 0, 1), (last, last - 1, 0))
@@ -91,10 +91,13 @@
     for side in copies:
         for copy in side:
             copy.start()
+    plane = pltpu.make_async_copy(d_ref, ds, sems.at[6])
+    plane.start()
+    plane.wait()
     cells = d_ref.shape[0]
     none = jnp.zeros((R, depth), F32)
     for i, (out_ref, start) in enumerate(((xlo_ref, 0), (xhi_ref, cells - R))):
-        strip = jnp.concatenate([paired(d_ref[start : start + R, :]), none], 0)
+        strip = jnp.concatenate([paired(ds[start : start + R, :]), none], 0)
         out_ref[PLANES * rows :] = strip.astype(BF16)
         for copy in copies[i]:
             copy.wait()
@@ -526,15 +529,16 @@
     xlo, xhi = local(
         x_kernel,
         "x_faces",
-        [far_away(a) for a in (fields, sources, material)] + [density],
-        [hbm] * 3 + [VMEM_SPEC],
+        [far_away(a) for a in (fields, sources, material, density)],
+        [hbm] * 4,
         [x_shape] * 2,
         [VMEM_SPEC] * 2,
         [
             pltpu.VMEM((2, 4, 2, ny, nz), F32),
             pltpu.VMEM((2, 4, ny, nz), BF16),
             pltpu.VMEM((2, ny, nz), jnp.int32),
-            pltpu.SemaphoreType.DMA((6,)),
+            pltpu.VMEM(density.shape, F32),
+            pltpu.SemaphoreType.DMA((7,)),
         ],
         8,
         ny * nz * 100,
@@ -649,11 +653,12 @@
 STEPS = 32767.0
 
 
-def share_kernel(got_ref, out_ref):
-    half = got_ref.shape[1] - 8
-    both = got_ref[0]
-    for part in range(1, got_ref.shape[0]):
-        both = both + got_ref[part]
+def share_kernel(*refs):
+    *parts, out_ref = refs
+    half = parts[0].shape[0] - 8
+    both = parts[0][...]
+    for part in parts[1:]:
+        both = both + part[...]
     value = both[:half]
     top = jnp.max(jnp.abs(value), axis=0, keepdims=True)
     power = jnp.floor(jnp.log(jnp.maximum(top, 1e-30)) * (1.0 / math.log(2.0))) + 1.0
@@ -735,13 +740,17 @@
     tables = (shift_real, shift_imag)
     owners = jnp.broadcast_to(owner_map.reshape(1, -1), (8, cells))
     final, partial = sweeps(tables, design_share, fields, sources, material, density, owners)
-    partial = lax.all_gather(partial, "gz")
+    if lax.axis_size("gz") == 2:
+        parts = [partial, shift_z(partial)[0]]
+    else:
+        gathered = lax.all_gather(partial, "gz")
+        parts = [gathered[i] for i in range(gathered.shape[0])]
     copies = local(
         share_kernel,
         "share",
-        [partial],
-        [VMEM_SPEC],
-        jax.ShapeDtypeStruct((columns, partial.shape[1] + 8, partial.shape[2]), jnp.int16),
+        parts,
+        [VMEM_SPEC] * len(parts),
+        jax.ShapeDtypeStruct((columns, partial.shape[0] + 8, partial.shape[1]), jnp.int16),
         VMEM_SPEC,
         [],
         8,

time: 65.7 us -> 64.2 us (0.977)
  blocking collectives: 1.83 us -> 0 us
  waiting for transfers between devices: 15.2 us -> 16.3 us
  local copies, waits for them, and re-layouts: 0.94 us -> 0.04 us
    all_gather x1 -> x0, blocking collectives: 1.83 us -> none  [on_device(): partial = lax.all_gather(partial, 'gz')]
    ppermute x2 -> x3, waiting for transfers between devices: 2.45 us -> 3.47 us  [shift_z(): other = lax.ppermute(g, 'gz', [(0, 1), (1, 0)])]
    unnamed x18 -> x16, local copies, waits for them, and re-layouts: 0.94 us -> 0.04 us
  transfers between devices with their start and end apart: 7 -> 8, of which waited for: 5 -> 6; matrix products, arithmetic and copies ran while one was open for 0% -> 0% of each run, Pallas kernels for 10% -> 11%
where the time goes in v9:
time: 64.2 us; the launch traced here: 63.8 us
  Pallas kernels  27.1 us (42%)
  starting transfers between devices  19.6 us (31%)
  waiting for transfers between devices  16.3 us (25%)
  between operations  0.84 us (1%)
    pallas_call x9, Pallas kernels, local(): pl.pallas_call(kernel, in_specs=specs, out_specs=out_specs, out_shape=sha...  24.8 us
    ppermute x4, starting transfers between devices, shift(): lax.ppermute(value, axis, pairs if up else [(j, i) for i, j in pairs])  12.2 us
    all_to_all x1, waiting for transfers between devices, on_device(): plane = lax.all_to_all(copies, ('gx', 'gy'), split_axis=0, concat_axis=0)  9.49 us
    all_to_all x1, starting transfers between devices, on_device(): plane = lax.all_to_all(copies, ('gx', 'gy'), split_axis=0, concat_axis=0)  6.82 us
    ppermute x3, waiting for transfers between devices, shift_z(): other = lax.ppermute(g, 'gz', [(0, 1), (1, 0)])  3.47 us
    ppermute x4, waiting for transfers between devices, shift(): lax.ppermute(value, axis, pairs if up else [(j, i) for i, j in pairs])  3.38 us
    pallas_call x1, Pallas kernels, on_device(): pl.pallas_call(functools.partial(plane_kernel, ngx, ngy), in_specs=[SMEM_...  2.27 us
  transfers between devices with their start and end apart: 8, of which 6 were waited for; matrix products, arithmetic and copies ran while one was open for 0% of the time, Pallas kernels for 11%

profile of v9, /device:TPU:0, one launch (start us, length us, event | category | flops | bytes accessed | tf_op | source)
XLA Modules:
  0.0 63.8 jit_solution(14691787888646184408)
XLA Ops:
  0.6 0.0 copy-start.2
  0.6 0.0 copy-start
  0.6 0.0 copy-start.1
  0.7 1.4 %x_faces.1 = (bf16[592,128]{1,0:T(8,128)(2,1)S(1)}, bf16[592,128]{1,0:T(8,128)(2,1)S(1)}) custom-call(f32[4,64,64,128]{3,2,1,0:T(8,128)} %refs_2_.1, bf16[4,64,64,128]{3,2,1,0:T(8,128)(2,1)} %refs_3_.3, s32[64,64,128]{2,1,0:T(8,128)} %refs_4_.3, f32[64,64]{1,0:T(8,128)} %refs_3_.2), custom_call_target="tpu_custom_call" | custom-call | flops 819200 | bytes 819200 | tf_op jit(solution)/shard_map/x_faces/pallas_call | solution.py:494
  2.1 5.1 %collective-permute-start = (bf16[592,128]{1,0:T(8,128)(2,1)S(1)}, bf16[592,128]{1,0:T(8,128)(2,1)S(1)}, u32[]{:S(2)}, u32[]{:S(2)}) collective-permute-start(bf16[592,128]{1,0:T(8,128)(2,1)S(1)} %get-tuple-element.19), channel_id=1, source_target_pairs={{0,8},{8,16},{16,24},{1,9},{9,17},{17,25},{2,10},{10,18},{18,26},{... | collective-permute-start | bytes 454664 | tf_op jit(solution)/shard_map/ppermute | solution.py:509
  7.2 1.3 %collective-permute-start.1 = (bf16[592,128]{1,0:T(8,128)(2,1)S(1)}, bf16[592,128]{1,0:T(8,128)(2,1)S(1)}, u32[]{:S(2)}, u32[]{:S(2)}) collective-permute-start(bf16[592,128]{1,0:T(8,128)(2,1)S(1)} %get-tuple-element.20), channel_id=1, source_target_pairs={{8,0},{16,8},{24,16},{9,1},{17,9},{25,17},{10,2},{18,10},{26,18},{... | collective-permute-start | bytes 454664 | tf_op jit(solution)/shard_map/ppermute | solution.py:509
  8.5 0.0 copy-done.2
  8.5 0.0 copy-done
  8.5 0.0 copy-done.1
  8.5 2.6 %pack_faces.1 = (bf16[576,128]{1,0:T(8,128)(2,1)S(1)}, bf16[576,128]{1,0:T(8,128)(2,1)S(1)}, bf16[4,64,128]{2,1,0:T(8,128)(2,1)S(1)}) custom-call(f32[4,64,64,128]{3,2,1,0:T(8,128)S(1)} %copy-done, bf16[4,64,64,128]{3,2,1,0:T(8,128)(2,1)S(1)} %copy-done.1, s32[64,64,128]{2,1,0:T(8,128)S(1)} %copy-done.2), custom_call_target="tpu_custom_call" | custom-call | flops 8388608 | bytes 8388608 | tf_op jit(solution)/shard_map/pack_faces/pallas_call | solution.py:494
  11.1 0.0 copy-start.3
  11.1 2.1 %inside.2 = (f32[4,32,64,128]{3,2,1,0:T(8,128)S(1)}, f32[8,128]{1,0:T(8,128)S(1)}) custom-call(f32[4,64,64,128]{3,2,1,0:T(8,128)S(1)} %copy-done, bf16[4,64,64,128]{3,2,1,0:T(8,128)(2,1)S(1)} %copy-done.1), custom_call_target="tpu_custom_call" | custom-call | flops 10485760 | bytes 10485760 | tf_op jit(solution)/shard_map/inside/pallas_call | solution.py:494
  13.2 0.0 collective-permute-done.xl_ref.refs_7_
  13.2 2.5 %collective-permute-done.1.xr_ref.refs_8_ = bf16[592,128]{1,0:T(8,128)(2,1)S(1)} collective-permute-done((bf16[592,128]{1,0:T(8,128)(2,1)S(1)}, bf16[592,128]{1,0:T(8,128)(2,1)S(1)}, u32[]{:S(2)}, u32[]{:S(2)}) %collective-permute-start.1) | collective-permute-done | bytes 151584 | tf_op jit(solution)/shard_map/ppermute | solution.py:509
  15.7 0.0 copy-done.3
  15.7 0.1 corners.1
  15.8 1.3 %collective-permute-start.3 = (bf16[720,128]{1,0:T(8,128)(2,1)S(1)}, bf16[720,128]{1,0:T(8,128)(2,1)S(1)}, u32[]{:S(2)}, u32[]{:S(2)}) collective-permute-start(bf16[720,128]{1,0:T(8,128)(2,1)S(1)} %get-tuple-element.25.refs_11_.refs_8_), channel_id=1, source_target_pairs={{2,0},{4,2},{6,4},{3,1},{5,3},{7,5},{10,8},{12,10},{14,12},{11,9},... | collective-permute-start | bytes 552968 | tf_op jit(solution)/shard_map/ppermute | solution.py:509
  17.1 0.0 copy-start.4
  17.1 0.0 copy-start.5
  17.1 4.6 %collective-permute-start.2 = (bf16[720,128]{1,0:T(8,128)(2,1)S(1)}, bf16[720,128]{1,0:T(8,128)(2,1)S(1)}, u32[]{:S(2)}, u32[]{:S(2)}) collective-permute-start(bf16[720,128]{1,0:T(8,128)(2,1)S(1)} %get-tuple-element.24.refs_12_), channel_id=1, source_target_pairs={{0,2},{2,4},{4,6},{1,3},{3,5},{5,7},{8,10},{10,12},{12,14},{9,11},... | collective-permute-start | bytes 552968 | tf_op jit(solution)/shard_map/ppermute | solution.py:509
  21.7 2.1 %inside.3 = (f32[4,32,64,128]{3,2,1,0:T(8,128)S(1)}, f32[8,128]{1,0:T(8,128)S(1)}) custom-call(f32[4,64,64,128]{3,2,1,0:T(8,128)S(1)} %copy-done, bf16[4,64,64,128]{3,2,1,0:T(8,128)(2,1)S(1)} %copy-done.1), custom_call_target="tpu_custom_call" | custom-call | flops 10485760 | bytes 10485760 | tf_op jit(solution)/shard_map/inside/pallas_call | solution.py:494
  23.7 0.0 collective-permute-done.3.yr_ref.refs_10_
  23.8 0.9 %collective-permute-done.2.yl_ref.refs_9_ = bf16[720,128]{1,0:T(8,128)(2,1)S(1)} collective-permute-done((bf16[720,128]{1,0:T(8,128)(2,1)S(1)}, bf16[720,128]{1,0:T(8,128)(2,1)S(1)}, u32[]{:S(2)}, u32[]{:S(2)}) %collective-permute-start.2) | collective-permute-done | bytes 184352 | tf_op jit(solution)/shard_map/ppermute | solution.py:509
  24.7 0.2 edge_faces.1
  24.9 0.1 collective-permute-start.4
  25.0 1.3 %collective-permute-done.4.refs_5_.refs_6_ = bf16[8,64,128]{2,1,0:T(8,128)(2,1)S(1)} collective-permute-done((bf16[8,64,128]{2,1,0:T(8,128)(2,1)S(1)}, bf16[8,64,128]{2,1,0:T(8,128)(2,1)S(1)}, u32[]{:S(2)}, u32[]{:S(2)}) %collective-permute-start.4) | collective-permute-done | bytes 131104 | tf_op jit(solution)/shard_map/ppermute | solution.py:514
  26.3 0.0 copy-done.4
  26.3 0.0 copy-done.5
  26.3 0.0 copy-start.7
  26.3 0.0 copy-start.6
  26.3 6.0 %sweep_first.1 = (f32[4,64,64,128]{3,2,1,0:T(8,128)S(1)}, f32[1024,128]{1,0:T(8,128)S(1)}, bf16[4,64,128]{2,1,0:T(8,128)(2,1)S(1)}) custom-call(f32[4]{0:T(128)S(1)} %copy-done.4, f32[4]{0:T(128)S(1)} %copy-done.5, f32[4,64,64,128]{3,2,1,0:T(8,128)S(1)} %copy-done, f32[64,64]{1,0:T(8,128)S(1)} %copy-done.3, s32[64,64,128]{2,1,0:T(8,128)S(1)} %copy-done.2, ...), custom_call_target="tpu_custom_call" | custom-call | flops 41943040 | bytes 41943040 | tf_op jit(solution)/shard_map/sweep_first/pallas_call | solution.py:494
  32.4 0.2 collective-permute-start.5
  32.6 1.1 %collective-permute-done.5.refs_5_.refs_6_ = bf16[4,64,128]{2,1,0:T(8,128)(2,1)S(1)} collective-permute-done((bf16[4,64,128]{2,1,0:T(8,128)(2,1)S(1)}, bf16[4,64,128]{2,1,0:T(8,128)(2,1)S(1)}, u32[]{:S(2)}, u32[]{:S(2)}) %collective-permute-start.5) | collective-permute-done | bytes 65568 | tf_op jit(solution)/shard_map/ppermute | solution.py:514
  33.7 0.0 copy-done.7
  33.7 0.0 copy-done.6
  33.7 9.6 %sweep_last.1 = (f32[4,64,64,128]{3,2,1,0:T(8,128)}, f32[40,128]{1,0:T(8,128)S(1)}) custom-call(f32[4]{0:T(128)S(1)} %copy-done.4, f32[4]{0:T(128)S(1)} %copy-done.5, f32[4,64,64,128]{3,2,1,0:T(8,128)S(1)} %get-tuple-element.29.refs_2_, bf16[4,64,64,128]{3,2,1,0:T(8,128)(2,1)S(1)} %copy-done.1, s32[64,64,128]{2,1,0:T(8,128)S(1)} %copy-done.2, ...), custom_call_target="tpu_custom_call" | custom-call | flops 41943040 | bytes 41943040 | tf_op jit(solution)/shard_map/sweep_last/pallas_call | solution.py:494
  43.3 0.2 collective-permute-start.6
  43.5 1.0 %collective-permute-done.6.refs_1_ = f32[40,128]{1,0:T(8,128)S(1)} collective-permute-done((f32[40,128]{1,0:T(8,128)S(1)}, f32[40,128]{1,0:T(8,128)S(1)}, u32[]{:S(2)}, u32[]{:S(2)}) %collective-permute-start.6) | collective-permute-done | bytes 20512 | tf_op jit(solution)/shard_map/ppermute | solution.py:514
  44.5 0.7 %share.1 = s16[16,48,128]{2,1,0:T(8,128)(2,1)} custom-call(f32[40,128]{1,0:T(8,128)S(1)} %get-tuple-element.33.refs_0_, f32[40,128]{1,0:T(8,128)S(1)} %collective-permute-done.6.refs_1_), custom_call_target="tpu_custom_call" | custom-call | flops 81920 | bytes 81920 | tf_op jit(solution)/shard_map/share/pallas_call | solution.py:494
  45.3 6.8 %all-to-all-start = ((s16[16,48,128]{2,1,0:T(8,128)(2,1)}), s16[16,48,128]{2,1,0:T(8,128)(2,1)S(1)}, u32[]{:S(2)}, u32[]{:S(2)}) async-start(s16[16,48,128]{2,1,0:T(8,128)(2,1)} %share.1), calls=%async_computation | async-start | bytes 393216 | tf_op jit(solution)/shard_map/all_to_all | solution.py:759
  52.1 9.5 %all-to-all-done.got_ref = s16[16,48,128]{2,1,0:T(8,128)(2,1)S(1)} async-done(((s16[16,48,128]{2,1,0:T(8,128)(2,1)}), s16[16,48,128]{2,1,0:T(8,128)(2,1)S(1)}, u32[]{:S(2)}, u32[]{:S(2)}) %all-to-all-start) | async-done | bytes 196640 | tf_op jit(solution)/shard_map/all_to_all | solution.py:759
  61.6 2.3 %plane.1 = f32[1,16,512]{2,1,0:T(8,128)} custom-call(s32[1]{0:T(128)} %bitcast.1.me_ref, s16[16,48,128]{2,1,0:T(8,128)(2,1)S(1)} %all-to-all-done.got_ref), custom_call_target="tpu_custom_call" | custom-call | tf_op jit(solution)/shard_map/plane/pallas_call | solution.py:761
  (1 shorter events, 0.0 us)
Async XLA Ops:
  0.6 7.9 %copy-start.2 = (s32[64,64,128]{2,1,0:T(8,128)S(1)}, s32[64,64,128]{2,1,0:T(8,128)}, u32[]{:S(2)}) copy-start(s32[64,64,128]{2,1,0:T(8,128)} %refs_4_.3) | copy-start | bytes 6291460
  0.6 7.9 %copy-start = (f32[4,64,64,128]{3,2,1,0:T(8,128)S(1)}, f32[4,64,64,128]{3,2,1,0:T(8,128)}, u32[]{:S(2)}) copy-start(f32[4,64,64,128]{3,2,1,0:T(8,128)} %refs_2_.1) | copy-start | bytes 25165828
  0.6 7.9 %copy-start.1 = (bf16[4,64,64,128]{3,2,1,0:T(8,128)(2,1)S(1)}, bf16[4,64,64,128]{3,2,1,0:T(8,128)(2,1)}, u32[]{:S(2)}) copy-start(bf16[4,64,64,128]{3,2,1,0:T(8,128)(2,1)} %refs_3_.3) | copy-start | bytes 12582916
  2.1 11.2 %collective-permute-start = (bf16[592,128]{1,0:T(8,128)(2,1)S(1)}, bf16[592,128]{1,0:T(8,128)(2,1)S(1)}, u32[]{:S(2)}, u32[]{:S(2)}) collective-permute-start(bf16[592,128]{1,0:T(8,128)(2,1)S(1)} %get-tuple-element.19), channel_id=1, source_target_pairs={{0,8},{8,16},{16,24},{1,9},{9,17},{17,25},{2,10},{10,18},{18,26},{... | collective-permute-start | bytes 454664 | tf_op jit(solution)/shard_map/ppermute | solution.py:509
  7.2 8.5 %collective-permute-start.1 = (bf16[592,128]{1,0:T(8,128)(2,1)S(1)}, bf16[592,128]{1,0:T(8,128)(2,1)S(1)}, u32[]{:S(2)}, u32[]{:S(2)}) collective-permute-start(bf16[592,128]{1,0:T(8,128)(2,1)S(1)} %get-tuple-element.20), channel_id=1, source_target_pairs={{8,0},{16,8},{24,16},{9,1},{17,9},{25,17},{10,2},{18,10},{26,18},{... | collective-permute-start | bytes 454664 | tf_op jit(solution)/shard_map/ppermute | solution.py:509
  11.1 4.6 %copy-start.3 = (f32[64,64]{1,0:T(8,128)S(1)}, f32[64,64]{1,0:T(8,128)}, u32[]{:S(2)}) copy-start(f32[64,64]{1,0:T(8,128)} %refs_3_.2) | copy-start | bytes 49156
  15.8 8.0 %collective-permute-start.3 = (bf16[720,128]{1,0:T(8,128)(2,1)S(1)}, bf16[720,128]{1,0:T(8,128)(2,1)S(1)}, u32[]{:S(2)}, u32[]{:S(2)}) collective-permute-start(bf16[720,128]{1,0:T(8,128)(2,1)S(1)} %get-tuple-element.25.refs_11_.refs_8_), channel_id=1, source_target_pairs={{2,0},{4,2},{6,4},{3,1},{5,3},{7,5},{10,8},{12,10},{14,12},{11,9},... | collective-permute-start | bytes 552968 | tf_op jit(solution)/shard_map/ppermute | solution.py:509
  17.1 9.3 %copy-start.4 = (f32[4]{0:T(128)S(1)}, f32[4]{0:T(128)}, u32[]{:S(2)}) copy-start(f32[4]{0:T(128)} %refs_0_.3) | copy-start | bytes 52
  17.1 9.3 %copy-start.5 = (f32[4]{0:T(128)S(1)}, f32[4]{0:T(128)}, u32[]{:S(2)}) copy-start(f32[4]{0:T(128)} %refs_1_.3) | copy-start | bytes 52
  17.1 7.6 %collective-permute-start.2 = (bf16[720,128]{1,0:T(8,128)(2,1)S(1)}, bf16[720,128]{1,0:T(8,128)(2,1)S(1)}, u32[]{:S(2)}, u32[]{:S(2)}) collective-permute-start(bf16[720,128]{1,0:T(8,128)(2,1)S(1)} %get-tuple-element.24.refs_12_), channel_id=1, source_target_pairs={{0,2},{2,4},{4,6},{1,3},{3,5},{5,7},{8,10},{10,12},{12,14},{9,11},... | collective-permute-start | bytes 552968 | tf_op jit(solution)/shard_map/ppermute | solution.py:509
  24.9 1.4 %collective-permute-start.4 = (bf16[8,64,128]{2,1,0:T(8,128)(2,1)S(1)}, bf16[8,64,128]{2,1,0:T(8,128)(2,1)S(1)}, u32[]{:S(2)}, u32[]{:S(2)}) collective-permute-start(bf16[8,64,128]{2,1,0:T(8,128)(2,1)S(1)} %edge_faces.1), channel_id=1, source_target_pairs={{0,1},{1,0},{2,3},{3,2},{4,5},{5,4},{6,7},{7,6},{8,9},{9,8},{10,11... | collective-permute-start | bytes 393224 | tf_op jit(solution)/shard_map/ppermute | solution.py:514
  26.3 7.4 %copy-start.7 = (s32[1,1,64,1]{2,3,1,0:T(1,128)S(1)}, s32[1,1,64,1]{2,3,1,0:T(1,128)}, u32[]{:S(2)}) copy-start(s32[1,1,64,1]{2,3,1,0:T(1,128)} %param.15) | copy-start | bytes 772
  26.3 7.4 %copy-start.6 = (f32[4]{0:T(128)S(1)}, f32[4]{0:T(128)}, u32[]{:S(2)}) copy-start(f32[4]{0:T(128)} %refs_11_.1) | copy-start | bytes 52
  32.4 1.3 %collective-permute-start.5 = (bf16[4,64,128]{2,1,0:T(8,128)(2,1)S(1)}, bf16[4,64,128]{2,1,0:T(8,128)(2,1)S(1)}, u32[]{:S(2)}, u32[]{:S(2)}) collective-permute-start(bf16[4,64,128]{2,1,0:T(8,128)(2,1)S(1)} %get-tuple-element.30), channel_id=1, source_target_pairs={{0,1},{1,0},{2,3},{3,2},{4,5},{5,4},{6,7},{7,6},{8,9},{9,8},{10,11... | collective-permute-start | bytes 196616 | tf_op jit(solution)/shard_map/ppermute | solution.py:514
  43.3 1.3 %collective-permute-start.6 = (f32[40,128]{1,0:T(8,128)S(1)}, f32[40,128]{1,0:T(8,128)S(1)}, u32[]{:S(2)}, u32[]{:S(2)}) collective-permute-start(f32[40,128]{1,0:T(8,128)S(1)} %get-tuple-element.33.refs_0_), channel_id=1, source_target_pairs={{0,1},{1,0},{2,3},{3,2},{4,5},{5,4},{6,7},{7,6},{8,9},{9,8},{10,11... | collective-permute-start | bytes 61448 | tf_op jit(solution)/shard_map/ppermute | solution.py:514
  45.3 16.3 %all-to-all-start = ((s16[16,48,128]{2,1,0:T(8,128)(2,1)}), s16[16,48,128]{2,1,0:T(8,128)(2,1)S(1)}, u32[]{:S(2)}, u32[]{:S(2)}) async-start(s16[16,48,128]{2,1,0:T(8,128)(2,1)} %share.1), calls=%async_computation | async-start | bytes 393216 | tf_op jit(solution)/shard_map/all_to_all | solution.py:759

commit v10 on v9

--- a/solution.py
+++ b/solution.py
@@ -664,8 +664,9 @@
     power = jnp.floor(jnp.log(jnp.maximum(top, 1e-30)) * (1.0 / math.log(2.0))) + 1.0
     steps = jnp.floor(value * (STEPS * jnp.exp2(-power)) + 0.5)
     steps = jnp.clip(steps, -STEPS, STEPS)
-    power = jnp.broadcast_to(power, (8, value.shape[1]))
-    block = jnp.concatenate([steps, power, both[half:]], 0).astype(jnp.int32).astype(jnp.int16)
+    row = lax.broadcasted_iota(jnp.int32, (8, value.shape[1]), 0)
+    known = jnp.where(row < 4, power, both[half:])
+    block = jnp.concatenate([steps, known], 0).astype(jnp.int32).astype(jnp.int16)
     for c in range(out_ref.shape[0]):
         out_ref[c] = block
 
@@ -685,7 +686,7 @@
                 w_ref[pl.ds(cy * cells + part * half, half), pl.ds(cx * cells, cells)] = value[
                     :, part * cells : (part + 1) * cells
                 ]
-            owners.append(got[half + 8 : half + 9, :cells])
+            owners.append(got[half + 7 : half + 8, :cells])
 
     def band(n):
         i = lax.broadcasted_iota(jnp.int32, (n, n), 0)
@@ -750,7 +751,7 @@
         "share",
         parts,
         [VMEM_SPEC] * len(parts),
-        jax.ShapeDtypeStruct((columns, partial.shape[0] + 8, partial.shape[1]), jnp.int16),
+        jax.ShapeDtypeStruct((columns, *partial.shape), jnp.int16),
         VMEM_SPEC,
         [],
         8,

time: 64.2 us -> 63.4 us (0.988)
  waiting for transfers between devices: 16.3 us -> 15.6 us
    all_to_all x1, waiting for transfers between devices: 9.49 us -> 8.7 us  [on_device(): plane = lax.all_to_all(copies, ('gx', 'gy'), split_axis=0, concat_axis=0)]
where the time goes in v10:
time: 63.4 us; the launch traced here: 63 us
  Pallas kernels  27 us (43%)
  starting transfers between devices  19.6 us (31%)
  waiting for transfers between devices  15.6 us (25%)
  between operations  0.84 us (1%)
    pallas_call x9, Pallas kernels, local(): pl.pallas_call(kernel, in_specs=specs, out_specs=out_specs, out_shape=sha...  24.8 us
    ppermute x4, starting transfers between devices, shift(): lax.ppermute(value, axis, pairs if up else [(j, i) for i, j in pairs])  12.2 us
    all_to_all x1, waiting for transfers between devices, on_device(): plane = lax.all_to_all(copies, ('gx', 'gy'), split_axis=0, concat_axis=0)  8.7 us
    all_to_all x1, starting transfers between devices, on_device(): plane = lax.all_to_all(copies, ('gx', 'gy'), split_axis=0, concat_axis=0)  6.82 us
    ppermute x3, waiting for transfers between devices, shift_z(): other = lax.ppermute(g, 'gz', [(0, 1), (1, 0)])  3.47 us
    ppermute x4, waiting for transfers between devices, shift(): lax.ppermute(value, axis, pairs if up else [(j, i) for i, j in pairs])  3.38 us
    pallas_call x1, Pallas kernels, on_device(): pl.pallas_call(functools.partial(plane_kernel, ngx, ngy), in_specs=[SMEM_...  2.26 us
  transfers between devices with their start and end apart: 8, of which 6 were waited for; matrix products, arithmetic and copies ran while one was open for 0% of the time, Pallas kernels for 11%

profile of v10, /device:TPU:0, one launch (start us, length us, event | category | flops | bytes accessed | tf_op | source)
XLA Modules:
  0.0 63.0 jit_solution(13295606482948363589)
XLA Ops:
  0.6 0.0 copy-start.2
  0.6 0.0 copy-start
  0.6 0.0 copy-start.1
  0.7 1.4 %x_faces.1 = (bf16[592,128]{1,0:T(8,128)(2,1)S(1)}, bf16[592,128]{1,0:T(8,128)(2,1)S(1)}) custom-call(f32[4,64,64,128]{3,2,1,0:T(8,128)} %refs_2_.1, bf16[4,64,64,128]{3,2,1,0:T(8,128)(2,1)} %refs_3_.3, s32[64,64,128]{2,1,0:T(8,128)} %refs_4_.3, f32[64,64]{1,0:T(8,128)} %refs_3_.2), custom_call_target="tpu_custom_call" | custom-call | flops 819200 | bytes 819200 | tf_op jit(solution)/shard_map/x_faces/pallas_call | solution.py:494
  2.1 5.1 %collective-permute-start = (bf16[592,128]{1,0:T(8,128)(2,1)S(1)}, bf16[592,128]{1,0:T(8,128)(2,1)S(1)}, u32[]{:S(2)}, u32[]{:S(2)}) collective-permute-start(bf16[592,128]{1,0:T(8,128)(2,1)S(1)} %get-tuple-element.19), channel_id=1, source_target_pairs={{0,8},{8,16},{16,24},{1,9},{9,17},{17,25},{2,10},{10,18},{18,26},{... | collective-permute-start | bytes 454664 | tf_op jit(solution)/shard_map/ppermute | solution.py:509
  7.2 1.3 %collective-permute-start.1 = (bf16[592,128]{1,0:T(8,128)(2,1)S(1)}, bf16[592,128]{1,0:T(8,128)(2,1)S(1)}, u32[]{:S(2)}, u32[]{:S(2)}) collective-permute-start(bf16[592,128]{1,0:T(8,128)(2,1)S(1)} %get-tuple-element.20), channel_id=1, source_target_pairs={{8,0},{16,8},{24,16},{9,1},{17,9},{25,17},{10,2},{18,10},{26,18},{... | collective-permute-start | bytes 454664 | tf_op jit(solution)/shard_map/ppermute | solution.py:509
  8.5 0.0 copy-done.2
  8.5 0.0 copy-done
  8.5 0.0 copy-done.1
  8.5 2.6 %pack_faces.1 = (bf16[576,128]{1,0:T(8,128)(2,1)S(1)}, bf16[576,128]{1,0:T(8,128)(2,1)S(1)}, bf16[4,64,128]{2,1,0:T(8,128)(2,1)S(1)}) custom-call(f32[4,64,64,128]{3,2,1,0:T(8,128)S(1)} %copy-done, bf16[4,64,64,128]{3,2,1,0:T(8,128)(2,1)S(1)} %copy-done.1, s32[64,64,128]{2,1,0:T(8,128)S(1)} %copy-done.2), custom_call_target="tpu_custom_call" | custom-call | flops 8388608 | bytes 8388608 | tf_op jit(solution)/shard_map/pack_faces/pallas_call | solution.py:494
  11.1 0.0 copy-start.3
  11.1 2.1 %inside.2 = (f32[4,32,64,128]{3,2,1,0:T(8,128)S(1)}, f32[8,128]{1,0:T(8,128)S(1)}) custom-call(f32[4,64,64,128]{3,2,1,0:T(8,128)S(1)} %copy-done, bf16[4,64,64,128]{3,2,1,0:T(8,128)(2,1)S(1)} %copy-done.1), custom_call_target="tpu_custom_call" | custom-call | flops 10485760 | bytes 10485760 | tf_op jit(solution)/shard_map/inside/pallas_call | solution.py:494
  13.2 0.0 collective-permute-done.xl_ref.refs_7_
  13.2 2.5 %collective-permute-done.1.xr_ref.refs_8_ = bf16[592,128]{1,0:T(8,128)(2,1)S(1)} collective-permute-done((bf16[592,128]{1,0:T(8,128)(2,1)S(1)}, bf16[592,128]{1,0:T(8,128)(2,1)S(1)}, u32[]{:S(2)}, u32[]{:S(2)}) %collective-permute-start.1) | collective-permute-done | bytes 151584 | tf_op jit(solution)/shard_map/ppermute | solution.py:509
  15.7 0.0 copy-done.3
  15.7 0.1 corners.1
  15.8 1.3 %collective-permute-start.3 = (bf16[720,128]{1,0:T(8,128)(2,1)S(1)}, bf16[720,128]{1,0:T(8,128)(2,1)S(1)}, u32[]{:S(2)}, u32[]{:S(2)}) collective-permute-start(bf16[720,128]{1,0:T(8,128)(2,1)S(1)} %get-tuple-element.25.refs_11_.refs_8_), channel_id=1, source_target_pairs={{2,0},{4,2},{6,4},{3,1},{5,3},{7,5},{10,8},{12,10},{14,12},{11,9},... | collective-permute-start | bytes 552968 | tf_op jit(solution)/shard_map/ppermute | solution.py:509
  17.1 0.0 copy-start.4
  17.1 0.0 copy-start.5
  17.1 4.6 %collective-permute-start.2 = (bf16[720,128]{1,0:T(8,128)(2,1)S(1)}, bf16[720,128]{1,0:T(8,128)(2,1)S(1)}, u32[]{:S(2)}, u32[]{:S(2)}) collective-permute-start(bf16[720,128]{1,0:T(8,128)(2,1)S(1)} %get-tuple-element.24.refs_12_), channel_id=1, source_target_pairs={{0,2},{2,4},{4,6},{1,3},{3,5},{5,7},{8,10},{10,12},{12,14},{9,11},... | collective-permute-start | bytes 552968 | tf_op jit(solution)/shard_map/ppermute | solution.py:509
  21.7 2.1 %inside.3 = (f32[4,32,64,128]{3,2,1,0:T(8,128)S(1)}, f32[8,128]{1,0:T(8,128)S(1)}) custom-call(f32[4,64,64,128]{3,2,1,0:T(8,128)S(1)} %copy-done, bf16[4,64,64,128]{3,2,1,0:T(8,128)(2,1)S(1)} %copy-done.1), custom_call_target="tpu_custom_call" | custom-call | flops 10485760 | bytes 10485760 | tf_op jit(solution)/shard_map/inside/pallas_call | solution.py:494
  23.7 0.0 collective-permute-done.3.yr_ref.refs_10_
  23.8 0.9 %collective-permute-done.2.yl_ref.refs_9_ = bf16[720,128]{1,0:T(8,128)(2,1)S(1)} collective-permute-done((bf16[720,128]{1,0:T(8,128)(2,1)S(1)}, bf16[720,128]{1,0:T(8,128)(2,1)S(1)}, u32[]{:S(2)}, u32[]{:S(2)}) %collective-permute-start.2) | collective-permute-done | bytes 184352 | tf_op jit(solution)/shard_map/ppermute | solution.py:509
  24.7 0.2 edge_faces.1
  24.9 0.1 collective-permute-start.4
  25.0 1.3 %collective-permute-done.4.refs_5_.refs_6_ = bf16[8,64,128]{2,1,0:T(8,128)(2,1)S(1)} collective-permute-done((bf16[8,64,128]{2,1,0:T(8,128)(2,1)S(1)}, bf16[8,64,128]{2,1,0:T(8,128)(2,1)S(1)}, u32[]{:S(2)}, u32[]{:S(2)}) %collective-permute-start.4) | collective-permute-done | bytes 131104 | tf_op jit(solution)/shard_map/ppermute | solution.py:514
  26.3 0.0 copy-done.4
  26.3 0.0 copy-done.5
  26.3 0.0 copy-start.7
  26.3 0.0 copy-start.6
  26.3 6.0 %sweep_first.1 = (f32[4,64,64,128]{3,2,1,0:T(8,128)S(1)}, f32[1024,128]{1,0:T(8,128)S(1)}, bf16[4,64,128]{2,1,0:T(8,128)(2,1)S(1)}) custom-call(f32[4]{0:T(128)S(1)} %copy-done.4, f32[4]{0:T(128)S(1)} %copy-done.5, f32[4,64,64,128]{3,2,1,0:T(8,128)S(1)} %copy-done, f32[64,64]{1,0:T(8,128)S(1)} %copy-done.3, s32[64,64,128]{2,1,0:T(8,128)S(1)} %copy-done.2, ...), custom_call_target="tpu_custom_call" | custom-call | flops 41943040 | bytes 41943040 | tf_op jit(solution)/shard_map/sweep_first/pallas_call | solution.py:494
  32.4 0.2 collective-permute-start.5
  32.6 1.1 %collective-permute-done.5.refs_5_.refs_6_ = bf16[4,64,128]{2,1,0:T(8,128)(2,1)S(1)} collective-permute-done((bf16[4,64,128]{2,1,0:T(8,128)(2,1)S(1)}, bf16[4,64,128]{2,1,0:T(8,128)(2,1)S(1)}, u32[]{:S(2)}, u32[]{:S(2)}) %collective-permute-start.5) | collective-permute-done | bytes 65568 | tf_op jit(solution)/shard_map/ppermute | solution.py:514
  33.7 0.0 copy-done.7
  33.7 0.0 copy-done.6
  33.7 9.6 %sweep_last.1 = (f32[4,64,64,128]{3,2,1,0:T(8,128)}, f32[40,128]{1,0:T(8,128)S(1)}) custom-call(f32[4]{0:T(128)S(1)} %copy-done.4, f32[4]{0:T(128)S(1)} %copy-done.5, f32[4,64,64,128]{3,2,1,0:T(8,128)S(1)} %get-tuple-element.29.refs_2_, bf16[4,64,64,128]{3,2,1,0:T(8,128)(2,1)S(1)} %copy-done.1, s32[64,64,128]{2,1,0:T(8,128)S(1)} %copy-done.2, ...), custom_call_target="tpu_custom_call" | custom-call | flops 41943040 | bytes 41943040 | tf_op jit(solution)/shard_map/sweep_last/pallas_call | solution.py:494
  43.3 0.2 collective-permute-start.6
  43.5 1.0 %collective-permute-done.6.refs_1_ = f32[40,128]{1,0:T(8,128)S(1)} collective-permute-done((f32[40,128]{1,0:T(8,128)S(1)}, f32[40,128]{1,0:T(8,128)S(1)}, u32[]{:S(2)}, u32[]{:S(2)}) %collective-permute-start.6) | collective-permute-done | bytes 20512 | tf_op jit(solution)/shard_map/ppermute | solution.py:514
  44.5 0.7 %share.1 = s16[16,40,128]{2,1,0:T(8,128)(2,1)} custom-call(f32[40,128]{1,0:T(8,128)S(1)} %get-tuple-element.33.refs_0_, f32[40,128]{1,0:T(8,128)S(1)} %collective-permute-done.6.refs_1_), custom_call_target="tpu_custom_call" | custom-call | flops 81920 | bytes 81920 | tf_op jit(solution)/shard_map/share/pallas_call | solution.py:494
  45.2 6.8 %all-to-all-start = ((s16[16,40,128]{2,1,0:T(8,128)(2,1)}), s16[16,40,128]{2,1,0:T(8,128)(2,1)S(1)}, u32[]{:S(2)}, u32[]{:S(2)}) async-start(s16[16,40,128]{2,1,0:T(8,128)(2,1)} %share.1), calls=%async_computation | async-start | bytes 327680 | tf_op jit(solution)/shard_map/all_to_all | solution.py:760
  52.1 8.7 %all-to-all-done.got_ref = s16[16,40,128]{2,1,0:T(8,128)(2,1)S(1)} async-done(((s16[16,40,128]{2,1,0:T(8,128)(2,1)}), s16[16,40,128]{2,1,0:T(8,128)(2,1)S(1)}, u32[]{:S(2)}, u32[]{:S(2)}) %all-to-all-start) | async-done | bytes 163872 | tf_op jit(solution)/shard_map/all_to_all | solution.py:760
  60.8 2.3 %plane.1 = f32[1,16,512]{2,1,0:T(8,128)} custom-call(s32[1]{0:T(128)} %bitcast.1.me_ref, s16[16,40,128]{2,1,0:T(8,128)(2,1)S(1)} %all-to-all-done.got_ref), custom_call_target="tpu_custom_call" | custom-call | tf_op jit(solution)/shard_map/plane/pallas_call | solution.py:762
  (1 shorter events, 0.0 us)
Async XLA Ops:
  0.6 7.9 %copy-start.2 = (s32[64,64,128]{2,1,0:T(8,128)S(1)}, s32[64,64,128]{2,1,0:T(8,128)}, u32[]{:S(2)}) copy-start(s32[64,64,128]{2,1,0:T(8,128)} %refs_4_.3) | copy-start | bytes 6291460
  0.6 7.9 %copy-start = (f32[4,64,64,128]{3,2,1,0:T(8,128)S(1)}, f32[4,64,64,128]{3,2,1,0:T(8,128)}, u32[]{:S(2)}) copy-start(f32[4,64,64,128]{3,2,1,0:T(8,128)} %refs_2_.1) | copy-start | bytes 25165828
  0.6 7.9 %copy-start.1 = (bf16[4,64,64,128]{3,2,1,0:T(8,128)(2,1)S(1)}, bf16[4,64,64,128]{3,2,1,0:T(8,128)(2,1)}, u32[]{:S(2)}) copy-start(bf16[4,64,64,128]{3,2,1,0:T(8,128)(2,1)} %refs_3_.3) | copy-start | bytes 12582916
  2.1 11.2 %collective-permute-start = (bf16[592,128]{1,0:T(8,128)(2,1)S(1)}, bf16[592,128]{1,0:T(8,128)(2,1)S(1)}, u32[]{:S(2)}, u32[]{:S(2)}) collective-permute-start(bf16[592,128]{1,0:T(8,128)(2,1)S(1)} %get-tuple-element.19), channel_id=1, source_target_pairs={{0,8},{8,16},{16,24},{1,9},{9,17},{17,25},{2,10},{10,18},{18,26},{... | collective-permute-start | bytes 454664 | tf_op jit(solution)/shard_map/ppermute | solution.py:509
  7.2 8.5 %collective-permute-start.1 = (bf16[592,128]{1,0:T(8,128)(2,1)S(1)}, bf16[592,128]{1,0:T(8,128)(2,1)S(1)}, u32[]{:S(2)}, u32[]{:S(2)}) collective-permute-start(bf16[592,128]{1,0:T(8,128)(2,1)S(1)} %get-tuple-element.20), channel_id=1, source_target_pairs={{8,0},{16,8},{24,16},{9,1},{17,9},{25,17},{10,2},{18,10},{26,18},{... | collective-permute-start | bytes 454664 | tf_op jit(solution)/shard_map/ppermute | solution.py:509
  11.1 4.6 %copy-start.3 = (f32[64,64]{1,0:T(8,128)S(1)}, f32[64,64]{1,0:T(8,128)}, u32[]{:S(2)}) copy-start(f32[64,64]{1,0:T(8,128)} %refs_3_.2) | copy-start | bytes 49156
  15.8 8.0 %collective-permute-start.3 = (bf16[720,128]{1,0:T(8,128)(2,1)S(1)}, bf16[720,128]{1,0:T(8,128)(2,1)S(1)}, u32[]{:S(2)}, u32[]{:S(2)}) collective-permute-start(bf16[720,128]{1,0:T(8,128)(2,1)S(1)} %get-tuple-element.25.refs_11_.refs_8_), channel_id=1, source_target_pairs={{2,0},{4,2},{6,4},{3,1},{5,3},{7,5},{10,8},{12,10},{14,12},{11,9},... | collective-permute-start | bytes 552968 | tf_op jit(solution)/shard_map/ppermute | solution.py:509
  17.1 9.3 %copy-start.4 = (f32[4]{0:T(128)S(1)}, f32[4]{0:T(128)}, u32[]{:S(2)}) copy-start(f32[4]{0:T(128)} %refs_0_.3) | copy-start | bytes 52
  17.1 9.3 %copy-start.5 = (f32[4]{0:T(128)S(1)}, f32[4]{0:T(128)}, u32[]{:S(2)}) copy-start(f32[4]{0:T(128)} %refs_1_.3) | copy-start | bytes 52
  17.1 7.6 %collective-permute-start.2 = (bf16[720,128]{1,0:T(8,128)(2,1)S(1)}, bf16[720,128]{1,0:T(8,128)(2,1)S(1)}, u32[]{:S(2)}, u32[]{:S(2)}) collective-permute-start(bf16[720,128]{1,0:T(8,128)(2,1)S(1)} %get-tuple-element.24.refs_12_), channel_id=1, source_target_pairs={{0,2},{2,4},{4,6},{1,3},{3,5},{5,7},{8,10},{10,12},{12,14},{9,11},... | collective-permute-start | bytes 552968 | tf_op jit(solution)/shard_map/ppermute | solution.py:509
  24.9 1.4 %collective-permute-start.4 = (bf16[8,64,128]{2,1,0:T(8,128)(2,1)S(1)}, bf16[8,64,128]{2,1,0:T(8,128)(2,1)S(1)}, u32[]{:S(2)}, u32[]{:S(2)}) collective-permute-start(bf16[8,64,128]{2,1,0:T(8,128)(2,1)S(1)} %edge_faces.1), channel_id=1, source_target_pairs={{0,1},{1,0},{2,3},{3,2},{4,5},{5,4},{6,7},{7,6},{8,9},{9,8},{10,11... | collective-permute-start | bytes 393224 | tf_op jit(solution)/shard_map/ppermute | solution.py:514
  26.3 7.4 %copy-start.7 = (s32[1,1,64,1]{2,3,1,0:T(1,128)S(1)}, s32[1,1,64,1]{2,3,1,0:T(1,128)}, u32[]{:S(2)}) copy-start(s32[1,1,64,1]{2,3,1,0:T(1,128)} %param.15) | copy-start | bytes 772
  26.3 7.4 %copy-start.6 = (f32[4]{0:T(128)S(1)}, f32[4]{0:T(128)}, u32[]{:S(2)}) copy-start(f32[4]{0:T(128)} %refs_11_.1) | copy-start | bytes 52
  32.4 1.3 %collective-permute-start.5 = (bf16[4,64,128]{2,1,0:T(8,128)(2,1)S(1)}, bf16[4,64,128]{2,1,0:T(8,128)(2,1)S(1)}, u32[]{:S(2)}, u32[]{:S(2)}) collective-permute-start(bf16[4,64,128]{2,1,0:T(8,128)(2,1)S(1)} %get-tuple-element.30), channel_id=1, source_target_pairs={{0,1},{1,0},{2,3},{3,2},{4,5},{5,4},{6,7},{7,6},{8,9},{9,8},{10,11... | collective-permute-start | bytes 196616 | tf_op jit(solution)/shard_map/ppermute | solution.py:514
  43.3 1.3 %collective-permute-start.6 = (f32[40,128]{1,0:T(8,128)S(1)}, f32[40,128]{1,0:T(8,128)S(1)}, u32[]{:S(2)}, u32[]{:S(2)}) collective-permute-start(f32[40,128]{1,0:T(8,128)S(1)} %get-tuple-element.33.refs_0_), channel_id=1, source_target_pairs={{0,1},{1,0},{2,3},{3,2},{4,5},{5,4},{6,7},{7,6},{8,9},{9,8},{10,11... | collective-permute-start | bytes 61448 | tf_op jit(solution)/shard_map/ppermute | solution.py:514
  45.2 15.5 %all-to-all-start = ((s16[16,40,128]{2,1,0:T(8,128)(2,1)}), s16[16,40,128]{2,1,0:T(8,128)(2,1)S(1)}, u32[]{:S(2)}, u32[]{:S(2)}) async-start(s16[16,40,128]{2,1,0:T(8,128)(2,1)} %share.1), calls=%async_computation | async-start | bytes 327680 | tf_op jit(solution)/shard_map/all_to_all | solution.py:760
